TPU v7x, 32 devices: a whole 2x2x4 slice. The times are simulated.
32 devices in a mesh: seq: 16 (over z, y, x), batch: 2 (over core).
Axes of the slice: x: 2, y: 2, z: 4, core: 2. Of those that a mesh axis runs over, the one named last changes fastest.
Arguments:
- tokens: bfloat16 [2, 2048, 768], P('batch', 'seq'), may hold values from -6 to 6
- cotangent: bfloat16 [2, 2048, 768], P('batch', 'seq'), may hold values from -6 to 6
- prefix_len: int32 [2], P('batch'), may hold values from 204 to 1024
- gain_one: bfloat16 [768], P(('seq', 'batch')), may hold values from 0.25 to 1.75
- shift_one: bfloat16 [768], P(('seq', 'batch')), may hold values from -1.75 to 1.75
- w_query: bfloat16 [768, 768], P(('seq', 'batch')), may hold values from -0.21875 to 0.21875
- b_query: bfloat16 [768], P(('seq', 'batch')), may hold values from -3 to 3
- w_key: bfloat16 [768, 768], P(('seq', 'batch')), may hold values from -0.21875 to 0.21875
- w_value: bfloat16 [768, 768], P(('seq', 'batch')), may hold values from -0.21875 to 0.21875
- b_value: bfloat16 [768], P(('seq', 'batch')), may hold values from -3 to 3
- w_output: bfloat16 [768, 768], P(('seq', 'batch')), may hold values from -3.5 to 3.5
- b_output: bfloat16 [768], P(('seq', 'batch')), may hold values from -1.75 to 1.75
- gain_two: bfloat16 [768], P(('seq', 'batch')), may hold values from 0.25 to 1.75
- shift_two: bfloat16 [768], P(('seq', 'batch')), may hold values from -1.75 to 1.75
- w_up: bfloat16 [768, 3072], P(('seq', 'batch')), may hold values from -0.21875 to 0.21875
- b_up: bfloat16 [3072], P(('seq', 'batch')), may hold values from -3 to 3
- w_down: bfloat16 [3072, 768], P(('seq', 'batch')), may hold values from -0.109375 to 0.109375
- b_down: bfloat16 [768], P(('seq', 'batch')), may hold values from -1.75 to 1.75
Outputs:
- layer_out: bfloat16 [2, 2048, 768], P('batch', 'seq')
- grad_tokens: float32 [2, 2048, 768], P('batch', 'seq')
- grad_gain_one: float32 [768], P(('seq', 'batch'))
- grad_shift_one: float32 [768], P(('seq', 'batch'))
- grad_w_query: float32 [768, 768], P(('seq', 'batch'))
- grad_b_query: float32 [768], P(('seq', 'batch'))
- grad_w_key: float32 [768, 768], P(('seq', 'batch'))
- grad_w_value: float32 [768, 768], P(('seq', 'batch'))
- grad_b_value: float32 [768], P(('seq', 'batch'))
- grad_w_output: float32 [768, 768], P(('seq', 'batch'))
- grad_b_output: float32 [768], P(('seq', 'batch'))
- grad_gain_two: float32 [768], P(('seq', 'batch'))
- grad_shift_two: float32 [768], P(('seq', 'batch'))
- grad_w_up: float32 [768, 3072], P(('seq', 'batch'))
- grad_b_up: float32 [3072], P(('seq', 'batch'))
- grad_w_down: float32 [3072, 768], P(('seq', 'batch'))
- grad_b_down: float32 [768], P(('seq', 'batch'))
Inputs may be any that keep to these rules, and one draw needn't show every extreme that they name: `prefix_len`: one prefix length per sequence.
All inputs are finite; a program needn't handle non-finite values.
Results may differ from a plain program's by a relative error of at most 0.014.
Values may be sent and summed in bfloat16 or wider, within the bound.
No kernel may reach another device: no remote copies, remote signals or barrier semaphores. Data moves between devices by JAX's collectives and lax.ppermute only.
A program may use at most 192 MiB of HBM per device.

v0:
```python
import jax
import jax.numpy as jnp
from jax import lax
from jax.sharding import PartitionSpec as P

HD = 64


EPS = 1e-05


def normalize(values):
    centre = jnp.mean(values, axis=-1, keepdims=True)
    centred = values - centre
    spread = jnp.mean(centred * centred, axis=-1, keepdims=True)
    factor = lax.rsqrt(spread + EPS)
    return (centred * factor, factor)


def norm_backward(grad_out, normed, factor, gain):
    grad_gain = jnp.sum(grad_out * normed, axis=0)
    grad_shift = jnp.sum(grad_out, axis=0)
    scaled = grad_out * gain.astype(jnp.float32)
    grad_in = factor * (
        scaled
        - jnp.mean(scaled, axis=-1, keepdims=True)
        - normed * jnp.mean(scaled * normed, axis=-1, keepdims=True)
    )
    return (grad_in, grad_gain, grad_shift)


def over_rows(left, right):
    return lax.dot_general(
        left, right, (((0,), (0,)), ((), ())), preferred_element_type=jnp.float32
    )


def over_cols(left, right):
    return lax.dot_general(
        left, right, (((1,), (1,)), ((), ())), preferred_element_type=jnp.float32
    )


def pair_scores(q_part, k_part, row_ids, col_ids, prefix):
    scores = jnp.einsum("qhd,khd->hqk", q_part, k_part, preferred_element_type=jnp.float32) * 0.125
    allowed = (col_ids[None, :] <= row_ids[:, None]) | (col_ids[None, :] < prefix)
    return (jnp.where(allowed[None], scores, -1e30), allowed)


def grad_terms(q_part, do_part, lse_part, delta_part, k_part, v_part, row_ids, col_ids, prefix):
    scores, allowed = pair_scores(q_part, k_part, row_ids, col_ids, prefix)
    attn_prob = jnp.where(allowed[None], jnp.exp(scores - lse_part[:, :, None]), 0.0)
    prob_low = attn_prob.astype(jnp.bfloat16)
    d_prob = jnp.einsum("qhd,khd->hqk", do_part, v_part, preferred_element_type=jnp.float32)
    d_score = (attn_prob * (d_prob - delta_part[:, :, None])).astype(jnp.bfloat16)
    return (prob_low, d_score)


def body(
    tokens,
    cotangent,
    prefix_len,
    gain_one,
    shift_one,
    w_query,
    b_query,
    w_key,
    w_value,
    b_value,
    w_output,
    b_output,
    gain_two,
    shift_two,
    w_up,
    b_up,
    w_down,
    b_down,
):
    shards = (
        gain_one,
        shift_one,
        w_query,
        b_query,
        w_key,
        w_value,
        b_value,
        w_output,
        b_output,
        gain_two,
        shift_two,
        w_up,
        b_up,
        w_down,
        b_down,
    )
    gathered = (
        lax.all_gather(shards[0], ("seq", "batch"), axis=0, tiled=True),
        lax.all_gather(shards[1], ("seq", "batch"), axis=0, tiled=True),
        lax.all_gather(shards[2], ("seq", "batch"), axis=0, tiled=True),
        lax.all_gather(shards[3], ("seq", "batch"), axis=0, tiled=True),
        lax.all_gather(shards[4], ("seq", "batch"), axis=0, tiled=True),
        lax.all_gather(shards[5], ("seq", "batch"), axis=0, tiled=True),
        lax.all_gather(shards[6], ("seq", "batch"), axis=0, tiled=True),
        lax.all_gather(shards[7], ("seq", "batch"), axis=0, tiled=True),
        lax.all_gather(shards[8], ("seq", "batch"), axis=0, tiled=True),
        lax.all_gather(shards[9], ("seq", "batch"), axis=0, tiled=True),
        lax.all_gather(shards[10], ("seq", "batch"), axis=0, tiled=True),
        lax.all_gather(shards[11], ("seq", "batch"), axis=0, tiled=True),
        lax.all_gather(shards[12], ("seq", "batch"), axis=0, tiled=True),
        lax.all_gather(shards[13], ("seq", "batch"), axis=0, tiled=True),
        lax.all_gather(shards[14], ("seq", "batch"), axis=0, tiled=True),
    )
    (
        ga_full,
        sa_full,
        wq_full,
        bq_full,
        wk_full,
        wv_full,
        bv_full,
        wo_full,
        bo_full,
        gb_full,
        sb_full,
        wu_full,
        bu_full,
        wd_full,
        bd_full,
    ) = gathered
    hidden = tokens[0].astype(jnp.float32)
    local_rows = hidden.shape[0]
    width = hidden.shape[1]
    heads = width // HD
    prefix = prefix_len[0]
    start_row = lax.axis_index("seq") * local_rows
    last_row = start_row + local_rows - 1
    length = local_rows * lax.axis_size("seq")
    block_rows = min(512, length)
    block_count = length // block_rows
    row_ids = start_row + jnp.arange(local_rows, dtype=jnp.int32)
    block_ids = jnp.arange(block_count, dtype=jnp.int32)
    normed_one, factor_one = normalize(hidden)
    norm_one = (normed_one * ga_full.astype(jnp.float32) + sa_full.astype(jnp.float32)).astype(
        jnp.bfloat16
    )
    q_low = (
        jnp.dot(norm_one, wq_full, preferred_element_type=jnp.float32) + bq_full.astype(jnp.float32)
    ).astype(jnp.bfloat16)
    k_low = jnp.dot(norm_one, wk_full, preferred_element_type=jnp.float32).astype(jnp.bfloat16)
    v_low = (
        jnp.dot(norm_one, wv_full, preferred_element_type=jnp.float32) + bv_full.astype(jnp.float32)
    ).astype(jnp.bfloat16)
    k_all, v_all = (
        lax.all_gather(k_low, "seq", axis=0, tiled=True),
        lax.all_gather(v_low, "seq", axis=0, tiled=True),
    )
    q_heads = q_low.reshape(local_rows, heads, HD)

    def lse_step(state, item):
        k_part, index = item
        col_ids = index * block_rows + jnp.arange(block_rows, dtype=jnp.int32)

        def lse_update(current):
            scores, allowed = pair_scores(q_heads, k_part, row_ids, col_ids, prefix)
            new_top = jnp.maximum(current[0], jnp.max(scores, axis=-1))
            total = current[1] * jnp.exp(current[0] - new_top) + jnp.sum(
                jnp.exp(scores - new_top[:, :, None]), axis=-1
            )
            return (new_top, total)

        needed = (index * block_rows <= last_row) | (index * block_rows < prefix)
        return (lax.cond(needed, lse_update, lambda current: current, state), None)

    k_blocks = k_all.reshape(block_count, block_rows, heads, HD)
    v_blocks = v_all.reshape(block_count, block_rows, heads, HD)
    lse_start = (
        jnp.full((heads, local_rows), -1e30, jnp.float32),
        jnp.zeros((heads, local_rows), jnp.float32),
    )
    (top_all, total_all), _ = lax.scan(lse_step, lse_start, (k_blocks, block_ids))
    lse = top_all + jnp.log(total_all)

    def out_step(acc, item):
        k_part, v_part, index = item
        col_ids = index * block_rows + jnp.arange(block_rows, dtype=jnp.int32)

        def out_update(current):
            scores, allowed = pair_scores(q_heads, k_part, row_ids, col_ids, prefix)
            attn_prob = jnp.where(allowed[None], jnp.exp(scores - lse[:, :, None]), 0.0).astype(
                jnp.bfloat16
            )
            return current + jnp.einsum(
                "hqk,khd->qhd", attn_prob, v_part, preferred_element_type=jnp.float32
            )

        needed = (index * block_rows <= last_row) | (index * block_rows < prefix)
        return (lax.cond(needed, out_update, lambda current: current, acc), None)

    ctx_acc, _ = lax.scan(
        out_step, jnp.zeros((local_rows, heads, HD), jnp.float32), (k_blocks, v_blocks, block_ids)
    )
    ctx_low = ctx_acc.reshape(local_rows, width).astype(jnp.bfloat16)
    middle = (
        hidden
        + jnp.dot(ctx_low, wo_full, preferred_element_type=jnp.float32)
        + bo_full.astype(jnp.float32)
    )
    normed_two, factor_two = normalize(middle)
    norm_two = (normed_two * gb_full.astype(jnp.float32) + sb_full.astype(jnp.float32)).astype(
        jnp.bfloat16
    )
    pre_act = jnp.dot(norm_two, wu_full, preferred_element_type=jnp.float32) + bu_full.astype(
        jnp.float32
    )
    cdf_part = 0.5 * (1.0 + jax.scipy.special.erf(pre_act * 0.7071067811865476))
    act_low = (pre_act * cdf_part).astype(jnp.bfloat16)
    layer_out = (
        middle
        + jnp.dot(act_low, wd_full, preferred_element_type=jnp.float32)
        + bd_full.astype(jnp.float32)
    ).astype(jnp.bfloat16)
    regathered = (
        lax.all_gather(shards[0], ("seq", "batch"), axis=0, tiled=True),
        lax.all_gather(shards[1], ("seq", "batch"), axis=0, tiled=True),
        lax.all_gather(shards[2], ("seq", "batch"), axis=0, tiled=True),
        lax.all_gather(shards[3], ("seq", "batch"), axis=0, tiled=True),
        lax.all_gather(shards[4], ("seq", "batch"), axis=0, tiled=True),
        lax.all_gather(shards[5], ("seq", "batch"), axis=0, tiled=True),
        lax.all_gather(shards[6], ("seq", "batch"), axis=0, tiled=True),
        lax.all_gather(shards[7], ("seq", "batch"), axis=0, tiled=True),
        lax.all_gather(shards[8], ("seq", "batch"), axis=0, tiled=True),
        lax.all_gather(shards[9], ("seq", "batch"), axis=0, tiled=True),
        lax.all_gather(shards[10], ("seq", "batch"), axis=0, tiled=True),
        lax.all_gather(shards[11], ("seq", "batch"), axis=0, tiled=True),
        lax.all_gather(shards[12], ("seq", "batch"), axis=0, tiled=True),
        lax.all_gather(shards[13], ("seq", "batch"), axis=0, tiled=True),
        lax.all_gather(shards[14], ("seq", "batch"), axis=0, tiled=True),
    )
    (
        ga_back,
        sa_back,
        wq_back,
        bq_back,
        wk_back,
        wv_back,
        bv_back,
        wo_back,
        bo_back,
        gb_back,
        sb_back,
        wu_back,
        bu_back,
        wd_back,
        bd_back,
    ) = regathered
    d_out = cotangent[0]
    grad_wd = over_rows(act_low, d_out)
    grad_bd = jnp.sum(d_out.astype(jnp.float32), axis=0)
    d_act = over_cols(d_out, wd_back)
    slope = cdf_part + pre_act * jnp.exp(-0.5 * pre_act * pre_act) * 0.3989422804014327
    d_pre = (d_act * slope).astype(jnp.bfloat16)
    grad_wu = over_rows(norm_two, d_pre)
    grad_bu = jnp.sum(d_pre.astype(jnp.float32), axis=0)
    d_norm_two = over_cols(d_pre, wu_back)
    d_mid_norm, grad_gb, grad_sb = norm_backward(d_norm_two, normed_two, factor_two, gb_back)
    d_middle = d_out.astype(jnp.float32) + d_mid_norm
    d_branch = d_middle.astype(jnp.bfloat16)
    grad_wo = over_rows(ctx_low, d_branch)
    grad_bo = jnp.sum(d_branch.astype(jnp.float32), axis=0)
    d_ctx = over_cols(d_branch, wo_back).astype(jnp.bfloat16)
    do_heads = d_ctx.reshape(local_rows, heads, HD)
    delta = jnp.sum(d_ctx.astype(jnp.float32).reshape(local_rows, heads, HD) * ctx_acc, axis=-1).T
    k_back, v_back = (k_blocks, v_blocks)
    zero_heads = jnp.zeros((local_rows, heads, HD), jnp.float32)

    def grad_step(acc, item):
        k_part, v_part, index = item
        col_ids = index * block_rows + jnp.arange(block_rows, dtype=jnp.int32)

        def work(current):
            prob_low, d_score = grad_terms(
                q_heads, do_heads, lse, delta, k_part, v_part, row_ids, col_ids, prefix
            )
            current = current + 0.125 * jnp.einsum(
                "hqk,khd->qhd", d_score, k_part, preferred_element_type=jnp.float32
            )
            d_key = 0.125 * jnp.einsum(
                "hqk,qhd->khd", d_score, q_heads, preferred_element_type=jnp.float32
            )
            d_value = jnp.einsum(
                "hqk,qhd->khd", prob_low, do_heads, preferred_element_type=jnp.float32
            )
            return (current, (d_key, d_value))

        def skip(current):
            empty = jnp.zeros((block_rows, heads, HD), jnp.float32)
            return (current, (empty, empty))

        needed = (index * block_rows <= last_row) | (index * block_rows < prefix)
        return lax.cond(needed, work, skip, acc)

    dq_acc, (dk_blocks, dv_blocks) = lax.scan(grad_step, zero_heads, (k_back, v_back, block_ids))
    dk_local, dv_local = (
        lax.psum_scatter(
            dk_blocks.reshape(length, width).astype(jnp.bfloat16),
            "seq",
            scatter_dimension=0,
            tiled=True,
        ).astype(jnp.float32),
        lax.psum_scatter(
            dv_blocks.reshape(length, width).astype(jnp.bfloat16),
            "seq",
            scatter_dimension=0,
            tiled=True,
        ).astype(jnp.float32),
    )
    dq_low = dq_acc.reshape(local_rows, width).astype(jnp.bfloat16)
    dk_low = dk_local.astype(jnp.bfloat16)
    dv_low = dv_local.astype(jnp.bfloat16)
    grad_wq = over_rows(norm_one, dq_low)
    grad_bq = jnp.sum(dq_low.astype(jnp.float32), axis=0)
    grad_wk = over_rows(norm_one, dk_low)
    grad_wv = over_rows(norm_one, dv_low)
    grad_bv = jnp.sum(dv_low.astype(jnp.float32), axis=0)
    d_norm_one = (
        over_cols(dq_low, wq_back) + over_cols(dk_low, wk_back) + over_cols(dv_low, wv_back)
    )
    d_in_norm, grad_ga, grad_sa = norm_backward(d_norm_one, normed_one, factor_one, ga_back)
    grad_tokens = d_middle + d_in_norm
    summed = (
        lax.psum_scatter(grad_ga, ("seq", "batch"), scatter_dimension=0, tiled=True),
        lax.psum_scatter(grad_sa, ("seq", "batch"), scatter_dimension=0, tiled=True),
        lax.psum_scatter(grad_wq, ("seq", "batch"), scatter_dimension=0, tiled=True),
        lax.psum_scatter(grad_bq, ("seq", "batch"), scatter_dimension=0, tiled=True),
        lax.psum_scatter(grad_wk, ("seq", "batch"), scatter_dimension=0, tiled=True),
        lax.psum_scatter(grad_wv, ("seq", "batch"), scatter_dimension=0, tiled=True),
        lax.psum_scatter(grad_bv, ("seq", "batch"), scatter_dimension=0, tiled=True),
        lax.psum_scatter(grad_wo, ("seq", "batch"), scatter_dimension=0, tiled=True),
        lax.psum_scatter(grad_bo, ("seq", "batch"), scatter_dimension=0, tiled=True),
        lax.psum_scatter(grad_gb, ("seq", "batch"), scatter_dimension=0, tiled=True),
        lax.psum_scatter(grad_sb, ("seq", "batch"), scatter_dimension=0, tiled=True),
        lax.psum_scatter(grad_wu, ("seq", "batch"), scatter_dimension=0, tiled=True),
        lax.psum_scatter(grad_bu, ("seq", "batch"), scatter_dimension=0, tiled=True),
        lax.psum_scatter(grad_wd, ("seq", "batch"), scatter_dimension=0, tiled=True),
        lax.psum_scatter(grad_bd, ("seq", "batch"), scatter_dimension=0, tiled=True),
    )
    return (
        layer_out[None],
        grad_tokens[None],
        summed[0],
        summed[1],
        summed[2],
        summed[3],
        summed[4],
        summed[5],
        summed[6],
        summed[7],
        summed[8],
        summed[9],
        summed[10],
        summed[11],
        summed[12],
        summed[13],
        summed[14],
    )


def solution(mesh):
    placed = (
        P("batch", "seq", None),
        P("batch", "seq", None),
        P("batch"),
        P(("seq", "batch")),
        P(("seq", "batch")),
        P(("seq", "batch"), None),
        P(("seq", "batch")),
        P(("seq", "batch"), None),
        P(("seq", "batch"), None),
        P(("seq", "batch")),
        P(("seq", "batch"), None),
        P(("seq", "batch")),
        P(("seq", "batch")),
        P(("seq", "batch")),
        P(("seq", "batch"), None),
        P(("seq", "batch")),
        P(("seq", "batch"), None),
        P(("seq", "batch")),
    )
    return jax.shard_map(
        body,
        mesh=mesh,
        in_specs=placed,
        out_specs=(
            P("batch", "seq", None),
            P("batch", "seq", None),
            P(("seq", "batch")),
            P(("seq", "batch")),
            P(("seq", "batch"), None),
            P(("seq", "batch")),
            P(("seq", "batch"), None),
            P(("seq", "batch"), None),
            P(("seq", "batch")),
            P(("seq", "batch"), None),
            P(("seq", "batch")),
            P(("seq", "batch")),
            P(("seq", "batch")),
            P(("seq", "batch"), None),
            P(("seq", "batch")),
            P(("seq", "batch"), None),
            P(("seq", "batch")),
        ),
        check_vma=False,
    )
```

profile of v0, /device:TPU:0, one launch (start us, length us, event | category | flops | bytes accessed | tf_op | source)
XLA Modules:
  0.0 1545.9 jit_solution(5383057277159908306)
XLA Ops:
  17.0 42.6 %all-reduce.19 = (bf16[768]{0:T(1024)(128)(2,1)S(1)}, bf16[768]{0:T(1024)(128)(2,1)S(1)}, bf16[768]{0:T(1024)(128)(2,1)S(1)}, bf16[768]{0:T(1024)(128)(2,1)S(1)}...) all-reduce(bf16[768]{0:T(1024)(128)(2,1)S(1)} %dynamic-update-slice, ...), channel_id=1, replica_groups=mesh['seq'=16,'batch'=2] {'seq','batch'}, use_global_device_ids=true, to_apply=%add.1 | all-reduce | flops 9216 | bytes 36864
  61.9 6.2 all-gather.15.cloned.1.call-done
  70.6 53.2 %all-gather.9.cloned.1.call-done = bf16[768,768]{1,0:T(8,128)(2,1)} async-done(((bf16[24,768]{1,0:T(8,128)(2,1)}), bf16[768,768]{1,0:T(8,128)(2,1)}) %all-gather.9.cloned.1.call-update) | async-done | bytes 1179664 | tf_op jit(solution)/shard_map/all_gather | solution.py:101
  129.8 49.9 %all-gather.13.cloned.1.call-done = bf16[768,768]{1,0:T(8,128)(2,1)} async-done(((bf16[24,768]{1,0:T(8,128)(2,1)}), bf16[768,768]{1,0:T(8,128)(2,1)}) %all-gather.13.cloned.1.call-update) | async-done | bytes 1179664 | tf_op jit(solution)/shard_map/all_gather | solution.py:99
  181.5 68.5 %all-gather.17.cloned.1.call-done = bf16[2048,768]{1,0:T(8,128)(2,1)} async-done(((bf16[128,768]{1,0:T(8,128)(2,1)}), bf16[2048,768]{1,0:T(8,128)(2,1)}) %all-gather.17.cloned.1.call-update) | async-done | bytes 3145744 | tf_op jit(solution)/shard_map/all_gather | solution.py:155
  257.2 4.2 copy.70
  261.4 58.4 %all-gather.11.cloned.1.call-done = bf16[2048,768]{1,0:T(8,128)(2,1)} async-done(((bf16[128,768]{1,0:T(8,128)(2,1)}), bf16[2048,768]{1,0:T(8,128)(2,1)}) %all-gather.11.cloned.1.call-update) | async-done | bytes 3145744 | tf_op jit(solution)/shard_map/all_gather | solution.py:154
  327.1 4.4 copy.69
  331.4 11.3 while.45
  342.8 11.4 while.46
  354.3 20.9 %all-gather.19.cloned.1.call-done = bf16[768,768]{1,0:T(8,128)(2,1)} async-done(((bf16[24,768]{1,0:T(8,128)(2,1)}), bf16[768,768]{1,0:T(8,128)(2,1)}) %all-gather.19.cloned.1.call-update) | async-done | bytes 1179664 | tf_op jit(solution)/shard_map/all_gather | solution.py:104
  377.2 63.5 %all-gather.21.cloned.1.call-done = bf16[768,3072]{1,0:T(8,128)(2,1)} async-done(((bf16[24,3072]{1,0:T(8,128)(2,1)}), bf16[768,3072]{1,0:T(8,128)(2,1)}) %all-gather.21.cloned.1.call-update) | async-done | bytes 4718608 | tf_op jit(solution)/shard_map/all_gather | solution.py:108
  444.0 62.1 %all-gather.23.cloned.1.call-done = bf16[3072,768]{1,0:T(8,128)(2,1)} async-done(((bf16[96,768]{1,0:T(8,128)(2,1)}), bf16[3072,768]{1,0:T(8,128)(2,1)}) %all-gather.23.cloned.1.call-update) | async-done | bytes 4718608 | tf_op jit(solution)/shard_map/all_gather | solution.py:110
  506.1 4.9 convert_reduce_fusion
  515.0 22.2 %while.47 = (s32[]{:T(128)}, f32[128,12,64]{0,2,1:T(8,128)S(1)}, bf16[4,512,12,64]{1,3,2,0:T(8,128)(2,1)}, bf16[4,512,12,64]{1,3,2,0:T(8,128)(2,1)}, s32[4]{0:T(...) while((s32[]{:T(128)}, f32[128,12,64]{0,2,1:T(8,128)S(1)}, ...), condition=%wide.region_20.21_spmd.clone, body=%wide.region_17.20_spmd.clone.sunk | while | flops 513868928 | bytes 23059832 | solution.py:302
  517.2 8.6 conditional.11
  537.3 4.3 copy.75
  544.3 4.7 copy.82
  549.0 4.3 copy.74
  556.1 4.9 copy.80
  566.1 137.8 %reduce-scatter.27.cloned.1.call-done = bf16[128,768]{1,0:T(8,128)(2,1)} async-done(((bf16[2048,768]{1,0:T(8,128)(2,1)}), bf16[128,768]{1,0:T(8,128)(2,1)}) %reduce-scatter.27.cloned.1.call-update) | async-done | bytes 196624
  707.1 131.5 %reduce-scatter.25.cloned.1.call-done = bf16[128,768]{1,0:T(8,128)(2,1)} async-done(((bf16[2048,768]{1,0:T(8,128)(2,1)}), bf16[128,768]{1,0:T(8,128)(2,1)}) %reduce-scatter.25.cloned.1.call-update) | async-done | bytes 196624
  841.6 5.1 fusion.93
  847.3 6.3 fusion.103
  856.2 4.0 fusion.69
  864.5 41.4 %all-reduce.18 = (f32[768]{0:T(1024)S(1)}, f32[768]{0:T(1024)S(1)}, f32[768]{0:T(1024)S(1)}, f32[768]{0:T(1024)S(1)}, f32[768]{0:T(1024)S(1)}, /*index=5*/f32[76...) all-reduce(f32[768]{0:T(1024)S(1)} %get-tuple-element.633, ...), channel_id=4, replica_groups=mesh['seq'=16,'batch'=2] {'seq','batch'}, use_global_device_ids=true, to_apply=%region_26.27.clone | all-reduce | flops 9216 | bytes 73728
  912.0 30.7 %reduce-scatter.19.cloned.1.call-done = f32[24,768]{1,0:T(8,128)} async-done(((f32[768,768]{1,0:T(8,128)}), f32[24,768]{1,0:T(8,128)}) %reduce-scatter.19.cloned.1.call-update) | async-done | bytes 73744 | tf_op jit(solution)/shard_map/reduce_scatter | solution.py:338
  942.7 104.6 %reduce-scatter.13.cloned.1.call-done = f32[24,768]{1,0:T(8,128)} async-done(((f32[768,768]{1,0:T(8,128)}), f32[24,768]{1,0:T(8,128)}) %reduce-scatter.13.cloned.1.call-update) | async-done | bytes 73744 | tf_op jit(solution)/shard_map/reduce_scatter | solution.py:333
  1047.3 103.9 %reduce-scatter.17.cloned.1.call-done = f32[24,768]{1,0:T(8,128)} async-done(((f32[768,768]{1,0:T(8,128)}), f32[24,768]{1,0:T(8,128)}) %reduce-scatter.17.cloned.1.call-update) | async-done | bytes 73744 | tf_op jit(solution)/shard_map/reduce_scatter | solution.py:336
  1151.2 104.7 %reduce-scatter.15.cloned.1.call-done = f32[24,768]{1,0:T(8,128)} async-done(((f32[768,768]{1,0:T(8,128)}), f32[24,768]{1,0:T(8,128)}) %reduce-scatter.15.cloned.1.call-update) | async-done | bytes 73744 | tf_op jit(solution)/shard_map/reduce_scatter | solution.py:335
  1255.9 141.0 %reduce-scatter.23.cloned.1.call-done = f32[96,768]{1,0:T(8,128)} async-done(((f32[3072,768]{1,0:T(8,128)}), f32[96,768]{1,0:T(8,128)}) %reduce-scatter.23.cloned.1.call-update) | async-done | bytes 294928 | tf_op jit(solution)/shard_map/reduce_scatter | solution.py:344
  1396.9 142.0 %reduce-scatter.21.cloned.1.call-done = f32[24,3072]{1,0:T(8,128)} async-done(((f32[768,3072]{1,0:T(8,128)}), f32[24,3072]{1,0:T(8,128)}) %reduce-scatter.21.cloned.1.call-update) | async-done | bytes 294928 | tf_op jit(solution)/shard_map/reduce_scatter | solution.py:342
  (263 shorter events, 111.8 us)
Async XLA Ops:
  7.2 172.5 %copy-start.3 = (bf16[1,128,768]{2,1,0:T(8,128)(2,1)S(1)}, bf16[1,128,768]{2,1,0:T(8,128)(2,1)}, u32[]{:S(2)}) copy-start(bf16[1,128,768]{2,1,0:T(8,128)(2,1)} %param.30) | copy-start | bytes 589828
  7.2 60.9 %all-gather.15.cloned.1.call-start = ((), (), s32[]{:S(2)}) async-start(), calls=%async_computation.11 | async-start | bytes 1216512 | tf_op jit(solution)/shard_map/all_gather | solution.py:102
  7.9 115.9 %all-gather.9.cloned.1.call-start = ((), (), s32[]{:S(2)}) async-start(), calls=%async_computation.8 | async-start | bytes 1216512 | tf_op jit(solution)/shard_map/all_gather | solution.py:101
  8.7 171.0 %all-gather.13.cloned.1.call-start = ((), (), s32[]{:S(2)}) async-start(), calls=%async_computation.10 | async-start | bytes 1216512 | tf_op jit(solution)/shard_map/all_gather | solution.py:99
  9.4 240.6 %all-gather.17.cloned.1.call-start = ((), (), s32[]{:S(2)}) async-start(), calls=%async_computation.12 | async-start | bytes 3342336 | tf_op jit(solution)/shard_map/all_gather | solution.py:155
  60.7 119.0 %copy-start.16 = (f32[128]{0:T(128)}, f32[128]{0:T(128)S(1)}, u32[]{:S(2)}) copy-start(f32[128]{0:T(128)S(1)} %broadcast_multiply_fusion.5) | copy-start | bytes 1540
  61.9 117.8 %copy-start.27 = (f32[128]{0:T(128)}, f32[128]{0:T(128)S(1)}, u32[]{:S(2)}) copy-start(f32[128]{0:T(128)S(1)} %add_rsqrt_fusion.1) | copy-start | bytes 1540
  70.5 249.3 %all-gather.11.cloned.1.call-start = ((), (), s32[]{:S(2)}) async-start(), calls=%async_computation.9 | async-start | bytes 3342336 | tf_op jit(solution)/shard_map/all_gather | solution.py:154
  126.3 249.0 %all-gather.19.cloned.1.call-start = ((), (), s32[]{:S(2)}) async-start(), calls=%async_computation.13 | async-start | bytes 1216512 | tf_op jit(solution)/shard_map/all_gather | solution.py:104
  126.8 313.9 %all-gather.21.cloned.1.call-start = ((), (), s32[]{:S(2)}) async-start(), calls=%async_computation.14 | async-start | bytes 4866048 | tf_op jit(solution)/shard_map/all_gather | solution.py:108
  127.6 378.5 %all-gather.23.cloned.1.call-start = ((), (), s32[]{:S(2)}) async-start(), calls=%async_computation.15 | async-start | bytes 4866048 | tf_op jit(solution)/shard_map/all_gather | solution.py:110
  128.3 575.6 %reduce-scatter.27.cloned.1.call-start = ((), (), s32[]{:S(2)}) async-start(), calls=%async_computation.23 | async-start | bytes 3342336
  342.8 32.4 %copy-start.19 = (f32[768]{0:T(1024)S(1)}, f32[768]{0:T(1024)}, u32[]{:S(2)}) copy-start(f32[768]{0:T(1024)} %convert_element_type.155) | copy-start | bytes 9220
  342.8 97.9 %copy-start.12 = (f32[3072]{0:T(1024)S(1)}, f32[3072]{0:T(1024)}, u32[]{:S(2)}) copy-start(f32[3072]{0:T(1024)} %convert_element_type.159) | copy-start | bytes 36868
  354.3 21.0 %copy-start.31 = (f32[12,128]{1,0:T(8,128)}, f32[12,128]{1,0:T(8,128)S(1)}, u32[]{:S(2)}) copy-start(f32[12,128]{1,0:T(8,128)S(1)} %get-tuple-element.1153) | copy-start | bytes 18436
  354.3 89.6 %copy-start.6 = (bf16[128,12,64]{0,2,1:T(8,128)(2,1)}, bf16[128,12,64]{0,2,1:T(8,128)(2,1)S(1)}, u32[]{:S(2)}) copy-start(bf16[128,12,64]{0,2,1:T(8,128)(2,1)S(1)} %convert_element_type.153) | copy-start | bytes 589828
  377.0 67.0 %copy-start.13 = (f32[128]{0:T(128)}, f32[128]{0:T(128)S(1)}, u32[]{:S(2)}) copy-start(f32[128]{0:T(128)S(1)} %broadcast_multiply_fusion.4) | copy-start | bytes 1540
  377.2 66.8 %copy-start.24 = (f32[128]{0:T(128)}, f32[128]{0:T(128)S(1)}, u32[]{:S(2)}) copy-start(f32[128]{0:T(128)S(1)} %add_rsqrt_fusion) | copy-start | bytes 1540
  443.9 67.1 %copy-start = (f32[128,3072]{1,0:T(8,128)}, f32[128,3072]{1,0:T(8,128)S(1)}, u32[]{:S(2)}) copy-start(f32[128,3072]{1,0:T(8,128)S(1)} %convolution_add_fusion) | copy-start | bytes 4718596
  506.1 4.9 copy-start.14
  506.1 4.9 copy-start.25
  549.0 289.6 %reduce-scatter.25.cloned.1.call-start = ((), (), s32[]{:S(2)}) async-start(), calls=%async_computation.22 | async-start | bytes 3342336
  561.0 381.7 %reduce-scatter.19.cloned.1.call-start = ((), (), s32[]{:S(2)}) async-start(), calls=%async_computation.19 | async-start | bytes 2433024 | tf_op jit(solution)/shard_map/reduce_scatter | solution.py:338
  563.8 483.6 %reduce-scatter.13.cloned.1.call-start = ((), (), s32[]{:S(2)}) async-start(), calls=%async_computation.16 | async-start | bytes 2433024 | tf_op jit(solution)/shard_map/reduce_scatter | solution.py:333
  566.1 585.1 %reduce-scatter.17.cloned.1.call-start = ((), (), s32[]{:S(2)}) async-start(), calls=%async_computation.18 | async-start | bytes 2433024 | tf_op jit(solution)/shard_map/reduce_scatter | solution.py:336
  707.0 134.6 %copy-start.1 = (f32[128,3072]{1,0:T(8,128)S(1)}, f32[128,3072]{1,0:T(8,128)}, u32[]{:S(2)}) copy-start(f32[128,3072]{1,0:T(8,128)} %copy-done) | copy-start | bytes 4718596
  707.0 134.6 %copy-start.10 = (bf16[1,128,768]{2,1,0:T(8,128)(2,1)S(1)}, bf16[1,128,768]{2,1,0:T(8,128)(2,1)}, u32[]{:S(2)}) copy-start(bf16[1,128,768]{2,1,0:T(8,128)(2,1)} %param.31) | copy-start | bytes 589828
  707.0 548.9 %reduce-scatter.15.cloned.1.call-start = ((), (), s32[]{:S(2)}) async-start(), calls=%async_computation.17 | async-start | bytes 2433024 | tf_op jit(solution)/shard_map/reduce_scatter | solution.py:335
  841.5 555.4 %reduce-scatter.23.cloned.1.call-start = ((), (), s32[]{:S(2)}) async-start(), calls=%async_computation.21 | async-start | bytes 9732096 | tf_op jit(solution)/shard_map/reduce_scatter | solution.py:344
  846.7 692.2 %reduce-scatter.21.cloned.1.call-start = ((), (), s32[]{:S(2)}) async-start(), calls=%async_computation.20 | async-start | bytes 9732096 | tf_op jit(solution)/shard_map/reduce_scatter | solution.py:342
  856.2 6.3 copy-start.18
  856.2 6.3 copy-start.29
  (18 other events, 53.8 us)
Sparse Core Ops, SparseCore 0:
  10.9 57.0 all-gather.14
  71.0 52.7 all-gather.8
  126.7 52.9 all-gather.12
  182.9 67.0 all-gather.16
  253.2 66.6 all-gather.10
  322.6 52.5 all-gather.18
  378.1 62.5 all-gather.20
  443.6 62.4 all-gather.22
  549.1 154.7 reduce-scatter.26
  708.7 129.7 reduce-scatter.24
  844.4 98.2 reduce-scatter.18
  949.3 97.9 reduce-scatter.12
  1053.2 97.9 reduce-scatter.16
  1157.8 98.0 reduce-scatter.14
  1262.2 134.6 reduce-scatter.22
  1404.3 134.5 reduce-scatter.20
where the time goes:
time: 1550 us
  waiting for transfers between devices  1280 us (83%)
  blocking collectives  84 us (5%)
  local copies, waits for them, and re-layouts  74.9 us (5%)
  matrix products  62.4 us (4%)
  loops' own time  16.7 us (1%)
    unnamed x18, waiting for transfers between devices  273 us
    reduce_scatter x1, waiting for transfers between devices, body(): lax.psum_scatter(grad_wu, ('seq', 'batch'), scatter_dimension=0, tiled=True)  142 us
    reduce_scatter x1, waiting for transfers between devices, body(): lax.psum_scatter(grad_wd, ('seq', 'batch'), scatter_dimension=0, tiled=True)  141 us
    reduce_scatter x1, waiting for transfers between devices, body(): lax.psum_scatter(grad_wk, ('seq', 'batch'), scatter_dimension=0, tiled=True)  105 us
    reduce_scatter x1, waiting for transfers between devices, body(): lax.psum_scatter(grad_wq, ('seq', 'batch'), scatter_dimension=0, tiled=True)  105 us
    reduce_scatter x1, waiting for transfers between devices, body(): lax.psum_scatter(grad_wv, ('seq', 'batch'), scatter_dimension=0, tiled=True)  104 us
    unnamed x2, blocking collectives  84 us
    all_gather x1, waiting for transfers between devices, body(): lax.all_gather(v_low, 'seq', axis=0, tiled=True)  68.5 us
  transfers between devices with their start and end apart: 16, of which 16 were waited for; matrix products, arithmetic and copies ran while one was open for 7% of the time, Pallas kernels for 0%

commit v1 on v0

v1 whole, which is shorter than its diff:
```python
import functools

import jax
import jax.numpy as jnp
from jax import lax
from jax.experimental import pallas as pl
from jax.experimental.pallas import tpu as pltpu
from jax.sharding import Mesh
from jax.sharding import PartitionSpec as P

HD = 64
EPS = 1e-05
LOG2E = 1.4426950408889634
SEQ = ("zo", "y", "x")
BAT = ("bo", "bi")
ALL = SEQ + BAT
TP = ("x", "bi")
WIDE = 4 * HD
NVEC = 12
F32 = jnp.float32
BF16 = jnp.bfloat16


def normalize(values):
    centre = jnp.mean(values, axis=-1, keepdims=True)
    centred = values - centre
    spread = jnp.mean(centred * centred, axis=-1, keepdims=True)
    factor = lax.rsqrt(spread + EPS)
    return (centred * factor, factor)


def norm_backward(grad_out, normed, factor, gain):
    grad_gain = jnp.sum(grad_out * normed, axis=0)
    grad_shift = jnp.sum(grad_out, axis=0)
    scaled = grad_out * gain
    grad_in = factor * (
        scaled
        - jnp.mean(scaled, axis=-1, keepdims=True)
        - normed * jnp.mean(scaled * normed, axis=-1, keepdims=True)
    )
    return (grad_in, grad_gain, grad_shift)


def dot(left, right, dims=((1,), (0,))):
    return lax.dot_general(left, right, (dims, ((), ())), preferred_element_type=F32)


NN = ((1,), (0,))
NT = ((1,), (1,))
TN = ((0,), (0,))


def swap(value, axis, step=1):
    size = lax.axis_size(axis)
    return lax.ppermute(value, axis, [(i, i ^ step) for i in range(size)])


def pick(value, index, axis):
    return lax.dynamic_index_in_dim(value, index, axis, keepdims=False)


def split(length):
    return 512 if length % 512 == 0 else length


def forward_kernel(
    outer, heads, scal, zc, xc, yc, xya, xyb, w, n1, qkvt, ctxc, ctxt, lse, wt_s, k_s
):
    place, prefix = (scal[0], scal[1])
    rows = zc.shape[1]
    length = n1.shape[0]
    blk = split(length)
    wide = jnp.transpose(w[...].astype(F32))
    wt_s[...] = wide[: 3 * HD].astype(BF16)
    gain = wide[3 * HD : 3 * HD + 1]
    shift = wide[3 * HD + 1 : 3 * HD + 2]

    def norm_piece(src, first, low):
        def one(k, carry):
            value = src[k].astype(F32)
            normed, _ = normalize(value)
            at = jnp.bitwise_xor(place, (first + k) * 4 + low) * rows
            n1[pl.ds(pl.multiple_of(at, rows), rows), :] = (normed * gain + shift).astype(BF16)
            return carry

        lax.fori_loop(0, src.shape[0], one, 0)

    norm_piece(zc, 0, 0)
    norm_piece(xc, 0, 1)
    norm_piece(yc, 0, 2)
    norm_piece(xya, 0, 3)
    norm_piece(xyb, outer // 2, 3)
    head = jnp.minimum(place, heads - 1)
    at = pl.multiple_of(head * HD, HD)
    bias_q = w[pl.ds(at, HD), 3 * HD + 2 : 3 * HD + 3].astype(F32)
    bias_v = w[pl.ds(at, HD), 3 * HD + 3 : 3 * HD + 4].astype(F32)
    for i in range(length // blk):
        part = dot(wt_s[...], n1[i * blk : (i + 1) * blk, :], NT)
        q_part = (part[:HD] + bias_q).astype(BF16)
        k_part = part[HD : 2 * HD].astype(BF16)
        v_part = (part[2 * HD :] + bias_v).astype(BF16)
        qkvt[:HD, i * blk : (i + 1) * blk] = q_part
        qkvt[HD : 2 * HD, i * blk : (i + 1) * blk] = k_part
        qkvt[2 * HD :, i * blk : (i + 1) * blk] = v_part
        k_s[i * blk : (i + 1) * blk, :] = jnp.transpose(k_part.astype(F32)).astype(BF16)
    scale = 0.125 * LOG2E

    def one_query(i, carry):
        first = pl.multiple_of(i * blk, blk)
        q_now = qkvt[:HD, pl.ds(first, blk)]

        def step(masked, j, state):
            top, total, acc = state
            start = pl.multiple_of(j * blk, blk)
            scores = dot(k_s[pl.ds(start, blk), :], q_now) * scale
            if masked:
                key = start + lax.broadcasted_iota(jnp.int32, (blk, blk), 0)
                query = first + lax.broadcasted_iota(jnp.int32, (blk, blk), 1)
                scores = jnp.where((key <= query) | (key < prefix), scores, -1e30)
            new_top = jnp.maximum(top, jnp.max(scores, axis=0, keepdims=True))
            prob = jnp.exp2(scores - new_top)
            fade = jnp.exp2(top - new_top)
            total = total * fade + jnp.sum(prob, axis=0, keepdims=True)
            acc = acc * fade + dot(qkvt[2 * HD :, pl.ds(start, blk)], prob.astype(BF16))
            return (new_top, total, acc)

        state = (
            jnp.full((1, blk), -1e30, F32),
            jnp.zeros((1, blk), F32),
            jnp.zeros((HD, blk), F32),
        )
        full = jnp.maximum(prefix // blk, i)
        needed = jnp.maximum((prefix + blk - 1) // blk, i + 1)
        state = lax.fori_loop(0, full, functools.partial(step, False), state)
        top, total, acc = lax.fori_loop(full, needed, functools.partial(step, True), state)
        out = acc / total
        ctxt[:, pl.ds(first, blk)] = out
        lse[:, pl.ds(first, blk)] = top + jnp.log2(total)
        for r in range(blk // rows):
            ctxc[i * (blk // rows) + r] = out[:, r * rows : (r + 1) * rows].astype(BF16)
        return carry

    lax.fori_loop(0, length // blk, one_query, 0)


def backward_kernel(
    scal, qkvt, dcr, ctxt, lse, dchunk, dall, q_s, k_s, v_s, dc_s, dct_s, del_s, dq_s, dk_s, dv_s
):
    prefix = scal[1]
    rows = dcr.shape[2]
    length = qkvt.shape[1]
    blk = split(length)
    count = length // blk
    for i in range(count):
        sl = slice(i * blk, (i + 1) * blk)
        turned = jnp.transpose(qkvt[:, sl].astype(F32)).astype(BF16)
        q_s[sl, :] = turned[:, :HD]
        k_s[sl, :] = turned[:, HD : 2 * HD]
        v_s[sl, :] = turned[:, 2 * HD :]
    for i in range(length // rows):
        sl = slice(i * rows, (i + 1) * rows)
        dct_s[:, sl] = dcr[i]
        dc_s[sl, :] = jnp.transpose(dcr[i].astype(F32)).astype(BF16)
    del_s[...] = jnp.sum(dct_s[...].astype(F32) * ctxt[...], axis=0, keepdims=True)
    dq_s[...] = jnp.zeros_like(dq_s)
    scale = 0.125 * LOG2E

    def one_key(j, carry):
        start = pl.multiple_of(j * blk, blk)
        dk_s[...] = jnp.zeros_like(dk_s)
        dv_s[...] = jnp.zeros_like(dv_s)

        def step(masked, i, inner):
            first = pl.multiple_of(i * blk, blk)
            here = pl.ds(first, blk)
            scores = dot(k_s[pl.ds(start, blk), :], qkvt[:HD, here]) * scale
            prob = jnp.exp2(scores - lse[:, here])
            if masked:
                key = start + lax.broadcasted_iota(jnp.int32, (blk, blk), 0)
                query = first + lax.broadcasted_iota(jnp.int32, (blk, blk), 1)
                prob = jnp.where((key <= query) | (key < prefix), prob, 0.0)
            d_prob = dot(v_s[pl.ds(start, blk), :], dct_s[:, here])
            d_score = (prob * (d_prob - del_s[:, here])).astype(BF16)
            dv_s[...] += dot(prob.astype(BF16), dc_s[here, :])
            dk_s[...] += dot(d_score, q_s[here, :])
            dq_s[:, here] += dot(qkvt[HD : 2 * HD, pl.ds(start, blk)], d_score)
            return inner

        begin = jnp.where(start < prefix, 0, j)
        middle = jnp.where(start + blk <= prefix, begin, j + 1)
        lax.fori_loop(begin, middle, functools.partial(step, True), 0)
        lax.fori_loop(middle, count, functools.partial(step, False), 0)
        d_key = jnp.transpose(dk_s[...] * 0.125).astype(BF16)
        d_value = jnp.transpose(dv_s[...]).astype(BF16)
        dall[HD : 2 * HD, pl.ds(start, blk)] = d_key
        dall[2 * HD :, pl.ds(start, blk)] = d_value
        for r in range(blk // rows):
            at = j * (blk // rows) + r
            dchunk[at, HD : 2 * HD, :] = d_key[:, r * rows : (r + 1) * rows]
            dchunk[at, 2 * HD :, :] = d_value[:, r * rows : (r + 1) * rows]
        return carry

    lax.fori_loop(0, count, one_key, 0)
    for i in range(count):
        sl = slice(i * blk, (i + 1) * blk)
        d_query = (dq_s[:, sl] * 0.125).astype(BF16)
        dall[:HD, sl] = d_query
        for r in range(blk // rows):
            dchunk[i * (blk // rows) + r, :HD, :] = d_query[:, r * rows : (r + 1) * rows]


def vmem(count):
    return [pl.BlockSpec(memory_space=pltpu.VMEM)] * count


SMEM_SPEC = pl.BlockSpec(memory_space=pltpu.SMEM)


def attend_forward(scal, zc, xc, yc, xya, xyb, w, heads):
    outer, rows, width = zc.shape
    seq = 4 * outer
    length = seq * rows
    return pl.pallas_call(
        functools.partial(forward_kernel, outer, heads),
        out_shape=(
            jax.ShapeDtypeStruct((length, width), BF16),
            jax.ShapeDtypeStruct((3 * HD, length), BF16),
            jax.ShapeDtypeStruct((seq, HD, rows), BF16),
            jax.ShapeDtypeStruct((HD, length), F32),
            jax.ShapeDtypeStruct((1, length), F32),
        ),
        in_specs=[SMEM_SPEC] + vmem(6),
        out_specs=tuple(vmem(5)),
        scratch_shapes=[pltpu.VMEM((3 * HD, width), BF16), pltpu.VMEM((length, HD), BF16)],
        compiler_params=pltpu.CompilerParams(vmem_limit_bytes=40 << 20),
        cost_estimate=pl.CostEstimate(
            flops=2 * length * width * 3 * HD + 4 * length * length * HD,
            bytes_accessed=6 * length * width,
            transcendentals=length * length,
        ),
    )(scal, zc, xc, yc, xya, xyb, w)


def attend_backward(scal, qkvt, dcr, ctxt, lse):
    seq, _, rows = dcr.shape
    length = seq * rows
    blk = split(length)
    return pl.pallas_call(
        backward_kernel,
        out_shape=(
            jax.ShapeDtypeStruct((seq, 3 * HD, rows), BF16),
            jax.ShapeDtypeStruct((3 * HD, length), BF16),
        ),
        in_specs=[SMEM_SPEC] + vmem(4),
        out_specs=tuple(vmem(2)),
        scratch_shapes=[
            pltpu.VMEM((length, HD), BF16),
            pltpu.VMEM((length, HD), BF16),
            pltpu.VMEM((length, HD), BF16),
            pltpu.VMEM((length, HD), BF16),
            pltpu.VMEM((HD, length), BF16),
            pltpu.VMEM((1, length), F32),
            pltpu.VMEM((HD, length), F32),
            pltpu.VMEM((blk, HD), F32),
            pltpu.VMEM((blk, HD), F32),
        ],
        compiler_params=pltpu.CompilerParams(vmem_limit_bytes=40 << 20),
        cost_estimate=pl.CostEstimate(
            flops=10 * length * length * HD,
            bytes_accessed=16 * length * HD,
            transcendentals=length * length,
        ),
    )(scal, qkvt, dcr, ctxt, lse)


def body(
    tokens, cotangent, prefix_len, gain_one, shift_one, w_query, b_query, w_key, w_value, b_value,
    w_output, b_output, gain_two, shift_two, w_up, b_up, w_down, b_down,
):
    outer, pairs = (lax.axis_size("zo"), lax.axis_size("bo"))
    seq, batch = (4 * outer, 2 * pairs)
    zi, yi, xi, ci = (lax.axis_index(a) for a in ("zo", "y", "x", "bi"))
    si = lax.axis_index(SEQ)
    token, d_out = (tokens[0], cotangent[0])
    rows, width = token.shape
    heads = width // HD
    cut = w_query.shape[0]
    wide_cut = w_down.shape[0]
    hidden_width = w_up.shape[1]
    local_width = hidden_width // 4

    zc = jnp.stack([token] + [swap(token, "zo", k) for k in range(1, outer)])
    xc = swap(zc, "x")
    yc = swap(zc, "y")
    xya = swap(xc[: outer // 2], "y")
    xyb = swap(yc[outer // 2 :], "x")

    vectors = jnp.stack(
        [gain_one, shift_one, b_query, b_value, b_output, gain_two, shift_two, b_down], axis=1
    )
    vectors = jnp.concatenate([vectors, b_up.reshape(4, cut).T], axis=1)
    vectors = jnp.pad(vectors, ((0, 0), (0, HD - NVEC)))
    by_head = jnp.concatenate(
        [w.reshape(cut, heads, HD) for w in (w_query, w_key, w_value)], axis=2
    ).transpose(1, 0, 2)
    by_head = jnp.pad(by_head, ((0, seq - heads), (0, 0), (0, 0)))
    send = jnp.concatenate(
        [by_head, jnp.broadcast_to(vectors[None], (seq, cut, HD))], axis=2
    )
    head_w = lax.all_to_all(send, SEQ, split_axis=0, concat_axis=0, tiled=True)
    head_w = lax.all_gather(head_w, BAT, axis=0, tiled=False)
    head_w = head_w.transpose(1, 0, 2, 3).reshape(width, WIDE)
    full = head_w[:, 3 * HD : 3 * HD + NVEC].astype(F32).T
    gain_one_f, shift_one_f, _, _, b_out_f, gain_two_f, shift_two_f, b_down_f = (
        full[i : i + 1] for i in range(8)
    )
    up = head_w[:, 3 * HD + 8 : 3 * HD + NVEC].reshape(outer, 2, 2, pairs, 2, cut, 4)
    up = pick(pick(up, xi, 2), ci, 3)
    b_up_t = up.transpose(0, 1, 2, 4, 3).reshape(1, local_width).astype(F32)

    up_send = (
        w_up.reshape(cut, outer, 2, 2, pairs, 2, wide_cut)
        .transpose(3, 5, 0, 1, 2, 4, 6)
        .reshape(4, cut, local_width)
    )
    up_part = lax.all_to_all(up_send, TP, split_axis=0, concat_axis=0, tiled=True)
    ff = jnp.concatenate([w_down, up_part.reshape(4 * cut, local_width)])
    ff = jnp.stack([ff] + [swap(ff, "zo", k) for k in range(1, outer)])
    ff = jnp.stack([ff, swap(ff, "y")])
    ff = jnp.stack(
        [
            pick(pick(ff, jnp.bitwise_xor(yi, b), 0), jnp.bitwise_xor(zi, a), 0)
            for a in range(outer)
            for b in range(2)
        ]
    )
    if pairs > 1:
        ff = lax.all_gather(ff, "bo", axis=1)
    ff = ff.reshape(2 * outer, pairs, wide_cut + 4 * cut, width)
    down_t = ff[:, :, :wide_cut].reshape(local_width, width)
    up_t = (
        ff[:, :, wide_cut:]
        .reshape(2 * outer, pairs, 2, 2, cut, local_width)
        .transpose(0, 2, 1, 3, 4, 5)
        .reshape(width, local_width)
    )

    square = lax.all_gather(
        jnp.concatenate([w_query, w_key, w_value, w_output]), ALL, axis=0, tiled=False
    )
    square = square.reshape(-1, 4, cut, width).transpose(1, 0, 2, 3).reshape(4, width, width)
    w_out_f = square[3]

    def group(value):
        both = jnp.stack([value, swap(value, "x")])
        return jnp.stack([both, swap(both, "bi")]).reshape(4 * rows, width)

    d_out_t = group(d_out)

    scal = jnp.stack([si, prefix_len[0]]).astype(jnp.int32)
    norm_one, qkvt, ctxc, ctxt, lse = attend_forward(scal, zc, xc, yc, xya, xyb, head_w, heads)
    ctx = lax.all_to_all(ctxc, SEQ, split_axis=0, concat_axis=0, tiled=True)
    ctx = ctx[:heads].reshape(width, rows)
    middle = token.astype(F32) + dot(ctx, w_out_f, TN) + b_out_f
    normed_two, factor_two = normalize(middle)
    norm_two = (normed_two * gain_two_f + shift_two_f).astype(BF16)
    norm_two_t = group(norm_two)

    pre_act = dot(norm_two_t, up_t) + b_up_t
    cdf = 0.5 * (1.0 + lax.erf(pre_act * 0.7071067811865476))
    act = (pre_act * cdf).astype(BF16)
    slope = cdf + pre_act * jnp.exp(-0.5 * pre_act * pre_act) * 0.3989422804014327
    d_pre = (dot(d_out_t, down_t, NT) * slope).astype(BF16)

    def ungroup(value):
        value = value.reshape(2, 2, rows, width)
        value = value[0] + swap(value[1].astype(BF16), "bi").astype(F32)
        return value[0] + swap(value[1].astype(BF16), "x").astype(F32)

    d_norm_two = ungroup(dot(d_pre, up_t, NT))
    d_mid_norm, grad_gain_two, grad_shift_two = norm_backward(
        d_norm_two, normed_two, factor_two, gain_two_f
    )
    d_middle = d_out.astype(F32) + d_mid_norm
    d_branch = d_middle.astype(BF16)
    d_ctx = dot(w_out_f, d_branch, NT).astype(BF16).reshape(heads, HD, rows)
    d_ctx = jnp.pad(d_ctx, ((0, seq - heads), (0, 0), (0, 0)))
    d_ctx = lax.all_to_all(d_ctx, SEQ, split_axis=0, concat_axis=0, tiled=True)

    layer_out = (middle + ungroup(dot(act, down_t)) + b_down_f).astype(BF16)

    grad_down = dot(act, d_out_t, TN).reshape(outer, 2, pairs, wide_cut, width)
    grad_up = dot(norm_two_t, d_pre, TN)
    grad_up = (
        grad_up.reshape(2 * outer, 2, pairs, 2, cut, local_width)
        .transpose(0, 2, 1, 3, 4, 5)
        .reshape(outer, 2, pairs, 4 * cut, local_width)
    )
    grad_b_up = jnp.sum(d_pre.astype(F32), axis=0)
    grad_out = dot(ctx, d_branch).reshape(outer, 2, 2, pairs, 2, cut, width)
    grad_out = pick(grad_out, ci, 4) + swap(
        pick(grad_out, 1 - ci, 4).astype(BF16), "bi"
    ).astype(F32)
    grad_out = pick(grad_out, xi, 2) + swap(
        pick(grad_out, 1 - xi, 2).astype(BF16), "x"
    ).astype(F32)
    grads = jnp.concatenate([grad_down, grad_up, grad_out], axis=3)
    if pairs > 1:
        grads = lax.psum_scatter(grads, "bo", scatter_dimension=2, tiled=True)
    grads = grads.reshape(outer, 2, wide_cut + 5 * cut, width)
    grads = pick(grads, yi, 1) + swap(pick(grads, 1 - yi, 1).astype(BF16), "y").astype(F32)
    total = pick(grads, zi, 0)
    for k in range(1, outer):
        away = pick(grads, jnp.bitwise_xor(zi, k), 0).astype(BF16)
        total = total + swap(away, "zo", k).astype(F32)
    grad_w_down = total[:wide_cut]
    grad_w_output = total[wide_cut + 4 * cut :]
    up_back = total[wide_cut : wide_cut + 4 * cut].astype(BF16).reshape(4, cut, local_width)
    up_back = lax.all_to_all(up_back, TP, split_axis=0, concat_axis=0, tiled=True)
    grad_w_up = (
        up_back.reshape(2, 2, cut, outer, 2, pairs, wide_cut)
        .transpose(2, 3, 4, 0, 5, 1, 6)
        .reshape(cut, hidden_width)
        .astype(F32)
    )

    dchunk, dall = attend_backward(scal, qkvt, d_ctx, ctxt, lse)
    d_rows = lax.all_to_all(dchunk, SEQ, split_axis=0, concat_axis=0, tiled=True)
    d_rows = d_rows[:heads].reshape(heads, 3, HD, rows).transpose(1, 0, 2, 3)
    d_rows = d_rows.reshape(3, width, rows)
    grad_head = dot(dall, norm_one)
    grad_b_qv = jnp.sum(d_rows.astype(F32), axis=2)
    d_norm_one = sum(dot(d_rows[i], square[i], ((0,), (1,))) for i in range(3))
    normed_one, factor_one = normalize(token.astype(F32))
    d_in_norm, grad_gain_one, grad_shift_one = norm_backward(
        d_norm_one, normed_one, factor_one, gain_one_f
    )
    grad_tokens = d_middle + d_in_norm

    mine = (
        (jnp.arange(2, dtype=jnp.int32)[:, None] == xi)
        & (jnp.arange(2, dtype=jnp.int32)[None, :] == ci)
    ).astype(F32)
    b_up_cols = grad_b_up.reshape(outer, 2, 1, pairs, 1, 4, cut).transpose(0, 1, 2, 3, 4, 6, 5)
    b_up_cols = b_up_cols * mine[None, None, :, None, :, None, None]
    vec_cols = jnp.stack(
        [
            grad_gain_one,
            grad_shift_one,
            grad_b_qv[0],
            grad_b_qv[2],
            jnp.sum(d_branch.astype(F32), axis=0),
            grad_gain_two,
            grad_shift_two,
            jnp.sum(d_out.astype(F32), axis=0),
        ],
        axis=1,
    )
    vec_cols = jnp.concatenate([vec_cols, b_up_cols.reshape(width, 4)], axis=1)
    vec_cols = jnp.pad(vec_cols, ((0, 0), (0, HD - NVEC)))
    last = jnp.concatenate([grad_head.T, vec_cols], axis=1).reshape(seq, batch, cut, WIDE)
    if pairs > 1:
        last = lax.psum_scatter(last, BAT, scatter_dimension=1, tiled=True)[:, 0]
    else:
        last = pick(last, ci, 1) + swap(pick(last, 1 - ci, 1).astype(BF16), "bi").astype(F32)
    last = lax.all_to_all(last.astype(BF16), SEQ, split_axis=0, concat_axis=0, tiled=True)
    last = last.astype(F32)
    grad_qkv = last[:heads, :, : 3 * HD].reshape(heads, cut, 3, HD).transpose(2, 1, 0, 3)
    grad_qkv = grad_qkv.reshape(3, cut, width)
    vec = jnp.sum(last[:, :, 3 * HD : 3 * HD + NVEC], axis=0)
    vec_of = [vec[:, i] for i in range(8)]
    grad_bu = vec[:, 8:].T.reshape(4 * cut)
    return (
        layer_out[None],
        grad_tokens[None],
        vec_of[0],
        vec_of[1],
        grad_qkv[0],
        vec_of[2],
        grad_qkv[1],
        grad_qkv[2],
        vec_of[3],
        grad_w_output,
        vec_of[4],
        vec_of[5],
        vec_of[6],
        grad_w_up,
        grad_bu,
        grad_w_down,
        vec_of[7],
    )


def solution(mesh):
    seq, batch = (mesh.shape["seq"], mesh.shape["batch"])
    fine = Mesh(mesh.devices.reshape(seq // 4, 2, 2, batch // 2, 2), ALL)
    act, mat, vec = (P(BAT, SEQ, None), P(ALL, None), P(ALL))
    return jax.shard_map(
        body,
        mesh=fine,
        in_specs=(
            act, act, P(BAT), vec, vec, mat, vec, mat, mat, vec, mat, vec, vec, vec, mat, vec, mat, vec,
        ),
        out_specs=(
            act, act, vec, vec, mat, vec, mat, mat, vec, mat, vec, vec, vec, mat, vec, mat, vec,
        ),
        check_vma=False,
    )
```

time: 1550 us -> 348 us (0.22)
  waiting for transfers between devices: 1280 us -> 111 us
  blocking collectives: 84 us -> 2.21 us
  starting transfers between devices: 0.81 us -> 81.8 us
  matrix products: 62.4 us -> 17.1 us
  other arithmetic: 9 us -> 36 us
  Pallas kernels: 0 us -> 24.1 us
  local copies, waits for them, and re-layouts: 74.9 us -> 58.1 us
  loops' own time: 16.7 us -> 0 us
    reduce_scatter x6 -> x0, waiting for transfers between devices: 627 us -> none  [the longest x1 142 us: body(): lax.psum_scatter(grad_wu, ('seq', 'batch'), scatter_dimension=0, tiled=True)]
    all_gather x8 -> x1, waiting for transfers between devices: 383 us -> 0.01 us  [body(): lax.all_gather(jnp.concatenate([w_query, w_key, w_value, w_output]), ALL,...]
    unnamed x18 -> x1, waiting for transfers between devices: 273 us -> 0.02 us
    ppermute x0 -> x26, waiting for transfers between devices: none -> 101 us  [swap(): return lax.ppermute(value, axis, [(i, i ^ step) for i in range(size)])]
    unnamed x2 -> x0, blocking collectives: 84 us -> none
    all_to_all x0 -> x7, starting transfers between devices: none -> 51.4 us  [the longest x1 19.7 us: body(): ctx = lax.all_to_all(ctxc, SEQ, split_axis=0, concat_axis=0, tiled=True)]
    dot_general x25 -> x13, matrix products: 62.4 us -> 17.1 us  [dot(): lax.dot_general(left, right, (dims, ((), ())), preferred_element_type=F32)]
    ppermute x0 -> x26, starting transfers between devices: none -> 30.4 us  [swap(): return lax.ppermute(value, axis, [(i, i ^ step) for i in range(size)])]
  transfers between devices with their start and end apart: 16 -> 34, of which waited for: 16 -> 13; matrix products, arithmetic and copies ran while one was open for 7% -> 22% of each run, Pallas kernels for 0% -> 7%
where the time goes in v1:
time: 348 us; the launch traced here: 346 us
  waiting for transfers between devices  111 us (32%)
  starting transfers between devices  81.8 us (24%)
  local copies, waits for them, and re-layouts  58.1 us (17%)
  other arithmetic  36 us (10%)
  Pallas kernels  24.1 us (7%)
  matrix products  17.1 us (5%)
  between operations  15.9 us (5%)
    ppermute x26, waiting for transfers between devices, swap(): return lax.ppermute(value, axis, [(i, i ^ step) for i in range(size)])  101 us
    ppermute x26, starting transfers between devices, swap(): return lax.ppermute(value, axis, [(i, i ^ step) for i in range(size)])  30.4 us
    all_to_all x1, starting transfers between devices, body(): ctx = lax.all_to_all(ctxc, SEQ, split_axis=0, concat_axis=0, tiled=True)  19.7 us
    unnamed x158, local copies, waits for them, and re-layouts  17.7 us
    dot_general x13, matrix products, dot(): lax.dot_general(left, right, (dims, ((), ())), preferred_element_type=F32)  17.1 us
    pallas_call x1, Pallas kernels, attend_forward(): pl.pallas_call(functools.partial(forward_kernel, outer, heads), out_shape...  12.9 us
    pallas_call x1, Pallas kernels, attend_backward(): pl.pallas_call(backward_kernel, out_shape=(jax.ShapeDtypeStruct((seq, 3 *...  11.1 us
    unnamed x7, other arithmetic  9.76 us
  transfers between devices with their start and end apart: 34, of which 13 were waited for; matrix products, arithmetic and copies ran while one was open for 22% of the time, Pallas kernels for 7%

profile of v1, /device:TPU:0, one launch (start us, length us, event | category | flops | bytes accessed | tf_op | source)
XLA Modules:
  0.0 346.4 jit_solution(6251782054062481827)
XLA Ops:
  8.9 5.1 %collective-permute-start.2 = (bf16[128,768]{1,0:T(8,128)(2,1)}, bf16[128,768]{1,0:T(8,128)(2,1)S(1)}, u32[]{:S(2)}, u32[]{:S(2)}) collective-permute-start(bf16[128,768]{1,0:T(8,128)(2,1)} %bitcast.241), channel_id=1, source_target_pairs={{0,24},{8,16},{16,8},{24,0},{1,25},{9,17},{17,9},{25,1},{2,26},{10... | collective-permute-start | bytes 589832 | tf_op jit(solution)/shard_map/ppermute | solution.py:55
  16.8 3.5 %all-to-all-start.2 = ((bf16[4,24,768]{2,1,0:T(8,128)(2,1)}), bf16[4,24,768]{2,1,0:T(8,128)(2,1)S(1)}, u32[]{:S(2)}, u32[]{:S(2)}) async-start(bf16[4,24,768]{2,1,0:T(8,128)(2,1)} %reshape.319), calls=%async_computation.2 | async-start | bytes 294912 | tf_op jit(solution)/shard_map/all_to_all | solution.py:326
  22.4 2.7 all-to-all-done.2
  25.1 7.1 %all-to-all-start = ((bf16[16,24,256]{2,1,0:T(8,128)(2,1)}), bf16[16,24,256]{2,1,0:T(8,128)(2,1)S(1)}, u32[]{:S(2)}, u32[]{:S(2)}) async-start(bf16[16,24,256]{2,1,0:T(8,128)(2,1)} %copy.104), calls=%async_computation | async-start | bytes 393216 | tf_op jit(solution)/shard_map/all_to_all | solution.py:310
  33.0 3.7 %collective-permute-start.11 = (bf16[192,768]{1,0:T(8,128)(2,1)}, bf16[192,768]{1,0:T(8,128)(2,1)S(1)}, u32[]{:S(2)}, u32[]{:S(2)}) collective-permute-start(bf16[192,768]{1,0:T(8,128)(2,1)} %get-tuple-element.79), channel_id=1, source_target_pairs={{0,24},{8,16},{16,8},{24,0},{1,25},{9,17},{17,9},{25,1},{2,26},{10... | collective-permute-start | bytes 884744 | tf_op jit(solution)/shard_map/ppermute | solution.py:55
  40.8 9.0 %collective-permute-done.11 = bf16[192,768]{1,0:T(8,128)(2,1)S(1)} collective-permute-done((bf16[192,768]{1,0:T(8,128)(2,1)}, bf16[192,768]{1,0:T(8,128)(2,1)S(1)}, u32[]{:S(2)}, u32[]{:S(2)}) %collective-permute-start.11) | collective-permute-done | bytes 294944 | tf_op jit(solution)/shard_map/ppermute | solution.py:55
  52.1 24.8 %collective-permute-done.10 = bf16[192,768]{1,0:T(8,128)(2,1)} collective-permute-done((bf16[192,768]{1,0:T(8,128)(2,1)}, bf16[192,768]{1,0:T(8,128)(2,1)}, u32[]{:S(2)}, u32[]{:S(2)}) %collective-permute-start.10) | collective-permute-done | bytes 294944 | tf_op jit(solution)/shard_map/ppermute | solution.py:55
  76.9 2.6 fusion.61
  83.0 2.2 all-gather
  95.6 14.2 %collective-permute-done.5.xya = bf16[2,128,768]{2,1,0:T(8,128)(2,1)S(1)} collective-permute-done((bf16[2,128,768]{2,1,0:T(8,128)(2,1)}, bf16[2,128,768]{2,1,0:T(8,128)(2,1)S(1)}, u32[]{:S(2)}, u32[]{:S(2)}) %collective-permute-start.5) | collective-permute-done | bytes 393248 | tf_op jit(solution)/shard_map/ppermute | solution.py:55
  114.4 12.9 %shard_map.305 = (bf16[2048,768]{1,0:T(8,128)(2,1)S(1)}, bf16[192,2048]{1,0:T(8,128)(2,1)S(1)}, bf16[16,64,128]{2,1,0:T(8,128)(2,1)S(1)}, f32[64,2048]{1,0:T(8,128)S(1)}, f32[1,2048]{1,0:T(1,128)S(1)}) custom-call(s32[2]{0:T(128)S(1)} %pad_add_fusion.scal, bf16[4,128,768]{2,1,0:T(8,128)(2,1)S(1)} %copy-done.1, bf16[4,128,768]{2,1,0:T(8,128)(2,1)S(1)} %copy-done.7, ...), custom_call_target="tpu_custom_call" | custom-call | flops 1677721600 | bytes 9437184 | tf_op jit(solution)/shard_map/pallas_call | solution.py:223
  129.8 19.7 %all-to-all-start.1 = ((bf16[16,64,128]{2,1,0:T(8,128)(2,1)}), bf16[16,64,128]{2,1,0:T(8,128)(2,1)S(1)}, u32[]{:S(2)}, u32[]{:S(2)}) async-start(bf16[16,64,128]{2,1,0:T(8,128)(2,1)} %copy-done.5), calls=%async_computation.1 | async-start | bytes 524288 | tf_op jit(solution)/shard_map/all_to_all | solution.py:362
  160.0 4.3 %fusion.62 = (bf16[1,32,24,768]{3,2,0,1:T(8,128)(2,1)}, bf16[1,32,24,768]{3,2,0,1:T(8,128)(2,1)}, bf16[1,32,24,768]{3,2,0,1:T(8,128)(2,1)}, bf16[1,32,24,768]{3,2,0,1:T(8,128)(2,1)S(1)}) fusion(bf16[4,32,24,768]{3,2,0,1:T(8,128)(2,1)} %bitcast.249), kind=kLoop, calls=%fused_computation.180 | loop fusion | bytes 9437184 | tf_op jit(solution)/shard_map/slice | solution.py:433
  167.3 3.6 %collective-permute-done.7 = bf16[128,768]{1,0:T(8,128)(2,1)S(1)} collective-permute-done((bf16[128,768]{1,0:T(8,128)(2,1)S(1)}, bf16[128,768]{1,0:T(8,128)(2,1)S(1)}, u32[]{:S(2)}, u32[]{:S(2)}) %collective-permute-start.7) | collective-permute-done | bytes 196640 | tf_op jit(solution)/shard_map/ppermute | solution.py:55
  184.0 2.3 copy.114
  186.3 2.3 copy.113
  188.7 3.7 %convolution_bitcast_fusion = f32[4,2,1,96,768]{4,3,1,0,2:T(8,128)} fusion(bf16[4,2,96,512]{3,2,1,0:T(8,128)(2,1)} %bitcast.257, bf16[512,768]{1,0:T(8,128)(2,1)} %copy-done.43), kind=kOutput, calls=%fused_computation.20 | convolution fusion | flops 603979776 | bytes 3932160 | tf_op jit(solution)/shard_map/dot_general | solution.py:45
  196.9 4.5 %collective-permute-done.18 = bf16[128,768]{1,0:T(8,128)(2,1)S(1)} collective-permute-done((bf16[128,768]{1,0:T(8,128)(2,1)S(1)}, bf16[128,768]{1,0:T(8,128)(2,1)S(1)}, u32[]{:S(2)}, u32[]{:S(2)}) %collective-permute-start.18) | collective-permute-done | bytes 196640 | tf_op jit(solution)/shard_map/ppermute | solution.py:55
  202.2 3.1 collective-permute-done.14
  208.3 5.8 %all-to-all-start.3 = ((bf16[16,64,128]{2,1,0:T(8,128)(2,1)}), bf16[16,64,128]{2,1,0:T(8,128)(2,1)S(1)}, u32[]{:S(2)}, u32[]{:S(2)}) async-start(bf16[16,64,128]{2,1,0:T(8,128)(2,1)} %pad.18), calls=%async_computation.3 | async-start | bytes 524288 | tf_op jit(solution)/shard_map/all_to_all | solution.py:388
  216.8 2.2 convolution_bitcast_fusion.1
  219.3 4.6 %all-to-all-done.3.dcr = bf16[16,64,128]{2,1,0:T(8,128)(2,1)S(1)} async-done(((bf16[16,64,128]{2,1,0:T(8,128)(2,1)}), bf16[16,64,128]{2,1,0:T(8,128)(2,1)S(1)}, u32[]{:S(2)}, u32[]{:S(2)}) %all-to-all-start.3) | async-done | bytes 262176 | tf_op jit(solution)/shard_map/all_to_all | solution.py:388
  226.0 11.1 %shard_map.306 = (bf16[16,192,128]{2,1,0:T(8,128)(2,1)S(1)}, bf16[192,2048]{1,0:T(8,128)(2,1)S(1)}) custom-call(s32[2]{0:T(128)S(1)} %pad_add_fusion.scal, bf16[192,2048]{1,0:T(8,128)(2,1)S(1)} %copy-done.15, bf16[16,64,128]{2,1,0:T(8,128)(2,1)S(1)} %all-to-all-done.3.dcr, f32[64,2048]{1,0:T(8,128)S(1)} %copy-done.17, f32[1,2048]{1,0:T(1,128)S(1)} %get-tuple-element.27.lse), custom_call_target="tpu_custom_call" | custom-call | flops 2684354560 | bytes 2097152 | tf_op jit(solution)/shard_map/pallas_call | solution.py:248
  239.0 4.4 %all-to-all-start.4 = ((bf16[16,192,128]{2,1,0:T(8,128)(2,1)}), bf16[16,192,128]{2,1,0:T(8,128)(2,1)}, u32[]{:S(2)}, u32[]{:S(2)}) async-start(bf16[16,192,128]{2,1,0:T(8,128)(2,1)} %copy-done.2), calls=%async_computation.4 | async-start | bytes 1572864 | tf_op jit(solution)/shard_map/all_to_all | solution.py:428
  248.8 8.9 %collective-permute-done.21 = bf16[4,2,1,24,768]{4,3,1,0,2:T(8,128)(2,1)S(1)} collective-permute-done((bf16[4,2,1,24,768]{4,3,1,0,2:T(8,128)(2,1)S(1)}, bf16[4,2,1,24,768]{4,3,1,0,2:T(8,128)(2,1)S(1)}, u32[]{:S(2)}, u32[]{:S(2)}) %collective-permute-start.21) | collective-permute-done | bytes 294944 | tf_op jit(solution)/shard_map/ppermute | solution.py:55
  258.3 2.4 copy-done.20
  271.0 5.7 %all-to-all-start.5 = ((bf16[16,24,256]{2,1,0:T(8,128)(2,1)}), bf16[16,24,256]{2,1,0:T(8,128)(2,1)S(1)}, u32[]{:S(2)}, u32[]{:S(2)}) async-start(bf16[16,24,256]{2,1,0:T(8,128)(2,1)} %fusion.33), calls=%async_computation.5 | async-start | bytes 393216 | tf_op jit(solution)/shard_map/all_to_all | solution.py:466
  276.7 16.4 %collective-permute-done.22 = bf16[4,216,768]{2,1,0:T(8,128)(2,1)} collective-permute-done((bf16[4,216,768]{2,1,0:T(8,128)(2,1)}, bf16[4,216,768]{2,1,0:T(8,128)(2,1)}, u32[]{:S(2)}, u32[]{:S(2)}) %collective-permute-start.22) | collective-permute-done | bytes 1327136 | tf_op jit(solution)/shard_map/ppermute | solution.py:55
  293.1 2.4 bitcast_add_fusion
  309.4 16.2 %collective-permute-done.24 = bf16[216,768]{1,0:T(8,128)(2,1)} collective-permute-done((bf16[216,768]{1,0:T(8,128)(2,1)}, bf16[216,768]{1,0:T(8,128)(2,1)}, u32[]{:S(2)}, u32[]{:S(2)}) %collective-permute-start.24) | collective-permute-done | bytes 331808 | tf_op jit(solution)/shard_map/ppermute | solution.py:55
  327.5 5.2 %all-to-all-start.6 = ((bf16[4,24,768]{2,1,0:T(8,128)(2,1)}), bf16[4,24,768]{2,1,0:T(8,128)(2,1)S(1)}, u32[]{:S(2)}, u32[]{:S(2)}) async-start(bf16[4,24,768]{2,1,0:T(8,128)(2,1)} %bitcast.103), calls=%async_computation.6 | async-start | bytes 294912 | tf_op jit(solution)/shard_map/all_to_all | solution.py:419
  334.9 2.6 all-to-all-done.6
  (337 shorter events, 111.1 us)
Async XLA Ops:
  7.3 152.7 %all-gather.4.cloned.1.call-start = ((), (), s32[]{:S(2)}) async-start(), calls=%async_computation.7 | async-start | bytes 4866048 | tf_op jit(solution)/shard_map/all_gather | solution.py:348
  8.9 27.8 %collective-permute-start.2 = (bf16[128,768]{1,0:T(8,128)(2,1)}, bf16[128,768]{1,0:T(8,128)(2,1)S(1)}, u32[]{:S(2)}, u32[]{:S(2)}) collective-permute-start(bf16[128,768]{1,0:T(8,128)(2,1)} %bitcast.241), channel_id=1, source_target_pairs={{0,24},{8,16},{16,8},{24,0},{1,25},{9,17},{17,9},{25,1},{2,26},{10... | collective-permute-start | bytes 589832 | tf_op jit(solution)/shard_map/ppermute | solution.py:55
  14.0 24.5 %collective-permute-start.1 = (bf16[128,768]{1,0:T(8,128)(2,1)}, bf16[128,768]{1,0:T(8,128)(2,1)S(1)}, u32[]{:S(2)}, u32[]{:S(2)}) collective-permute-start(bf16[128,768]{1,0:T(8,128)(2,1)} %bitcast.242), channel_id=1, source_target_pairs={{0,16},{8,24},{16,0},{24,8},{1,17},{9,25},{17,1},{25,9},{2,18},{10... | collective-permute-start | bytes 589832 | tf_op jit(solution)/shard_map/ppermute | solution.py:55
  14.0 26.5 %collective-permute-start = (bf16[128,768]{1,0:T(8,128)(2,1)}, bf16[128,768]{1,0:T(8,128)(2,1)S(1)}, u32[]{:S(2)}, u32[]{:S(2)}) collective-permute-start(bf16[128,768]{1,0:T(8,128)(2,1)} %bitcast.243), channel_id=1, source_target_pairs={{0,8},{8,0},{16,24},{24,16},{1,9},{9,1},{17,25},{25,17},{2,10},{10... | collective-permute-start | bytes 589832 | tf_op jit(solution)/shard_map/ppermute | solution.py:55
  16.8 8.3 %all-to-all-start.2 = ((bf16[4,24,768]{2,1,0:T(8,128)(2,1)}), bf16[4,24,768]{2,1,0:T(8,128)(2,1)S(1)}, u32[]{:S(2)}, u32[]{:S(2)}) async-start(bf16[4,24,768]{2,1,0:T(8,128)(2,1)} %reshape.319), calls=%async_computation.2 | async-start | bytes 294912 | tf_op jit(solution)/shard_map/all_to_all | solution.py:326
  25.1 57.9 %all-to-all-start = ((bf16[16,24,256]{2,1,0:T(8,128)(2,1)}), bf16[16,24,256]{2,1,0:T(8,128)(2,1)S(1)}, u32[]{:S(2)}, u32[]{:S(2)}) async-start(bf16[16,24,256]{2,1,0:T(8,128)(2,1)} %copy.104), calls=%async_computation | async-start | bytes 393216 | tf_op jit(solution)/shard_map/all_to_all | solution.py:310
  33.0 16.9 %collective-permute-start.11 = (bf16[192,768]{1,0:T(8,128)(2,1)}, bf16[192,768]{1,0:T(8,128)(2,1)S(1)}, u32[]{:S(2)}, u32[]{:S(2)}) collective-permute-start(bf16[192,768]{1,0:T(8,128)(2,1)} %get-tuple-element.79), channel_id=1, source_target_pairs={{0,24},{8,16},{16,8},{24,0},{1,25},{9,17},{17,9},{25,1},{2,26},{10... | collective-permute-start | bytes 884744 | tf_op jit(solution)/shard_map/ppermute | solution.py:55
  36.7 40.2 %collective-permute-start.10 = (bf16[192,768]{1,0:T(8,128)(2,1)}, bf16[192,768]{1,0:T(8,128)(2,1)}, u32[]{:S(2)}, u32[]{:S(2)}) collective-permute-start(bf16[192,768]{1,0:T(8,128)(2,1)} %get-tuple-element.79), channel_id=1, source_target_pairs={{0,16},{8,24},{16,0},{24,8},{1,17},{9,25},{17,1},{25,9},{2,18},{10... | collective-permute-start | bytes 884744 | tf_op jit(solution)/shard_map/ppermute | solution.py:55
  36.7 40.2 %collective-permute-start.9 = (bf16[192,768]{1,0:T(8,128)(2,1)}, bf16[192,768]{1,0:T(8,128)(2,1)}, u32[]{:S(2)}, u32[]{:S(2)}) collective-permute-start(bf16[192,768]{1,0:T(8,128)(2,1)} %get-tuple-element.79), channel_id=1, source_target_pairs={{0,8},{8,0},{16,24},{24,16},{1,9},{9,1},{17,25},{25,17},{2,10},{10... | collective-permute-start | bytes 884744 | tf_op jit(solution)/shard_map/ppermute | solution.py:55
  38.5 42.6 %collective-permute-start.15 = (bf16[128,768]{1,0:T(8,128)(2,1)S(1)}, bf16[128,768]{1,0:T(8,128)(2,1)}, u32[]{:S(2)}, u32[]{:S(2)}) collective-permute-start(bf16[128,768]{1,0:T(8,128)(2,1)S(1)} %bitcast.273), channel_id=1, source_target_pairs={{0,2},{2,0},{1,3},{3,1},{4,6},{6,4},{5,7},{7,5},{8,10},{10,8},{9,1... | collective-permute-start | bytes 589832 | tf_op jit(solution)/shard_map/ppermute | solution.py:55
  40.7 46.3 %collective-permute-start.3 = (bf16[4,128,768]{2,1,0:T(8,128)(2,1)S(1)}, bf16[4,128,768]{2,1,0:T(8,128)(2,1)S(1)}, u32[]{:S(2)}, u32[]{:S(2)}) collective-permute-start(bf16[4,128,768]{2,1,0:T(8,128)(2,1)S(1)} %pad_maximum_fusion.2.zc), channel_id=1, source_target_pairs={{0,2},{2,0},{1,3},{3,1},{4,6},{6,4},{5,7},{7,5},{8,10},{10,8},{9,1... | collective-permute-start | bytes 2359304 | tf_op jit(solution)/shard_map/ppermute | solution.py:55
  49.8 38.4 %collective-permute-start.4 = (bf16[4,128,768]{2,1,0:T(8,128)(2,1)S(1)}, bf16[4,128,768]{2,1,0:T(8,128)(2,1)S(1)}, u32[]{:S(2)}, u32[]{:S(2)}) collective-permute-start(bf16[4,128,768]{2,1,0:T(8,128)(2,1)S(1)} %pad_maximum_fusion.2.zc), channel_id=1, source_target_pairs={{0,4},{4,0},{1,5},{5,1},{2,6},{6,2},{3,7},{7,3},{8,12},{12,8},{9,1... | collective-permute-start | bytes 2359304 | tf_op jit(solution)/shard_map/ppermute | solution.py:55
  79.5 70.0 %collective-permute-start.12 = (bf16[4,192,768]{2,1,0:T(8,128)(2,1)}, bf16[4,192,768]{2,1,0:T(8,128)(2,1)}, u32[]{:S(2)}, u32[]{:S(2)}) collective-permute-start(bf16[4,192,768]{2,1,0:T(8,128)(2,1)} %get-tuple-element.66), channel_id=1, source_target_pairs={{0,4},{4,0},{1,5},{5,1},{2,6},{6,2},{3,7},{7,3},{8,12},{12,8},{9,1... | collective-permute-start | bytes 3538952 | tf_op jit(solution)/shard_map/ppermute | solution.py:55
  83.0 10.4 %collective-permute-start.16 = (bf16[2,128,768]{2,1,0:T(8,128)(2,1)}, bf16[2,128,768]{2,1,0:T(8,128)(2,1)}, u32[]{:S(2)}, u32[]{:S(2)}) collective-permute-start(bf16[2,128,768]{2,1,0:T(8,128)(2,1)} %get-tuple-element.75), channel_id=1, source_target_pairs={{0,1},{1,0},{2,3},{3,2},{4,5},{5,4},{6,7},{7,6},{8,9},{9,8},{10,11... | collective-permute-start | bytes 1179656 | tf_op jit(solution)/shard_map/ppermute | solution.py:55
  87.8 22.0 %collective-permute-start.5 = (bf16[2,128,768]{2,1,0:T(8,128)(2,1)}, bf16[2,128,768]{2,1,0:T(8,128)(2,1)S(1)}, u32[]{:S(2)}, u32[]{:S(2)}) collective-permute-start(bf16[2,128,768]{2,1,0:T(8,128)(2,1)} %slice.209), channel_id=1, source_target_pairs={{0,4},{4,0},{1,5},{5,1},{2,6},{6,2},{3,7},{7,3},{8,12},{12,8},{9,1... | collective-permute-start | bytes 1179656 | tf_op jit(solution)/shard_map/ppermute | solution.py:55
  88.3 22.3 %collective-permute-start.6 = (bf16[2,128,768]{2,1,0:T(8,128)(2,1)S(1)}, bf16[2,128,768]{2,1,0:T(8,128)(2,1)S(1)}, u32[]{:S(2)}, u32[]{:S(2)}) collective-permute-start(bf16[2,128,768]{2,1,0:T(8,128)(2,1)S(1)} %slice.210), channel_id=1, source_target_pairs={{0,2},{2,0},{1,3},{3,1},{4,6},{6,4},{5,7},{7,5},{8,10},{10,8},{9,1... | collective-permute-start | bytes 1179656 | tf_op jit(solution)/shard_map/ppermute | solution.py:55
  129.8 29.5 %all-to-all-start.1 = ((bf16[16,64,128]{2,1,0:T(8,128)(2,1)}), bf16[16,64,128]{2,1,0:T(8,128)(2,1)S(1)}, u32[]{:S(2)}, u32[]{:S(2)}) async-start(bf16[16,64,128]{2,1,0:T(8,128)(2,1)} %copy-done.5), calls=%async_computation.1 | async-start | bytes 524288 | tf_op jit(solution)/shard_map/all_to_all | solution.py:362
  165.2 5.7 %collective-permute-start.7 = (bf16[128,768]{1,0:T(8,128)(2,1)S(1)}, bf16[128,768]{1,0:T(8,128)(2,1)S(1)}, u32[]{:S(2)}, u32[]{:S(2)}) collective-permute-start(bf16[128,768]{1,0:T(8,128)(2,1)S(1)} %add_convert_fusion), channel_id=1, source_target_pairs={{0,2},{2,0},{1,3},{3,1},{4,6},{6,4},{5,7},{7,5},{8,10},{10,8},{9,1... | collective-permute-start | bytes 589832 | tf_op jit(solution)/shard_map/ppermute | solution.py:55
  180.6 11.7 %collective-permute-start.17 = (bf16[2,128,768]{2,1,0:T(8,128)(2,1)}, bf16[2,128,768]{2,1,0:T(8,128)(2,1)}, u32[]{:S(2)}, u32[]{:S(2)}) collective-permute-start(bf16[2,128,768]{2,1,0:T(8,128)(2,1)} %bitcast.61), channel_id=1, source_target_pairs={{0,1},{1,0},{2,3},{3,2},{4,5},{5,4},{6,7},{7,6},{8,9},{9,8},{10,11... | collective-permute-start | bytes 1179656 | tf_op jit(solution)/shard_map/ppermute | solution.py:55
  184.0 11.6 %collective-permute-start.13 = (bf16[2,128,768]{2,1,0:T(8,128)(2,1)}, bf16[2,128,768]{2,1,0:T(8,128)(2,1)}, u32[]{:S(2)}, u32[]{:S(2)}) collective-permute-start(bf16[2,128,768]{2,1,0:T(8,128)(2,1)} %bitcast.51), channel_id=1, source_target_pairs={{0,1},{1,0},{2,3},{3,2},{4,5},{5,4},{6,7},{7,6},{8,9},{9,8},{10,11... | collective-permute-start | bytes 1179656 | tf_op jit(solution)/shard_map/ppermute | solution.py:55
  193.6 7.8 %collective-permute-start.18 = (bf16[128,768]{1,0:T(8,128)(2,1)S(1)}, bf16[128,768]{1,0:T(8,128)(2,1)S(1)}, u32[]{:S(2)}, u32[]{:S(2)}) collective-permute-start(bf16[128,768]{1,0:T(8,128)(2,1)S(1)} %fusion.51), channel_id=1, source_target_pairs={{0,2},{2,0},{1,3},{3,1},{4,6},{6,4},{5,7},{7,5},{8,10},{10,8},{9,1... | collective-permute-start | bytes 589832 | tf_op jit(solution)/shard_map/ppermute | solution.py:55
  196.7 8.6 %collective-permute-start.14 = (bf16[128,768]{1,0:T(8,128)(2,1)S(1)}, bf16[128,768]{1,0:T(8,128)(2,1)S(1)}, u32[]{:S(2)}, u32[]{:S(2)}) collective-permute-start(bf16[128,768]{1,0:T(8,128)(2,1)S(1)} %fusion.50), channel_id=1, source_target_pairs={{0,2},{2,0},{1,3},{3,1},{4,6},{6,4},{5,7},{7,5},{8,10},{10,8},{9,1... | collective-permute-start | bytes 589832 | tf_op jit(solution)/shard_map/ppermute | solution.py:55
  208.3 15.6 %all-to-all-start.3 = ((bf16[16,64,128]{2,1,0:T(8,128)(2,1)}), bf16[16,64,128]{2,1,0:T(8,128)(2,1)S(1)}, u32[]{:S(2)}, u32[]{:S(2)}) async-start(bf16[16,64,128]{2,1,0:T(8,128)(2,1)} %pad.18), calls=%async_computation.3 | async-start | bytes 524288 | tf_op jit(solution)/shard_map/all_to_all | solution.py:388
  216.8 26.7 %collective-permute-start.20 = (bf16[4,2,2,1,24,768]{5,4,1,0,3,2:T(8,128)(2,1)}, bf16[4,2,2,1,24,768]{5,4,1,0,3,2:T(8,128)(2,1)}, u32[]{:S(2)}, u32[]{:S(2)}) collective-permute-start(bf16[4,2,2,1,24,768]{5,4,1,0,3,2:T(8,128)(2,1)} %dynamic-slice_convert_fusion.1), channel_id=1, source_target_pairs={{0,1},{1,0},{2,3},{3,2},{4,5},{5,4},{6,7},{7,6},{8,9},{9,8},{10,11... | collective-permute-start | bytes 1769480 | tf_op jit(solution)/shard_map/ppermute | solution.py:55
  239.0 25.0 %all-to-all-start.4 = ((bf16[16,192,128]{2,1,0:T(8,128)(2,1)}), bf16[16,192,128]{2,1,0:T(8,128)(2,1)}, u32[]{:S(2)}, u32[]{:S(2)}) async-start(bf16[16,192,128]{2,1,0:T(8,128)(2,1)} %copy-done.2), calls=%async_computation.4 | async-start | bytes 1572864 | tf_op jit(solution)/shard_map/all_to_all | solution.py:428
  245.2 12.4 %collective-permute-start.21 = (bf16[4,2,1,24,768]{4,3,1,0,2:T(8,128)(2,1)S(1)}, bf16[4,2,1,24,768]{4,3,1,0,2:T(8,128)(2,1)S(1)}, u32[]{:S(2)}, u32[]{:S(2)}) collective-permute-start(bf16[4,2,1,24,768]{4,3,1,0,2:T(8,128)(2,1)S(1)} %fusion.46), channel_id=1, source_target_pairs={{0,2},{2,0},{1,3},{3,1},{4,6},{6,4},{5,7},{7,5},{8,10},{10,8},{9,1... | collective-permute-start | bytes 884744 | tf_op jit(solution)/shard_map/ppermute | solution.py:55
  262.0 31.1 %collective-permute-start.22 = (bf16[4,216,768]{2,1,0:T(8,128)(2,1)}, bf16[4,216,768]{2,1,0:T(8,128)(2,1)}, u32[]{:S(2)}, u32[]{:S(2)}) collective-permute-start(bf16[4,216,768]{2,1,0:T(8,128)(2,1)} %fusion.10), channel_id=1, source_target_pairs={{0,4},{4,0},{1,5},{5,1},{2,6},{6,2},{3,7},{7,3},{8,12},{12,8},{9,1... | collective-permute-start | bytes 3981320 | tf_op jit(solution)/shard_map/ppermute | solution.py:55
  271.0 30.0 %all-to-all-start.5 = ((bf16[16,24,256]{2,1,0:T(8,128)(2,1)}), bf16[16,24,256]{2,1,0:T(8,128)(2,1)S(1)}, u32[]{:S(2)}, u32[]{:S(2)}) async-start(bf16[16,24,256]{2,1,0:T(8,128)(2,1)} %fusion.33), calls=%async_computation.5 | async-start | bytes 393216 | tf_op jit(solution)/shard_map/all_to_all | solution.py:466
  296.5 12.9 %collective-permute-start.25 = (bf16[216,768]{1,0:T(8,128)(2,1)}, bf16[216,768]{1,0:T(8,128)(2,1)}, u32[]{:S(2)}, u32[]{:S(2)}) collective-permute-start(bf16[216,768]{1,0:T(8,128)(2,1)} %get-tuple-element.61), channel_id=1, source_target_pairs={{0,24},{8,16},{16,8},{24,0},{1,25},{9,17},{17,9},{25,1},{2,26},{10... | collective-permute-start | bytes 995336 | tf_op jit(solution)/shard_map/ppermute | solution.py:55
  297.6 28.0 %collective-permute-start.24 = (bf16[216,768]{1,0:T(8,128)(2,1)}, bf16[216,768]{1,0:T(8,128)(2,1)}, u32[]{:S(2)}, u32[]{:S(2)}) collective-permute-start(bf16[216,768]{1,0:T(8,128)(2,1)} %get-tuple-element.62), channel_id=1, source_target_pairs={{0,16},{8,24},{16,0},{24,8},{1,17},{9,25},{17,1},{25,9},{2,18},{10... | collective-permute-start | bytes 995336 | tf_op jit(solution)/shard_map/ppermute | solution.py:55
  299.7 25.9 %collective-permute-start.23 = (bf16[216,768]{1,0:T(8,128)(2,1)}, bf16[216,768]{1,0:T(8,128)(2,1)}, u32[]{:S(2)}, u32[]{:S(2)}) collective-permute-start(bf16[216,768]{1,0:T(8,128)(2,1)} %get-tuple-element.60), channel_id=1, source_target_pairs={{0,8},{8,0},{16,24},{24,16},{1,9},{9,1},{17,25},{25,17},{2,10},{10... | collective-permute-start | bytes 995336 | tf_op jit(solution)/shard_map/ppermute | solution.py:55
  327.5 10.0 %all-to-all-start.6 = ((bf16[4,24,768]{2,1,0:T(8,128)(2,1)}), bf16[4,24,768]{2,1,0:T(8,128)(2,1)S(1)}, u32[]{:S(2)}, u32[]{:S(2)}) async-start(bf16[4,24,768]{2,1,0:T(8,128)(2,1)} %bitcast.103), calls=%async_computation.6 | async-start | bytes 294912 | tf_op jit(solution)/shard_map/all_to_all | solution.py:419
  (82 other events, 511.0 us)
Sparse Core Ops, SparseCore 0:
  11.0 82.5 all-gather.3

commit v2 on v1

v2 whole, which is shorter than its diff:
```python
import functools

import jax
import jax.numpy as jnp
from jax import lax
from jax.experimental import pallas as pl
from jax.experimental.pallas import tpu as pltpu
from jax.sharding import Mesh
from jax.sharding import PartitionSpec as P

HD = 64
EPS = 1e-05
LOG2E = 1.4426950408889634
SEQ = ("zo", "y", "x")
BAT = ("bo", "bi")
ALL = SEQ + BAT
PLANE = ("y", "x", "bi")
WIDE = 4 * HD
F32 = jnp.float32
BF16 = jnp.bfloat16


def normalize(values):
    centre = jnp.mean(values, axis=-1, keepdims=True)
    centred = values - centre
    spread = jnp.mean(centred * centred, axis=-1, keepdims=True)
    factor = lax.rsqrt(spread + EPS)
    return (centred * factor, factor)


def norm_backward(grad_out, normed, factor, gain):
    grad_gain = jnp.sum(grad_out * normed, axis=0, keepdims=True)
    grad_shift = jnp.sum(grad_out, axis=0, keepdims=True)
    scaled = grad_out * gain
    grad_in = factor * (
        scaled
        - jnp.mean(scaled, axis=-1, keepdims=True)
        - normed * jnp.mean(scaled * normed, axis=-1, keepdims=True)
    )
    return (grad_in, grad_gain, grad_shift)


def dot(left, right, dims=((1,), (0,))):
    return lax.dot_general(left, right, (dims, ((), ())), preferred_element_type=F32)


NN = ((1,), (0,))
NT = ((1,), (1,))
TN = ((0,), (0,))


def swap(value, axis, step=1):
    size = lax.axis_size(axis)
    return lax.ppermute(value, axis, [(i, i ^ step) for i in range(size)])


def swap_plane(value, step):
    return lax.ppermute(value, ("y", "x"), [(i, i ^ step) for i in range(4)])


def after(value, *others):
    return lax.optimization_barrier((value,) + others)[0]


def pick(value, index, axis):
    return lax.dynamic_index_in_dim(value, index, axis, keepdims=False)


def split(length):
    return 512 if length % 512 == 0 else length


def assemble(parts, out):
    seq, cut = (parts.shape[1], parts.shape[2])
    for b in range(2):
        for i in range(seq):
            at = (2 * i + b) * cut
            out[at : at + cut, :] = parts[b, i].astype(F32)


def forward_kernel(
    outer, heads, scal, zc, xc, yc, xya, xyb, w, n1_out, n0_out, qkvt, ctxc, ctxt, lse, rows_out,
    w_head, *rest,
):
    place, prefix = (scal[0], scal[1])
    if w.ndim == 4:
        w_out, n1, n0, wt_s, k_s, sems = rest
        assemble(w, w_head)
    else:
        w_out, (n1, n0, wt_s, k_s, sems) = (None, rest)
        w_head[...] = w[...].astype(F32)
    rows = n1.shape[0] // (4 * outer)
    length = n1.shape[0]
    blk = split(length)
    turned = jnp.transpose(w_head[...])
    wt_s[...] = turned[: 3 * HD].astype(BF16)
    rows_in = turned[3 * HD : 3 * HD + 8]
    rows_out[...] = rows_in
    gain = rows_in[0:1]
    shift = rows_in[1:2]
    if w_out is not None:
        for src, first, low in ((zc, 0, 0), (xc, 0, 1), (yc, 0, 2), (xya, 0, 3), (xyb, outer // 2, 3)):
            for k in range(src.shape[0]):
                w_out[(first + k) * 4 + low] = src[k, rows:, :]

    def norm_piece(src, first, low):
        def one(k, carry):
            value = src[k, :rows, :].astype(F32)
            normed, _ = normalize(value)
            at = jnp.bitwise_xor(place, (first + k) * 4 + low) * rows
            here = pl.ds(pl.multiple_of(at, rows), rows)
            n0[here, :] = normed.astype(BF16)
            n1[here, :] = (normed * gain + shift).astype(BF16)
            return carry

        lax.fori_loop(0, src.shape[0], one, 0)

    norm_piece(zc, 0, 0)
    norm_piece(xc, 0, 1)
    norm_piece(yc, 0, 2)
    norm_piece(xya, 0, 3)
    norm_piece(xyb, outer // 2, 3)
    copies = (
        pltpu.make_async_copy(n1, n1_out, sems.at[0]),
        pltpu.make_async_copy(n0, n0_out, sems.at[1]),
    )
    for copy in copies:
        copy.start()
    head = jnp.minimum(place, heads - 1)
    at = pl.multiple_of(head * HD, HD)
    bias_q = w_head[pl.ds(at, HD), 3 * HD + 2 : 3 * HD + 3]
    bias_v = w_head[pl.ds(at, HD), 3 * HD + 3 : 3 * HD + 4]
    for i in range(length // blk):
        part = dot(wt_s[...], n1[i * blk : (i + 1) * blk, :], NT)
        q_part = (part[:HD] + bias_q).astype(BF16)
        k_part = part[HD : 2 * HD].astype(BF16)
        v_part = (part[2 * HD :] + bias_v).astype(BF16)
        qkvt[:HD, i * blk : (i + 1) * blk] = q_part
        qkvt[HD : 2 * HD, i * blk : (i + 1) * blk] = k_part
        qkvt[2 * HD :, i * blk : (i + 1) * blk] = v_part
        k_s[i * blk : (i + 1) * blk, :] = jnp.transpose(k_part.astype(F32)).astype(BF16)
    scale = 0.125 * LOG2E

    def one_query(i, carry):
        first = pl.multiple_of(i * blk, blk)
        q_now = qkvt[:HD, pl.ds(first, blk)]

        def step(masked, j, state):
            top, total, acc = state
            start = pl.multiple_of(j * blk, blk)
            scores = dot(k_s[pl.ds(start, blk), :], q_now) * scale
            if masked:
                key = start + lax.broadcasted_iota(jnp.int32, (blk, blk), 0)
                query = first + lax.broadcasted_iota(jnp.int32, (blk, blk), 1)
                scores = jnp.where((key <= query) | (key < prefix), scores, -1e30)
            new_top = jnp.maximum(top, jnp.max(scores, axis=0, keepdims=True))
            prob = jnp.exp2(scores - new_top)
            fade = jnp.exp2(top - new_top)
            total = total * fade + jnp.sum(prob, axis=0, keepdims=True)
            acc = acc * fade + dot(qkvt[2 * HD :, pl.ds(start, blk)], prob.astype(BF16))
            return (new_top, total, acc)

        state = (
            jnp.full((1, blk), -1e30, F32),
            jnp.zeros((1, blk), F32),
            jnp.zeros((HD, blk), F32),
        )
        full = jnp.maximum(prefix // blk, i)
        needed = jnp.maximum((prefix + blk - 1) // blk, i + 1)
        state = lax.fori_loop(0, full, functools.partial(step, False), state)
        top, total, acc = lax.fori_loop(full, needed, functools.partial(step, True), state)
        out = acc / total
        ctxt[:, pl.ds(first, blk)] = out
        lse[:, pl.ds(first, blk)] = top + jnp.log2(total)
        for r in range(blk // rows):
            ctxc[i * (blk // rows) + r] = out[:, r * rows : (r + 1) * rows].astype(BF16)
        return carry

    lax.fori_loop(0, length // blk, one_query, 0)
    for copy in copies:
        copy.wait()


def backward_kernel(
    scal, qkvt, dcr, ctxt, lse, dchunk, dall, q_s, k_s, v_s, dc_s, dct_s, del_s, dq_s, dk_s, dv_s
):
    prefix = scal[1]
    rows = dcr.shape[2]
    length = qkvt.shape[1]
    blk = split(length)
    count = length // blk
    for i in range(count):
        sl = slice(i * blk, (i + 1) * blk)
        turned = jnp.transpose(qkvt[:, sl].astype(F32)).astype(BF16)
        q_s[sl, :] = turned[:, :HD]
        k_s[sl, :] = turned[:, HD : 2 * HD]
        v_s[sl, :] = turned[:, 2 * HD :]
    for i in range(length // rows):
        sl = slice(i * rows, (i + 1) * rows)
        dct_s[:, sl] = dcr[i]
        dc_s[sl, :] = jnp.transpose(dcr[i].astype(F32)).astype(BF16)
    del_s[...] = jnp.sum(dct_s[...].astype(F32) * ctxt[...], axis=0, keepdims=True)
    dq_s[...] = jnp.zeros_like(dq_s)
    scale = 0.125 * LOG2E

    def one_key(j, carry):
        start = pl.multiple_of(j * blk, blk)
        dk_s[...] = jnp.zeros_like(dk_s)
        dv_s[...] = jnp.zeros_like(dv_s)

        def step(masked, i, inner):
            first = pl.multiple_of(i * blk, blk)
            here = pl.ds(first, blk)
            scores = dot(k_s[pl.ds(start, blk), :], qkvt[:HD, here]) * scale
            prob = jnp.exp2(scores - lse[:, here])
            if masked:
                key = start + lax.broadcasted_iota(jnp.int32, (blk, blk), 0)
                query = first + lax.broadcasted_iota(jnp.int32, (blk, blk), 1)
                prob = jnp.where((key <= query) | (key < prefix), prob, 0.0)
            d_prob = dot(v_s[pl.ds(start, blk), :], dct_s[:, here])
            d_score = (prob * (d_prob - del_s[:, here])).astype(BF16)
            dv_s[...] += dot(prob.astype(BF16), dc_s[here, :])
            dk_s[...] += dot(d_score, q_s[here, :])
            dq_s[:, here] += dot(qkvt[HD : 2 * HD, pl.ds(start, blk)], d_score)
            return inner

        begin = jnp.where(start < prefix, 0, j)
        middle = jnp.where(start + blk <= prefix, begin, j + 1)
        lax.fori_loop(begin, middle, functools.partial(step, True), 0)
        lax.fori_loop(middle, count, functools.partial(step, False), 0)
        d_key = jnp.transpose(dk_s[...] * 0.125).astype(BF16)
        d_value = jnp.transpose(dv_s[...]).astype(BF16)
        dall[HD : 2 * HD, pl.ds(start, blk)] = d_key
        dall[2 * HD :, pl.ds(start, blk)] = d_value
        for r in range(blk // rows):
            at = j * (blk // rows) + r
            dchunk[at, HD : 2 * HD, :] = d_key[:, r * rows : (r + 1) * rows]
            dchunk[at, 2 * HD :, :] = d_value[:, r * rows : (r + 1) * rows]
        return carry

    lax.fori_loop(0, count, one_key, 0)
    for i in range(count):
        sl = slice(i * blk, (i + 1) * blk)
        d_query = (dq_s[:, sl] * 0.125).astype(BF16)
        dall[:HD, sl] = d_query
        for r in range(blk // rows):
            dchunk[i * (blk // rows) + r, :HD, :] = d_query[:, r * rows : (r + 1) * rows]


def gather_rows(pieces, out):
    rows = pieces[0].shape[0]
    for i, piece in enumerate(pieces):
        out[i * rows : (i + 1) * rows, :] = piece[...]


def feed_kernel(packed, *refs):
    scal, n2_a, n2_b, n2_c, n2_d, dy_a, dy_b, dy_c, dy_d = refs[:9]
    if packed:
        ffz, ffc, w_own = refs[9:12]
        outs, (n2, dy, down, up, bias) = (refs[12:-5], refs[-5:])
        outs, w_qkv = (outs[:-1], outs[-1])
        zi, ci = (scal[0], scal[1])
        outer = ffz.shape[0]
        cut = (ffz.shape[1] - 8) // 8
        half = 4 * cut
        rows = []
        for src, flip in ((ffz, 0), (ffc, 1)):
            for k in range(outer):
                at = jnp.bitwise_xor(zi, k) * 2 + jnp.bitwise_xor(ci, flip)
                here = pl.ds(pl.multiple_of(at * half, half), half)
                down[here, :] = src[k, :half, :]
                up[here, :] = src[k, half : 2 * half, :]
                rows.append((at, src[k, 2 * half : 2 * half + 8, :half].astype(F32)[:1]))
        for d, src in enumerate((None, dy_b, dy_c, dy_d)):
            for k in range(outer):
                if src is None:
                    w_qkv[k * 4] = w_own[k]
                else:
                    w_qkv[k * 4 + d] = src[k * 3 * cut : (k + 1) * 3 * cut, :]
        behind = 3 * cut * outer
        for q in range(2 * outer):
            bias[:, q * half : (q + 1) * half] = sum(
                jnp.where(at == q, row, 0.0) for at, row in rows
            )
    else:
        down, up, bias = refs[9:12]
        outs, (n2, dy) = (refs[12:-2], refs[-2:])
        behind = 0
    gather_rows((n2_a, n2_b, n2_c, n2_d), n2)
    rows = n2_a.shape[0]
    dy[:rows, :] = dy_a[...]
    for d, src in enumerate((dy_b, dy_c, dy_d)):
        dy[(d + 1) * rows : (d + 2) * rows, :] = src[behind:, :]
    act, d_pre, out_keep, out_b, out_c, out_d, dn_keep, dn_b, dn_c, dn_d = outs
    width = down.shape[0]
    tile = 256
    for c in range(width // tile):
        sl = slice(c * tile, (c + 1) * tile)
        pre = dot(n2[...], up[:, sl]) + bias[:, sl]
        cdf = 0.5 * (1.0 + lax.erf(pre * 0.7071067811865476))
        act[:, sl] = (pre * cdf).astype(BF16)
        slope = cdf + pre * jnp.exp(-0.5 * pre * pre) * 0.3989422804014327
        d_pre[:, sl] = (dot(dy[...], down[sl, :], NT) * slope).astype(BF16)
    back = dot(d_pre[...], up[...], NT)
    for i, ref in enumerate((dn_keep, dn_b, dn_c, dn_d)):
        ref[...] = back[i * rows : (i + 1) * rows].astype(ref.dtype)
    out = dot(act[...], down[...])
    for i, ref in enumerate((out_keep, out_b, out_c, out_d)):
        ref[...] = out[i * rows : (i + 1) * rows].astype(ref.dtype)


def feed_forward(scal, n2, dy, weights, local):
    rows, width = n2[0].shape
    packed = weights[0].ndim == 3
    wide = [pltpu.VMEM((4 * rows, width), BF16)] * 2
    if packed:
        wide = wide + [
            pltpu.VMEM((local, width), BF16),
            pltpu.VMEM((width, local), BF16),
            pltpu.VMEM((1, local), F32),
        ]
    more = []
    if packed:
        outer = weights[0].shape[0]
        cut = (weights[0].shape[1] - 8) // 8
        more = [jax.ShapeDtypeStruct((4 * outer, 3 * cut, width), BF16)]
    part = [jax.ShapeDtypeStruct((rows, width), F32)]
    part = part + [jax.ShapeDtypeStruct((rows, width), BF16)] * 3
    return pl.pallas_call(
        functools.partial(feed_kernel, packed),
        out_shape=tuple([jax.ShapeDtypeStruct((4 * rows, local), BF16)] * 2 + part + part + more),
        in_specs=[SMEM_SPEC] + vmem(8 + len(weights)),
        out_specs=tuple(vmem(10 + len(more))),
        scratch_shapes=wide,
        compiler_params=pltpu.CompilerParams(vmem_limit_bytes=14 << 20),
        cost_estimate=SMALL,
        name="feed",
    )(scal, *n2, *dy, *weights)


def rank_row(scal, seq, low, core, cut):
    return pl.multiple_of((2 * jnp.bitwise_xor(scal[0], low) + jnp.bitwise_xor(scal[2], core)) * cut, cut)


def stacked(own, other, first, last):
    rows = [ref[i, first:last, :].astype(F32) for ref in (own, other) for i in range(own.shape[0])]
    return jnp.concatenate(rows, axis=0).astype(BF16)


def middle_kernel(heads, scal, ctx, own, other, token, rows_in, middle, norm_two, plain, moved):
    seq, cut, _ = own.shape
    plain[...] = ctx[:heads].reshape(plain.shape).astype(F32)
    for b in range(2):
        for i in range(seq):
            at = (b * seq + i) * cut
            moved[at : at + cut, :] = plain[pl.ds(rank_row(scal, seq, i, b, cut), cut), :]
    turned = jnp.transpose(moved[...]).astype(BF16)
    product = dot(turned, stacked(own, other, 0, cut))
    value = token[...].astype(F32) + product + rows_in[4:5, :]
    middle[...] = value
    normed, _ = normalize(value)
    norm_two[...] = (normed * rows_in[5:6, :] + rows_in[6:7, :]).astype(BF16)


def attend_output(scal, ctx, own, other, token, rows_in, heads):
    rows, width = token.shape
    return pl.pallas_call(
        functools.partial(middle_kernel, heads),
        out_shape=(
            jax.ShapeDtypeStruct((rows, width), F32),
            jax.ShapeDtypeStruct((rows, width), BF16),
        ),
        in_specs=[SMEM_SPEC] + vmem(5),
        out_specs=tuple(vmem(2)),
        scratch_shapes=[pltpu.VMEM((width, rows), F32)] * 2,
        compiler_params=pltpu.CompilerParams(vmem_limit_bytes=8 << 20),
        cost_estimate=SMALL,
        name="middle",
    )(scal, ctx, own, other, token, rows_in)


def turn_math(keep, got, middle, d_out, rows_in):
    d_norm = keep + (got[0].astype(F32) + got[1].astype(F32)) + got[2].astype(F32)
    normed, factor = normalize(middle)
    grad_in, grad_gain, grad_shift = norm_backward(d_norm, normed, factor, rows_in[5:6])
    grad_up = d_out.astype(F32)
    total = grad_up + grad_in
    low = total.astype(BF16)
    sums = (
        jnp.sum(low.astype(F32), axis=0, keepdims=True),
        grad_gain,
        grad_shift,
        jnp.sum(grad_up, axis=0, keepdims=True),
        jnp.zeros((4, total.shape[1]), F32),
    )
    return (total, low, jnp.concatenate(sums, axis=0))


def turn_kernel(
    heads, scal, keep, got_b, got_c, got_d, middle, d_out, own, other, rows_in,
    d_middle, d_branch, d_ctx, sums, plain,
):
    got = (got_b[...], got_c[...], got_d[...])
    d_middle[...], low, sums[...] = turn_math(keep[...], got, middle[...], d_out[...], rows_in[...])
    d_branch[...] = low
    seq, cut, _ = own.shape
    back = dot(stacked(own, other, 0, cut), low, NT)
    for b in range(2):
        for i in range(seq):
            at = (b * seq + i) * cut
            plain[pl.ds(rank_row(scal, seq, i, b, cut), cut), :] = back[at : at + cut]
    rows = d_ctx.shape[2]
    d_ctx[:heads] = plain[...].astype(BF16).reshape(heads, HD, rows)
    d_ctx[heads:] = jnp.zeros((seq - heads, HD, rows), BF16)


def turn_back(scal, keep, got, middle, d_out, own, other, rows_in, heads, seq):
    rows, width = middle.shape
    return pl.pallas_call(
        functools.partial(turn_kernel, heads),
        out_shape=(
            jax.ShapeDtypeStruct((rows, width), F32),
            jax.ShapeDtypeStruct((rows, width), BF16),
            jax.ShapeDtypeStruct((seq, HD, rows), BF16),
            jax.ShapeDtypeStruct((8, width), F32),
        ),
        in_specs=[SMEM_SPEC] + vmem(9),
        out_specs=tuple(vmem(4)),
        scratch_shapes=[pltpu.VMEM((width, rows), F32)],
        compiler_params=pltpu.CompilerParams(vmem_limit_bytes=8 << 20),
        cost_estimate=SMALL,
        name="turn",
    )(scal, keep, *got, middle, d_out, own, other, rows_in)


def last_kernel(heads, scal, d_rows, own, other, token, d_middle, rows_in, grad_tokens, plain):
    seq, cut = (own.shape[0], own.shape[1] // 3)
    total = 0.0
    for i in range(3):
        part = jnp.concatenate(
            [d_rows[h, i * HD : (i + 1) * HD, :].astype(F32) for h in range(heads)], axis=0
        )
        total = total + dot(stacked(own, other, i * cut, (i + 1) * cut), part.astype(BF16))
    for b in range(2):
        for i in range(seq):
            at = (b * seq + i) * cut
            plain[pl.ds(rank_row(scal, seq, i, b, cut), cut), :] = total[at : at + cut]
    normed, factor = normalize(token[...].astype(F32))
    grad_in, _, _ = norm_backward(jnp.transpose(plain[...]), normed, factor, rows_in[0:1, :])
    grad_tokens[...] = d_middle[...] + grad_in


def input_grad(scal, d_rows, own, other, token, d_middle, rows_in, heads):
    rows, width = token.shape
    return pl.pallas_call(
        functools.partial(last_kernel, heads),
        out_shape=jax.ShapeDtypeStruct((rows, width), F32),
        in_specs=[SMEM_SPEC] + vmem(6),
        out_specs=vmem(1)[0],
        scratch_shapes=[pltpu.VMEM((width, rows), F32)],
        compiler_params=pltpu.CompilerParams(vmem_limit_bytes=12 << 20),
        cost_estimate=SMALL,
        name="last",
    )(scal, d_rows, own, other, token, d_middle, rows_in)


def grads_kernel(
    scal, act, d_pre, n2_a, n2_b, n2_c, n2_d, dy_a, dy_b, dy_c, dy_d, send, keep, n2, dy, down_s, up_s
):
    zi, ci = (scal[0], scal[1])
    outer, rows, width = keep.shape
    half = (rows - 8) // 2
    gather_rows((n2_a, n2_b, n2_c, n2_d), n2)
    count = dy_a.shape[0]
    dy[:count, :] = dy_a[...]
    for d, src in enumerate((dy_b, dy_c, dy_d)):
        dy[(d + 1) * count : (d + 2) * count, :] = src[src.shape[0] - count :, :]
    down_s[...] = dot(act[...], dy[...], TN)
    up_s[...] = dot(n2[...], d_pre[...], TN)
    bias = jnp.sum(d_pre[...].astype(F32), axis=0, keepdims=True)
    for k in range(outer):
        for flip, out in ((0, keep), (1, send)):
            at = jnp.bitwise_xor(zi, k) * 2 + jnp.bitwise_xor(ci, flip)
            here = pl.ds(pl.multiple_of(at * half, half), half)
            out[k, :half, :] = down_s[here, :].astype(out.dtype)
            out[k, half : 2 * half, :] = up_s[here, :].astype(out.dtype)
            part = sum(
                jnp.where(at == q, bias[:, q * half : (q + 1) * half], 0.0)
                for q in range(2 * outer)
            )
            part = jnp.concatenate([part, jnp.zeros((1, width - half), F32)], axis=1)
            out[k, 2 * half :, :] = jnp.broadcast_to(part, (8, width)).astype(out.dtype)


def feed_grads(scal, act, d_pre, n2, dy, outer, half):
    rows, width = n2[0].shape
    local = act.shape[1]
    return pl.pallas_call(
        grads_kernel,
        out_shape=(
            jax.ShapeDtypeStruct((outer, 2 * half + 8, width), BF16),
            jax.ShapeDtypeStruct((outer, 2 * half + 8, width), F32),
        ),
        in_specs=[SMEM_SPEC] + vmem(10),
        out_specs=tuple(vmem(2)),
        scratch_shapes=[
            pltpu.VMEM((4 * rows, width), BF16),
            pltpu.VMEM((4 * rows, width), BF16),
            pltpu.VMEM((local, width), F32),
            pltpu.VMEM((width, local), F32),
        ],
        compiler_params=pltpu.CompilerParams(vmem_limit_bytes=16 << 20),
        cost_estimate=SMALL,
        name="grads",
    )(scal, act, d_pre, *n2, *dy)


def fold_kernel(keep, got, own, *away):
    own[...] = keep[0] + got[0].astype(F32)
    for k, ref in enumerate(away):
        ref[...] = (keep[k + 1] + got[k + 1].astype(F32)).astype(BF16)


def fold(keep, got):
    outer, rows, width = keep.shape
    part = jax.ShapeDtypeStruct((rows, width), BF16)
    own, *away = pl.pallas_call(
        fold_kernel,
        out_shape=tuple([jax.ShapeDtypeStruct((rows, width), F32)] + [part] * (outer - 1)),
        in_specs=vmem(2),
        out_specs=tuple(vmem(outer)),
        compiler_params=pltpu.CompilerParams(vmem_limit_bytes=4 << 20),
        cost_estimate=SMALL,
        name="fold",
    )(keep, got)
    return (own, away)


def pack_kernel(outer, heads, w_up, w_q, w_k, w_v, vec, up_send, send):
    wide = up_send.shape[2] // outer
    for t in range(4):
        for z in range(outer):
            at = (z * 4 + t) * wide
            piece = w_up[:, at : at + wide]
            for b in range(2):
                up_send[t * 2 + b, :, z * wide : (z + 1) * wide] = piece
    for h in range(send.shape[0]):
        for i, w in enumerate((w_q, w_k, w_v)):
            if h < heads:
                piece = w[:, h * HD : (h + 1) * HD]
            else:
                piece = jnp.zeros((w.shape[0], HD), BF16)
            send[h, :, i * HD : (i + 1) * HD] = piece
        send[h, :, 3 * HD :] = vec[...]


def pack(w_up, w_q, w_k, w_v, vec, outer, heads):
    cut = w_up.shape[0]
    return pl.pallas_call(
        functools.partial(pack_kernel, outer, heads),
        out_shape=(
            jax.ShapeDtypeStruct((8, cut, w_up.shape[1] // 4), BF16),
            jax.ShapeDtypeStruct((4 * outer, cut, WIDE), BF16),
        ),
        in_specs=vmem(5),
        out_specs=tuple(vmem(2)),
        compiler_params=pltpu.CompilerParams(vmem_limit_bytes=4 << 20),
        cost_estimate=SMALL,
        name="pack",
    )(w_up, w_q, w_k, w_v, vec)


def unpack_up_kernel(outer, scal, got, out):
    wide = got.shape[2] // outer
    for t in range(4):
        piece = got[2 * t + scal[0]].astype(F32)
        for z in range(outer):
            at = (z * 4 + t) * wide
            out[:, at : at + wide] = piece[:, z * wide : (z + 1) * wide]


def unpack_up(scal, got, outer):
    _, cut, local = got.shape
    return pl.pallas_call(
        functools.partial(unpack_up_kernel, outer),
        out_shape=jax.ShapeDtypeStruct((cut, 4 * local), F32),
        in_specs=[SMEM_SPEC] + vmem(1),
        out_specs=vmem(1)[0],
        compiler_params=pltpu.CompilerParams(vmem_limit_bytes=4 << 20),
        cost_estimate=SMALL,
        name="unpack_up",
    )(scal, got)


def heads_kernel(
    heads, batch, scal, dall, n1, n0, w_head, sums, *refs
):
    outs, (gh, gm, cs, full) = (refs[:-4], refs[-4:])
    step = pl.program_id(0)

    @pl.when(step == 0)
    def _():
        gh[...] = jnp.zeros_like(gh)
        gm[...] = jnp.zeros_like(gm)
        cs[...] = jnp.zeros_like(cs)

    gh[...] += dot(dall[...], n1[...])
    gm[...] += dot(dall[...], n0[...])
    cs[...] += dot(jnp.ones((8, dall.shape[1]), BF16), dall[...], NT)

    @pl.when(step == pl.num_programs(0) - 1)
    def _():
        place, core = (scal[0], scal[2])
        width = gh.shape[1]
        wide = w_head[:, : 3 * HD]
        turned = jnp.transpose(gm[...])
        total = cs[0:1, :]
        gain = jnp.sum(wide * turned, axis=1, keepdims=True)
        shift = jnp.sum(wide * total, axis=1, keepdims=True)
        column = jnp.transpose(cs[...])[:, 0:1]
        head_of = lax.broadcasted_iota(jnp.int32, (width, 1), 0) // HD
        b_q = jnp.where(head_of == place, jnp.concatenate([column[:HD]] * heads, axis=0), 0.0)
        b_v = jnp.where(head_of == place, jnp.concatenate([column[2 * HD :]] * heads, axis=0), 0.0)
        others = jnp.transpose(sums[...])
        pad = jnp.zeros((width, HD - 8), F32)
        vec = jnp.concatenate([gain, shift, b_q, b_v, others[:, :4], pad], axis=1)
        block = jnp.concatenate([jnp.transpose(gh[...]), vec], axis=1)
        if len(outs) == 1:
            outs[0][...] = block
        else:
            full[...] = block.reshape(full.shape)
            keep, send = outs
            for i in range(keep.shape[0]):
                keep[i] = full[i * batch + core]
                send[i] = full[i * batch + 1 - core].astype(BF16)


def head_grads(scal, dall, n1, n0, w_head, sums, heads, seq, batch):
    length, width = n1.shape
    blk = split(length)
    cut = width // (seq * batch)
    if batch == 2:
        shapes = (
            jax.ShapeDtypeStruct((seq, cut, WIDE), F32),
            jax.ShapeDtypeStruct((seq, cut, WIDE), BF16),
        )
        full = (seq * batch, cut, WIDE)
    else:
        shapes = (jax.ShapeDtypeStruct((width, WIDE), F32),)
        full = (8, WIDE)
    return pl.pallas_call(
        functools.partial(heads_kernel, heads, batch),
        out_shape=shapes,
        grid=(length // blk,),
        in_specs=[
            SMEM_SPEC,
            pl.BlockSpec((3 * HD, blk), lambda i: (0, i)),
            pl.BlockSpec((blk, width), lambda i: (i, 0)),
            pl.BlockSpec((blk, width), lambda i: (i, 0)),
            whole((width, WIDE)),
            whole((8, width)),
        ],
        out_specs=tuple(whole(shape.shape) for shape in shapes),
        scratch_shapes=[
            pltpu.VMEM((3 * HD, width), F32),
            pltpu.VMEM((3 * HD, width), F32),
            pltpu.VMEM((8, 3 * HD), F32),
            pltpu.VMEM(full, F32),
        ],
        compiler_params=pltpu.CompilerParams(vmem_limit_bytes=14 << 20),
        cost_estimate=SMALL,
        name="heads",
    )(scal, dall, n1, n0, w_head, sums)


def unpack_heads_kernel(heads, got, g_q, g_k, g_v, vec):
    for i, out in enumerate((g_q, g_k, g_v)):
        for h in range(heads):
            out[:, h * HD : (h + 1) * HD] = got[h, :, i * HD : (i + 1) * HD].astype(F32)
    total = got[0, :, 3 * HD :].astype(F32)
    for s in range(1, got.shape[0]):
        total = total + got[s, :, 3 * HD :].astype(F32)
    vec[...] = total


def unpack_heads(got, heads):
    _, cut, _ = got.shape
    mat = jax.ShapeDtypeStruct((cut, heads * HD), F32)
    return pl.pallas_call(
        functools.partial(unpack_heads_kernel, heads),
        out_shape=(mat, mat, mat, jax.ShapeDtypeStruct((cut, HD), F32)),
        in_specs=vmem(1),
        out_specs=tuple(vmem(4)),
        compiler_params=pltpu.CompilerParams(vmem_limit_bytes=4 << 20),
        cost_estimate=SMALL,
        name="unpack_heads",
    )(got)


def out_grad_kernel(heads, batch, scal, ctx, d_branch, keep, send, full):
    rows = ctx.shape[2]
    turned = ctx[:heads].reshape(heads * HD, rows)
    full[...] = dot(turned, d_branch[...]).reshape(full.shape)
    core = scal[2]
    for i in range(keep.shape[0]):
        keep[i] = full[i * batch + core]
        send[i] = full[i * batch + 1 - core].astype(BF16)


def out_grad(scal, ctx, d_branch, heads, batch):
    seq = ctx.shape[0]
    width = d_branch.shape[1]
    cut = width // (seq * batch)
    return pl.pallas_call(
        functools.partial(out_grad_kernel, heads, batch),
        out_shape=(
            jax.ShapeDtypeStruct((seq, cut, width), F32),
            jax.ShapeDtypeStruct((seq, cut, width), BF16),
        ),
        in_specs=[SMEM_SPEC] + vmem(2),
        out_specs=tuple(vmem(2)),
        scratch_shapes=[pltpu.VMEM((seq * batch, cut, width), F32)],
        compiler_params=pltpu.CompilerParams(vmem_limit_bytes=6 << 20),
        cost_estimate=SMALL,
        name="out_grad",
    )(scal, ctx, d_branch)


def plane_kernel(scal, keep, got, own, *away):
    outer = own.shape[0]
    for z in range(outer):
        for k, ref in enumerate((own,) + away):
            at = z * 4 + jnp.bitwise_xor(scal[3], k)
            ref[z] = (keep[at] + got[at].astype(F32)).astype(ref.dtype)


def plane_fold(scal, keep, got):
    seq, cut, width = keep.shape
    part = (seq // 4, cut, width)
    return pl.pallas_call(
        plane_kernel,
        out_shape=tuple([jax.ShapeDtypeStruct(part, F32)] + [jax.ShapeDtypeStruct(part, BF16)] * 3),
        in_specs=[SMEM_SPEC] + vmem(2),
        out_specs=tuple(vmem(4)),
        compiler_params=pltpu.CompilerParams(vmem_limit_bytes=4 << 20),
        cost_estimate=SMALL,
        name="plane_fold",
    )(scal, keep, got)


def line_kernel(scal, keep, got_b, got_c, got_d, own, *away):
    for k, ref in enumerate((own,) + away):
        at = jnp.bitwise_xor(scal[4], k)
        total = keep[at] + (got_b[at].astype(F32) + got_c[at].astype(F32))
        ref[...] = (total + got_d[at].astype(F32)).astype(ref.dtype)


def line_fold(scal, keep, got):
    outer, cut, width = keep.shape
    part = (cut, width)
    shapes = [jax.ShapeDtypeStruct(part, F32)] + [jax.ShapeDtypeStruct(part, BF16)] * (outer - 1)
    own, *away = pl.pallas_call(
        line_kernel,
        out_shape=tuple(shapes),
        in_specs=[SMEM_SPEC] + vmem(4),
        out_specs=tuple(vmem(outer)),
        compiler_params=pltpu.CompilerParams(vmem_limit_bytes=4 << 20),
        cost_estimate=SMALL,
        name="line_fold",
    )(scal, keep, *got)
    return (own, away)


def vmem(count):
    return [pl.BlockSpec(memory_space=pltpu.VMEM)] * count


SMALL = pl.CostEstimate(flops=1, bytes_accessed=1, transcendentals=0)
SMEM_SPEC = pl.BlockSpec(memory_space=pltpu.SMEM)


def whole(shape):
    return pl.BlockSpec(shape, lambda i: (0,) * len(shape))


def attend_forward(scal, zc, xc, yc, xya, xyb, w, heads, rows):
    outer, extra, width = zc.shape
    seq = 4 * outer
    length = seq * rows
    shapes = [
        jax.ShapeDtypeStruct((length, width), BF16),
        jax.ShapeDtypeStruct((length, width), BF16),
        jax.ShapeDtypeStruct((3 * HD, length), BF16),
        jax.ShapeDtypeStruct((seq, HD, rows), BF16),
        jax.ShapeDtypeStruct((HD, length), F32),
        jax.ShapeDtypeStruct((1, length), F32),
        jax.ShapeDtypeStruct((8, width), F32),
        jax.ShapeDtypeStruct((width, WIDE), F32),
    ]
    if extra > rows:
        shapes.append(jax.ShapeDtypeStruct((seq, extra - rows, width), BF16))
    return pl.pallas_call(
        functools.partial(forward_kernel, outer, heads),
        out_shape=tuple(shapes),
        in_specs=[SMEM_SPEC] + vmem(6),
        out_specs=tuple([pl.BlockSpec(memory_space=pl.ANY)] * 2 + vmem(len(shapes) - 2)),
        scratch_shapes=[
            pltpu.VMEM((length, width), BF16),
            pltpu.VMEM((length, width), BF16),
            pltpu.VMEM((3 * HD, width), BF16),
            pltpu.VMEM((length, HD), BF16),
            pltpu.SemaphoreType.DMA((2,)),
        ],
        compiler_params=pltpu.CompilerParams(vmem_limit_bytes=(14 << 20) + 4 * length * width),
        cost_estimate=SMALL,
        name="forward",
    )(scal, zc, xc, yc, xya, xyb, w)


def attend_backward(scal, qkvt, dcr, ctxt, lse):
    seq, _, rows = dcr.shape
    length = seq * rows
    blk = split(length)
    return pl.pallas_call(
        backward_kernel,
        out_shape=(
            jax.ShapeDtypeStruct((seq, 3 * HD, rows), BF16),
            jax.ShapeDtypeStruct((3 * HD, length), BF16),
        ),
        in_specs=[SMEM_SPEC] + vmem(4),
        out_specs=tuple(vmem(2)),
        scratch_shapes=[
            pltpu.VMEM((length, HD), BF16),
            pltpu.VMEM((length, HD), BF16),
            pltpu.VMEM((length, HD), BF16),
            pltpu.VMEM((length, HD), BF16),
            pltpu.VMEM((HD, length), BF16),
            pltpu.VMEM((1, length), F32),
            pltpu.VMEM((HD, length), F32),
            pltpu.VMEM((blk, HD), F32),
            pltpu.VMEM((blk, HD), F32),
        ],
        compiler_params=pltpu.CompilerParams(vmem_limit_bytes=12 << 20),
        cost_estimate=SMALL,
    )(scal, qkvt, dcr, ctxt, lse)


def body(
    tokens, cotangent, prefix_len, gain_one, shift_one, w_query, b_query, w_key, w_value, b_value,
    w_output, b_output, gain_two, shift_two, w_up, b_up, w_down, b_down,
):
    outer, pairs = (lax.axis_size("zo"), lax.axis_size("bo"))
    seq, batch = (4 * outer, 2 * pairs)
    zi, yi, ci = (lax.axis_index(a) for a in ("zo", "y", "bi"))
    si = lax.axis_index(SEQ)
    token, d_out = (tokens[0], cotangent[0])
    rows, width = token.shape
    heads = width // HD
    cut = w_query.shape[0]
    wide_cut = w_down.shape[0]
    hidden_width = w_up.shape[1]
    local_width = hidden_width // 4

    packed = pairs == 1

    ahead = jnp.concatenate([token, w_output]) if packed else token
    zc = jnp.stack([ahead] + [swap(ahead, "zo", k) for k in range(1, outer)])
    xc = swap(zc, "x")
    yc = swap(zc, "y")
    xya = swap(xc[: outer // 2], "y")
    xyb = swap(yc[outer // 2 :], "x")

    vectors = jnp.stack(
        [gain_one, shift_one, b_query, b_value, b_output, gain_two, shift_two, b_down], axis=1
    )
    vectors = jnp.pad(vectors, ((0, 0), (0, HD - 8)))
    if packed:
        up_send, send = pack(w_up, w_query, w_key, w_value, vectors, outer, heads)
    else:
        by_head = jnp.concatenate(
            [w.reshape(cut, heads, HD) for w in (w_query, w_key, w_value)], axis=2
        ).transpose(1, 0, 2)
        by_head = jnp.pad(by_head, ((0, seq - heads), (0, 0), (0, 0)))
        send = jnp.concatenate(
            [by_head, jnp.broadcast_to(vectors[None], (seq, cut, HD))], axis=2
        )
        up_send = w_up.reshape(cut, outer, 4, local_width // outer).transpose(2, 0, 1, 3)
        up_send = jnp.repeat(up_send.reshape(4, cut, local_width), 2, axis=0)
    head_w = lax.all_to_all(after(send, zc), SEQ, split_axis=0, concat_axis=0, tiled=True)
    up_part = lax.all_to_all(after(up_send, head_w), PLANE, split_axis=0, concat_axis=0, tiled=True)
    head_w = lax.all_gather(head_w, BAT, axis=0, tiled=False)
    if not packed:
        head_w = head_w.transpose(1, 0, 2, 3).reshape(width, WIDE)

    up_part = lax.dynamic_slice_in_dim(up_part, 4 * ci, 4, 0).reshape(4 * cut, local_width)
    b_up_row = jnp.pad(b_up[None], ((0, 7), (0, width - wide_cut)))
    ff = jnp.concatenate([w_down, up_part, b_up_row])
    ff = after(ff, xc, yc)
    ff_got = [swap(ff, "zo", k) for k in range(1, outer)]
    if packed:
        w_qkv = after(jnp.concatenate([w_query, w_key, w_value]), zc)
        w_qkv = jnp.stack([w_qkv] + [swap(w_qkv, "zo", k) for k in range(1, outer)])
        side = jnp.concatenate([w_qkv.reshape(3 * cut * outer, width), d_out])
    else:
        side = d_out
        square = jnp.concatenate([w_query, w_key, w_value, w_output], axis=1)
        square = lax.all_gather(square, ALL, axis=0, tiled=True)
    side = after(side, xya, xyb)
    d_out_t = [d_out] + [swap_plane(side, k) for k in range(1, 4)]

    def group(value):
        return [value] + [swap_plane(value, k) for k in range(1, 4)]

    flat = lax.axis_index(("y", "x"))
    scal = jnp.stack([si, prefix_len[0], ci, flat, zi]).astype(jnp.int32)
    norm_one, norm_raw, qkvt, ctxc, ctxt, lse, rows_in, head_f, *w_out_own = attend_forward(
        scal, zc, xc, yc, xya, xyb, head_w, heads, rows
    )
    b_down_f = rows_in[7:8]
    ctxc, d_out_t, ff_got = lax.optimization_barrier((ctxc, d_out_t, ff_got))
    ffz = jnp.stack([ff] + ff_got)
    ctx = lax.all_to_all(ctxc, SEQ, split_axis=0, concat_axis=0, tiled=True)
    ffc = swap(ffz, "bi")
    if pairs > 1:
        ff = jnp.stack([ffz, ffc])
        ff = jnp.stack(
            [
                pick(pick(ff, jnp.bitwise_xor(ci, b), 0), jnp.bitwise_xor(zi, a), 0)
                for a in range(outer)
                for b in range(2)
            ]
        )
        ff = lax.all_gather(ff, "bo", axis=0).reshape(pairs, outer, 2, 8 * cut + 8, width)
        down_t = ff[:, :, :, :wide_cut].transpose(1, 0, 2, 3, 4).reshape(local_width, width)
        up_t = ff[:, :, :, wide_cut : 2 * wide_cut].reshape(
            pairs, outer, 2, 2, 2, cut, local_width
        )
        up_t = up_t.transpose(1, 2, 3, 0, 4, 5, 6).reshape(width, local_width)
        bias_t = ff[:, :, :, 2 * wide_cut, :wide_cut].transpose(1, 0, 2, 3).reshape(1, local_width)
        weights = (down_t, up_t, bias_t.astype(F32))
    else:
        weights = (ffz, ffc, w_qkv)
    if packed:
        w_out_own = w_out_own[0]
        w_out_other = swap(w_out_own, "bi")
        middle, norm_two = attend_output(
            scal, ctx, w_out_own, w_out_other, token, rows_in, heads
        )
    else:
        ctx_flat = ctx[:heads].reshape(width, rows)
        middle = token.astype(F32) + dot(ctx_flat, square[:, 3 * width :], TN) + rows_in[4:5]
        norm_two = (normalize(middle)[0] * rows_in[5:6] + rows_in[6:7]).astype(BF16)
    norm_two_t = group(norm_two)

    places = jnp.stack([zi, ci]).astype(jnp.int32)
    fed = feed_forward(places, norm_two_t, d_out_t, weights, local_width)
    act, d_pre, out_keep, *out_send = fed[:6]
    dn_keep, *dn_send = fed[6:10]
    dn_got = [swap_plane(part, k + 1) for k, part in enumerate(dn_send)]
    if packed:
        d_middle, d_branch, d_ctx, sums = turn_back(
            scal, dn_keep, dn_got, middle, d_out, w_out_own, w_out_other, rows_in, heads, seq
        )
    else:
        d_middle, d_branch, sums = turn_math(dn_keep, dn_got, middle, d_out, rows_in)
        d_ctx = dot(square[:, 3 * width :], d_branch, NT).astype(BF16).reshape(heads, HD, rows)
        d_ctx = jnp.pad(d_ctx, ((0, seq - heads), (0, 0), (0, 0)))
    act, d_pre = lax.optimization_barrier((act, d_pre, d_ctx))[:2]

    if packed:
        send, keep = feed_grads(places, act, d_pre, norm_two_t, d_out_t, outer, wide_cut)
    else:
        n2_all, dy_all = (jnp.concatenate(norm_two_t), jnp.concatenate(d_out_t))
        grad_down = dot(act, dy_all, TN).reshape(outer, pairs, 2, wide_cut, width)
        grad_up = dot(n2_all, d_pre, TN).reshape(outer, 2, 2, pairs, 2, cut, local_width)
        grad_up = grad_up.transpose(0, 3, 1, 2, 4, 5, 6)
        grad_up = grad_up.reshape(outer, pairs, 2, 4 * cut, local_width)
        grad_b_up = jnp.sum(d_pre.astype(F32), axis=0).reshape(outer, pairs, 2, 1, wide_cut)
        grad_b_up = jnp.pad(
            grad_b_up, ((0, 0), (0, 0), (0, 0), (0, 7), (0, width - wide_cut))
        )
        grads = jnp.concatenate([grad_down, grad_up, grad_b_up], axis=3)
        grads = lax.psum_scatter(grads, "bo", scatter_dimension=1, tiled=True)[:, 0]
        grads = jnp.stack([pick(grads, jnp.bitwise_xor(zi, k), 0) for k in range(outer)])
        send, keep = (pick(grads, 1 - ci, 1).astype(BF16), pick(grads, ci, 1))
    keep, away = fold(keep, swap(send, "bi"))
    back = [swap(part, "zo", k + 1) for k, part in enumerate(away)]
    d_ctx = lax.all_to_all(d_ctx, SEQ, split_axis=0, concat_axis=0, tiled=True)

    scal = after(scal, *away)
    if packed:
        w_qkv_other = swap(after(fed[10], *away), "bi")

    dchunk, dall = attend_backward(scal, qkvt, d_ctx, ctxt, lse)
    *back, dchunk = lax.optimization_barrier(tuple(back) + (dchunk,))
    d_rows = lax.all_to_all(dchunk, SEQ, split_axis=0, concat_axis=0, tiled=True)
    d_branch_late = after(d_branch, dall)
    if packed:
        grad_out, part = out_grad(scal, ctx, d_branch_late, heads, batch)
        grad_out, *part = plane_fold(scal, grad_out, swap(part, "bi"))
        got = [swap_plane(value, k + 1) for k, value in enumerate(part)]
        grad_out, part = line_fold(scal, grad_out, got)
        grad_w_output = grad_out + sum(
            swap(value, "zo", k + 1).astype(F32) for k, value in enumerate(part)
        )
    else:
        grad_out = dot(ctx[:heads].reshape(width, rows), d_branch_late)
        grad_w_output = lax.psum_scatter(grad_out, ALL, scatter_dimension=0, tiled=True)
    out_got = [swap_plane(after(part, dall), k + 1) for k, part in enumerate(out_send)]
    layer_out = middle + out_keep + sum(part.astype(F32) for part in out_got) + b_down_f
    layer_out = layer_out.astype(BF16)
    total = keep + sum(part.astype(F32) for part in back)
    grad_w_down = total[:wide_cut]
    grad_bu = total[wide_cut + 4 * cut, :wide_cut]
    up_back = total[wide_cut : 2 * wide_cut].astype(BF16).reshape(4, cut, local_width)
    up_back = after(jnp.concatenate([up_back, up_back]), d_rows)
    up_back = lax.all_to_all(up_back, PLANE, split_axis=0, concat_axis=0, tiled=True)
    if packed:
        grad_w_up = unpack_up(yi[None].astype(jnp.int32), up_back, outer)
    else:
        up_back = pick(up_back.reshape(4, 2, cut, local_width), yi, 1)
        grad_w_up = (
            up_back.reshape(4, cut, outer, local_width // outer)
            .transpose(1, 2, 0, 3)
            .reshape(cut, hidden_width)
            .astype(F32)
        )
    if packed:
        grad_tokens = input_grad(
            scal, d_rows, fed[10], w_qkv_other, token, d_middle, rows_in, heads
        )
    else:
        d_flat = d_rows[:heads].reshape(heads, 3, HD, rows).transpose(1, 0, 2, 3)
        d_flat = d_flat.reshape(3, width, rows)
        d_norm_one = sum(
            dot(d_flat[i], square[:, i * width : (i + 1) * width], ((0,), (1,)))
            for i in range(3)
        )
        normed_one, factor_one = normalize(token.astype(F32))
        d_in_norm, _, _ = norm_backward(d_norm_one, normed_one, factor_one, rows_in[0:1])
        grad_tokens = d_middle + d_in_norm

    last = head_grads(scal, dall, norm_one, norm_raw, head_f, sums, heads, seq, batch)
    if packed:
        last = last[0] + swap(last[1], "bi").astype(F32)
    else:
        last = last[0].reshape(seq, batch, cut, WIDE)
        last = lax.psum_scatter(last, BAT, scatter_dimension=1, tiled=True)[:, 0]
    last = after(last.astype(BF16), d_rows)
    last = lax.all_to_all(last, SEQ, split_axis=0, concat_axis=0, tiled=True)
    if packed:
        *grad_qkv, vec = unpack_heads(last, heads)
        vec = vec.T
        vec_of = [vec[i] for i in range(8)]
    else:
        last = last.astype(F32)
        grad_qkv = last[:heads, :, : 3 * HD].reshape(heads, cut, 3, HD).transpose(2, 1, 0, 3)
        grad_qkv = grad_qkv.reshape(3, cut, width)
        vec = jnp.sum(last[:, :, 3 * HD : 3 * HD + 8], axis=0)
        vec_of = [vec[:, i] for i in range(8)]
    return (
        layer_out[None],
        grad_tokens[None],
        vec_of[0],
        vec_of[1],
        grad_qkv[0],
        vec_of[2],
        grad_qkv[1],
        grad_qkv[2],
        vec_of[3],
        grad_w_output,
        vec_of[4],
        vec_of[5],
        vec_of[6],
        grad_w_up,
        grad_bu,
        grad_w_down,
        vec_of[7],
    )


def solution(mesh):
    seq, batch = (mesh.shape["seq"], mesh.shape["batch"])
    fine = Mesh(mesh.devices.reshape(seq // 4, 2, 2, batch // 2, 2), ALL)
    act, mat, vec = (P(BAT, SEQ, None), P(ALL, None), P(ALL))
    return jax.shard_map(
        body,
        mesh=fine,
        in_specs=(
            act, act, P(BAT), vec, vec, mat, vec, mat, mat, vec, mat, vec, vec, vec, mat, vec, mat, vec,
        ),
        out_specs=(
            act, act, vec, vec, mat, vec, mat, mat, vec, mat, vec, vec, vec, mat, vec, mat, vec,
        ),
        check_vma=False,
    )
```

time: 348 us -> 275 us (0.79)
  waiting for transfers between devices: 111 us -> 74.5 us
  Pallas kernels: 24.1 us -> 53.4 us
  local copies, waits for them, and re-layouts: 58.1 us -> 34.9 us
  other arithmetic: 36 us -> 13.1 us
  matrix products: 17.1 us -> 0 us
  between operations: 15.9 us -> 2.08 us
  starting transfers between devices: 81.8 us -> 92.7 us
    ppermute x26 -> x25, waiting for transfers between devices: 101 us -> 37.5 us  [swap(): return lax.ppermute(value, axis, [(i, i ^ step) for i in range(size)])]
    pallas_call x0 -> x13, Pallas kernels: none -> 27.5 us  [the longest x1 4.55 us: feed_forward(): pl.pallas_call(functools.partial(feed_kernel, packed), out_shape=tuple([j...]
    ppermute x0 -> x15, waiting for transfers between devices: none -> 19.2 us  [swap_plane(): return lax.ppermute(value, ('y', 'x'), [(i, i ^ step) for i in range(4)])]
    ppermute x0 -> x15, starting transfers between devices: none -> 17.6 us  [swap_plane(): return lax.ppermute(value, ('y', 'x'), [(i, i ^ step) for i in range(4)])]
    dot_general x13 -> x0, matrix products: 17.1 us -> none  [dot(): lax.dot_general(left, right, (dims, ((), ())), preferred_element_type=F32)]
    slice x22 -> x3, local copies, waits for them, and re-layouts: 17.1 us -> 0.85 us  [the longest x1 0.82 us: body(): vec_of = [vec[i] for i in range(8)]]
    all_to_all x1, starting transfers between devices: 19.7 us -> 5.08 us  [body(): ctx = lax.all_to_all(ctxc, SEQ, split_axis=0, concat_axis=0, tiled=True)]
    unnamed x158 -> x130, local copies, waits for them, and re-layouts: 17.7 us -> 29.3 us
  transfers between devices with their start and end apart: 34 -> 47, of which waited for: 13 -> 14; matrix products, arithmetic and copies ran while one was open for 22% -> 5% of each run, Pallas kernels for 7% -> 15%
where the time goes in v2:
time: 275 us; the launch traced here: 273 us
  starting transfers between devices  92.7 us (34%)
  waiting for transfers between devices  74.5 us (27%)
  Pallas kernels  53.4 us (19%)
  local copies, waits for them, and re-layouts  34.9 us (13%)
  other arithmetic  13.1 us (5%)
    ppermute x25, waiting for transfers between devices, swap(): return lax.ppermute(value, axis, [(i, i ^ step) for i in range(size)])  37.5 us
    ppermute x25, starting transfers between devices, swap(): return lax.ppermute(value, axis, [(i, i ^ step) for i in range(size)])  35.5 us
    unnamed x130, local copies, waits for them, and re-layouts  29.3 us
    ppermute x15, waiting for transfers between devices, swap_plane(): return lax.ppermute(value, ('y', 'x'), [(i, i ^ step) for i in range(4)])  19.2 us
    ppermute x15, starting transfers between devices, swap_plane(): return lax.ppermute(value, ('y', 'x'), [(i, i ^ step) for i in range(4)])  17.6 us
    pallas_call x1, Pallas kernels, attend_forward(): pl.pallas_call(functools.partial(forward_kernel, outer, heads), out_shape...  14.8 us
    pallas_call x1, Pallas kernels, attend_backward(): pl.pallas_call(backward_kernel, out_shape=(jax.ShapeDtypeStruct((seq, 3 *...  11.1 us
    all_to_all x1, waiting for transfers between devices, body(): ctx = lax.all_to_all(ctxc, SEQ, split_axis=0, concat_axis=0, tiled=True)  10.2 us
  transfers between devices with their start and end apart: 47, of which 14 were waited for; matrix products, arithmetic and copies ran while one was open for 5% of the time, Pallas kernels for 15%

profile of v2, /device:TPU:0, one launch (start us, length us, event | category | flops | bytes accessed | tf_op | source)
XLA Modules:
  0.0 272.9 jit_solution(4489339936015687308)
XLA Ops:
  1.8 3.1 %collective-permute-start = (bf16[152,768]{1,0:T(8,128)(2,1)S(1)}, bf16[152,768]{1,0:T(8,128)(2,1)S(1)}, u32[]{:S(2)}, u32[]{:S(2)}) collective-permute-start(bf16[152,768]{1,0:T(8,128)(2,1)S(1)} %get-tuple-element.184), channel_id=1, source_target_pairs={{0,8},{8,0},{16,24},{24,16},{1,9},{9,1},{17,25},{25,17},{2,10},{10... | collective-permute-start | bytes 700424 | tf_op jit(solution)/shard_map/ppermute | solution.py:54
  4.9 2.6 collective-permute-start.1
  7.5 7.3 %collective-permute-done = bf16[152,768]{1,0:T(8,128)(2,1)S(1)} collective-permute-done((bf16[152,768]{1,0:T(8,128)(2,1)S(1)}, bf16[152,768]{1,0:T(8,128)(2,1)S(1)}, u32[]{:S(2)}, u32[]{:S(2)}) %collective-permute-start) | collective-permute-done | bytes 233504 | tf_op jit(solution)/shard_map/ppermute | solution.py:54
  14.9 9.6 %collective-permute-done.1 = bf16[152,768]{1,0:T(8,128)(2,1)S(1)} collective-permute-done((bf16[152,768]{1,0:T(8,128)(2,1)S(1)}, bf16[152,768]{1,0:T(8,128)(2,1)S(1)}, u32[]{:S(2)}, u32[]{:S(2)}) %collective-permute-start.1) | collective-permute-done | bytes 233504 | tf_op jit(solution)/shard_map/ppermute | solution.py:54
  29.5 6.5 %all-to-all-start = ((bf16[16,24,256]{2,1,0:T(8,128)(2,1)}), bf16[16,24,256]{2,1,0:T(8,128)(2,1)S(1)}, u32[]{:S(2)}, u32[]{:S(2)}) async-start(bf16[16,24,256]{2,1,0:T(8,128)(2,1)} %get-tuple-element.97), calls=%async_computation | async-start | bytes 393216 | tf_op jit(solution)/shard_map/all_to_all | solution.py:889
  38.6 2.4 collective-permute-start.8
  41.1 5.4 %collective-permute-done.3.xc = bf16[4,152,768]{2,1,0:T(8,128)(2,1)S(1)} collective-permute-done((bf16[4,152,768]{2,1,0:T(8,128)(2,1)S(1)}, bf16[4,152,768]{2,1,0:T(8,128)(2,1)S(1)}, u32[]{:S(2)}, u32[]{:S(2)}) %collective-permute-start.3) | collective-permute-done | bytes 933920 | tf_op jit(solution)/shard_map/ppermute | solution.py:54
  52.1 3.4 %all-to-all-start.1 = ((bf16[8,24,768]{2,1,0:T(8,128)(2,1)}), bf16[8,24,768]{2,1,0:T(8,128)(2,1)S(1)}, u32[]{:S(2)}, u32[]{:S(2)}) async-start(bf16[8,24,768]{2,1,0:T(8,128)(2,1)} %copy-done.38), calls=%async_computation.1 | async-start | bytes 589824 | tf_op jit(solution)/shard_map/all_to_all | solution.py:890
  57.6 5.1 %all-to-all-done.1 = bf16[8,24,768]{2,1,0:T(8,128)(2,1)S(1)} async-done(((bf16[8,24,768]{2,1,0:T(8,128)(2,1)}), bf16[8,24,768]{2,1,0:T(8,128)(2,1)S(1)}, u32[]{:S(2)}, u32[]{:S(2)}) %all-to-all-start.1) | async-done | bytes 294944 | tf_op jit(solution)/shard_map/all_to_all | solution.py:890
  68.7 6.5 %collective-permute-start.13 = (bf16[200,768]{1,0:T(8,128)(2,1)}, bf16[200,768]{1,0:T(8,128)(2,1)}, u32[]{:S(2)}, u32[]{:S(2)}) collective-permute-start(bf16[200,768]{1,0:T(8,128)(2,1)} %fusion.1), channel_id=1, source_target_pairs={{0,8},{8,0},{16,24},{24,16},{1,9},{9,1},{17,25},{25,17},{2,10},{10... | collective-permute-start | bytes 921608 | tf_op jit(solution)/shard_map/ppermute | solution.py:54
  76.2 11.4 %collective-permute-done.13 = bf16[200,768]{1,0:T(8,128)(2,1)} collective-permute-done((bf16[200,768]{1,0:T(8,128)(2,1)}, bf16[200,768]{1,0:T(8,128)(2,1)}, u32[]{:S(2)}, u32[]{:S(2)}) %collective-permute-start.13) | collective-permute-done | bytes 307232 | tf_op jit(solution)/shard_map/ppermute | solution.py:54
  95.2 14.8 %forward.1 = (bf16[2048,768]{1,0:T(8,128)(2,1)S(1)}, bf16[2048,768]{1,0:T(8,128)(2,1)S(1)}, bf16[192,2048]{1,0:T(8,128)(2,1)S(1)}, bf16[16,64,128]{2,1,0:T(8,128...) custom-call(s32[5]{0:T(128)S(1)} %stack.96.scal, ...), custom_call_target="tpu_custom_call" | custom-call | flops 1 | bytes 1 | tf_op jit(solution)/shard_map/forward/pallas_call | solution.py:802
  116.3 5.1 %all-to-all-start.2 = ((bf16[16,64,128]{2,1,0:T(8,128)(2,1)}), bf16[16,64,128]{2,1,0:T(8,128)(2,1)S(1)}, u32[]{:S(2)}, u32[]{:S(2)}) async-start(bf16[16,64,128]{2,1,0:T(8,128)(2,1)} %copy-done.40), calls=%async_computation.2 | async-start | bytes 524288 | tf_op jit(solution)/shard_map/all_to_all | solution.py:922
  121.4 10.2 %all-to-all-done.2.ctx = bf16[16,64,128]{2,1,0:T(8,128)(2,1)S(1)} async-done(((bf16[16,64,128]{2,1,0:T(8,128)(2,1)}), bf16[16,64,128]{2,1,0:T(8,128)(2,1)S(1)}, u32[]{:S(2)}, u32[]{:S(2)}) %all-to-all-start.2) | async-done | bytes 262176 | tf_op jit(solution)/shard_map/all_to_all | solution.py:922
  138.0 3.9 %collective-permute-done.17.refs_2_.n2_b = bf16[128,768]{1,0:T(8,128)(2,1)S(1)} collective-permute-done((bf16[128,768]{1,0:T(8,128)(2,1)S(1)}, bf16[128,768]{1,0:T(8,128)(2,1)S(1)}, u32[]{:S(2)}, u32[]{:S(2)}) %collective-permute-start.17) | collective-permute-done | bytes 196640 | tf_op jit(solution)/shard_map/ppermute | solution.py:58
  141.9 3.0 %collective-permute-done.18.refs_3_.n2_c = bf16[128,768]{1,0:T(8,128)(2,1)S(1)} collective-permute-done((bf16[128,768]{1,0:T(8,128)(2,1)S(1)}, bf16[128,768]{1,0:T(8,128)(2,1)S(1)}, u32[]{:S(2)}, u32[]{:S(2)}) %collective-permute-start.18) | collective-permute-done | bytes 196640 | tf_op jit(solution)/shard_map/ppermute | solution.py:58
  144.9 4.5 %feed.1 = (bf16[512,768]{1,0:T(8,128)(2,1)S(1)}, bf16[512,768]{1,0:T(8,128)(2,1)S(1)}, f32[128,768]{1,0:T(8,128)S(1)}, bf16[128,768]{1,0:T(8,128)(2,1)S(1)}, bf1...) custom-call(s32[2]{0:T(128)S(1)} %pad_add_fusion.refs_0_.scal, ...), custom_call_target="tpu_custom_call" | custom-call | flops 1 | bytes 1 | tf_op jit(solution)/shard_map/feed/pallas_call | solution.py:329
  153.1 2.3 collective-permute-done.21.got_b
  155.4 3.4 %collective-permute-done.22.got_c = bf16[128,768]{1,0:T(8,128)(2,1)S(1)} collective-permute-done((bf16[128,768]{1,0:T(8,128)(2,1)S(1)}, bf16[128,768]{1,0:T(8,128)(2,1)S(1)}, u32[]{:S(2)}, u32[]{:S(2)}) %collective-permute-start.22) | collective-permute-done | bytes 196640 | tf_op jit(solution)/shard_map/ppermute | solution.py:58
  163.8 3.7 %grads.1 = (bf16[4,200,768]{2,1,0:T(8,128)(2,1)}, f32[4,200,768]{2,1,0:T(8,128)S(1)}) custom-call(s32[2]{0:T(128)S(1)} %pad_add_fusion.refs_0_.scal, bf16[512,768]{1,0:T(8,128)(2,1)S(1)} %get-tuple-element.125.act, bf16[512,768]{1,0:T(8,128)(2,1)S(1)} %get-tuple-element.126.d_pre, bf16[128,768]{1,0:T(8,128)(2,1)S(1)} %get-tuple-element.108.refs_1_.n2_a, ...), custom_call_target="tpu_custom_call" | custom-call | flops 1 | bytes 1 | tf_op jit(solution)/shard_map/grads/pallas_call | solution.py:498
  169.0 5.0 %all-to-all-start.3 = ((bf16[16,64,128]{2,1,0:T(8,128)(2,1)}), bf16[16,64,128]{2,1,0:T(8,128)(2,1)S(1)}, u32[]{:S(2)}, u32[]{:S(2)}) async-start(bf16[16,64,128]{2,1,0:T(8,128)(2,1)} %copy-done.39), calls=%async_computation.3 | async-start | bytes 524288 | tf_op jit(solution)/shard_map/all_to_all | solution.py:988
  179.5 2.4 collective-permute-start.29
  181.9 2.6 all-to-all-done.3.dcr
  188.3 11.1 %shard_map.305 = (bf16[16,192,128]{2,1,0:T(8,128)(2,1)S(1)}, bf16[192,2048]{1,0:T(8,128)(2,1)S(1)}) custom-call(s32[5]{0:T(128)S(1)} %stack.96.scal, bf16[192,2048]{1,0:T(8,128)(2,1)S(1)} %copy-done.26, bf16[16,64,128]{2,1,0:T(8,128)(2,1)S(1)} %copy-done.20, f32[64,2048]{1,0:T(8,128)S(1)} %copy-done.31, f32[1,2048]{1,0:T(1,128)S(1)} %get-tuple-element.135.lse), custom_call_target="tpu_custom_call" | custom-call | flops 1 | bytes 1 | tf_op jit(solution)/shard_map/pallas_call | solution.py:824
  200.4 3.6 %collective-permute-done.29 = bf16[200,768]{1,0:T(8,128)(2,1)} collective-permute-done((bf16[200,768]{1,0:T(8,128)(2,1)}, bf16[200,768]{1,0:T(8,128)(2,1)}, u32[]{:S(2)}, u32[]{:S(2)}) %collective-permute-start.29) | collective-permute-done | bytes 307232 | tf_op jit(solution)/shard_map/ppermute | solution.py:54
  204.0 10.0 %all-to-all-start.4 = ((bf16[16,192,128]{2,1,0:T(8,128)(2,1)}), bf16[16,192,128]{2,1,0:T(8,128)(2,1)}, u32[]{:S(2)}, u32[]{:S(2)}) async-start(bf16[16,192,128]{2,1,0:T(8,128)(2,1)} %copy-done.27), calls=%async_computation.4 | async-start | bytes 1572864 | tf_op jit(solution)/shard_map/all_to_all | solution.py:996
  226.9 4.0 %heads.1 = (f32[16,24,256]{2,1,0:T(8,128)S(1)}, bf16[16,24,256]{2,1,0:T(8,128)(2,1)S(1)}) custom-call(s32[5]{0:T(128)S(1)} %stack.96.scal, bf16[192,2048]{1,0:T(8,128)(2,1)S(1)} %copy-done.24, bf16[2048,768]{1,0:T(8,128)(2,1)S(1)} %copy-done.2, bf16[2048,768]{1,0:T(8,128)(2,1)S(1)} %copy-done.4, f32[768,256]{1,0:T(8,128)S(1)} %copy-done.22, ...), custom_call_target="tpu_custom_call" | custom-call | flops 1 | bytes 1 | tf_op jit(solution)/shard_map/heads/pallas_call | solution.py:651
  234.0 4.0 %all-to-all-start.6 = ((bf16[8,24,768]{2,1,0:T(8,128)(2,1)}), bf16[8,24,768]{2,1,0:T(8,128)(2,1)S(1)}, u32[]{:S(2)}, u32[]{:S(2)}) async-start(bf16[8,24,768]{2,1,0:T(8,128)(2,1)} %pad_maximum_fusion.4), calls=%async_computation.6 | async-start | bytes 589824 | tf_op jit(solution)/shard_map/all_to_all | solution.py:1017
  248.2 4.2 %collective-permute-done.35.got_c = bf16[4,24,768]{2,1,0:T(8,128)(2,1)S(1)} collective-permute-done((bf16[4,24,768]{2,1,0:T(8,128)(2,1)S(1)}, bf16[4,24,768]{2,1,0:T(8,128)(2,1)S(1)}, u32[]{:S(2)}, u32[]{:S(2)}) %collective-permute-start.35) | collective-permute-done | bytes 147488 | tf_op jit(solution)/shard_map/ppermute | solution.py:58
  254.5 2.4 collective-permute-start.38
  257.5 5.6 %all-to-all-start.5 = ((bf16[16,24,256]{2,1,0:T(8,128)(2,1)}), bf16[16,24,256]{2,1,0:T(8,128)(2,1)S(1)}, u32[]{:S(2)}, u32[]{:S(2)}) async-start(bf16[16,24,256]{2,1,0:T(8,128)(2,1)} %add_convert_fusion), calls=%async_computation.5 | async-start | bytes 393216 | tf_op jit(solution)/shard_map/all_to_all | solution.py:1050
  266.6 3.9 %last.1 = f32[128,768]{1,0:T(8,128)} custom-call(s32[5]{0:T(128)S(1)} %stack.96.scal, bf16[16,192,128]{2,1,0:T(8,128)(2,1)} %all-to-all-done.4.d_rows, bf16[16,72,768]{2,1,0:T(8,128)(2,1)S(1)} %copy-done.14, bf16[16,72,768]{2,1,0:T(8,128)(2,1)} %collective-permute-done.31.other, bf16[128,768]{1,0:T(8,128)(2,1)S(1)} %bitcast.46, f32[128,768]{1,0:T(8,128)S(1)} %copy-done.37, ...), custom_call_target="tpu_custom_call" | custom-call | flops 1 | bytes 1 | tf_op jit(solution)/shard_map/last/pallas_call | solution.py:455
  (233 shorter events, 97.7 us)
Async XLA Ops:
  1.8 13.0 %collective-permute-start = (bf16[152,768]{1,0:T(8,128)(2,1)S(1)}, bf16[152,768]{1,0:T(8,128)(2,1)S(1)}, u32[]{:S(2)}, u32[]{:S(2)}) collective-permute-start(bf16[152,768]{1,0:T(8,128)(2,1)S(1)} %get-tuple-element.184), channel_id=1, source_target_pairs={{0,8},{8,0},{16,24},{24,16},{1,9},{9,1},{17,25},{25,17},{2,10},{10... | collective-permute-start | bytes 700424 | tf_op jit(solution)/shard_map/ppermute | solution.py:54
  4.9 19.5 %collective-permute-start.1 = (bf16[152,768]{1,0:T(8,128)(2,1)S(1)}, bf16[152,768]{1,0:T(8,128)(2,1)S(1)}, u32[]{:S(2)}, u32[]{:S(2)}) collective-permute-start(bf16[152,768]{1,0:T(8,128)(2,1)S(1)} %get-tuple-element.184), channel_id=1, source_target_pairs={{0,16},{8,24},{16,0},{24,8},{1,17},{9,25},{17,1},{25,9},{2,18},{10... | collective-permute-start | bytes 700424 | tf_op jit(solution)/shard_map/ppermute | solution.py:54
  7.5 16.9 %collective-permute-start.2 = (bf16[152,768]{1,0:T(8,128)(2,1)S(1)}, bf16[152,768]{1,0:T(8,128)(2,1)S(1)}, u32[]{:S(2)}, u32[]{:S(2)}) collective-permute-start(bf16[152,768]{1,0:T(8,128)(2,1)S(1)} %get-tuple-element.184), channel_id=1, source_target_pairs={{0,24},{8,16},{16,8},{24,0},{1,25},{9,17},{17,9},{25,1},{2,26},{10... | collective-permute-start | bytes 700424 | tf_op jit(solution)/shard_map/ppermute | solution.py:54
  24.6 21.9 %collective-permute-start.3 = (bf16[4,152,768]{2,1,0:T(8,128)(2,1)S(1)}, bf16[4,152,768]{2,1,0:T(8,128)(2,1)S(1)}, u32[]{:S(2)}, u32[]{:S(2)}) collective-permute-start(bf16[4,152,768]{2,1,0:T(8,128)(2,1)S(1)} %pad_maximum_fusion.1.zc), channel_id=1, source_target_pairs={{0,2},{2,0},{1,3},{3,1},{4,6},{6,4},{5,7},{7,5},{8,10},{10,8},{9,1... | collective-permute-start | bytes 2801672 | tf_op jit(solution)/shard_map/ppermute | solution.py:54
  26.1 23.6 %collective-permute-start.4 = (bf16[4,152,768]{2,1,0:T(8,128)(2,1)S(1)}, bf16[4,152,768]{2,1,0:T(8,128)(2,1)S(1)}, u32[]{:S(2)}, u32[]{:S(2)}) collective-permute-start(bf16[4,152,768]{2,1,0:T(8,128)(2,1)S(1)} %pad_maximum_fusion.1.zc), channel_id=1, source_target_pairs={{0,4},{4,0},{1,5},{5,1},{2,6},{6,2},{3,7},{7,3},{8,12},{12,8},{9,1... | collective-permute-start | bytes 2801672 | tf_op jit(solution)/shard_map/ppermute | solution.py:54
  29.5 22.6 %all-to-all-start = ((bf16[16,24,256]{2,1,0:T(8,128)(2,1)}), bf16[16,24,256]{2,1,0:T(8,128)(2,1)S(1)}, u32[]{:S(2)}, u32[]{:S(2)}) async-start(bf16[16,24,256]{2,1,0:T(8,128)(2,1)} %get-tuple-element.97), calls=%async_computation | async-start | bytes 393216 | tf_op jit(solution)/shard_map/all_to_all | solution.py:889
  36.7 18.9 %collective-permute-start.7 = (bf16[72,768]{1,0:T(8,128)(2,1)}, bf16[72,768]{1,0:T(8,128)(2,1)}, u32[]{:S(2)}, u32[]{:S(2)}) collective-permute-start(bf16[72,768]{1,0:T(8,128)(2,1)} %pad_maximum_fusion.6), channel_id=1, source_target_pairs={{0,8},{8,0},{16,24},{24,16},{1,9},{9,1},{17,25},{25,17},{2,10},{10... | collective-permute-start | bytes 331784 | tf_op jit(solution)/shard_map/ppermute | solution.py:54
  38.6 17.0 %collective-permute-start.8 = (bf16[72,768]{1,0:T(8,128)(2,1)}, bf16[72,768]{1,0:T(8,128)(2,1)}, u32[]{:S(2)}, u32[]{:S(2)}) collective-permute-start(bf16[72,768]{1,0:T(8,128)(2,1)} %pad_maximum_fusion.6), channel_id=1, source_target_pairs={{0,16},{8,24},{16,0},{24,8},{1,17},{9,25},{17,1},{25,9},{2,18},{10... | collective-permute-start | bytes 331784 | tf_op jit(solution)/shard_map/ppermute | solution.py:54
  41.0 14.6 %collective-permute-start.9 = (bf16[72,768]{1,0:T(8,128)(2,1)}, bf16[72,768]{1,0:T(8,128)(2,1)}, u32[]{:S(2)}, u32[]{:S(2)}) collective-permute-start(bf16[72,768]{1,0:T(8,128)(2,1)} %pad_maximum_fusion.6), channel_id=1, source_target_pairs={{0,24},{8,16},{16,8},{24,0},{1,25},{9,17},{17,9},{25,1},{2,26},{10... | collective-permute-start | bytes 331784 | tf_op jit(solution)/shard_map/ppermute | solution.py:54
  48.2 14.6 %collective-permute-start.5 = (bf16[2,152,768]{2,1,0:T(8,128)(2,1)}, bf16[2,152,768]{2,1,0:T(8,128)(2,1)S(1)}, u32[]{:S(2)}, u32[]{:S(2)}) collective-permute-start(bf16[2,152,768]{2,1,0:T(8,128)(2,1)} %slice.57), channel_id=1, source_target_pairs={{0,4},{4,0},{1,5},{5,1},{2,6},{6,2},{3,7},{7,3},{8,12},{12,8},{9,1... | collective-permute-start | bytes 1400840 | tf_op jit(solution)/shard_map/ppermute | solution.py:54
  50.6 13.0 %collective-permute-start.6 = (bf16[2,152,768]{2,1,0:T(8,128)(2,1)}, bf16[2,152,768]{2,1,0:T(8,128)(2,1)}, u32[]{:S(2)}, u32[]{:S(2)}) collective-permute-start(bf16[2,152,768]{2,1,0:T(8,128)(2,1)} %slice.58), channel_id=1, source_target_pairs={{0,2},{2,0},{1,3},{3,1},{4,6},{6,4},{5,7},{7,5},{8,10},{10,8},{9,1... | collective-permute-start | bytes 1400840 | tf_op jit(solution)/shard_map/ppermute | solution.py:54
  63.6 49.8 %collective-permute-start.10 = (bf16[416,768]{1,0:T(8,128)(2,1)}, bf16[416,768]{1,0:T(8,128)(2,1)S(1)}, u32[]{:S(2)}, u32[]{:S(2)}) collective-permute-start(bf16[416,768]{1,0:T(8,128)(2,1)} %pad_maximum_fusion.2), channel_id=1, source_target_pairs={{0,2},{2,0},{4,6},{6,4},{1,3},{3,1},{5,7},{7,5},{8,10},{10,8},{12,... | collective-permute-start | bytes 1916936 | tf_op jit(solution)/shard_map/ppermute | solution.py:58
  64.9 48.6 %collective-permute-start.11 = (bf16[416,768]{1,0:T(8,128)(2,1)}, bf16[416,768]{1,0:T(8,128)(2,1)S(1)}, u32[]{:S(2)}, u32[]{:S(2)}) collective-permute-start(bf16[416,768]{1,0:T(8,128)(2,1)} %pad_maximum_fusion.2), channel_id=1, source_target_pairs={{0,4},{2,6},{4,0},{6,2},{1,5},{3,7},{5,1},{7,3},{8,12},{10,14},{12... | collective-permute-start | bytes 1916936 | tf_op jit(solution)/shard_map/ppermute | solution.py:58
  65.9 47.5 %collective-permute-start.12 = (bf16[416,768]{1,0:T(8,128)(2,1)}, bf16[416,768]{1,0:T(8,128)(2,1)}, u32[]{:S(2)}, u32[]{:S(2)}) collective-permute-start(bf16[416,768]{1,0:T(8,128)(2,1)} %pad_maximum_fusion.2), channel_id=1, source_target_pairs={{0,6},{2,4},{4,2},{6,0},{1,7},{3,5},{5,3},{7,1},{8,14},{10,12},{12... | collective-permute-start | bytes 1916936 | tf_op jit(solution)/shard_map/ppermute | solution.py:58
  68.7 18.9 %collective-permute-start.13 = (bf16[200,768]{1,0:T(8,128)(2,1)}, bf16[200,768]{1,0:T(8,128)(2,1)}, u32[]{:S(2)}, u32[]{:S(2)}) collective-permute-start(bf16[200,768]{1,0:T(8,128)(2,1)} %fusion.1), channel_id=1, source_target_pairs={{0,8},{8,0},{16,24},{24,16},{1,9},{9,1},{17,25},{25,17},{2,10},{10... | collective-permute-start | bytes 921608 | tf_op jit(solution)/shard_map/ppermute | solution.py:54
  75.2 38.2 %collective-permute-start.14 = (bf16[200,768]{1,0:T(8,128)(2,1)}, bf16[200,768]{1,0:T(8,128)(2,1)}, u32[]{:S(2)}, u32[]{:S(2)}) collective-permute-start(bf16[200,768]{1,0:T(8,128)(2,1)} %fusion.1), channel_id=1, source_target_pairs={{0,16},{8,24},{16,0},{24,8},{1,17},{9,25},{17,1},{25,9},{2,18},{10... | collective-permute-start | bytes 921608 | tf_op jit(solution)/shard_map/ppermute | solution.py:54
  87.6 25.8 %collective-permute-start.15 = (bf16[200,768]{1,0:T(8,128)(2,1)}, bf16[200,768]{1,0:T(8,128)(2,1)}, u32[]{:S(2)}, u32[]{:S(2)}) collective-permute-start(bf16[200,768]{1,0:T(8,128)(2,1)} %fusion.1), channel_id=1, source_target_pairs={{0,24},{8,16},{16,8},{24,0},{1,25},{9,17},{17,9},{25,1},{2,26},{10... | collective-permute-start | bytes 921608 | tf_op jit(solution)/shard_map/ppermute | solution.py:54
  115.7 29.2 %collective-permute-start.20 = (bf16[4,200,768]{2,1,0:T(8,128)(2,1)S(1)}, bf16[4,200,768]{2,1,0:T(8,128)(2,1)}, u32[]{:S(2)}, u32[]{:S(2)}) collective-permute-start(bf16[4,200,768]{2,1,0:T(8,128)(2,1)S(1)} %pad_maximum_fusion.refs_9_), channel_id=1, source_target_pairs={{0,1},{1,0},{2,3},{3,2},{4,5},{5,4},{6,7},{7,6},{8,9},{9,8},{10,11... | collective-permute-start | bytes 3686408 | tf_op jit(solution)/shard_map/ppermute | solution.py:54
  116.3 15.3 %all-to-all-start.2 = ((bf16[16,64,128]{2,1,0:T(8,128)(2,1)}), bf16[16,64,128]{2,1,0:T(8,128)(2,1)S(1)}, u32[]{:S(2)}, u32[]{:S(2)}) async-start(bf16[16,64,128]{2,1,0:T(8,128)(2,1)} %copy-done.40), calls=%async_computation.2 | async-start | bytes 524288 | tf_op jit(solution)/shard_map/all_to_all | solution.py:922
  169.0 15.5 %all-to-all-start.3 = ((bf16[16,64,128]{2,1,0:T(8,128)(2,1)}), bf16[16,64,128]{2,1,0:T(8,128)(2,1)S(1)}, u32[]{:S(2)}, u32[]{:S(2)}) async-start(bf16[16,64,128]{2,1,0:T(8,128)(2,1)} %copy-done.39), calls=%async_computation.3 | async-start | bytes 524288 | tf_op jit(solution)/shard_map/all_to_all | solution.py:988
  177.5 22.8 %collective-permute-start.28 = (bf16[200,768]{1,0:T(8,128)(2,1)}, bf16[200,768]{1,0:T(8,128)(2,1)}, u32[]{:S(2)}, u32[]{:S(2)}) collective-permute-start(bf16[200,768]{1,0:T(8,128)(2,1)} %get-tuple-element.129), channel_id=1, source_target_pairs={{0,8},{8,0},{16,24},{24,16},{1,9},{9,1},{17,25},{25,17},{2,10},{10... | collective-permute-start | bytes 921608 | tf_op jit(solution)/shard_map/ppermute | solution.py:54
  179.5 24.6 %collective-permute-start.29 = (bf16[200,768]{1,0:T(8,128)(2,1)}, bf16[200,768]{1,0:T(8,128)(2,1)}, u32[]{:S(2)}, u32[]{:S(2)}) collective-permute-start(bf16[200,768]{1,0:T(8,128)(2,1)} %get-tuple-element.130), channel_id=1, source_target_pairs={{0,16},{8,24},{16,0},{24,8},{1,17},{9,25},{17,1},{25,9},{2,18},{10... | collective-permute-start | bytes 921608 | tf_op jit(solution)/shard_map/ppermute | solution.py:54
  181.8 22.2 %collective-permute-start.30 = (bf16[200,768]{1,0:T(8,128)(2,1)}, bf16[200,768]{1,0:T(8,128)(2,1)}, u32[]{:S(2)}, u32[]{:S(2)}) collective-permute-start(bf16[200,768]{1,0:T(8,128)(2,1)} %get-tuple-element.131), channel_id=1, source_target_pairs={{0,24},{8,16},{16,8},{24,0},{1,25},{9,17},{17,9},{25,1},{2,26},{10... | collective-permute-start | bytes 921608 | tf_op jit(solution)/shard_map/ppermute | solution.py:54
  204.0 29.9 %all-to-all-start.4 = ((bf16[16,192,128]{2,1,0:T(8,128)(2,1)}), bf16[16,192,128]{2,1,0:T(8,128)(2,1)}, u32[]{:S(2)}, u32[]{:S(2)}) async-start(bf16[16,192,128]{2,1,0:T(8,128)(2,1)} %copy-done.27), calls=%async_computation.4 | async-start | bytes 1572864 | tf_op jit(solution)/shard_map/all_to_all | solution.py:996
  214.0 52.5 %collective-permute-start.31 = (bf16[16,72,768]{2,1,0:T(8,128)(2,1)}, bf16[16,72,768]{2,1,0:T(8,128)(2,1)}, u32[]{:S(2)}, u32[]{:S(2)}) collective-permute-start(bf16[16,72,768]{2,1,0:T(8,128)(2,1)} %copy-done.13), channel_id=1, source_target_pairs={{0,1},{1,0},{2,3},{3,2},{4,5},{5,4},{6,7},{7,6},{8,9},{9,8},{10,11... | collective-permute-start | bytes 5308424 | tf_op jit(solution)/shard_map/ppermute | solution.py:54
  218.1 22.4 %collective-permute-start.33 = (bf16[16,24,768]{2,1,0:T(8,128)(2,1)}, bf16[16,24,768]{2,1,0:T(8,128)(2,1)}, u32[]{:S(2)}, u32[]{:S(2)}) collective-permute-start(bf16[16,24,768]{2,1,0:T(8,128)(2,1)} %get-tuple-element.161), channel_id=1, source_target_pairs={{0,1},{1,0},{2,3},{3,2},{4,5},{5,4},{6,7},{7,6},{8,9},{9,8},{10,11... | collective-permute-start | bytes 1769480 | tf_op jit(solution)/shard_map/ppermute | solution.py:54
  218.5 19.5 %collective-permute-start.25 = (bf16[128,768]{1,0:T(8,128)(2,1)}, bf16[128,768]{1,0:T(8,128)(2,1)}, u32[]{:S(2)}, u32[]{:S(2)}) collective-permute-start(bf16[128,768]{1,0:T(8,128)(2,1)} %copy-done.53), channel_id=1, source_target_pairs={{0,2},{2,0},{4,6},{6,4},{1,3},{3,1},{5,7},{7,5},{8,10},{10,8},{12,... | collective-permute-start | bytes 589832 | tf_op jit(solution)/shard_map/ppermute | solution.py:58
  220.4 18.1 %collective-permute-start.26 = (bf16[128,768]{1,0:T(8,128)(2,1)}, bf16[128,768]{1,0:T(8,128)(2,1)}, u32[]{:S(2)}, u32[]{:S(2)}) collective-permute-start(bf16[128,768]{1,0:T(8,128)(2,1)} %copy-done.52), channel_id=1, source_target_pairs={{0,4},{2,6},{4,0},{6,2},{1,5},{3,7},{5,1},{7,3},{8,12},{10,14},{12... | collective-permute-start | bytes 589832 | tf_op jit(solution)/shard_map/ppermute | solution.py:58
  221.9 16.6 %collective-permute-start.27 = (bf16[128,768]{1,0:T(8,128)(2,1)}, bf16[128,768]{1,0:T(8,128)(2,1)}, u32[]{:S(2)}, u32[]{:S(2)}) collective-permute-start(bf16[128,768]{1,0:T(8,128)(2,1)} %copy-done.51), channel_id=1, source_target_pairs={{0,6},{2,4},{4,2},{6,0},{1,7},{3,5},{5,3},{7,1},{8,14},{10,12},{12... | collective-permute-start | bytes 589832 | tf_op jit(solution)/shard_map/ppermute | solution.py:58
  234.0 23.5 %all-to-all-start.6 = ((bf16[8,24,768]{2,1,0:T(8,128)(2,1)}), bf16[8,24,768]{2,1,0:T(8,128)(2,1)S(1)}, u32[]{:S(2)}, u32[]{:S(2)}) async-start(bf16[8,24,768]{2,1,0:T(8,128)(2,1)} %pad_maximum_fusion.4), calls=%async_computation.6 | async-start | bytes 589824 | tf_op jit(solution)/shard_map/all_to_all | solution.py:1017
  253.0 12.9 %collective-permute-start.37 = (bf16[24,768]{1,0:T(8,128)(2,1)S(1)}, bf16[24,768]{1,0:T(8,128)(2,1)S(1)}, u32[]{:S(2)}, u32[]{:S(2)}) collective-permute-start(bf16[24,768]{1,0:T(8,128)(2,1)S(1)} %get-tuple-element.167), channel_id=1, source_target_pairs={{0,8},{8,0},{16,24},{24,16},{1,9},{9,1},{17,25},{25,17},{2,10},{10... | collective-permute-start | bytes 110600 | tf_op jit(solution)/shard_map/ppermute | solution.py:54
  257.5 13.8 %all-to-all-start.5 = ((bf16[16,24,256]{2,1,0:T(8,128)(2,1)}), bf16[16,24,256]{2,1,0:T(8,128)(2,1)S(1)}, u32[]{:S(2)}, u32[]{:S(2)}) async-start(bf16[16,24,256]{2,1,0:T(8,128)(2,1)} %add_convert_fusion), calls=%async_computation.5 | async-start | bytes 393216 | tf_op jit(solution)/shard_map/all_to_all | solution.py:1050
  (80 other events, 845.5 us)

commit v3 on v0

--- a/solution.py
+++ b/solution.py
@@ -1,12 +1,25 @@
+import functools
+
 import jax
 import jax.numpy as jnp
 from jax import lax
+from jax.experimental import pallas as pl
+from jax.experimental.pallas import tpu as pltpu
+from jax.sharding import Mesh
 from jax.sharding import PartitionSpec as P
 
 HD = 64
-
-
 EPS = 1e-05
+LOG2E = 1.4426950408889634
+SEQ = ("z", "y", "x")
+ALL = SEQ + ("batch",)
+WIDE = 4 * HD
+LIMIT = 58
+F32 = jnp.float32
+BF16 = jnp.bfloat16
+NN = ((1,), (0,))
+NT = ((1,), (1,))
+TN = ((0,), (0,))
 
 
 def normalize(values):
@@ -18,15 +31,794 @@
 
 
 def norm_backward(grad_out, normed, factor, gain):
-    grad_gain = jnp.sum(grad_out * normed, axis=0)
-    grad_shift = jnp.sum(grad_out, axis=0)
-    scaled = grad_out * gain.astype(jnp.float32)
+    grad_gain = jnp.sum(grad_out * normed, axis=0, keepdims=True)
+    grad_shift = jnp.sum(grad_out, axis=0, keepdims=True)
+    scaled = grad_out * gain.astype(F32)
     grad_in = factor * (
         scaled
         - jnp.mean(scaled, axis=-1, keepdims=True)
         - normed * jnp.mean(scaled * normed, axis=-1, keepdims=True)
     )
     return (grad_in, grad_gain, grad_shift)
+
+
+def dot(left, right, dims=NN):
+    return lax.dot_general(left, right, (dims, ((), ())), preferred_element_type=F32)
+
+
+def swap(value, axis, step=1):
+    size = lax.axis_size(axis)
+    return lax.ppermute(value, axis, [(i, i ^ step) for i in range(size)])
+
+
+def swap_plane(value, step):
+    return lax.ppermute(value, ("y", "x"), [(i, i ^ step) for i in range(4)])
+
+
+def after(value, *others):
+    return lax.optimization_barrier((value,) + others)[0]
+
+
+def split(length):
+    return 512 if length % 512 == 0 else length
+
+
+SMALL = pl.CostEstimate(flops=1, bytes_accessed=1, transcendentals=0)
+SMEM_SPEC = pl.BlockSpec(memory_space=pltpu.SMEM)
+HBM_SPEC = pl.BlockSpec(memory_space=pltpu.HBM)
+
+
+def full_block(shape):
+    zeros = (0,) * len(shape)
+    return pl.BlockSpec(shape, lambda i: zeros, pipeline_mode=pl.Buffered(1))
+
+
+def like(shape, dtype):
+    return jax.ShapeDtypeStruct(shape, dtype)
+
+
+def once(name, kernel, args, outs, scratch=(), limit=LIMIT, left=()):
+    in_specs = [SMEM_SPEC if a.dtype == jnp.int32 else full_block(a.shape) for a in args]
+    out_specs = [HBM_SPEC if i in left else full_block(o.shape) for i, o in enumerate(outs)]
+    return pl.pallas_call(
+        kernel,
+        grid=(1,),
+        out_shape=tuple(outs),
+        in_specs=in_specs,
+        out_specs=tuple(out_specs),
+        scratch_shapes=list(scratch),
+        compiler_params=pltpu.CompilerParams(vmem_limit_bytes=limit << 20),
+        cost_estimate=SMALL,
+        name=name,
+    )(*args)
+
+
+PLACE, PREFIX, CORE, FLAT, LINE = range(5)
+
+
+def rank_of(scal, k, d, other):
+    line = jnp.bitwise_xor(scal[LINE], k)
+    flat = jnp.bitwise_xor(scal[FLAT], d)
+    return (line * 4 + flat) * 2 + jnp.bitwise_xor(scal[CORE], other)
+
+
+def rows_at(index, size):
+    return pl.ds(pl.multiple_of(index * size, size), size)
+
+
+def square_pieces(wq, other):
+    outer = other.shape[0] // 4
+    for d in range(4):
+        for k in range(outer):
+            yield (k, d, 0, wq[d].at[k])
+            yield (k, d, 1, other.at[d * outer + k])
+
+
+def pack_kernel(lines, heads, scal, token, w_out, w_up, w_q, w_k, w_v, *refs):
+    vectors, (up_own, out_b, out_c, out_d, send) = (refs[:8], refs[8:])
+    wide = w_up.shape[1] // (4 * lines)
+    rows, cut = (token.shape[0], w_up.shape[0])
+    for out in (out_b, out_c, out_d):
+        out[:rows, :] = token[...]
+        out[rows : rows + cut, :] = w_out[...]
+    for z in range(lines):
+        pieces = [w_up[:, (z * 4 + t) * wide : (z * 4 + t + 1) * wide] for t in range(4)]
+        for k, (out, first) in enumerate(
+            ((up_own, 0), (out_b, rows + cut), (out_c, rows + cut), (out_d, rows + cut))
+        ):
+            target = jnp.bitwise_xor(scal[FLAT], k)
+            value = pieces[0]
+            for t in range(1, 4):
+                value = jnp.where(target == t, pieces[t], value)
+            out[first : first + cut, z * wide : (z + 1) * wide] = value
+    lane = jnp.concatenate([ref[...].astype(F32) for ref in vectors], axis=0)
+    lane = jnp.concatenate([lane, jnp.zeros((8, 2 * HD - cut), F32)], axis=1)
+    vec = jnp.concatenate([jnp.transpose(lane)[:cut], jnp.zeros((cut, HD - 8), F32)], axis=1)
+    vec = vec.astype(BF16)
+    for h in range(send.shape[0]):
+        for i, w in enumerate((w_q, w_k, w_v)):
+            if h < heads:
+                piece = w[:, h * HD : (h + 1) * HD]
+            else:
+                piece = jnp.zeros((cut, HD), BF16)
+            send[h, :, i * HD : (i + 1) * HD] = piece
+        send[h, :, 3 * HD :] = vec
+
+
+def forward_kernel(
+    heads, scal, ahead, own_b, own_c, own_d, zc, xc, yc, xya, xyb, w,
+    n1_out, n0_out, qkvt, ctxc, ctxt, lse, rows_out, wt_out, wo_out,
+    n1, n0, k_s, w_s, sems,
+):
+    place, prefix = (scal[PLACE], scal[PREFIX])
+    outer = zc.shape[0] + 1
+    length, width = n1.shape
+    rows = length // (4 * outer)
+    cut = w.shape[2]
+    blk = split(length)
+    copies = []
+    near = ((ahead, 0), (own_b, 1), (own_c, 2), (own_d, 3))
+    along = ((zc, 1, 0), (xc, 1, 1), (yc, 1, 2), (xya, 1, 3), (xyb, outer // 2 + 1, 3))
+    for src, d in near:
+        pair = (src.at[rows : rows + cut, :], wo_out.at[d * outer])
+        copies.append(pltpu.make_async_copy(*pair, sems.at[2 + len(copies)]))
+    for src, k, d in along:
+        target = wo_out.at[d * outer + k : d * outer + k + src.shape[0]]
+        copies.append(pltpu.make_async_copy(src.at[:, rows:, :], target, sems.at[2 + len(copies)]))
+    for copy in copies:
+        copy.start()
+    head = jnp.minimum(place, heads - 1)
+    for b in range(2):
+        for i in range(w.shape[1]):
+            at = (2 * i + b) * cut
+            w_s[at : at + cut, :] = w[b, i].astype(F32)
+    turned = jnp.transpose(w_s[...])
+    wt_out[...] = turned[: 3 * HD].astype(BF16)
+    rows_in = turned[3 * HD : 3 * HD + 8]
+    rows_out[...] = rows_in
+    gain = rows_in[0:1]
+    shift = rows_in[1:2]
+
+    def norm_rows(value, k, d):
+        normed, _ = normalize(value.astype(F32))
+        here = rows_at(jnp.bitwise_xor(place, k * 4 + d), rows)
+        n0[here, :] = normed.astype(BF16)
+        n1[here, :] = (normed * gain + shift).astype(BF16)
+
+    for src, d in near:
+        norm_rows(src[:rows, :], 0, d)
+    for src, first, d in along:
+
+        def one(k, carry, src=src, first=first, d=d):
+            norm_rows(src[k, :rows, :], first + k, d)
+            return carry
+
+        lax.fori_loop(0, src.shape[0], one, 0)
+    for i, (src, dst) in enumerate(((n1, n1_out), (n0, n0_out))):
+        copy = pltpu.make_async_copy(src, dst, sems.at[i])
+        copy.start()
+        copies.append(copy)
+    bias_q = w_s[rows_at(head, HD), 3 * HD + 2 : 3 * HD + 3]
+    bias_v = w_s[rows_at(head, HD), 3 * HD + 3 : 3 * HD + 4]
+    for i in range(length // blk):
+        sl = slice(i * blk, (i + 1) * blk)
+        part = dot(wt_out[...], n1[sl, :], NT)
+        k_part = part[HD : 2 * HD].astype(BF16)
+        qkvt[:HD, sl] = (part[:HD] + bias_q).astype(BF16)
+        qkvt[HD : 2 * HD, sl] = k_part
+        qkvt[2 * HD :, sl] = (part[2 * HD :] + bias_v).astype(BF16)
+        k_s[sl, :] = jnp.transpose(k_part.astype(F32)).astype(BF16)
+    scale = 0.125 * LOG2E
+
+    def one_query(i, carry):
+        first = pl.multiple_of(i * blk, blk)
+        q_now = qkvt[:HD, pl.ds(first, blk)]
+
+        def step(masked, j, state):
+            top, total, acc = state
+            start = pl.multiple_of(j * blk, blk)
+            scores = dot(k_s[pl.ds(start, blk), :], q_now) * scale
+            if masked:
+                key = start + lax.broadcasted_iota(jnp.int32, (blk, blk), 0)
+                query = first + lax.broadcasted_iota(jnp.int32, (blk, blk), 1)
+                scores = jnp.where((key <= query) | (key < prefix), scores, -1e30)
+            new_top = jnp.maximum(top, jnp.max(scores, axis=0, keepdims=True))
+            prob = jnp.exp2(scores - new_top)
+            fade = jnp.exp2(top - new_top)
+            total = total * fade + jnp.sum(prob, axis=0, keepdims=True)
+            acc = acc * fade + dot(qkvt[2 * HD :, pl.ds(start, blk)], prob.astype(BF16))
+            return (new_top, total, acc)
+
+        state = (
+            jnp.full((1, blk), -1e30, F32),
+            jnp.zeros((1, blk), F32),
+            jnp.zeros((HD, blk), F32),
+        )
+        full = jnp.maximum(prefix // blk, i)
+        needed = jnp.maximum((prefix + blk - 1) // blk, i + 1)
+        state = lax.fori_loop(0, full, functools.partial(step, False), state)
+        top, total, acc = lax.fori_loop(full, needed, functools.partial(step, True), state)
+        out = acc / total
+        ctxt[:, pl.ds(first, blk)] = out
+        lse[:, pl.ds(first, blk)] = top + jnp.log2(total)
+        for r in range(blk // rows):
+            ctxc[i * (blk // rows) + r] = out[:, r * rows : (r + 1) * rows].astype(BF16)
+        return carry
+
+    lax.fori_loop(0, length // blk, one_query, 0)
+    for copy in copies:
+        copy.wait()
+
+
+def backward_kernel(
+    scal, qkvt, dcr, ctxt, lse, dchunk, dall, q_s, k_s, v_s, dc_s, dct_s, del_s, dq_s, dk_s, dv_s
+):
+    prefix = scal[PREFIX]
+    rows = dcr.shape[2]
+    length = qkvt.shape[1]
+    blk = split(length)
+    count = length // blk
+    for i in range(count):
+        sl = slice(i * blk, (i + 1) * blk)
+        turned = jnp.transpose(qkvt[:, sl].astype(F32)).astype(BF16)
+        q_s[sl, :] = turned[:, :HD]
+        k_s[sl, :] = turned[:, HD : 2 * HD]
+        v_s[sl, :] = turned[:, 2 * HD :]
+    for i in range(length // rows):
+        sl = slice(i * rows, (i + 1) * rows)
+        dct_s[:, sl] = dcr[i]
+        dc_s[sl, :] = jnp.transpose(dcr[i].astype(F32)).astype(BF16)
+    del_s[...] = jnp.sum(dct_s[...].astype(F32) * ctxt[...], axis=0, keepdims=True)
+    dq_s[...] = jnp.zeros_like(dq_s)
+    scale = 0.125 * LOG2E
+
+    def one_key(j, carry):
+        start = pl.multiple_of(j * blk, blk)
+        dk_s[...] = jnp.zeros_like(dk_s)
+        dv_s[...] = jnp.zeros_like(dv_s)
+
+        def step(masked, i, inner):
+            first = pl.multiple_of(i * blk, blk)
+            here = pl.ds(first, blk)
+            scores = dot(k_s[pl.ds(start, blk), :], qkvt[:HD, here]) * scale
+            prob = jnp.exp2(scores - lse[:, here])
+            if masked:
+                key = start + lax.broadcasted_iota(jnp.int32, (blk, blk), 0)
+                query = first + lax.broadcasted_iota(jnp.int32, (blk, blk), 1)
+                prob = jnp.where((key <= query) | (key < prefix), prob, 0.0)
+            d_prob = dot(v_s[pl.ds(start, blk), :], dct_s[:, here])
+            d_score = (prob * (d_prob - del_s[:, here])).astype(BF16)
+            dv_s[...] += dot(prob.astype(BF16), dc_s[here, :])
+            dk_s[...] += dot(d_score, q_s[here, :])
+            dq_s[:, here] += dot(qkvt[HD : 2 * HD, pl.ds(start, blk)], d_score)
+            return inner
+
+        begin = jnp.where(start < prefix, 0, j)
+        middle = jnp.where(start + blk <= prefix, begin, j + 1)
+        lax.fori_loop(begin, middle, functools.partial(step, True), 0)
+        lax.fori_loop(middle, count, functools.partial(step, False), 0)
+        d_key = jnp.transpose(dk_s[...] * 0.125).astype(BF16)
+        d_value = jnp.transpose(dv_s[...]).astype(BF16)
+        dall[HD : 2 * HD, pl.ds(start, blk)] = d_key
+        dall[2 * HD :, pl.ds(start, blk)] = d_value
+        for r in range(blk // rows):
+            at = j * (blk // rows) + r
+            dchunk[at, HD : 2 * HD, :] = d_key[:, r * rows : (r + 1) * rows]
+            dchunk[at, 2 * HD :, :] = d_value[:, r * rows : (r + 1) * rows]
+        return carry
+
+    lax.fori_loop(0, count, one_key, 0)
+    for i in range(count):
+        sl = slice(i * blk, (i + 1) * blk)
+        d_query = (dq_s[:, sl] * 0.125).astype(BF16)
+        dall[:HD, sl] = d_query
+        for r in range(blk // rows):
+            dchunk[i * (blk // rows) + r, :HD, :] = d_query[:, r * rows : (r + 1) * rows]
+
+
+def stacked(pieces, first, last):
+    return jnp.concatenate([piece[first:last, :].astype(F32) for piece in pieces]).astype(BF16)
+
+
+def out_pieces(own, other):
+    outer = own.shape[0] // 4
+    return [
+        (i % outer, i // outer, core, ref.at[i])
+        for core, ref in ((0, own), (1, other))
+        for i in range(own.shape[0])
+    ]
+
+
+def middle_kernel(heads, scal, ctx, own, other, token, rows_in, middle, norm_two, plain, moved):
+    pieces = out_pieces(own, other)
+    cut = own.shape[1]
+    plain[...] = ctx[:heads].reshape(plain.shape).astype(F32)
+    for n, (k, d, core, _) in enumerate(pieces):
+        moved[n * cut : (n + 1) * cut, :] = plain[rows_at(rank_of(scal, k, d, core), cut), :]
+    turned = jnp.transpose(moved[...]).astype(BF16)
+    product = dot(turned, stacked([p[3] for p in pieces], 0, cut))
+    value = token[...].astype(F32) + product + rows_in[4:5, :]
+    middle[...] = value
+    normed, _ = normalize(value)
+    norm_two[...] = (normed * rows_in[5:6, :] + rows_in[6:7, :]).astype(BF16)
+
+
+def feed_kernel(
+    scal, n2_a, n2_b, n2_c, n2_d, dy_a, dy_b, dy_c, dy_d, ffz, ffc,
+    out_keep, out_b, out_c, out_d, dn_keep, dn_b, dn_c, dn_d, send, keep,
+    n2, dy, down, up, act, d_pre, down_s, up_s, bias,
+):
+    outer = ffz.shape[0]
+    cut = (ffz.shape[1] - 8) // 8
+    half = 4 * cut
+    sources = [(src, k, core) for core, src in ((0, ffz), (1, ffc)) for k in range(outer)]
+
+    def block_of(k, core):
+        line = jnp.bitwise_xor(scal[LINE], k)
+        return line * 2 + jnp.bitwise_xor(scal[CORE], core)
+
+    rows = []
+    for src, k, core in sources:
+        down[rows_at(block_of(k, core), half), :] = src[k, :half, :]
+        for d in range(4):
+            here = rows_at(rank_of(scal, k, d, core), cut)
+            up_s[here, :] = src[k, half + d * cut : half + (d + 1) * cut, :].astype(F32)
+        rows.append((block_of(k, core), src[k, 2 * half :, :half].astype(F32)[:1]))
+    up[...] = up_s[...].astype(BF16)
+    for q in range(2 * outer):
+        bias[:, q * half : (q + 1) * half] = sum(jnp.where(at == q, row, 0.0) for at, row in rows)
+    count = n2_a.shape[0]
+    for i, piece in enumerate((n2_a, n2_b, n2_c, n2_d)):
+        n2[i * count : (i + 1) * count, :] = piece[...]
+    for i, piece in enumerate((dy_a, dy_b, dy_c, dy_d)):
+        dy[i * count : (i + 1) * count, :] = piece[piece.shape[0] - count :, :]
+    tile = 256
+    for c in range(down.shape[0] // tile):
+        sl = slice(c * tile, (c + 1) * tile)
+        pre = dot(n2[...], up[:, sl]) + bias[:, sl]
+        cdf = 0.5 * (1.0 + lax.erf(pre * 0.7071067811865476))
+        act[:, sl] = (pre * cdf).astype(BF16)
+        slope = cdf + pre * jnp.exp(-0.5 * pre * pre) * 0.3989422804014327
+        d_pre[:, sl] = (dot(dy[...], down[sl, :], NT) * slope).astype(BF16)
+    back = dot(d_pre[...], up[...], NT)
+    for i, ref in enumerate((dn_keep, dn_b, dn_c, dn_d)):
+        ref[...] = back[i * count : (i + 1) * count].astype(ref.dtype)
+    out = dot(act[...], down[...])
+    for i, ref in enumerate((out_keep, out_b, out_c, out_d)):
+        ref[...] = out[i * count : (i + 1) * count].astype(ref.dtype)
+    down_s[...] = dot(act[...], dy[...], TN)
+    up_s[...] = dot(n2[...], d_pre[...], TN)
+    total = jnp.sum(d_pre[...].astype(F32), axis=0, keepdims=True)
+    width = keep.shape[2]
+    for k in range(outer):
+        for core, ref in ((0, keep), (1, send)):
+            at = block_of(k, core)
+            ref[k, :half, :] = down_s[rows_at(at, half), :].astype(ref.dtype)
+            for t in range(4):
+                line = jnp.bitwise_xor(scal[LINE], k)
+                rank = (line * 4 + t) * 2 + jnp.bitwise_xor(scal[CORE], core)
+                here = slice(half + t * cut, half + (t + 1) * cut)
+                ref[k, here, :] = up_s[rows_at(rank, cut), :].astype(ref.dtype)
+            part = sum(
+                jnp.where(at == q, total[:, q * half : (q + 1) * half], 0.0)
+                for q in range(2 * outer)
+            )
+            part = jnp.concatenate([part, jnp.zeros((1, width - half), F32)], axis=1)
+            ref[k, 2 * half :, :] = jnp.broadcast_to(part, (8, width)).astype(ref.dtype)
+
+
+def turn_kernel(
+    heads, scal, keep, got_b, got_c, got_d, middle, d_out, own, other, rows_in, ctx,
+    d_middle, d_branch_out, d_ctx, sums, wo_keep, wo_send, plain, full,
+):
+    d_norm = keep[...] + (got_b[...].astype(F32) + got_c[...].astype(F32)) + got_d[...].astype(F32)
+    normed, factor = normalize(middle[...])
+    grad_in, grad_gain, grad_shift = norm_backward(d_norm, normed, factor, rows_in[5:6, :])
+    grad_up = d_out[...].astype(F32)
+    total = grad_up + grad_in
+    low = total.astype(BF16)
+    d_middle[...] = total
+    d_branch_out[...] = low[:8]
+    pieces = out_pieces(own, other)
+    cut = own.shape[1]
+    back = dot(stacked([p[3] for p in pieces], 0, cut), low, NT)
+    for n, (k, d, core, _) in enumerate(pieces):
+        plain[rows_at(rank_of(scal, k, d, core), cut), :] = back[n * cut : (n + 1) * cut]
+    seq, rows = (d_ctx.shape[0], d_ctx.shape[2])
+    d_ctx[:heads] = plain[...].astype(BF16).reshape(heads, HD, rows)
+    d_ctx[heads:] = jnp.zeros((seq - heads, HD, rows), BF16)
+    sums[0:1, :] = jnp.sum(low.astype(F32), axis=0, keepdims=True)
+    sums[1:2, :] = grad_gain
+    sums[2:3, :] = grad_shift
+    sums[3:4, :] = jnp.sum(grad_up, axis=0, keepdims=True)
+    sums[4:, :] = jnp.zeros((4, sums.shape[1]), F32)
+    full[...] = dot(ctx[:heads].reshape(heads * HD, rows), low).reshape(full.shape)
+    for i in range(seq):
+        wo_keep[i] = full[2 * i + scal[CORE]]
+        wo_send[i] = full[2 * i + 1 - scal[CORE]].astype(BF16)
+
+
+def fold_kernel(keep, got, own, *away):
+    for k, ref in enumerate((own,) + away):
+        ref[...] = (keep[k] + got[k].astype(F32)).astype(ref.dtype)
+
+
+def finish_kernel(scal, keep, *refs):
+    got, (wo_keep, wo_got, out_b, out_c, out_d), outs = (refs[:-13], refs[-13:-8], refs[-8:])
+    grad_down, bias, own, wo_own, away_b, away_c, away_d, total = outs
+    value = keep[...]
+    for ref in got:
+        value = value + ref[...].astype(F32)
+    total[...] = value
+    half = grad_down.shape[0]
+    cut = half // 4
+    lines = wo_own.shape[0]
+    grad_down[...] = value[:half]
+    bias[...] = value[2 * half :, :half]
+    for k, ref in enumerate((own, away_b, away_c, away_d)):
+        at = jnp.bitwise_xor(scal[FLAT], k)
+        here = pl.ds(pl.multiple_of(half + at * cut, 8), cut)
+        ref[:cut, :] = total[here, :].astype(BF16)
+        for z in range(lines):
+            part = wo_keep[4 * z + at] + wo_got[4 * z + at].astype(F32)
+            if k:
+                ref[(1 + z) * cut : (2 + z) * cut, :] = part.astype(BF16)
+            else:
+                wo_own[z] = part
+    for src, ref in ((out_b, away_b), (out_c, away_c), (out_d, away_d)):
+        ref[(1 + lines) * cut :, :] = src[...]
+
+
+def close_kernel(
+    lines, scal, own, wo_own, got_b, got_c, got_d, middle, out_keep, rows_in,
+    layer_out, grad_up, grad_out, *away,
+):
+    cut = grad_out.shape[0]
+    got = (got_b, got_c, got_d)
+    value = middle[...] + out_keep[...] + rows_in[7:8, :]
+    pieces = [own[...].astype(F32)]
+    for ref in got:
+        value = value + ref[(1 + lines) * cut :, :].astype(F32)
+        pieces.append(ref[:cut, :].astype(F32))
+    layer_out[...] = value.astype(BF16)
+    for k, out in enumerate((grad_out,) + away):
+        at = jnp.bitwise_xor(scal[LINE], k)
+        here = pl.ds(pl.multiple_of((1 + at) * cut, 8), cut)
+        part = wo_own[at]
+        for ref in got:
+            part = part + ref[here, :].astype(F32)
+        out[...] = part.astype(out.dtype)
+    wide = own.shape[1] // lines
+    for t in range(4):
+        step = jnp.bitwise_xor(scal[FLAT], t)
+        piece = pieces[0]
+        for k in range(1, 4):
+            piece = jnp.where(step == k, pieces[k], piece)
+        for z in range(lines):
+            at = (z * 4 + t) * wide
+            grad_up[:, at : at + wide] = piece[:, z * wide : (z + 1) * wide]
+
+
+def heads_kernel(heads, scal, dall, n1, n0, wt, sums, keep, send, gh, gm, cs, full):
+    step = pl.program_id(0)
+
+    @pl.when(step == 0)
+    def _():
+        gh[...] = jnp.zeros_like(gh)
+        gm[...] = jnp.zeros_like(gm)
+        cs[...] = jnp.zeros_like(cs)
+
+    gh[...] += dot(dall[...], n1[...])
+    gm[...] += dot(dall[...], n0[...])
+    cs[...] += dot(dall[...], jnp.ones((dall.shape[1], 2 * HD), BF16))
+
+    @pl.when(step == pl.num_programs(0) - 1)
+    def _():
+        place = scal[PLACE]
+        width = gh.shape[1]
+        live = place < heads
+        wide = wt[...].astype(F32)
+        gain = jnp.where(live, jnp.sum(wide * gm[...], axis=0, keepdims=True), 0.0)
+        shift = jnp.where(live, jnp.sum(wide * cs[:, :1], axis=0, keepdims=True), 0.0)
+        line = jnp.transpose(cs[...])[0:1]
+        mine = lax.broadcasted_iota(jnp.int32, (1, width), 1) // HD == place
+        b_q = jnp.where(mine, jnp.concatenate([line[:, :HD]] * heads, axis=1), 0.0)
+        b_v = jnp.where(mine, jnp.concatenate([line[:, 2 * HD :]] * heads, axis=1), 0.0)
+        vec = jnp.concatenate([gain, shift, b_q, b_v, sums[:4, :]], axis=0)
+        pad = jnp.zeros((width, HD - 8), F32)
+        block = jnp.concatenate([jnp.transpose(gh[...]), jnp.transpose(vec), pad], axis=1)
+        full[...] = block.reshape(full.shape)
+        for i in range(keep.shape[0]):
+            keep[i] = full[2 * i + scal[CORE]]
+            send[i] = full[2 * i + 1 - scal[CORE]].astype(BF16)
+
+
+def head_grads(scal, dall, n1, n0, wt, sums, heads, seq):
+    length, width = n1.shape
+    blk = split(length)
+    cut = width // (2 * seq)
+    outs = (like((seq, cut, WIDE), F32), like((seq, cut, WIDE), BF16))
+    return pl.pallas_call(
+        functools.partial(heads_kernel, heads),
+        out_shape=outs,
+        grid=(length // blk,),
+        in_specs=[
+            SMEM_SPEC,
+            pl.BlockSpec((3 * HD, blk), lambda i: (0, i)),
+            pl.BlockSpec((blk, width), lambda i: (i, 0)),
+            pl.BlockSpec((blk, width), lambda i: (i, 0)),
+            full_block(wt.shape),
+            full_block(sums.shape),
+        ],
+        out_specs=tuple(full_block(out.shape) for out in outs),
+        scratch_shapes=[
+            pltpu.VMEM((3 * HD, width), F32),
+            pltpu.VMEM((3 * HD, width), F32),
+            pltpu.VMEM((3 * HD, 2 * HD), F32),
+            pltpu.VMEM((2 * seq, cut, WIDE), F32),
+        ],
+        compiler_params=pltpu.CompilerParams(vmem_limit_bytes=LIMIT << 20),
+        cost_estimate=SMALL,
+        name="heads",
+    )(scal, dall, n1, n0, wt, sums)
+
+
+def last_kernel(
+    heads, scal, d_rows, wq_a, wq_b, wq_c, wq_d, other, token, d_middle, rows_in, grad_tokens, plain
+):
+    cut = other.shape[1] // 3
+    pieces = list(square_pieces((wq_a, wq_b, wq_c, wq_d), other))
+    total = 0.0
+    for i in range(3):
+        part = jnp.concatenate(
+            [d_rows[h, i * HD : (i + 1) * HD, :].astype(F32) for h in range(heads)], axis=0
+        )
+        weights = stacked([p[3] for p in pieces], i * cut, (i + 1) * cut)
+        total = total + dot(weights, part.astype(BF16))
+    for n, (k, d, core, _) in enumerate(pieces):
+        plain[rows_at(rank_of(scal, k, d, core), cut), :] = total[n * cut : (n + 1) * cut]
+    normed, factor = normalize(token[...].astype(F32))
+    grad_in, _, _ = norm_backward(jnp.transpose(plain[...]), normed, factor, rows_in[0:1, :])
+    grad_tokens[...] = d_middle[...] + grad_in
+
+
+def unpack_kernel(heads, got, g_q, g_k, g_v, vec):
+    for i, out in enumerate((g_q, g_k, g_v)):
+        for h in range(heads):
+            out[:, h * HD : (h + 1) * HD] = got[h, :, i * HD : (i + 1) * HD].astype(F32)
+    total = got[0, :, 2 * HD :].astype(F32)
+    for s in range(1, got.shape[0]):
+        total = total + got[s, :, 2 * HD :].astype(F32)
+    cut = total.shape[0]
+    total = jnp.concatenate([total, jnp.zeros((2 * HD - cut, 2 * HD), F32)], axis=0)
+    vec[...] = jnp.transpose(total)[HD : HD + 8, :cut]
+
+
+def body(
+    tokens, cotangent, prefix_len, gain_one, shift_one, w_query, b_query, w_key, w_value, b_value,
+    w_output, b_output, gain_two, shift_two, w_up, b_up, w_down, b_down,
+):
+    outer = lax.axis_size("z")
+    seq = 4 * outer
+    token, d_out = (tokens[0], cotangent[0])
+    rows, width = token.shape
+    length = seq * rows
+    heads = width // HD
+    cut = w_query.shape[0]
+    half = w_down.shape[0]
+    local = w_up.shape[1] // 4
+    flat = lax.axis_index(("y", "x"))
+    places = (lax.axis_index(SEQ), prefix_len[0], lax.axis_index("batch"), flat, lax.axis_index("z"))
+    scal = jnp.stack(places).astype(jnp.int32)
+
+    ahead = jnp.concatenate([token, w_output])
+    zc = jnp.stack([swap(ahead, "z", k) for k in range(1, outer)])
+    vectors = (
+        gain_one, shift_one, b_query, b_value, b_output, gain_two, shift_two, b_down,
+    )
+    vectors = [value[None] for value in vectors]
+    up_own, *first, send = once(
+        "pack",
+        functools.partial(pack_kernel, outer, heads),
+        (scal, token, w_output, w_up, w_query, w_key, w_value, *vectors),
+        [like((cut, local), BF16)]
+        + [like((rows + 2 * cut, width), BF16)] * 3
+        + [like((seq, cut, WIDE), BF16)],
+    )
+    first = [swap_plane(part, k + 1) for k, part in enumerate(first)]
+    zc = after(zc, *first)
+    xc = swap(zc, "x")
+    yc = swap(zc, "y")
+    head_w = lax.all_to_all(after(send, zc), SEQ, split_axis=0, concat_axis=0, tiled=True)
+    wq = after(jnp.concatenate([w_query, w_key, w_value]), zc)
+    wq_got = [swap(wq, "z", k) for k in range(1, outer)]
+    xc, yc, head_w, wq_got = lax.optimization_barrier((xc, yc, head_w, wq_got))
+    xya = swap(xc[: outer // 2], "y")
+    xyb = swap(yc[outer // 2 :], "x")
+    head_w = lax.all_gather(head_w, "batch", axis=0, tiled=False)
+
+    b_up_row = jnp.pad(b_up[None], ((0, 7), (0, width - half)))
+    ff = [w_down, up_own] + [part[rows + cut :] for part in first] + [b_up_row]
+    ff = after(jnp.concatenate(ff), head_w, xc)
+    ff_got = [swap(ff, "z", k) for k in range(1, outer)]
+    wq = after(jnp.stack([wq] + wq_got), xya, xyb)
+    wq = [wq] + [swap_plane(wq, k) for k in range(1, 3)]
+
+    norm_one, norm_raw, qkvt, ctxc, ctxt, lse, rows_in, wt, w_out_own = once(
+        "forward",
+        functools.partial(forward_kernel, heads),
+        (scal, ahead, *first, zc, xc, yc, xya, xyb, head_w),
+        [
+            like((length, width), BF16),
+            like((length, width), BF16),
+            like((3 * HD, length), BF16),
+            like((seq, HD, rows), BF16),
+            like((HD, length), F32),
+            like((1, length), F32),
+            like((8, width), F32),
+            like((3 * HD, width), BF16),
+            like((seq, cut, width), BF16),
+        ],
+        [
+            pltpu.VMEM((length, width), BF16),
+            pltpu.VMEM((length, width), BF16),
+            pltpu.VMEM((length, HD), BF16),
+            pltpu.VMEM((width, WIDE), F32),
+            pltpu.SemaphoreType.DMA((11,)),
+        ],
+        left=(0, 1, 8),
+    )
+    w_out_other = swap(w_out_own, "batch")
+    ctxc, wq, ff_got = lax.optimization_barrier((ctxc, wq, ff_got))
+    ffz = jnp.stack([ff] + ff_got)
+    dy = [d_out] + [swap_plane(after(d_out, ctxc), k) for k in range(1, 4)]
+    ctx = lax.all_to_all(ctxc, SEQ, split_axis=0, concat_axis=0, tiled=True)
+    ffc = swap(ffz, "batch")
+    dy, ctx = lax.optimization_barrier((dy, ctx))
+    middle, norm_two = once(
+        "middle",
+        functools.partial(middle_kernel, heads),
+        (scal, ctx, w_out_own, w_out_other, token, rows_in),
+        [like((rows, width), F32), like((rows, width), BF16)],
+        [pltpu.VMEM((width, rows), F32)] * 2,
+    )
+    n2 = [norm_two] + [swap_plane(norm_two, k) for k in range(1, 4)]
+
+    part = [like((rows, width), F32)] + [like((rows, width), BF16)] * 3
+    fed = once(
+        "feed",
+        feed_kernel,
+        (scal, *n2, *dy, ffz, ffc),
+        part + part + [like(ffz.shape, BF16), like(ffz.shape, F32)],
+        [
+            pltpu.VMEM((4 * rows, width), BF16),
+            pltpu.VMEM((4 * rows, width), BF16),
+            pltpu.VMEM((local, width), BF16),
+            pltpu.VMEM((width, local), BF16),
+            pltpu.VMEM((4 * rows, local), BF16),
+            pltpu.VMEM((4 * rows, local), BF16),
+            pltpu.VMEM((local, width), F32),
+            pltpu.VMEM((width, local), F32),
+            pltpu.VMEM((1, local), F32),
+        ],
+    )
+    out_keep, *out_send = fed[:4]
+    dn_keep, *dn_send = fed[4:8]
+    send, keep = fed[8:]
+    dn_got = [swap_plane(value, k + 1) for k, value in enumerate(dn_send)]
+
+    count = 2 * half + 8
+    own, *away = once(
+        "fold",
+        fold_kernel,
+        (keep, swap(send, "batch")),
+        [like((count, width), F32)] + [like((count, width), BF16)] * (outer - 1),
+    )
+    back = [swap(value, "z", k + 1) for k, value in enumerate(away)]
+    dn_keep, _ = lax.optimization_barrier((dn_keep, away))
+    d_middle, _, d_ctx, sums, wo_keep, wo_send = once(
+        "turn",
+        functools.partial(turn_kernel, heads),
+        (scal, dn_keep, *dn_got, middle, d_out, w_out_own, w_out_other, rows_in, ctx),
+        [
+            like((rows, width), F32),
+            like((8, width), BF16),
+            like((seq, HD, rows), BF16),
+            like((8, width), F32),
+            like((seq, cut, width), F32),
+            like((seq, cut, width), BF16),
+        ],
+        [pltpu.VMEM((width, rows), F32), pltpu.VMEM((2 * seq, cut, width), F32)],
+    )
+    d_ctx = lax.all_to_all(d_ctx, SEQ, split_axis=0, concat_axis=0, tiled=True)
+
+    wo_got = swap(wo_send, "batch")
+    wq = wq + [swap_plane(after(wq[0], sums), 3)]
+
+    blk = split(length)
+    dchunk, dall = once(
+        "backward",
+        backward_kernel,
+        (scal, qkvt, d_ctx, ctxt, lse),
+        [like((seq, 3 * HD, rows), BF16), like((3 * HD, length), BF16)],
+        [
+            pltpu.VMEM((length, HD), BF16),
+            pltpu.VMEM((length, HD), BF16),
+            pltpu.VMEM((length, HD), BF16),
+            pltpu.VMEM((length, HD), BF16),
+            pltpu.VMEM((HD, length), BF16),
+            pltpu.VMEM((1, length), F32),
+            pltpu.VMEM((HD, length), F32),
+            pltpu.VMEM((blk, HD), F32),
+            pltpu.VMEM((blk, HD), F32),
+        ],
+    )
+    back, wq, dchunk = lax.optimization_barrier((back, wq, dchunk))
+    d_rows = lax.all_to_all(dchunk, SEQ, split_axis=0, concat_axis=0, tiled=True)
+
+    grad_w_down, bias, own, wo_own, *away = once(
+        "finish",
+        finish_kernel,
+        (scal, own, *back, wo_keep, wo_got, *out_send),
+        [
+            like((half, width), F32),
+            like((8, half), F32),
+            like((cut, width), BF16),
+            like((outer, cut, width), F32),
+        ]
+        + [like(((1 + outer) * cut + rows, width), BF16)] * 3,
+        [pltpu.VMEM((count, width), F32)],
+    )
+    got = [swap_plane(value, k + 1) for k, value in enumerate(away)]
+    layer_out, grad_w_up, grad_w_output, *away = once(
+        "close",
+        functools.partial(close_kernel, outer),
+        (scal, own, wo_own, *got, middle, out_keep, rows_in),
+        [like((rows, width), BF16), like((cut, 4 * local), F32), like((cut, width), F32)]
+        + [like((cut, width), BF16)] * (outer - 1),
+    )
+    grad_w_output = grad_w_output + sum(
+        swap(value, "z", k + 1).astype(F32) for k, value in enumerate(away)
+    )
+
+    last, send = head_grads(scal, after(dall, got[0]), norm_one, norm_raw, wt, sums, heads, seq)
+    last = last + swap(send, "batch").astype(F32)
+    last = after(last.astype(BF16), d_rows, *away)
+    other = swap(after(jnp.concatenate(wq), dall), "batch")
+    grad_tokens = once(
+        "last",
+        functools.partial(last_kernel, heads),
+        (scal, d_rows, *wq, other, token, d_middle, rows_in),
+        [like((rows, width), F32)],
+        [pltpu.VMEM((width, rows), F32)],
+    )[0]
+    last = lax.all_to_all(last, SEQ, split_axis=0, concat_axis=0, tiled=True)
+    mat = like((cut, width), F32)
+    grad_w_query, grad_w_key, grad_w_value, vec = once(
+        "unpack",
+        functools.partial(unpack_kernel, heads),
+        (last,),
+        [mat, mat, mat, like((8, cut), F32)],
+    )
+    return (
+        layer_out[None],
+        grad_tokens[None],
+        vec[0],
+        vec[1],
+        grad_w_query,
+        vec[2],
+        grad_w_key,
+        grad_w_value,
+        vec[3],
+        grad_w_output,
+        vec[4],
+        vec[5],
+        vec[6],
+        grad_w_up,
+        bias[0],
+        grad_w_down,
+        vec[7],
+    )
 
 
 def over_rows(left, right):
@@ -56,7 +848,7 @@
     return (prob_low, d_score)
 
 
-def body(
+def plain_body(
     tokens,
     cotangent,
     prefix_len,
@@ -263,6 +1055,7 @@
     grad_bu = jnp.sum(d_pre.astype(jnp.float32), axis=0)
     d_norm_two = over_cols(d_pre, wu_back)
     d_mid_norm, grad_gb, grad_sb = norm_backward(d_norm_two, normed_two, factor_two, gb_back)
+    grad_gb, grad_sb = (grad_gb[0], grad_sb[0])
     d_middle = d_out.astype(jnp.float32) + d_mid_norm
     d_branch = d_middle.astype(jnp.bfloat16)
     grad_wo = over_rows(ctx_low, d_branch)
@@ -326,6 +1119,7 @@
         over_cols(dq_low, wq_back) + over_cols(dk_low, wk_back) + over_cols(dv_low, wv_back)
     )
     d_in_norm, grad_ga, grad_sa = norm_backward(d_norm_one, normed_one, factor_one, ga_back)
+    grad_ga, grad_sa = (grad_ga[0], grad_sa[0])
     grad_tokens = d_middle + d_in_norm
     summed = (
         lax.psum_scatter(grad_ga, ("seq", "batch"), scatter_dimension=0, tiled=True),
@@ -366,48 +1160,23 @@
 
 
 def solution(mesh):
-    placed = (
-        P("batch", "seq", None),
-        P("batch", "seq", None),
-        P("batch"),
-        P(("seq", "batch")),
-        P(("seq", "batch")),
-        P(("seq", "batch"), None),
-        P(("seq", "batch")),
-        P(("seq", "batch"), None),
-        P(("seq", "batch"), None),
-        P(("seq", "batch")),
-        P(("seq", "batch"), None),
-        P(("seq", "batch")),
-        P(("seq", "batch")),
-        P(("seq", "batch")),
-        P(("seq", "batch"), None),
-        P(("seq", "batch")),
-        P(("seq", "batch"), None),
-        P(("seq", "batch")),
-    )
+    seq, batch = (mesh.shape["seq"], mesh.shape["batch"])
+    if batch == 2 and seq == 16:
+        fine = Mesh(mesh.devices.reshape(seq // 4, 2, 2, batch), ALL)
+        along, run = (SEQ, body)
+    else:
+        fine, along, run = (mesh, "seq", plain_body)
+    every = along + ("batch",) if run is body else ("seq", "batch")
+    act, mat, vec = (P("batch", along, None), P(every, None), P(every))
     return jax.shard_map(
-        body,
-        mesh=mesh,
-        in_specs=placed,
+        run,
+        mesh=fine,
+        in_specs=(
+            act, act, P("batch"), vec, vec, mat, vec, mat, mat, vec, mat, vec, vec, vec, mat, vec, mat,
+            vec,
+        ),
         out_specs=(
-            P("batch", "seq", None),
-            P("batch", "seq", None),
-            P(("seq", "batch")),
-            P(("seq", "batch")),
-            P(("seq", "batch"), None),
-            P(("seq", "batch")),
-            P(("seq", "batch"), None),
-            P(("seq", "batch"), None),
-            P(("seq", "batch")),
-            P(("seq", "batch"), None),
-            P(("seq", "batch")),
-            P(("seq", "batch")),
-            P(("seq", "batch")),
-            P(("seq", "batch"), None),
-            P(("seq", "batch")),
-            P(("seq", "batch"), None),
-            P(("seq", "batch")),
+            act, act, vec, vec, mat, vec, mat, mat, vec, mat, vec, vec, vec, mat, vec, mat, vec,
         ),
         check_vma=False,
     )

time: 1550 us -> 260 us (0.17)
  waiting for transfers between devices: 1280 us -> 80.9 us
  starting transfers between devices: 0.81 us -> 85.4 us
  blocking collectives: 84 us -> 2.21 us
  Pallas kernels: 0 us -> 68 us
  matrix products: 62.4 us -> 0 us
  local copies, waits for them, and re-layouts: 74.9 us -> 14.1 us
  loops' own time: 16.7 us -> 0 us
    reduce_scatter x6 -> x0, waiting for transfers between devices: 627 us -> none  [the longest x1 142 us: body(): lax.psum_scatter(grad_wu, ('seq', 'batch'), scatter_dimension=0, tiled=True)]
    all_gather x8 -> x0, waiting for transfers between devices: 383 us -> none  [the longest x1 68.5 us: body(): lax.all_gather(v_low, 'seq', axis=0, tiled=True)]
    unnamed x18 -> x0, waiting for transfers between devices: 273 us -> none
    unnamed x2 -> x0, blocking collectives: 84 us -> none
    ppermute x0 -> x43, waiting for transfers between devices: none -> 77.4 us  [the longest x18 38.8 us: swap_plane(): return lax.ppermute(value, ('y', 'x'), [(i, i ^ step) for i in range(4)])]
    pallas_call x0 -> x12, Pallas kernels: none -> 68 us  [the longest x11 61.2 us: once(): pl.pallas_call(kernel, grid=(1,), out_shape=tuple(outs), in_specs=in_spec...]
    dot_general x25 -> x0, matrix products: 62.4 us -> none  [the longest x6 21.2 us: over_rows(): lax.dot_general(left, right, (((0,), (0,)), ((), ())), preferred_element_...]
    ppermute x0 -> x43, starting transfers between devices: none -> 56.1 us  [the longest x25 31.4 us: swap(): return lax.ppermute(value, axis, [(i, i ^ step) for i in range(size)])]
  transfers between devices with their start and end apart: 16 -> 48, of which waited for: 16 -> 17; matrix products, arithmetic and copies ran while one was open for 7% -> 3% of each run, Pallas kernels for 0% -> 20%
where the time goes in v3:
time: 260 us; the launch traced here: 259 us
  starting transfers between devices  85.4 us (33%)
  waiting for transfers between devices  80.9 us (31%)
  Pallas kernels  68 us (26%)
  local copies, waits for them, and re-layouts  14.1 us (5%)
  other arithmetic  6.13 us (2%)
    pallas_call x11, Pallas kernels, once(): pl.pallas_call(kernel, grid=(1,), out_shape=tuple(outs), in_specs=in_spec...  61.2 us
    ppermute x18, waiting for transfers between devices, swap_plane(): return lax.ppermute(value, ('y', 'x'), [(i, i ^ step) for i in range(4)])  38.8 us
    ppermute x25, waiting for transfers between devices, swap(): return lax.ppermute(value, axis, [(i, i ^ step) for i in range(size)])  38.7 us
    ppermute x25, starting transfers between devices, swap(): return lax.ppermute(value, axis, [(i, i ^ step) for i in range(size)])  31.4 us
    ppermute x18, starting transfers between devices, swap_plane(): return lax.ppermute(value, ('y', 'x'), [(i, i ^ step) for i in range(4)])  24.7 us
    unnamed x101, local copies, waits for them, and re-layouts  10.8 us
    all_to_all x1, starting transfers between devices, body(): lax.all_to_all(dchunk, SEQ, split_axis=0, concat_axis=0, tiled=True)  9.3 us
    pallas_call x1, Pallas kernels, head_grads(): pl.pallas_call(functools.partial(heads_kernel, heads), out_shape=outs, gr...  6.75 us
  transfers between devices with their start and end apart: 48, of which 17 were waited for; matrix products, arithmetic and copies ran while one was open for 3% of the time, Pallas kernels for 20%

profile of v3, /device:TPU:0, one launch (start us, length us, event | category | flops | bytes accessed | tf_op | source)
XLA Modules:
  0.0 258.9 jit_solution(923155021188260524)
XLA Ops:
  1.7 5.1 %collective-permute-start.5 = (bf16[152,768]{1,0:T(8,128)(2,1)S(1)}, bf16[152,768]{1,0:T(8,128)(2,1)S(1)}, u32[]{:S(2)}, u32[]{:S(2)}) collective-permute-start(bf16[152,768]{1,0:T(8,128)(2,1)S(1)} %pad_maximum_fusion.4.ahead), channel_id=1, source_target_pairs={{0,24},{8,16},{16,8},{24,0},{1,25},{9,17},{17,9},{25,1},{2,26},{10... | collective-permute-start | bytes 700424 | tf_op jit(solution)/shard_map/ppermute | solution.py:51
  16.1 10.5 %collective-permute-done.4 = bf16[152,768]{1,0:T(8,128)(2,1)S(1)} collective-permute-done((bf16[152,768]{1,0:T(8,128)(2,1)S(1)}, bf16[152,768]{1,0:T(8,128)(2,1)S(1)}, u32[]{:S(2)}, u32[]{:S(2)}) %collective-permute-start.4) | collective-permute-done | bytes 233504 | tf_op jit(solution)/shard_map/ppermute | solution.py:51
  29.9 6.5 %all-to-all-start = ((bf16[16,24,256]{2,1,0:T(8,128)(2,1)}), bf16[16,24,256]{2,1,0:T(8,128)(2,1)S(1)}, u32[]{:S(2)}, u32[]{:S(2)}) async-start(bf16[16,24,256]{2,1,0:T(8,128)(2,1)} %get-tuple-element.115), calls=%async_computation | async-start | bytes 393216 | tf_op jit(solution)/shard_map/all_to_all | solution.py:632
  36.6 3.8 %collective-permute-start.10 = (bf16[72,768]{1,0:T(8,128)(2,1)S(1)}, bf16[72,768]{1,0:T(8,128)(2,1)S(1)}, u32[]{:S(2)}, u32[]{:S(2)}) collective-permute-start(bf16[72,768]{1,0:T(8,128)(2,1)S(1)} %pad_maximum_fusion.5), channel_id=1, source_target_pairs={{0,24},{8,16},{16,8},{24,0},{1,25},{9,17},{17,9},{25,1},{2,26},{10... | collective-permute-start | bytes 331784 | tf_op jit(solution)/shard_map/ppermute | solution.py:51
  41.0 3.8 %collective-permute-done.10 = bf16[72,768]{1,0:T(8,128)(2,1)S(1)} collective-permute-done((bf16[72,768]{1,0:T(8,128)(2,1)S(1)}, bf16[72,768]{1,0:T(8,128)(2,1)S(1)}, u32[]{:S(2)}, u32[]{:S(2)}) %collective-permute-start.10) | collective-permute-done | bytes 110624 | tf_op jit(solution)/shard_map/ppermute | solution.py:51
  44.8 4.8 %collective-permute-done.9 = bf16[72,768]{1,0:T(8,128)(2,1)S(1)} collective-permute-done((bf16[72,768]{1,0:T(8,128)(2,1)S(1)}, bf16[72,768]{1,0:T(8,128)(2,1)S(1)}, u32[]{:S(2)}, u32[]{:S(2)}) %collective-permute-start.9) | collective-permute-done | bytes 110624 | tf_op jit(solution)/shard_map/ppermute | solution.py:51
  55.4 2.7 %collective-permute-done.12.xyb = bf16[1,152,768]{2,1,0:T(8,128)(2,1)S(1)} collective-permute-done((bf16[1,152,768]{2,1,0:T(8,128)(2,1)S(1)}, bf16[1,152,768]{2,1,0:T(8,128)(2,1)S(1)}, u32[]{:S(2)}, u32[]{:S(2)}) %collective-permute-start.12) | collective-permute-done | bytes 233504 | tf_op jit(solution)/shard_map/ppermute | solution.py:51
  67.2 2.9 %collective-permute-start.15 = (bf16[200,768]{1,0:T(8,128)(2,1)S(1)}, bf16[200,768]{1,0:T(8,128)(2,1)S(1)}, u32[]{:S(2)}, u32[]{:S(2)}) collective-permute-start(bf16[200,768]{1,0:T(8,128)(2,1)S(1)} %constant_dynamic-update-slice_fusion), channel_id=1, source_target_pairs={{0,8},{8,0},{16,24},{24,16},{1,9},{9,1},{17,25},{25,17},{2,10},{10... | collective-permute-start | bytes 921608 | tf_op jit(solution)/shard_map/ppermute | solution.py:51
  70.2 15.0 %forward.1 = (bf16[2048,768]{1,0:T(8,128)(2,1)}, bf16[2048,768]{1,0:T(8,128)(2,1)}, bf16[192,2048]{1,0:T(8,128)(2,1)}, bf16[16,64,128]{2,1,0:T(8,128)(2,1)}, f32...) custom-call(s32[5]{0:T(128)} %stack.61.scal, ...), custom_call_target="tpu_custom_call" | custom-call | flops 1 | bytes 1 | tf_op jit(solution)/shard_map/forward/pallas_call | solution.py:83
  85.2 8.6 %collective-permute-done.16 = bf16[200,768]{1,0:T(8,128)(2,1)S(1)} collective-permute-done((bf16[200,768]{1,0:T(8,128)(2,1)S(1)}, bf16[200,768]{1,0:T(8,128)(2,1)S(1)}, u32[]{:S(2)}, u32[]{:S(2)}) %collective-permute-start.16) | collective-permute-done | bytes 307232 | tf_op jit(solution)/shard_map/ppermute | solution.py:51
  95.4 3.7 %all-to-all-start.1 = ((bf16[16,64,128]{2,1,0:T(8,128)(2,1)}), bf16[16,64,128]{2,1,0:T(8,128)(2,1)S(1)}, u32[]{:S(2)}, u32[]{:S(2)}) async-start(bf16[16,64,128]{2,1,0:T(8,128)(2,1)} %get-tuple-element.127), calls=%async_computation.1 | async-start | bytes 524288 | tf_op jit(solution)/shard_map/all_to_all | solution.py:675
  99.1 2.6 %collective-permute-start.20 = (bf16[128,768]{1,0:T(8,128)(2,1)}, bf16[128,768]{1,0:T(8,128)(2,1)S(1)}, u32[]{:S(2)}, u32[]{:S(2)}) collective-permute-start(bf16[128,768]{1,0:T(8,128)(2,1)} %bitcast.52), channel_id=1, source_target_pairs={{0,6},{2,4},{4,2},{6,0},{1,7},{3,5},{5,3},{7,1},{8,14},{10,12},{12... | collective-permute-start | bytes 589832 | tf_op jit(solution)/shard_map/ppermute | solution.py:55
  102.6 7.7 %collective-permute-done.20.dy_d = bf16[128,768]{1,0:T(8,128)(2,1)S(1)} collective-permute-done((bf16[128,768]{1,0:T(8,128)(2,1)}, bf16[128,768]{1,0:T(8,128)(2,1)S(1)}, u32[]{:S(2)}, u32[]{:S(2)}) %collective-permute-start.20) | collective-permute-done | bytes 196640 | tf_op jit(solution)/shard_map/ppermute | solution.py:55
  110.3 3.2 %collective-permute-done.19.dy_c = bf16[128,768]{1,0:T(8,128)(2,1)S(1)} collective-permute-done((bf16[128,768]{1,0:T(8,128)(2,1)}, bf16[128,768]{1,0:T(8,128)(2,1)S(1)}, u32[]{:S(2)}, u32[]{:S(2)}) %collective-permute-start.19) | collective-permute-done | bytes 196640 | tf_op jit(solution)/shard_map/ppermute | solution.py:55
  115.1 2.7 %middle.1 = (f32[128,768]{1,0:T(8,128)}, bf16[128,768]{1,0:T(8,128)(2,1)}) custom-call(s32[5]{0:T(128)} %stack.61.scal, bf16[16,64,128]{2,1,0:T(8,128)(2,1)} %copy-done.6, bf16[16,24,768]{2,1,0:T(8,128)(2,1)} %get-tuple-element.130.own, bf16[16,24,768]{2,1,0:T(8,128)(2,1)} %copy-done.5, bf16[128,768]{1,0:T(8,128)(2,1)} %bitcast.49, ...), custom_call_target="tpu_custom_call" | custom-call | flops 1 | bytes 1 | tf_op jit(solution)/shard_map/middle/pallas_call | solution.py:83
  121.3 5.4 %collective-permute-done.24.n2_d = bf16[128,768]{1,0:T(8,128)(2,1)S(1)} collective-permute-done((bf16[128,768]{1,0:T(8,128)(2,1)}, bf16[128,768]{1,0:T(8,128)(2,1)S(1)}, u32[]{:S(2)}, u32[]{:S(2)}) %collective-permute-start.24) | collective-permute-done | bytes 196640 | tf_op jit(solution)/shard_map/ppermute | solution.py:55
  126.7 3.2 %collective-permute-done.23.n2_c = bf16[128,768]{1,0:T(8,128)(2,1)S(1)} collective-permute-done((bf16[128,768]{1,0:T(8,128)(2,1)}, bf16[128,768]{1,0:T(8,128)(2,1)S(1)}, u32[]{:S(2)}, u32[]{:S(2)}) %collective-permute-start.23) | collective-permute-done | bytes 196640 | tf_op jit(solution)/shard_map/ppermute | solution.py:55
  130.6 8.7 %feed.1 = (f32[128,768]{1,0:T(8,128)}, bf16[128,768]{1,0:T(8,128)(2,1)}, bf16[128,768]{1,0:T(8,128)(2,1)}, bf16[128,768]{1,0:T(8,128)(2,1)}, f32[128,768]{1,0:T(...) custom-call(s32[5]{0:T(128)} %stack.61.scal, ...), custom_call_target="tpu_custom_call" | custom-call | flops 1 | bytes 1 | tf_op jit(solution)/shard_map/feed/pallas_call | solution.py:83
  144.0 3.3 %fold.1 = (f32[200,768]{1,0:T(8,128)}, bf16[200,768]{1,0:T(8,128)(2,1)}, bf16[200,768]{1,0:T(8,128)(2,1)}, bf16[200,768]{1,0:T(8,128)(2,1)}) custom-call(f32[4,200,768]{2,1,0:T(8,128)} %get-tuple-element.140.keep, bf16[4,200,768]{2,1,0:T(8,128)(2,1)} %copy-done.14), custom_call_target="tpu_custom_call" | custom-call | flops 1 | bytes 1 | tf_op jit(solution)/shard_map/fold/pallas_call | solution.py:83
  147.4 4.9 %collective-permute-done.31.got_c = bf16[128,768]{1,0:T(8,128)(2,1)S(1)} collective-permute-done((bf16[128,768]{1,0:T(8,128)(2,1)}, bf16[128,768]{1,0:T(8,128)(2,1)S(1)}, u32[]{:S(2)}, u32[]{:S(2)}) %collective-permute-start.31) | collective-permute-done | bytes 196640 | tf_op jit(solution)/shard_map/ppermute | solution.py:55
  153.0 4.5 %turn.1 = (f32[128,768]{1,0:T(8,128)}, bf16[8,768]{1,0:T(8,128)(2,1)}, bf16[16,64,128]{2,1,0:T(8,128)(2,1)}, f32[8,768]{1,0:T(8,128)}, f32[16,24,768]{2,1,0:T(8,128)}, /*index=5*/bf16[16,24,768]{2,1,0:T(8,128)(2,1)}) custom-call(s32[5]{0:T(128)} %stack.61.scal, f32[128,768]{1,0:T(8,128)} %get-tuple-element.150.keep, bf16[128,768]{1,0:T(8,128)(2,1)} %copy-done.35, ...), custom_call_target="tpu_custom_call" | custom-call | flops 1 | bytes 1 | tf_op jit(solution)/shard_map/turn/pallas_call | solution.py:83
  157.5 4.8 %all-to-all-start.2 = ((bf16[16,64,128]{2,1,0:T(8,128)(2,1)}), bf16[16,64,128]{2,1,0:T(8,128)(2,1)S(1)}, u32[]{:S(2)}, u32[]{:S(2)}) async-start(bf16[16,64,128]{2,1,0:T(8,128)(2,1)} %get-tuple-element.158), calls=%async_computation.2 | async-start | bytes 524288 | tf_op jit(solution)/shard_map/all_to_all | solution.py:733
  162.3 2.8 %collective-permute-start.33 = (bf16[4,72,768]{2,1,0:T(8,128)(2,1)S(1)}, bf16[4,72,768]{2,1,0:T(8,128)(2,1)S(1)}, u32[]{:S(2)}, u32[]{:S(2)}) collective-permute-start(bf16[4,72,768]{2,1,0:T(8,128)(2,1)S(1)} %pad_maximum_fusion.3.wq_a), channel_id=1, source_target_pairs={{0,6},{2,4},{4,2},{6,0},{1,7},{3,5},{5,3},{7,1},{8,14},{10,12},{12... | collective-permute-start | bytes 1327112 | tf_op jit(solution)/shard_map/ppermute | solution.py:55
  169.5 3.5 %all-to-all-done.2.dcr = bf16[16,64,128]{2,1,0:T(8,128)(2,1)S(1)} async-done(((bf16[16,64,128]{2,1,0:T(8,128)(2,1)}), bf16[16,64,128]{2,1,0:T(8,128)(2,1)S(1)}, u32[]{:S(2)}, u32[]{:S(2)}) %all-to-all-start.2) | async-done | bytes 262176 | tf_op jit(solution)/shard_map/all_to_all | solution.py:733
  173.7 12.3 %backward.1 = (bf16[16,192,128]{2,1,0:T(8,128)(2,1)}, bf16[192,2048]{1,0:T(8,128)(2,1)}) custom-call(s32[5]{0:T(128)} %stack.61.scal, bf16[192,2048]{1,0:T(8,128)(2,1)} %get-tuple-element.157.qkvt, bf16[16,64,128]{2,1,0:T(8,128)(2,1)} %copy-done.15, f32[64,2048]{1,0:T(8,128)} %get-tuple-element.159.ctxt, f32[1,2048]{1,0:T(1,128)} %get-tuple-element.160.lse), custom_call_target="tpu_custom_call" | custom-call | flops 1 | bytes 1 | tf_op jit(solution)/shard_map/backward/pallas_call | solution.py:83
  186.0 5.6 %collective-permute-done.28.refs_1_ = bf16[200,768]{1,0:T(8,128)(2,1)S(1)} collective-permute-done((bf16[200,768]{1,0:T(8,128)(2,1)}, bf16[200,768]{1,0:T(8,128)(2,1)S(1)}, u32[]{:S(2)}, u32[]{:S(2)}) %collective-permute-start.28) | collective-permute-done | bytes 307232 | tf_op jit(solution)/shard_map/ppermute | solution.py:51
  191.7 9.3 %all-to-all-start.3 = ((bf16[16,192,128]{2,1,0:T(8,128)(2,1)}), bf16[16,192,128]{2,1,0:T(8,128)(2,1)S(1)}, u32[]{:S(2)}, u32[]{:S(2)}) async-start(bf16[16,192,128]{2,1,0:T(8,128)(2,1)} %get-tuple-element.177), calls=%async_computation.3 | async-start | bytes 1572864 | tf_op jit(solution)/shard_map/all_to_all | solution.py:757
  204.2 3.4 %finish.1 = (f32[96,768]{1,0:T(8,128)}, f32[8,96]{1,0:T(8,128)}, bf16[24,768]{1,0:T(8,128)(2,1)}, f32[4,24,768]{2,1,0:T(8,128)}, bf16[248,768]{1,0:T(8,128)(2,1)...) custom-call(s32[5]{0:T(128)} %stack.61.scal, f32[200,768]{1,0:T(8,128)} %get-tuple-element.142.keep, ...), custom_call_target="tpu_custom_call" | custom-call | flops 1 | bytes 1 | tf_op jit(solution)/shard_map/finish/pallas_call | solution.py:83
  211.0 13.1 %collective-permute-done.35.got_b = bf16[248,768]{1,0:T(8,128)(2,1)S(1)} collective-permute-done((bf16[248,768]{1,0:T(8,128)(2,1)}, bf16[248,768]{1,0:T(8,128)(2,1)S(1)}, u32[]{:S(2)}, u32[]{:S(2)}) %collective-permute-start.35) | collective-permute-done | bytes 380960 | tf_op jit(solution)/shard_map/ppermute | solution.py:55
  224.1 6.7 %heads.1 = (f32[16,24,256]{2,1,0:T(8,128)}, bf16[16,24,256]{2,1,0:T(8,128)(2,1)}) custom-call(s32[5]{0:T(128)} %stack.61.scal, bf16[192,2048]{1,0:T(8,128)(2,1)} %get-tuple-element.185.dall, bf16[2048,768]{1,0:T(8,128)(2,1)} %get-tuple-element.186.n1, bf16[2048,768]{1,0:T(8,128)(2,1)} %get-tuple-element.187.n0, bf16[192,768]{1,0:T(8,128)(2,1)} %get-tuple-element.188.wt, ...), custom_call_target="tpu_custom_call" | custom-call | flops 1 | bytes 1 | tf_op jit(solution)/shard_map/heads/pallas_call | solution.py:541
  241.3 5.1 %all-to-all-start.4 = ((bf16[16,24,256]{2,1,0:T(8,128)(2,1)}), bf16[16,24,256]{2,1,0:T(8,128)(2,1)S(1)}, u32[]{:S(2)}, u32[]{:S(2)}) async-start(bf16[16,24,256]{2,1,0:T(8,128)(2,1)} %add_convert_fusion), calls=%async_computation.4 | async-start | bytes 393216 | tf_op jit(solution)/shard_map/all_to_all | solution.py:795
  250.3 4.5 %last.1 = f32[128,768]{1,0:T(8,128)} custom-call(s32[5]{0:T(128)} %stack.61.scal, bf16[16,192,128]{2,1,0:T(8,128)(2,1)} %copy-done.2, bf16[4,72,768]{2,1,0:T(8,128)(2,1)} %copy-done.1, bf16[4,72,768]{2,1,0:T(8,128)(2,1)} %copy-done.10, bf16[4,72,768]{2,1,0:T(8,128)(2,1)} %copy-done.9, bf16[4,72,768]{2,1,0:T(8,128)(2,1)} %copy-done.12, ...), custom_call_target="tpu_custom_call" | custom-call | flops 1 | bytes 1 | tf_op jit(solution)/shard_map/last/pallas_call | solution.py:83
  (192 shorter events, 72.0 us)
Async XLA Ops:
  1.7 12.8 %collective-permute-start.5 = (bf16[152,768]{1,0:T(8,128)(2,1)S(1)}, bf16[152,768]{1,0:T(8,128)(2,1)S(1)}, u32[]{:S(2)}, u32[]{:S(2)}) collective-permute-start(bf16[152,768]{1,0:T(8,128)(2,1)S(1)} %pad_maximum_fusion.4.ahead), channel_id=1, source_target_pairs={{0,24},{8,16},{16,8},{24,0},{1,25},{9,17},{17,9},{25,1},{2,26},{10... | collective-permute-start | bytes 700424 | tf_op jit(solution)/shard_map/ppermute | solution.py:51
  6.8 19.9 %collective-permute-start.4 = (bf16[152,768]{1,0:T(8,128)(2,1)S(1)}, bf16[152,768]{1,0:T(8,128)(2,1)S(1)}, u32[]{:S(2)}, u32[]{:S(2)}) collective-permute-start(bf16[152,768]{1,0:T(8,128)(2,1)S(1)} %pad_maximum_fusion.4.ahead), channel_id=1, source_target_pairs={{0,16},{8,24},{16,0},{24,8},{1,17},{9,25},{17,1},{25,9},{2,18},{10... | collective-permute-start | bytes 700424 | tf_op jit(solution)/shard_map/ppermute | solution.py:51
  6.8 19.9 %collective-permute-start.3 = (bf16[152,768]{1,0:T(8,128)(2,1)S(1)}, bf16[152,768]{1,0:T(8,128)(2,1)S(1)}, u32[]{:S(2)}, u32[]{:S(2)}) collective-permute-start(bf16[152,768]{1,0:T(8,128)(2,1)S(1)} %pad_maximum_fusion.4.ahead), channel_id=1, source_target_pairs={{0,8},{8,0},{16,24},{24,16},{1,9},{9,1},{17,25},{25,17},{2,10},{10... | collective-permute-start | bytes 700424 | tf_op jit(solution)/shard_map/ppermute | solution.py:51
  11.3 15.5 %collective-permute-start = (bf16[176,768]{1,0:T(8,128)(2,1)}, bf16[176,768]{1,0:T(8,128)(2,1)S(1)}, u32[]{:S(2)}, u32[]{:S(2)}) collective-permute-start(bf16[176,768]{1,0:T(8,128)(2,1)} %get-tuple-element.110), channel_id=1, source_target_pairs={{0,2},{2,0},{4,6},{6,4},{1,3},{3,1},{5,7},{7,5},{8,10},{10,8},{12,... | collective-permute-start | bytes 811016 | tf_op jit(solution)/shard_map/ppermute | solution.py:55
  13.0 13.8 %collective-permute-start.1 = (bf16[176,768]{1,0:T(8,128)(2,1)}, bf16[176,768]{1,0:T(8,128)(2,1)}, u32[]{:S(2)}, u32[]{:S(2)}) collective-permute-start(bf16[176,768]{1,0:T(8,128)(2,1)} %get-tuple-element.111), channel_id=1, source_target_pairs={{0,4},{2,6},{4,0},{6,2},{1,5},{3,7},{5,1},{7,3},{8,12},{10,14},{12... | collective-permute-start | bytes 811016 | tf_op jit(solution)/shard_map/ppermute | solution.py:55
  14.5 12.3 %collective-permute-start.2 = (bf16[176,768]{1,0:T(8,128)(2,1)}, bf16[176,768]{1,0:T(8,128)(2,1)S(1)}, u32[]{:S(2)}, u32[]{:S(2)}) collective-permute-start(bf16[176,768]{1,0:T(8,128)(2,1)} %get-tuple-element.112), channel_id=1, source_target_pairs={{0,6},{2,4},{4,2},{6,0},{1,7},{3,5},{5,3},{7,1},{8,14},{10,12},{12... | collective-permute-start | bytes 811016 | tf_op jit(solution)/shard_map/ppermute | solution.py:55
  26.8 22.8 %collective-permute-start.7 = (bf16[3,152,768]{2,1,0:T(8,128)(2,1)S(1)}, bf16[3,152,768]{2,1,0:T(8,128)(2,1)S(1)}, u32[]{:S(2)}, u32[]{:S(2)}) collective-permute-start(bf16[3,152,768]{2,1,0:T(8,128)(2,1)S(1)} %pad_maximum_fusion.2.zc), channel_id=1, source_target_pairs={{0,4},{4,0},{1,5},{5,1},{2,6},{6,2},{3,7},{7,3},{8,12},{12,8},{9,1... | collective-permute-start | bytes 2101256 | tf_op jit(solution)/shard_map/ppermute | solution.py:51
  28.4 21.2 %collective-permute-start.6 = (bf16[3,152,768]{2,1,0:T(8,128)(2,1)S(1)}, bf16[3,152,768]{2,1,0:T(8,128)(2,1)S(1)}, u32[]{:S(2)}, u32[]{:S(2)}) collective-permute-start(bf16[3,152,768]{2,1,0:T(8,128)(2,1)S(1)} %pad_maximum_fusion.2.zc), channel_id=1, source_target_pairs={{0,2},{2,0},{1,3},{3,1},{4,6},{6,4},{5,7},{7,5},{8,10},{10,8},{9,1... | collective-permute-start | bytes 2101256 | tf_op jit(solution)/shard_map/ppermute | solution.py:51
  29.9 19.7 %all-to-all-start = ((bf16[16,24,256]{2,1,0:T(8,128)(2,1)}), bf16[16,24,256]{2,1,0:T(8,128)(2,1)S(1)}, u32[]{:S(2)}, u32[]{:S(2)}) async-start(bf16[16,24,256]{2,1,0:T(8,128)(2,1)} %get-tuple-element.115), calls=%async_computation | async-start | bytes 393216 | tf_op jit(solution)/shard_map/all_to_all | solution.py:632
  60.6 33.2 %collective-permute-start.14 = (bf16[4,72,768]{2,1,0:T(8,128)(2,1)S(1)}, bf16[4,72,768]{2,1,0:T(8,128)(2,1)S(1)}, u32[]{:S(2)}, u32[]{:S(2)}) collective-permute-start(bf16[4,72,768]{2,1,0:T(8,128)(2,1)S(1)} %pad_maximum_fusion.3.wq_a), channel_id=1, source_target_pairs={{0,4},{2,6},{4,0},{6,2},{1,5},{3,7},{5,1},{7,3},{8,12},{10,14},{12... | collective-permute-start | bytes 1327112 | tf_op jit(solution)/shard_map/ppermute | solution.py:55
  62.1 31.7 %collective-permute-start.13 = (bf16[4,72,768]{2,1,0:T(8,128)(2,1)S(1)}, bf16[4,72,768]{2,1,0:T(8,128)(2,1)S(1)}, u32[]{:S(2)}, u32[]{:S(2)}) collective-permute-start(bf16[4,72,768]{2,1,0:T(8,128)(2,1)S(1)} %pad_maximum_fusion.3.wq_a), channel_id=1, source_target_pairs={{0,2},{2,0},{4,6},{6,4},{1,3},{3,1},{5,7},{7,5},{8,10},{10,8},{12,... | collective-permute-start | bytes 1327112 | tf_op jit(solution)/shard_map/ppermute | solution.py:55
  65.8 19.4 %collective-permute-start.17 = (bf16[200,768]{1,0:T(8,128)(2,1)S(1)}, bf16[200,768]{1,0:T(8,128)(2,1)S(1)}, u32[]{:S(2)}, u32[]{:S(2)}) collective-permute-start(bf16[200,768]{1,0:T(8,128)(2,1)S(1)} %constant_dynamic-update-slice_fusion), channel_id=1, source_target_pairs={{0,24},{8,16},{16,8},{24,0},{1,25},{9,17},{17,9},{25,1},{2,26},{10... | collective-permute-start | bytes 921608 | tf_op jit(solution)/shard_map/ppermute | solution.py:51
  67.2 26.5 %collective-permute-start.16 = (bf16[200,768]{1,0:T(8,128)(2,1)S(1)}, bf16[200,768]{1,0:T(8,128)(2,1)S(1)}, u32[]{:S(2)}, u32[]{:S(2)}) collective-permute-start(bf16[200,768]{1,0:T(8,128)(2,1)S(1)} %constant_dynamic-update-slice_fusion), channel_id=1, source_target_pairs={{0,16},{8,24},{16,0},{24,8},{1,17},{9,25},{17,1},{25,9},{2,18},{10... | collective-permute-start | bytes 921608 | tf_op jit(solution)/shard_map/ppermute | solution.py:51
  67.2 26.5 %collective-permute-start.15 = (bf16[200,768]{1,0:T(8,128)(2,1)S(1)}, bf16[200,768]{1,0:T(8,128)(2,1)S(1)}, u32[]{:S(2)}, u32[]{:S(2)}) collective-permute-start(bf16[200,768]{1,0:T(8,128)(2,1)S(1)} %constant_dynamic-update-slice_fusion), channel_id=1, source_target_pairs={{0,8},{8,0},{16,24},{24,16},{1,9},{9,1},{17,25},{25,17},{2,10},{10... | collective-permute-start | bytes 921608 | tf_op jit(solution)/shard_map/ppermute | solution.py:51
  94.8 35.1 %collective-permute-start.25 = (bf16[4,200,768]{2,1,0:T(8,128)(2,1)S(1)}, bf16[4,200,768]{2,1,0:T(8,128)(2,1)}, u32[]{:S(2)}, u32[]{:S(2)}) collective-permute-start(bf16[4,200,768]{2,1,0:T(8,128)(2,1)S(1)} %pad_maximum_fusion.1.ffz), channel_id=1, source_target_pairs={{0,1},{1,0},{2,3},{3,2},{4,5},{5,4},{6,7},{7,6},{8,9},{9,8},{10,11... | collective-permute-start | bytes 3686408 | tf_op jit(solution)/shard_map/ppermute | solution.py:51
  94.9 19.3 %collective-permute-start.21 = (bf16[16,24,768]{2,1,0:T(8,128)(2,1)S(1)}, bf16[16,24,768]{2,1,0:T(8,128)(2,1)S(1)}, u32[]{:S(2)}, u32[]{:S(2)}) collective-permute-start(bf16[16,24,768]{2,1,0:T(8,128)(2,1)S(1)} %copy-done.4), channel_id=1, source_target_pairs={{0,1},{1,0},{2,3},{3,2},{4,5},{5,4},{6,7},{7,6},{8,9},{9,8},{10,11... | collective-permute-start | bytes 1769480 | tf_op jit(solution)/shard_map/ppermute | solution.py:51
  95.4 18.8 %all-to-all-start.1 = ((bf16[16,64,128]{2,1,0:T(8,128)(2,1)}), bf16[16,64,128]{2,1,0:T(8,128)(2,1)S(1)}, u32[]{:S(2)}, u32[]{:S(2)}) async-start(bf16[16,64,128]{2,1,0:T(8,128)(2,1)} %get-tuple-element.127), calls=%async_computation.1 | async-start | bytes 524288 | tf_op jit(solution)/shard_map/all_to_all | solution.py:675
  101.7 11.8 %collective-permute-start.19 = (bf16[128,768]{1,0:T(8,128)(2,1)}, bf16[128,768]{1,0:T(8,128)(2,1)S(1)}, u32[]{:S(2)}, u32[]{:S(2)}) collective-permute-start(bf16[128,768]{1,0:T(8,128)(2,1)} %bitcast.53), channel_id=1, source_target_pairs={{0,4},{2,6},{4,0},{6,2},{1,5},{3,7},{5,1},{7,3},{8,12},{10,14},{12... | collective-permute-start | bytes 589832 | tf_op jit(solution)/shard_map/ppermute | solution.py:55
  102.2 12.0 %collective-permute-start.18 = (bf16[128,768]{1,0:T(8,128)(2,1)}, bf16[128,768]{1,0:T(8,128)(2,1)}, u32[]{:S(2)}, u32[]{:S(2)}) collective-permute-start(bf16[128,768]{1,0:T(8,128)(2,1)} %bitcast.54), channel_id=1, source_target_pairs={{0,2},{2,0},{4,6},{6,4},{1,3},{3,1},{5,7},{7,5},{8,10},{10,8},{12,... | collective-permute-start | bytes 589832 | tf_op jit(solution)/shard_map/ppermute | solution.py:55
  140.9 11.4 %collective-permute-start.31 = (bf16[128,768]{1,0:T(8,128)(2,1)}, bf16[128,768]{1,0:T(8,128)(2,1)S(1)}, u32[]{:S(2)}, u32[]{:S(2)}) collective-permute-start(bf16[128,768]{1,0:T(8,128)(2,1)} %get-tuple-element.152), channel_id=1, source_target_pairs={{0,4},{2,6},{4,0},{6,2},{1,5},{3,7},{5,1},{7,3},{8,12},{10,14},{12... | collective-permute-start | bytes 589832 | tf_op jit(solution)/shard_map/ppermute | solution.py:55
  157.5 15.5 %all-to-all-start.2 = ((bf16[16,64,128]{2,1,0:T(8,128)(2,1)}), bf16[16,64,128]{2,1,0:T(8,128)(2,1)S(1)}, u32[]{:S(2)}, u32[]{:S(2)}) async-start(bf16[16,64,128]{2,1,0:T(8,128)(2,1)} %get-tuple-element.158), calls=%async_computation.2 | async-start | bytes 524288 | tf_op jit(solution)/shard_map/all_to_all | solution.py:733
  162.3 29.4 %collective-permute-start.33 = (bf16[4,72,768]{2,1,0:T(8,128)(2,1)S(1)}, bf16[4,72,768]{2,1,0:T(8,128)(2,1)S(1)}, u32[]{:S(2)}, u32[]{:S(2)}) collective-permute-start(bf16[4,72,768]{2,1,0:T(8,128)(2,1)S(1)} %pad_maximum_fusion.3.wq_a), channel_id=1, source_target_pairs={{0,6},{2,4},{4,2},{6,0},{1,7},{3,5},{5,3},{7,1},{8,14},{10,12},{12... | collective-permute-start | bytes 1327112 | tf_op jit(solution)/shard_map/ppermute | solution.py:55
  165.1 20.9 %collective-permute-start.27 = (bf16[200,768]{1,0:T(8,128)(2,1)}, bf16[200,768]{1,0:T(8,128)(2,1)S(1)}, u32[]{:S(2)}, u32[]{:S(2)}) collective-permute-start(bf16[200,768]{1,0:T(8,128)(2,1)} %get-tuple-element.143), channel_id=1, source_target_pairs={{0,8},{8,0},{16,24},{24,16},{1,9},{9,1},{17,25},{25,17},{2,10},{10... | collective-permute-start | bytes 921608 | tf_op jit(solution)/shard_map/ppermute | solution.py:51
  166.6 25.1 %collective-permute-start.28 = (bf16[200,768]{1,0:T(8,128)(2,1)}, bf16[200,768]{1,0:T(8,128)(2,1)S(1)}, u32[]{:S(2)}, u32[]{:S(2)}) collective-permute-start(bf16[200,768]{1,0:T(8,128)(2,1)} %get-tuple-element.144), channel_id=1, source_target_pairs={{0,16},{8,24},{16,0},{24,8},{1,17},{9,25},{17,1},{25,9},{2,18},{10... | collective-permute-start | bytes 921608 | tf_op jit(solution)/shard_map/ppermute | solution.py:51
  169.0 22.7 %collective-permute-start.29 = (bf16[200,768]{1,0:T(8,128)(2,1)S(1)}, bf16[200,768]{1,0:T(8,128)(2,1)S(1)}, u32[]{:S(2)}, u32[]{:S(2)}) collective-permute-start(bf16[200,768]{1,0:T(8,128)(2,1)S(1)} %copy-done.47), channel_id=1, source_target_pairs={{0,24},{8,16},{16,8},{24,0},{1,25},{9,17},{17,9},{25,1},{2,26},{10... | collective-permute-start | bytes 921608 | tf_op jit(solution)/shard_map/ppermute | solution.py:51
  191.7 49.6 %all-to-all-start.3 = ((bf16[16,192,128]{2,1,0:T(8,128)(2,1)}), bf16[16,192,128]{2,1,0:T(8,128)(2,1)S(1)}, u32[]{:S(2)}, u32[]{:S(2)}) async-start(bf16[16,192,128]{2,1,0:T(8,128)(2,1)} %get-tuple-element.177), calls=%async_computation.3 | async-start | bytes 1572864 | tf_op jit(solution)/shard_map/all_to_all | solution.py:757
  202.7 46.4 %collective-permute-start.38 = (bf16[16,72,768]{2,1,0:T(8,128)(2,1)}, bf16[16,72,768]{2,1,0:T(8,128)(2,1)S(1)}, u32[]{:S(2)}, u32[]{:S(2)}) collective-permute-start(bf16[16,72,768]{2,1,0:T(8,128)(2,1)} %pad_maximum_fusion), channel_id=1, source_target_pairs={{0,1},{1,0},{2,3},{3,2},{4,5},{5,4},{6,7},{7,6},{8,9},{9,8},{10,11... | collective-permute-start | bytes 5308424 | tf_op jit(solution)/shard_map/ppermute | solution.py:51
  207.5 16.6 %collective-permute-start.35 = (bf16[248,768]{1,0:T(8,128)(2,1)}, bf16[248,768]{1,0:T(8,128)(2,1)S(1)}, u32[]{:S(2)}, u32[]{:S(2)}) collective-permute-start(bf16[248,768]{1,0:T(8,128)(2,1)} %get-tuple-element.172), channel_id=1, source_target_pairs={{0,2},{2,0},{4,6},{6,4},{1,3},{3,1},{5,7},{7,5},{8,10},{10,8},{12,... | collective-permute-start | bytes 1142792 | tf_op jit(solution)/shard_map/ppermute | solution.py:55
  209.5 21.5 %collective-permute-start.36 = (bf16[248,768]{1,0:T(8,128)(2,1)}, bf16[248,768]{1,0:T(8,128)(2,1)S(1)}, u32[]{:S(2)}, u32[]{:S(2)}) collective-permute-start(bf16[248,768]{1,0:T(8,128)(2,1)} %get-tuple-element.173), channel_id=1, source_target_pairs={{0,4},{2,6},{4,0},{6,2},{1,5},{3,7},{5,1},{7,3},{8,12},{10,14},{12... | collective-permute-start | bytes 1142792 | tf_op jit(solution)/shard_map/ppermute | solution.py:55
  210.9 21.2 %collective-permute-start.37 = (bf16[248,768]{1,0:T(8,128)(2,1)}, bf16[248,768]{1,0:T(8,128)(2,1)S(1)}, u32[]{:S(2)}, u32[]{:S(2)}) collective-permute-start(bf16[248,768]{1,0:T(8,128)(2,1)} %get-tuple-element.174), channel_id=1, source_target_pairs={{0,6},{2,4},{4,2},{6,0},{1,7},{3,5},{5,3},{7,1},{8,14},{10,12},{12... | collective-permute-start | bytes 1142792 | tf_op jit(solution)/shard_map/ppermute | solution.py:55
  235.5 12.1 %collective-permute-start.40 = (bf16[24,768]{1,0:T(8,128)(2,1)}, bf16[24,768]{1,0:T(8,128)(2,1)S(1)}, u32[]{:S(2)}, u32[]{:S(2)}) collective-permute-start(bf16[24,768]{1,0:T(8,128)(2,1)} %get-tuple-element.191), channel_id=1, source_target_pairs={{0,8},{8,0},{16,24},{24,16},{1,9},{9,1},{17,25},{25,17},{2,10},{10... | collective-permute-start | bytes 110600 | tf_op jit(solution)/shard_map/ppermute | solution.py:51
  241.3 13.5 %all-to-all-start.4 = ((bf16[16,24,256]{2,1,0:T(8,128)(2,1)}), bf16[16,24,256]{2,1,0:T(8,128)(2,1)S(1)}, u32[]{:S(2)}, u32[]{:S(2)}) async-start(bf16[16,24,256]{2,1,0:T(8,128)(2,1)} %add_convert_fusion), calls=%async_computation.4 | async-start | bytes 393216 | tf_op jit(solution)/shard_map/all_to_all | solution.py:795
  (64 other events, 939.8 us)

commit v4 on v3

--- a/solution.py
+++ b/solution.py
@@ -351,7 +351,10 @@
     outer = ffz.shape[0]
     cut = (ffz.shape[1] - 8) // 8
     half = 4 * cut
-    sources = [(src, k, core) for core, src in ((0, ffz), (1, ffc)) for k in range(outer)]
+    order = (0, 2, 1, 3)
+    sources = [
+        (src.at[i], k, core) for core, src in ((0, ffz), (1, ffc)) for i, k in enumerate(order)
+    ]
 
     def block_of(k, core):
         line = jnp.bitwise_xor(scal[LINE], k)
@@ -359,11 +362,11 @@
 
     rows = []
     for src, k, core in sources:
-        down[rows_at(block_of(k, core), half), :] = src[k, :half, :]
+        down[rows_at(block_of(k, core), half), :] = src[:half, :]
         for d in range(4):
             here = rows_at(rank_of(scal, k, d, core), cut)
-            up_s[here, :] = src[k, half + d * cut : half + (d + 1) * cut, :].astype(F32)
-        rows.append((block_of(k, core), src[k, 2 * half :, :half].astype(F32)[:1]))
+            up_s[here, :] = src[half + d * cut : half + (d + 1) * cut, :].astype(F32)
+        rows.append((block_of(k, core), src[2 * half :, :half].astype(F32)[:1]))
     up[...] = up_s[...].astype(BF16)
     for q in range(2 * outer):
         bias[:, q * half : (q + 1) * half] = sum(jnp.where(at == q, row, 0.0) for at, row in rows)
@@ -454,7 +457,7 @@
     cut = half // 4
     lines = wo_own.shape[0]
     grad_down[...] = value[:half]
-    bias[...] = value[2 * half :, :half]
+    bias[...] = value[2 * half : 2 * half + 1, :half]
     for k, ref in enumerate((own, away_b, away_c, away_d)):
         at = jnp.bitwise_xor(scal[FLAT], k)
         here = pl.ds(pl.multiple_of(half + at * cut, 8), cut)
@@ -582,7 +585,7 @@
     grad_tokens[...] = d_middle[...] + grad_in
 
 
-def unpack_kernel(heads, got, g_q, g_k, g_v, vec):
+def unpack_kernel(heads, got, g_q, g_k, g_v, *vec):
     for i, out in enumerate((g_q, g_k, g_v)):
         for h in range(heads):
             out[:, h * HD : (h + 1) * HD] = got[h, :, i * HD : (i + 1) * HD].astype(F32)
@@ -591,7 +594,9 @@
         total = total + got[s, :, 2 * HD :].astype(F32)
     cut = total.shape[0]
     total = jnp.concatenate([total, jnp.zeros((2 * HD - cut, 2 * HD), F32)], axis=0)
-    vec[...] = jnp.transpose(total)[HD : HD + 8, :cut]
+    total = jnp.transpose(total)
+    for i, out in enumerate(vec):
+        out[...] = total[HD + i : HD + i + 1, :cut]
 
 
 def body(
@@ -632,17 +637,18 @@
     head_w = lax.all_to_all(after(send, zc), SEQ, split_axis=0, concat_axis=0, tiled=True)
     wq = after(jnp.concatenate([w_query, w_key, w_value]), zc)
     wq_got = [swap(wq, "z", k) for k in range(1, outer)]
+    head_w = lax.all_gather(head_w, "batch", axis=0, tiled=False)
     xc, yc, head_w, wq_got = lax.optimization_barrier((xc, yc, head_w, wq_got))
     xya = swap(xc[: outer // 2], "y")
     xyb = swap(yc[outer // 2 :], "x")
-    head_w = lax.all_gather(head_w, "batch", axis=0, tiled=False)
 
     b_up_row = jnp.pad(b_up[None], ((0, 7), (0, width - half)))
     ff = [w_down, up_own] + [part[rows + cut :] for part in first] + [b_up_row]
     ff = after(jnp.concatenate(ff), head_w, xc)
-    ff_got = [swap(ff, "z", k) for k in range(1, outer)]
+    ff = jnp.stack([ff, swap(ff, "z", 2)])
+    ff_got = swap(ff, "z", 1)
     wq = after(jnp.stack([wq] + wq_got), xya, xyb)
-    wq = [wq] + [swap_plane(wq, k) for k in range(1, 3)]
+    wq = [wq] + [swap_plane(wq, k) for k in range(1, 4)]
 
     norm_one, norm_raw, qkvt, ctxc, ctxt, lse, rows_in, wt, w_out_own = once(
         "forward",
@@ -670,7 +676,7 @@
     )
     w_out_other = swap(w_out_own, "batch")
     ctxc, wq, ff_got = lax.optimization_barrier((ctxc, wq, ff_got))
-    ffz = jnp.stack([ff] + ff_got)
+    ffz = jnp.concatenate([ff, ff_got])
     dy = [d_out] + [swap_plane(after(d_out, ctxc), k) for k in range(1, 4)]
     ctx = lax.all_to_all(ctxc, SEQ, split_axis=0, concat_axis=0, tiled=True)
     ffc = swap(ffz, "batch")
@@ -733,7 +739,6 @@
     d_ctx = lax.all_to_all(d_ctx, SEQ, split_axis=0, concat_axis=0, tiled=True)
 
     wo_got = swap(wo_send, "batch")
-    wq = wq + [swap_plane(after(wq[0], sums), 3)]
 
     blk = split(length)
     dchunk, dall = once(
@@ -753,7 +758,7 @@
             pltpu.VMEM((blk, HD), F32),
         ],
     )
-    back, wq, dchunk = lax.optimization_barrier((back, wq, dchunk))
+    back, dchunk = lax.optimization_barrier((back, dchunk))
     d_rows = lax.all_to_all(dchunk, SEQ, split_axis=0, concat_axis=0, tiled=True)
 
     grad_w_down, bias, own, wo_own, *away = once(
@@ -762,7 +767,7 @@
         (scal, own, *back, wo_keep, wo_got, *out_send),
         [
             like((half, width), F32),
-            like((8, half), F32),
+            like((1, half), F32),
             like((cut, width), BF16),
             like((outer, cut, width), F32),
         ]
@@ -770,20 +775,9 @@
         [pltpu.VMEM((count, width), F32)],
     )
     got = [swap_plane(value, k + 1) for k, value in enumerate(away)]
-    layer_out, grad_w_up, grad_w_output, *away = once(
-        "close",
-        functools.partial(close_kernel, outer),
-        (scal, own, wo_own, *got, middle, out_keep, rows_in),
-        [like((rows, width), BF16), like((cut, 4 * local), F32), like((cut, width), F32)]
-        + [like((cut, width), BF16)] * (outer - 1),
-    )
-    grad_w_output = grad_w_output + sum(
-        swap(value, "z", k + 1).astype(F32) for k, value in enumerate(away)
-    )
-
-    last, send = head_grads(scal, after(dall, got[0]), norm_one, norm_raw, wt, sums, heads, seq)
+    last, send = head_grads(scal, dall, norm_one, norm_raw, wt, sums, heads, seq)
     last = last + swap(send, "batch").astype(F32)
-    last = after(last.astype(BF16), d_rows, *away)
+    last = after(last.astype(BF16), d_rows)
     other = swap(after(jnp.concatenate(wq), dall), "batch")
     grad_tokens = once(
         "last",
@@ -794,30 +788,41 @@
     )[0]
     last = lax.all_to_all(last, SEQ, split_axis=0, concat_axis=0, tiled=True)
     mat = like((cut, width), F32)
-    grad_w_query, grad_w_key, grad_w_value, vec = once(
+    grad_w_query, grad_w_key, grad_w_value, *vec = once(
         "unpack",
         functools.partial(unpack_kernel, heads),
         (last,),
-        [mat, mat, mat, like((8, cut), F32)],
-    )
+        [mat, mat, mat] + [like((1, cut), F32)] * 8,
+    )
+    layer_out, grad_w_up, grad_w_output, *away = once(
+        "close",
+        functools.partial(close_kernel, outer),
+        (scal, own, wo_own, *got, after(middle, grad_tokens), out_keep, rows_in),
+        [like((rows, width), BF16), like((cut, 4 * local), F32), like((cut, width), F32)]
+        + [like((cut, width), BF16)] * (outer - 1),
+    )
+    grad_w_output = grad_w_output + sum(
+        swap(value, "z", k + 1).astype(F32) for k, value in enumerate(away)
+    )
+
     return (
         layer_out[None],
         grad_tokens[None],
-        vec[0],
-        vec[1],
+        vec[0][0],
+        vec[1][0],
         grad_w_query,
-        vec[2],
+        vec[2][0],
         grad_w_key,
         grad_w_value,
-        vec[3],
+        vec[3][0],
         grad_w_output,
-        vec[4],
-        vec[5],
-        vec[6],
+        vec[4][0],
+        vec[5][0],
+        vec[6][0],
         grad_w_up,
         bias[0],
         grad_w_down,
-        vec[7],
+        vec[7][0],
     )
 
 

time: 260 us -> 250 us (0.962)
  starting transfers between devices: 85.4 us -> 78.9 us
  local copies, waits for them, and re-layouts: 14.1 us -> 9.54 us
    all_to_all x1, waiting for transfers between devices: 0.01 us -> 7.27 us  [body(): lax.all_to_all(after(send, zc), SEQ, split_axis=0, concat_axis=0, tiled=T...]
    ppermute x18, waiting for transfers between devices: 38.8 us -> 32.7 us  [swap_plane(): return lax.ppermute(value, ('y', 'x'), [(i, i ^ step) for i in range(4)])]
    ppermute x25 -> x24, waiting for transfers between devices: 38.7 us -> 33.1 us  [swap(): return lax.ppermute(value, axis, [(i, i ^ step) for i in range(size)])]
    all_to_all x1, waiting for transfers between devices: 0.01 us -> 3.76 us  [body(): lax.all_to_all(dchunk, SEQ, split_axis=0, concat_axis=0, tiled=True)]
    ppermute x18, starting transfers between devices: 24.7 us -> 21.6 us  [swap_plane(): return lax.ppermute(value, ('y', 'x'), [(i, i ^ step) for i in range(4)])]
    all_to_all x1, starting transfers between devices: 6.52 us -> 3.74 us  [body(): lax.all_to_all(after(send, zc), SEQ, split_axis=0, concat_axis=0, tiled=T...]
    squeeze x2 -> x0, local copies, waits for them, and re-layouts: 2.7 us -> none  [the longest x1 1.51 us: body(): vec[7]]
    unnamed x101 -> x77, local copies, waits for them, and re-layouts: 10.8 us -> 8.88 us
  transfers between devices with their start and end apart: 48 -> 47, of which waited for: 17 -> 19; matrix products, arithmetic and copies ran while one was open for 3% -> 3% of each run, Pallas kernels for 20% -> 21%
where the time goes in v4:
time: 250 us; the launch traced here: 249 us
  waiting for transfers between devices  82.9 us (33%)
  starting transfers between devices  78.9 us (32%)
  Pallas kernels  67.8 us (27%)
  local copies, waits for them, and re-layouts  9.54 us (4%)
  other arithmetic  5.6 us (2%)
    pallas_call x11, Pallas kernels, once(): pl.pallas_call(kernel, grid=(1,), out_shape=tuple(outs), in_specs=in_spec...  61.2 us
    ppermute x24, waiting for transfers between devices, swap(): return lax.ppermute(value, axis, [(i, i ^ step) for i in range(size)])  33.1 us
    ppermute x18, waiting for transfers between devices, swap_plane(): return lax.ppermute(value, ('y', 'x'), [(i, i ^ step) for i in range(4)])  32.7 us
    ppermute x24, starting transfers between devices, swap(): return lax.ppermute(value, axis, [(i, i ^ step) for i in range(size)])  29.6 us
    ppermute x18, starting transfers between devices, swap_plane(): return lax.ppermute(value, ('y', 'x'), [(i, i ^ step) for i in range(4)])  21.6 us
    all_to_all x1, starting transfers between devices, body(): lax.all_to_all(dchunk, SEQ, split_axis=0, concat_axis=0, tiled=True)  9.19 us
    unnamed x77, local copies, waits for them, and re-layouts  8.88 us
    all_to_all x1, waiting for transfers between devices, body(): lax.all_to_all(after(send, zc), SEQ, split_axis=0, concat_axis=0, tiled=T...  7.27 us
  transfers between devices with their start and end apart: 47, of which 19 were waited for; matrix products, arithmetic and copies ran while one was open for 3% of the time, Pallas kernels for 21%

profile of v4, /device:TPU:0, one launch (start us, length us, event | category | flops | bytes accessed | tf_op | source)
XLA Modules:
  0.0 248.9 jit_solution(11170464874120166568)
XLA Ops:
  1.6 5.1 %collective-permute-start.5 = (bf16[152,768]{1,0:T(8,128)(2,1)S(1)}, bf16[152,768]{1,0:T(8,128)(2,1)S(1)}, u32[]{:S(2)}, u32[]{:S(2)}) collective-permute-start(bf16[152,768]{1,0:T(8,128)(2,1)S(1)} %pad_maximum_fusion.5.ahead), channel_id=1, source_target_pairs={{0,24},{8,16},{16,8},{24,0},{1,25},{9,17},{17,9},{25,1},{2,26},{10... | collective-permute-start | bytes 700424 | tf_op jit(solution)/shard_map/ppermute | solution.py:51
  8.7 2.6 %pack.1 = (bf16[24,768]{1,0:T(8,128)(2,1)}, bf16[176,768]{1,0:T(8,128)(2,1)}, bf16[176,768]{1,0:T(8,128)(2,1)}, bf16[176,768]{1,0:T(8,128)(2,1)}, bf16[16,24,256]{2,1,0:T(8,128)(2,1)}) custom-call(s32[5]{0:T(128)} %stack.55.scal, bf16[128,768]{1,0:T(8,128)(2,1)} %bitcast.37, bf16[24,768]{1,0:T(8,128)(2,1)} %w_out.1, bf16[24,3072]{1,0:T(8,128)(2,1)} %w_up.1, ...), custom_call_target="tpu_custom_call" | custom-call | flops 1 | bytes 1 | tf_op jit(solution)/shard_map/pack/pallas_call | solution.py:83
  17.7 8.9 %collective-permute-done.4 = bf16[152,768]{1,0:T(8,128)(2,1)S(1)} collective-permute-done((bf16[152,768]{1,0:T(8,128)(2,1)S(1)}, bf16[152,768]{1,0:T(8,128)(2,1)S(1)}, u32[]{:S(2)}, u32[]{:S(2)}) %collective-permute-start.4) | collective-permute-done | bytes 233504 | tf_op jit(solution)/shard_map/ppermute | solution.py:51
  29.8 4.1 %collective-permute-start.8 = (bf16[72,768]{1,0:T(8,128)(2,1)S(1)}, bf16[72,768]{1,0:T(8,128)(2,1)}, u32[]{:S(2)}, u32[]{:S(2)}) collective-permute-start(bf16[72,768]{1,0:T(8,128)(2,1)S(1)} %pad_maximum_fusion.6), channel_id=1, source_target_pairs={{0,8},{8,0},{16,24},{24,16},{1,9},{9,1},{17,25},{25,17},{2,10},{10... | collective-permute-start | bytes 331784 | tf_op jit(solution)/shard_map/ppermute | solution.py:51
  37.1 3.7 %all-to-all-start = ((bf16[16,24,256]{2,1,0:T(8,128)(2,1)}), bf16[16,24,256]{2,1,0:T(8,128)(2,1)S(1)}, u32[]{:S(2)}, u32[]{:S(2)}) async-start(bf16[16,24,256]{2,1,0:T(8,128)(2,1)} %get-tuple-element.116), calls=%async_computation | async-start | bytes 393216 | tf_op jit(solution)/shard_map/all_to_all | solution.py:637
  41.7 7.3 %all-to-all-done = bf16[16,24,256]{2,1,0:T(8,128)(2,1)S(1)} async-done(((bf16[16,24,256]{2,1,0:T(8,128)(2,1)}), bf16[16,24,256]{2,1,0:T(8,128)(2,1)S(1)}, u32[]{:S(2)}, u32[]{:S(2)}) %all-to-all-start) | async-done | bytes 196640 | tf_op jit(solution)/shard_map/all_to_all | solution.py:637
  54.7 13.4 %collective-permute-done.16 = bf16[200,768]{1,0:T(8,128)(2,1)S(1)} collective-permute-done((bf16[200,768]{1,0:T(8,128)(2,1)S(1)}, bf16[200,768]{1,0:T(8,128)(2,1)S(1)}, u32[]{:S(2)}, u32[]{:S(2)}) %collective-permute-start.16) | collective-permute-done | bytes 307232 | tf_op jit(solution)/shard_map/ppermute | solution.py:51
  72.9 15.0 %forward.1 = (bf16[2048,768]{1,0:T(8,128)(2,1)}, bf16[2048,768]{1,0:T(8,128)(2,1)}, bf16[192,2048]{1,0:T(8,128)(2,1)}, bf16[16,64,128]{2,1,0:T(8,128)(2,1)}, f32...) custom-call(s32[5]{0:T(128)} %stack.55.scal, ...), custom_call_target="tpu_custom_call" | custom-call | flops 1 | bytes 1 | tf_op jit(solution)/shard_map/forward/pallas_call | solution.py:83
  88.0 3.6 %collective-permute-done.14.wq_c = bf16[4,72,768]{2,1,0:T(8,128)(2,1)S(1)} collective-permute-done((bf16[4,72,768]{2,1,0:T(8,128)(2,1)S(1)}, bf16[4,72,768]{2,1,0:T(8,128)(2,1)S(1)}, u32[]{:S(2)}, u32[]{:S(2)}) %collective-permute-start.14) | collective-permute-done | bytes 442400 | tf_op jit(solution)/shard_map/ppermute | solution.py:55
  93.1 3.9 %all-to-all-start.1 = ((bf16[16,64,128]{2,1,0:T(8,128)(2,1)}), bf16[16,64,128]{2,1,0:T(8,128)(2,1)S(1)}, u32[]{:S(2)}, u32[]{:S(2)}) async-start(bf16[16,64,128]{2,1,0:T(8,128)(2,1)} %get-tuple-element.128), calls=%async_computation.1 | async-start | bytes 524288 | tf_op jit(solution)/shard_map/all_to_all | solution.py:681
  100.6 7.1 %collective-permute-done.18.dy_b = bf16[128,768]{1,0:T(8,128)(2,1)S(1)} collective-permute-done((bf16[128,768]{1,0:T(8,128)(2,1)S(1)}, bf16[128,768]{1,0:T(8,128)(2,1)S(1)}, u32[]{:S(2)}, u32[]{:S(2)}) %collective-permute-start.18) | collective-permute-done | bytes 196640 | tf_op jit(solution)/shard_map/ppermute | solution.py:55
  112.6 2.7 %middle.1 = (f32[128,768]{1,0:T(8,128)}, bf16[128,768]{1,0:T(8,128)(2,1)}) custom-call(s32[5]{0:T(128)} %stack.55.scal, bf16[16,64,128]{2,1,0:T(8,128)(2,1)} %copy-done.6, bf16[16,24,768]{2,1,0:T(8,128)(2,1)} %get-tuple-element.131.own, bf16[16,24,768]{2,1,0:T(8,128)(2,1)} %copy-done.5, bf16[128,768]{1,0:T(8,128)(2,1)} %bitcast.38, ...), custom_call_target="tpu_custom_call" | custom-call | flops 1 | bytes 1 | tf_op jit(solution)/shard_map/middle/pallas_call | solution.py:83
  118.8 4.1 %collective-permute-done.22.n2_b = bf16[128,768]{1,0:T(8,128)(2,1)S(1)} collective-permute-done((bf16[128,768]{1,0:T(8,128)(2,1)}, bf16[128,768]{1,0:T(8,128)(2,1)S(1)}, u32[]{:S(2)}, u32[]{:S(2)}) %collective-permute-start.22) | collective-permute-done | bytes 196640 | tf_op jit(solution)/shard_map/ppermute | solution.py:55
  123.0 3.8 %collective-permute-done.23.n2_c = bf16[128,768]{1,0:T(8,128)(2,1)S(1)} collective-permute-done((bf16[128,768]{1,0:T(8,128)(2,1)}, bf16[128,768]{1,0:T(8,128)(2,1)S(1)}, u32[]{:S(2)}, u32[]{:S(2)}) %collective-permute-start.23) | collective-permute-done | bytes 196640 | tf_op jit(solution)/shard_map/ppermute | solution.py:55
  127.5 8.7 %feed.1 = (f32[128,768]{1,0:T(8,128)}, bf16[128,768]{1,0:T(8,128)(2,1)}, bf16[128,768]{1,0:T(8,128)(2,1)}, bf16[128,768]{1,0:T(8,128)(2,1)}, f32[128,768]{1,0:T(...) custom-call(s32[5]{0:T(128)} %stack.55.scal, ...), custom_call_target="tpu_custom_call" | custom-call | flops 1 | bytes 1 | tf_op jit(solution)/shard_map/feed/pallas_call | solution.py:83
  140.9 3.2 %fold.1 = (f32[200,768]{1,0:T(8,128)}, bf16[200,768]{1,0:T(8,128)(2,1)}, bf16[200,768]{1,0:T(8,128)(2,1)}, bf16[200,768]{1,0:T(8,128)(2,1)}) custom-call(f32[4,200,768]{2,1,0:T(8,128)} %get-tuple-element.139.keep, bf16[4,200,768]{2,1,0:T(8,128)(2,1)} %copy-done.15), custom_call_target="tpu_custom_call" | custom-call | flops 1 | bytes 1 | tf_op jit(solution)/shard_map/fold/pallas_call | solution.py:83
  144.3 3.3 %collective-permute-done.31.got_c = bf16[128,768]{1,0:T(8,128)(2,1)S(1)} collective-permute-done((bf16[128,768]{1,0:T(8,128)(2,1)}, bf16[128,768]{1,0:T(8,128)(2,1)S(1)}, u32[]{:S(2)}, u32[]{:S(2)}) %collective-permute-start.31) | collective-permute-done | bytes 196640 | tf_op jit(solution)/shard_map/ppermute | solution.py:55
  148.8 4.5 %turn.1 = (f32[128,768]{1,0:T(8,128)}, bf16[8,768]{1,0:T(8,128)(2,1)}, bf16[16,64,128]{2,1,0:T(8,128)(2,1)}, f32[8,768]{1,0:T(8,128)}, f32[16,24,768]{2,1,0:T(8,128)}, /*index=5*/bf16[16,24,768]{2,1,0:T(8,128)(2,1)}) custom-call(s32[5]{0:T(128)} %stack.55.scal, f32[128,768]{1,0:T(8,128)} %get-tuple-element.147.keep, bf16[128,768]{1,0:T(8,128)(2,1)} %copy-done.32, ...), custom_call_target="tpu_custom_call" | custom-call | flops 1 | bytes 1 | tf_op jit(solution)/shard_map/turn/pallas_call | solution.py:83
  153.3 5.8 %all-to-all-start.2 = ((bf16[16,64,128]{2,1,0:T(8,128)(2,1)}), bf16[16,64,128]{2,1,0:T(8,128)(2,1)}, u32[]{:S(2)}, u32[]{:S(2)}) async-start(bf16[16,64,128]{2,1,0:T(8,128)(2,1)} %get-tuple-element.152), calls=%async_computation.2 | async-start | bytes 524288 | tf_op jit(solution)/shard_map/all_to_all | solution.py:739
  163.8 6.0 %all-to-all-done.2.dcr = bf16[16,64,128]{2,1,0:T(8,128)(2,1)} async-done(((bf16[16,64,128]{2,1,0:T(8,128)(2,1)}), bf16[16,64,128]{2,1,0:T(8,128)(2,1)}, u32[]{:S(2)}, u32[]{:S(2)}) %all-to-all-start.2) | async-done | bytes 262176 | tf_op jit(solution)/shard_map/all_to_all | solution.py:739
  169.8 12.3 %backward.1 = (bf16[16,192,128]{2,1,0:T(8,128)(2,1)}, bf16[192,2048]{1,0:T(8,128)(2,1)}) custom-call(s32[5]{0:T(128)} %stack.55.scal, bf16[192,2048]{1,0:T(8,128)(2,1)} %get-tuple-element.145.qkvt, bf16[16,64,128]{2,1,0:T(8,128)(2,1)} %all-to-all-done.2.dcr, f32[64,2048]{1,0:T(8,128)} %get-tuple-element.153.ctxt, f32[1,2048]{1,0:T(1,128)} %get-tuple-element.154.lse), custom_call_target="tpu_custom_call" | custom-call | flops 1 | bytes 1 | tf_op jit(solution)/shard_map/backward/pallas_call | solution.py:83
  182.2 6.3 %collective-permute-done.28.refs_1_ = bf16[200,768]{1,0:T(8,128)(2,1)} collective-permute-done((bf16[200,768]{1,0:T(8,128)(2,1)}, bf16[200,768]{1,0:T(8,128)(2,1)}, u32[]{:S(2)}, u32[]{:S(2)}) %collective-permute-start.28) | collective-permute-done | bytes 307232 | tf_op jit(solution)/shard_map/ppermute | solution.py:51
  188.5 9.2 %all-to-all-start.3 = ((bf16[16,192,128]{2,1,0:T(8,128)(2,1)}), bf16[16,192,128]{2,1,0:T(8,128)(2,1)S(1)}, u32[]{:S(2)}, u32[]{:S(2)}) async-start(bf16[16,192,128]{2,1,0:T(8,128)(2,1)} %get-tuple-element.169), calls=%async_computation.3 | async-start | bytes 1572864 | tf_op jit(solution)/shard_map/all_to_all | solution.py:762
  197.8 6.6 %heads.1 = (f32[16,24,256]{2,1,0:T(8,128)}, bf16[16,24,256]{2,1,0:T(8,128)(2,1)}) custom-call(s32[5]{0:T(128)} %stack.55.scal, bf16[192,2048]{1,0:T(8,128)(2,1)} %get-tuple-element.174.dall, bf16[2048,768]{1,0:T(8,128)(2,1)} %get-tuple-element.180.n1, bf16[2048,768]{1,0:T(8,128)(2,1)} %get-tuple-element.181.n0, bf16[192,768]{1,0:T(8,128)(2,1)} %get-tuple-element.182.wt, ...), custom_call_target="tpu_custom_call" | custom-call | flops 1 | bytes 1 | tf_op jit(solution)/shard_map/heads/pallas_call | solution.py:544
  205.7 3.4 %finish.1 = (f32[96,768]{1,0:T(8,128)}, f32[1,96]{1,0:T(1,128)}, bf16[24,768]{1,0:T(8,128)(2,1)}, f32[4,24,768]{2,1,0:T(8,128)}, bf16[248,768]{1,0:T(8,128)(2,1)...) custom-call(s32[5]{0:T(128)} %stack.55.scal, f32[200,768]{1,0:T(8,128)} %get-tuple-element.141.keep, ...), custom_call_target="tpu_custom_call" | custom-call | flops 1 | bytes 1 | tf_op jit(solution)/shard_map/finish/pallas_call | solution.py:83
  213.4 3.8 %all-to-all-done.3.d_rows = bf16[16,192,128]{2,1,0:T(8,128)(2,1)S(1)} async-done(((bf16[16,192,128]{2,1,0:T(8,128)(2,1)}), bf16[16,192,128]{2,1,0:T(8,128)(2,1)S(1)}, u32[]{:S(2)}, u32[]{:S(2)}) %all-to-all-start.3) | async-done | bytes 786464 | tf_op jit(solution)/shard_map/all_to_all | solution.py:762
  217.1 5.1 %all-to-all-start.4 = ((bf16[16,24,256]{2,1,0:T(8,128)(2,1)}), bf16[16,24,256]{2,1,0:T(8,128)(2,1)S(1)}, u32[]{:S(2)}, u32[]{:S(2)}) async-start(bf16[16,24,256]{2,1,0:T(8,128)(2,1)} %add_convert_fusion), calls=%async_computation.4 | async-start | bytes 393216 | tf_op jit(solution)/shard_map/all_to_all | solution.py:789
  222.3 4.5 %last.1 = f32[128,768]{1,0:T(8,128)} custom-call(s32[5]{0:T(128)} %stack.55.scal, bf16[16,192,128]{2,1,0:T(8,128)(2,1)} %copy-done.2, bf16[4,72,768]{2,1,0:T(8,128)(2,1)} %copy-done.1, bf16[4,72,768]{2,1,0:T(8,128)(2,1)} %copy-done.8, bf16[4,72,768]{2,1,0:T(8,128)(2,1)} %copy-done.10, bf16[4,72,768]{2,1,0:T(8,128)(2,1)} %copy-done.12, ...), custom_call_target="tpu_custom_call" | custom-call | flops 1 | bytes 1 | tf_op jit(solution)/shard_map/last/pallas_call | solution.py:83
  226.8 5.3 %collective-permute-done.35.got_c = bf16[248,768]{1,0:T(8,128)(2,1)} collective-permute-done((bf16[248,768]{1,0:T(8,128)(2,1)}, bf16[248,768]{1,0:T(8,128)(2,1)}, u32[]{:S(2)}, u32[]{:S(2)}) %collective-permute-start.35) | collective-permute-done | bytes 380960 | tf_op jit(solution)/shard_map/ppermute | solution.py:55
  233.4 2.6 %close.1 = (bf16[128,768]{1,0:T(8,128)(2,1)}, f32[24,3072]{1,0:T(8,128)}, f32[24,768]{1,0:T(8,128)}, bf16[24,768]{1,0:T(8,128)(2,1)}, bf16[24,768]{1,0:T(8,128)(2,1)}, /*index=5*/bf16[24,768]{1,0:T(8,128)(2,1)}) custom-call(s32[5]{0:T(128)} %stack.55.scal, bf16[24,768]{1,0:T(8,128)(2,1)} %get-tuple-element.164.own, f32[4,24,768]{2,1,0:T(8,128)} %get-tuple-element.165.wo_own, ...), custom_call_target="tpu_custom_call" | custom-call | flops 1 | bytes 1 | tf_op jit(solution)/shard_map/close/pallas_call | solution.py:83
  236.0 3.8 %collective-permute-start.41 = (bf16[24,768]{1,0:T(8,128)(2,1)}, bf16[24,768]{1,0:T(8,128)(2,1)S(1)}, u32[]{:S(2)}, u32[]{:S(2)}) collective-permute-start(bf16[24,768]{1,0:T(8,128)(2,1)} %get-tuple-element.197), channel_id=1, source_target_pairs={{0,24},{8,16},{16,8},{24,0},{1,25},{9,17},{17,9},{25,1},{2,26},{10... | collective-permute-start | bytes 110600 | tf_op jit(solution)/shard_map/ppermute | solution.py:51
  242.3 2.5 %collective-permute-done.40 = bf16[24,768]{1,0:T(8,128)(2,1)S(1)} collective-permute-done((bf16[24,768]{1,0:T(8,128)(2,1)}, bf16[24,768]{1,0:T(8,128)(2,1)S(1)}, u32[]{:S(2)}, u32[]{:S(2)}) %collective-permute-start.40) | collective-permute-done | bytes 36896 | tf_op jit(solution)/shard_map/ppermute | solution.py:51
  (165 shorter events, 64.5 us)
Async XLA Ops:
  1.6 13.7 %collective-permute-start.5 = (bf16[152,768]{1,0:T(8,128)(2,1)S(1)}, bf16[152,768]{1,0:T(8,128)(2,1)S(1)}, u32[]{:S(2)}, u32[]{:S(2)}) collective-permute-start(bf16[152,768]{1,0:T(8,128)(2,1)S(1)} %pad_maximum_fusion.5.ahead), channel_id=1, source_target_pairs={{0,24},{8,16},{16,8},{24,0},{1,25},{9,17},{17,9},{25,1},{2,26},{10... | collective-permute-start | bytes 700424 | tf_op jit(solution)/shard_map/ppermute | solution.py:51
  6.8 19.9 %collective-permute-start.4 = (bf16[152,768]{1,0:T(8,128)(2,1)S(1)}, bf16[152,768]{1,0:T(8,128)(2,1)S(1)}, u32[]{:S(2)}, u32[]{:S(2)}) collective-permute-start(bf16[152,768]{1,0:T(8,128)(2,1)S(1)} %pad_maximum_fusion.5.ahead), channel_id=1, source_target_pairs={{0,16},{8,24},{16,0},{24,8},{1,17},{9,25},{17,1},{25,9},{2,18},{10... | collective-permute-start | bytes 700424 | tf_op jit(solution)/shard_map/ppermute | solution.py:51
  6.8 19.9 %collective-permute-start.3 = (bf16[152,768]{1,0:T(8,128)(2,1)S(1)}, bf16[152,768]{1,0:T(8,128)(2,1)S(1)}, u32[]{:S(2)}, u32[]{:S(2)}) collective-permute-start(bf16[152,768]{1,0:T(8,128)(2,1)S(1)} %pad_maximum_fusion.5.ahead), channel_id=1, source_target_pairs={{0,8},{8,0},{16,24},{24,16},{1,9},{9,1},{17,25},{25,17},{2,10},{10... | collective-permute-start | bytes 700424 | tf_op jit(solution)/shard_map/ppermute | solution.py:51
  11.2 15.5 %collective-permute-start = (bf16[176,768]{1,0:T(8,128)(2,1)}, bf16[176,768]{1,0:T(8,128)(2,1)S(1)}, u32[]{:S(2)}, u32[]{:S(2)}) collective-permute-start(bf16[176,768]{1,0:T(8,128)(2,1)} %get-tuple-element.111), channel_id=1, source_target_pairs={{0,2},{2,0},{4,6},{6,4},{1,3},{3,1},{5,7},{7,5},{8,10},{10,8},{12,... | collective-permute-start | bytes 811016 | tf_op jit(solution)/shard_map/ppermute | solution.py:55
  12.9 13.9 %collective-permute-start.1 = (bf16[176,768]{1,0:T(8,128)(2,1)}, bf16[176,768]{1,0:T(8,128)(2,1)S(1)}, u32[]{:S(2)}, u32[]{:S(2)}) collective-permute-start(bf16[176,768]{1,0:T(8,128)(2,1)} %get-tuple-element.112), channel_id=1, source_target_pairs={{0,4},{2,6},{4,0},{6,2},{1,5},{3,7},{5,1},{7,3},{8,12},{10,14},{12... | collective-permute-start | bytes 811016 | tf_op jit(solution)/shard_map/ppermute | solution.py:55
  15.3 11.4 %collective-permute-start.2 = (bf16[176,768]{1,0:T(8,128)(2,1)}, bf16[176,768]{1,0:T(8,128)(2,1)}, u32[]{:S(2)}, u32[]{:S(2)}) collective-permute-start(bf16[176,768]{1,0:T(8,128)(2,1)} %get-tuple-element.113), channel_id=1, source_target_pairs={{0,6},{2,4},{4,2},{6,0},{1,7},{3,5},{5,3},{7,1},{8,14},{10,12},{12... | collective-permute-start | bytes 811016 | tf_op jit(solution)/shard_map/ppermute | solution.py:55
  26.8 24.4 %collective-permute-start.6 = (bf16[3,152,768]{2,1,0:T(8,128)(2,1)S(1)}, bf16[3,152,768]{2,1,0:T(8,128)(2,1)S(1)}, u32[]{:S(2)}, u32[]{:S(2)}) collective-permute-start(bf16[3,152,768]{2,1,0:T(8,128)(2,1)S(1)} %pad_maximum_fusion.2.zc), channel_id=1, source_target_pairs={{0,2},{2,0},{1,3},{3,1},{4,6},{6,4},{5,7},{7,5},{8,10},{10,8},{9,1... | collective-permute-start | bytes 2101256 | tf_op jit(solution)/shard_map/ppermute | solution.py:51
  28.3 22.9 %collective-permute-start.7 = (bf16[3,152,768]{2,1,0:T(8,128)(2,1)S(1)}, bf16[3,152,768]{2,1,0:T(8,128)(2,1)S(1)}, u32[]{:S(2)}, u32[]{:S(2)}) collective-permute-start(bf16[3,152,768]{2,1,0:T(8,128)(2,1)S(1)} %pad_maximum_fusion.2.zc), channel_id=1, source_target_pairs={{0,4},{4,0},{1,5},{5,1},{2,6},{6,2},{3,7},{7,3},{8,12},{12,8},{9,1... | collective-permute-start | bytes 2101256 | tf_op jit(solution)/shard_map/ppermute | solution.py:51
  29.8 21.3 %collective-permute-start.8 = (bf16[72,768]{1,0:T(8,128)(2,1)S(1)}, bf16[72,768]{1,0:T(8,128)(2,1)}, u32[]{:S(2)}, u32[]{:S(2)}) collective-permute-start(bf16[72,768]{1,0:T(8,128)(2,1)S(1)} %pad_maximum_fusion.6), channel_id=1, source_target_pairs={{0,8},{8,0},{16,24},{24,16},{1,9},{9,1},{17,25},{25,17},{2,10},{10... | collective-permute-start | bytes 331784 | tf_op jit(solution)/shard_map/ppermute | solution.py:51
  34.0 17.2 %collective-permute-start.9 = (bf16[72,768]{1,0:T(8,128)(2,1)S(1)}, bf16[72,768]{1,0:T(8,128)(2,1)}, u32[]{:S(2)}, u32[]{:S(2)}) collective-permute-start(bf16[72,768]{1,0:T(8,128)(2,1)S(1)} %pad_maximum_fusion.6), channel_id=1, source_target_pairs={{0,16},{8,24},{16,0},{24,8},{1,17},{9,25},{17,1},{25,9},{2,18},{10... | collective-permute-start | bytes 331784 | tf_op jit(solution)/shard_map/ppermute | solution.py:51
  35.6 15.5 %collective-permute-start.10 = (bf16[72,768]{1,0:T(8,128)(2,1)S(1)}, bf16[72,768]{1,0:T(8,128)(2,1)}, u32[]{:S(2)}, u32[]{:S(2)}) collective-permute-start(bf16[72,768]{1,0:T(8,128)(2,1)S(1)} %pad_maximum_fusion.6), channel_id=1, source_target_pairs={{0,24},{8,16},{16,8},{24,0},{1,25},{9,17},{17,9},{25,1},{2,26},{10... | collective-permute-start | bytes 331784 | tf_op jit(solution)/shard_map/ppermute | solution.py:51
  37.1 11.8 %all-to-all-start = ((bf16[16,24,256]{2,1,0:T(8,128)(2,1)}), bf16[16,24,256]{2,1,0:T(8,128)(2,1)S(1)}, u32[]{:S(2)}, u32[]{:S(2)}) async-start(bf16[16,24,256]{2,1,0:T(8,128)(2,1)} %get-tuple-element.116), calls=%async_computation | async-start | bytes 393216 | tf_op jit(solution)/shard_map/all_to_all | solution.py:637
  51.2 16.9 %collective-permute-start.16 = (bf16[200,768]{1,0:T(8,128)(2,1)S(1)}, bf16[200,768]{1,0:T(8,128)(2,1)S(1)}, u32[]{:S(2)}, u32[]{:S(2)}) collective-permute-start(bf16[200,768]{1,0:T(8,128)(2,1)S(1)} %constant_dynamic-update-slice_fusion), channel_id=1, source_target_pairs={{0,16},{8,24},{16,0},{24,8},{1,17},{9,25},{17,1},{25,9},{2,18},{10... | collective-permute-start | bytes 921608 | tf_op jit(solution)/shard_map/ppermute | solution.py:51
  52.4 17.0 %collective-permute-start.11 = (bf16[2,152,768]{2,1,0:T(8,128)(2,1)S(1)}, bf16[2,152,768]{2,1,0:T(8,128)(2,1)}, u32[]{:S(2)}, u32[]{:S(2)}) collective-permute-start(bf16[2,152,768]{2,1,0:T(8,128)(2,1)S(1)} %slice.15), channel_id=1, source_target_pairs={{0,4},{4,0},{1,5},{5,1},{2,6},{6,2},{3,7},{7,3},{8,12},{12,8},{9,1... | collective-permute-start | bytes 1400840 | tf_op jit(solution)/shard_map/ppermute | solution.py:51
  53.6 15.7 %collective-permute-start.12 = (bf16[1,152,768]{2,1,0:T(8,128)(2,1)S(1)}, bf16[1,152,768]{2,1,0:T(8,128)(2,1)S(1)}, u32[]{:S(2)}, u32[]{:S(2)}) collective-permute-start(bf16[1,152,768]{2,1,0:T(8,128)(2,1)S(1)} %slice.16), channel_id=1, source_target_pairs={{0,2},{2,0},{1,3},{3,1},{4,6},{6,4},{5,7},{7,5},{8,10},{10,8},{9,1... | collective-permute-start | bytes 700424 | tf_op jit(solution)/shard_map/ppermute | solution.py:51
  68.2 23.4 %collective-permute-start.17 = (bf16[2,200,768]{2,1,0:T(8,128)(2,1)S(1)}, bf16[2,200,768]{2,1,0:T(8,128)(2,1)S(1)}, u32[]{:S(2)}, u32[]{:S(2)}) collective-permute-start(bf16[2,200,768]{2,1,0:T(8,128)(2,1)S(1)} %pad_maximum_fusion.3), channel_id=1, source_target_pairs={{0,8},{8,0},{16,24},{24,16},{1,9},{9,1},{17,25},{25,17},{2,10},{10... | collective-permute-start | bytes 1843208 | tf_op jit(solution)/shard_map/ppermute | solution.py:51
  69.3 18.6 %collective-permute-start.13 = (bf16[4,72,768]{2,1,0:T(8,128)(2,1)S(1)}, bf16[4,72,768]{2,1,0:T(8,128)(2,1)S(1)}, u32[]{:S(2)}, u32[]{:S(2)}) collective-permute-start(bf16[4,72,768]{2,1,0:T(8,128)(2,1)S(1)} %pad_maximum_fusion.4.wq_a), channel_id=1, source_target_pairs={{0,2},{2,0},{4,6},{6,4},{1,3},{3,1},{5,7},{7,5},{8,10},{10,8},{12,... | collective-permute-start | bytes 1327112 | tf_op jit(solution)/shard_map/ppermute | solution.py:55
  70.2 21.3 %collective-permute-start.14 = (bf16[4,72,768]{2,1,0:T(8,128)(2,1)S(1)}, bf16[4,72,768]{2,1,0:T(8,128)(2,1)S(1)}, u32[]{:S(2)}, u32[]{:S(2)}) collective-permute-start(bf16[4,72,768]{2,1,0:T(8,128)(2,1)S(1)} %pad_maximum_fusion.4.wq_a), channel_id=1, source_target_pairs={{0,4},{2,6},{4,0},{6,2},{1,5},{3,7},{5,1},{7,3},{8,12},{10,14},{12... | collective-permute-start | bytes 1327112 | tf_op jit(solution)/shard_map/ppermute | solution.py:55
  70.8 20.7 %collective-permute-start.15 = (bf16[4,72,768]{2,1,0:T(8,128)(2,1)S(1)}, bf16[4,72,768]{2,1,0:T(8,128)(2,1)S(1)}, u32[]{:S(2)}, u32[]{:S(2)}) collective-permute-start(bf16[4,72,768]{2,1,0:T(8,128)(2,1)S(1)} %pad_maximum_fusion.4.wq_a), channel_id=1, source_target_pairs={{0,6},{2,4},{4,2},{6,0},{1,7},{3,5},{5,3},{7,1},{8,14},{10,12},{12... | collective-permute-start | bytes 1327112 | tf_op jit(solution)/shard_map/ppermute | solution.py:55
  92.5 34.3 %collective-permute-start.25 = (bf16[4,200,768]{2,1,0:T(8,128)(2,1)S(1)}, bf16[4,200,768]{2,1,0:T(8,128)(2,1)}, u32[]{:S(2)}, u32[]{:S(2)}) collective-permute-start(bf16[4,200,768]{2,1,0:T(8,128)(2,1)S(1)} %pad_maximum_fusion.1.ffz), channel_id=1, source_target_pairs={{0,1},{1,0},{2,3},{3,2},{4,5},{5,4},{6,7},{7,6},{8,9},{9,8},{10,11... | collective-permute-start | bytes 3686408 | tf_op jit(solution)/shard_map/ppermute | solution.py:51
  92.6 19.2 %collective-permute-start.21 = (bf16[16,24,768]{2,1,0:T(8,128)(2,1)S(1)}, bf16[16,24,768]{2,1,0:T(8,128)(2,1)S(1)}, u32[]{:S(2)}, u32[]{:S(2)}) collective-permute-start(bf16[16,24,768]{2,1,0:T(8,128)(2,1)S(1)} %copy-done.4), channel_id=1, source_target_pairs={{0,1},{1,0},{2,3},{3,2},{4,5},{5,4},{6,7},{7,6},{8,9},{9,8},{10,11... | collective-permute-start | bytes 1769480 | tf_op jit(solution)/shard_map/ppermute | solution.py:51
  93.1 18.6 %all-to-all-start.1 = ((bf16[16,64,128]{2,1,0:T(8,128)(2,1)}), bf16[16,64,128]{2,1,0:T(8,128)(2,1)S(1)}, u32[]{:S(2)}, u32[]{:S(2)}) async-start(bf16[16,64,128]{2,1,0:T(8,128)(2,1)} %get-tuple-element.128), calls=%async_computation.1 | async-start | bytes 524288 | tf_op jit(solution)/shard_map/all_to_all | solution.py:681
  153.3 16.5 %all-to-all-start.2 = ((bf16[16,64,128]{2,1,0:T(8,128)(2,1)}), bf16[16,64,128]{2,1,0:T(8,128)(2,1)}, u32[]{:S(2)}, u32[]{:S(2)}) async-start(bf16[16,64,128]{2,1,0:T(8,128)(2,1)} %get-tuple-element.152), calls=%async_computation.2 | async-start | bytes 524288 | tf_op jit(solution)/shard_map/all_to_all | solution.py:739
  159.1 23.0 %collective-permute-start.27 = (bf16[200,768]{1,0:T(8,128)(2,1)}, bf16[200,768]{1,0:T(8,128)(2,1)}, u32[]{:S(2)}, u32[]{:S(2)}) collective-permute-start(bf16[200,768]{1,0:T(8,128)(2,1)} %get-tuple-element.142), channel_id=1, source_target_pairs={{0,8},{8,0},{16,24},{24,16},{1,9},{9,1},{17,25},{25,17},{2,10},{10... | collective-permute-start | bytes 921608 | tf_op jit(solution)/shard_map/ppermute | solution.py:51
  161.0 27.5 %collective-permute-start.28 = (bf16[200,768]{1,0:T(8,128)(2,1)}, bf16[200,768]{1,0:T(8,128)(2,1)}, u32[]{:S(2)}, u32[]{:S(2)}) collective-permute-start(bf16[200,768]{1,0:T(8,128)(2,1)} %get-tuple-element.143), channel_id=1, source_target_pairs={{0,16},{8,24},{16,0},{24,8},{1,17},{9,25},{17,1},{25,9},{2,18},{10... | collective-permute-start | bytes 921608 | tf_op jit(solution)/shard_map/ppermute | solution.py:51
  163.4 25.1 %collective-permute-start.29 = (bf16[200,768]{1,0:T(8,128)(2,1)}, bf16[200,768]{1,0:T(8,128)(2,1)}, u32[]{:S(2)}, u32[]{:S(2)}) collective-permute-start(bf16[200,768]{1,0:T(8,128)(2,1)} %get-tuple-element.144), channel_id=1, source_target_pairs={{0,24},{8,16},{16,8},{24,0},{1,25},{9,17},{17,9},{25,1},{2,26},{10... | collective-permute-start | bytes 921608 | tf_op jit(solution)/shard_map/ppermute | solution.py:51
  182.2 40.1 %collective-permute-start.37 = (bf16[16,72,768]{2,1,0:T(8,128)(2,1)S(1)}, bf16[16,72,768]{2,1,0:T(8,128)(2,1)}, u32[]{:S(2)}, u32[]{:S(2)}) collective-permute-start(bf16[16,72,768]{2,1,0:T(8,128)(2,1)S(1)} %pad_maximum_fusion), channel_id=1, source_target_pairs={{0,1},{1,0},{2,3},{3,2},{4,5},{5,4},{6,7},{7,6},{8,9},{9,8},{10,11... | collective-permute-start | bytes 5308424 | tf_op jit(solution)/shard_map/ppermute | solution.py:51
  188.5 28.6 %all-to-all-start.3 = ((bf16[16,192,128]{2,1,0:T(8,128)(2,1)}), bf16[16,192,128]{2,1,0:T(8,128)(2,1)S(1)}, u32[]{:S(2)}, u32[]{:S(2)}) async-start(bf16[16,192,128]{2,1,0:T(8,128)(2,1)} %get-tuple-element.169), calls=%async_computation.3 | async-start | bytes 1572864 | tf_op jit(solution)/shard_map/all_to_all | solution.py:762
  209.1 17.6 %collective-permute-start.34 = (bf16[248,768]{1,0:T(8,128)(2,1)}, bf16[248,768]{1,0:T(8,128)(2,1)S(1)}, u32[]{:S(2)}, u32[]{:S(2)}) collective-permute-start(bf16[248,768]{1,0:T(8,128)(2,1)} %get-tuple-element.166), channel_id=1, source_target_pairs={{0,2},{2,0},{4,6},{6,4},{1,3},{3,1},{5,7},{7,5},{8,10},{10,8},{12,... | collective-permute-start | bytes 1142792 | tf_op jit(solution)/shard_map/ppermute | solution.py:55
  211.1 21.0 %collective-permute-start.35 = (bf16[248,768]{1,0:T(8,128)(2,1)}, bf16[248,768]{1,0:T(8,128)(2,1)}, u32[]{:S(2)}, u32[]{:S(2)}) collective-permute-start(bf16[248,768]{1,0:T(8,128)(2,1)} %get-tuple-element.167), channel_id=1, source_target_pairs={{0,4},{2,6},{4,0},{6,2},{1,5},{3,7},{5,1},{7,3},{8,12},{10,14},{12... | collective-permute-start | bytes 1142792 | tf_op jit(solution)/shard_map/ppermute | solution.py:55
  212.5 20.9 %collective-permute-start.36 = (bf16[248,768]{1,0:T(8,128)(2,1)}, bf16[248,768]{1,0:T(8,128)(2,1)}, u32[]{:S(2)}, u32[]{:S(2)}) collective-permute-start(bf16[248,768]{1,0:T(8,128)(2,1)} %get-tuple-element.168), channel_id=1, source_target_pairs={{0,6},{2,4},{4,2},{6,0},{1,7},{3,5},{5,3},{7,1},{8,14},{10,12},{12... | collective-permute-start | bytes 1142792 | tf_op jit(solution)/shard_map/ppermute | solution.py:55
  217.1 29.3 %all-to-all-start.4 = ((bf16[16,24,256]{2,1,0:T(8,128)(2,1)}), bf16[16,24,256]{2,1,0:T(8,128)(2,1)S(1)}, u32[]{:S(2)}, u32[]{:S(2)}) async-start(bf16[16,24,256]{2,1,0:T(8,128)(2,1)} %add_convert_fusion), calls=%async_computation.4 | async-start | bytes 393216 | tf_op jit(solution)/shard_map/all_to_all | solution.py:789
  (51 other events, 681.5 us)

commit v5 on v4

--- a/solution.py
+++ b/solution.py
@@ -441,9 +441,14 @@
         wo_send[i] = full[2 * i + 1 - scal[CORE]].astype(BF16)
 
 
-def fold_kernel(keep, got, own, *away):
-    for k, ref in enumerate((own,) + away):
-        ref[...] = (keep[k] + got[k].astype(F32)).astype(ref.dtype)
+def fold_kernel(keep, got, own, away):
+    for i, (k, ref) in enumerate(((0, own), (2, own), (1, away), (3, away))):
+        ref[i % 2] = (keep[k] + got[k].astype(F32)).astype(ref.dtype)
+
+
+def second_kernel(keep, got, own, away):
+    own[...] = keep[0] + got[0].astype(F32)
+    away[...] = (keep[1] + got[1].astype(F32)).astype(BF16)
 
 
 def finish_kernel(scal, keep, *refs):
@@ -714,13 +719,13 @@
     dn_got = [swap_plane(value, k + 1) for k, value in enumerate(dn_send)]
 
     count = 2 * half + 8
-    own, *away = once(
+    pair = like((2, count, width), F32)
+    own, away = once(
         "fold",
         fold_kernel,
-        (keep, swap(send, "batch")),
-        [like((count, width), F32)] + [like((count, width), BF16)] * (outer - 1),
-    )
-    back = [swap(value, "z", k + 1) for k, value in enumerate(away)]
+        (keep, after(swap(send, "batch"), *dn_got)),
+        [pair, like(pair.shape, BF16)],
+    )
     dn_keep, _ = lax.optimization_barrier((dn_keep, away))
     d_middle, _, d_ctx, sums, wo_keep, wo_send = once(
         "turn",
@@ -739,12 +744,19 @@
     d_ctx = lax.all_to_all(d_ctx, SEQ, split_axis=0, concat_axis=0, tiled=True)
 
     wo_got = swap(wo_send, "batch")
+    own, away = once(
+        "second",
+        second_kernel,
+        (own, swap(away, "z", 1)),
+        [like((count, width), F32), like((count, width), BF16)],
+    )
+    back = [swap(away, "z", 2)]
 
     blk = split(length)
     dchunk, dall = once(
         "backward",
         backward_kernel,
-        (scal, qkvt, d_ctx, ctxt, lse),
+        (after(scal, away), qkvt, d_ctx, ctxt, lse),
         [like((seq, 3 * HD, rows), BF16), like((3 * HD, length), BF16)],
         [
             pltpu.VMEM((length, HD), BF16),

time: 250 us -> 246 us (0.984)
  starting transfers between devices: 78.9 us -> 73.2 us
  Pallas kernels: 67.8 us -> 71.5 us
    all_to_all x1, waiting for transfers between devices: 6.02 us -> 0.01 us  [body(): d_ctx = lax.all_to_all(d_ctx, SEQ, split_axis=0, concat_axis=0, tiled=True)]
    all_to_all x1, starting transfers between devices: 9.19 us -> 5.35 us  [body(): lax.all_to_all(dchunk, SEQ, split_axis=0, concat_axis=0, tiled=True)]
    pallas_call x11 -> x12, Pallas kernels: 61.2 us -> 64.9 us  [once(): pl.pallas_call(kernel, grid=(1,), out_shape=tuple(outs), in_specs=in_spec...]
    ppermute x18, waiting for transfers between devices: 32.7 us -> 35.4 us  [swap_plane(): return lax.ppermute(value, ('y', 'x'), [(i, i ^ step) for i in range(4)])]
    ppermute x24 -> x23, starting transfers between devices: 29.6 us -> 28.1 us  [swap(): return lax.ppermute(value, axis, [(i, i ^ step) for i in range(size)])]
    ppermute x24 -> x23, waiting for transfers between devices: 33.1 us -> 34 us  [swap(): return lax.ppermute(value, axis, [(i, i ^ step) for i in range(size)])]
    unnamed x77 -> x79, local copies, waits for them, and re-layouts: 8.88 us -> 9.08 us
  transfers between devices with their start and end apart: 47 -> 46, of which waited for: 19 -> 17; matrix products, arithmetic and copies ran while one was open for 3% -> 3% of each run, Pallas kernels for 21% -> 23%
where the time goes in v5:
time: 246 us
  waiting for transfers between devices  81.4 us (33%)
  starting transfers between devices  73.2 us (30%)
  Pallas kernels  71.5 us (29%)
  local copies, waits for them, and re-layouts  9.74 us (4%)
  other arithmetic  5.58 us (2%)
    pallas_call x12, Pallas kernels, once(): pl.pallas_call(kernel, grid=(1,), out_shape=tuple(outs), in_specs=in_spec...  64.9 us
    ppermute x18, waiting for transfers between devices, swap_plane(): return lax.ppermute(value, ('y', 'x'), [(i, i ^ step) for i in range(4)])  35.4 us
    ppermute x23, waiting for transfers between devices, swap(): return lax.ppermute(value, axis, [(i, i ^ step) for i in range(size)])  34 us
    ppermute x23, starting transfers between devices, swap(): return lax.ppermute(value, axis, [(i, i ^ step) for i in range(size)])  28.1 us
    ppermute x18, starting transfers between devices, swap_plane(): return lax.ppermute(value, ('y', 'x'), [(i, i ^ step) for i in range(4)])  21.6 us
    unnamed x79, local copies, waits for them, and re-layouts  9.08 us
    all_to_all x1, waiting for transfers between devices, body(): lax.all_to_all(after(send, zc), SEQ, split_axis=0, concat_axis=0, tiled=T...  7.27 us
    pallas_call x1, Pallas kernels, head_grads(): pl.pallas_call(functools.partial(heads_kernel, heads), out_shape=outs, gr...  6.59 us
  transfers between devices with their start and end apart: 46, of which 17 were waited for; matrix products, arithmetic and copies ran while one was open for 3% of the time, Pallas kernels for 23%

profile of v5, /device:TPU:0, one launch (start us, length us, event | category | flops | bytes accessed | tf_op | source)
XLA Modules:
  0.0 245.7 jit_solution(13867059085968768363)
XLA Ops:
  1.6 5.1 %collective-permute-start.5 = (bf16[152,768]{1,0:T(8,128)(2,1)S(1)}, bf16[152,768]{1,0:T(8,128)(2,1)S(1)}, u32[]{:S(2)}, u32[]{:S(2)}) collective-permute-start(bf16[152,768]{1,0:T(8,128)(2,1)S(1)} %pad_maximum_fusion.5.ahead), channel_id=1, source_target_pairs={{0,24},{8,16},{16,8},{24,0},{1,25},{9,17},{17,9},{25,1},{2,26},{10... | collective-permute-start | bytes 700424 | tf_op jit(solution)/shard_map/ppermute | solution.py:51
  8.7 2.6 %pack.1 = (bf16[24,768]{1,0:T(8,128)(2,1)}, bf16[176,768]{1,0:T(8,128)(2,1)}, bf16[176,768]{1,0:T(8,128)(2,1)}, bf16[176,768]{1,0:T(8,128)(2,1)}, bf16[16,24,256]{2,1,0:T(8,128)(2,1)}) custom-call(s32[5]{0:T(128)} %stack.55.scal, bf16[128,768]{1,0:T(8,128)(2,1)} %bitcast.37, bf16[24,768]{1,0:T(8,128)(2,1)} %w_out.1, bf16[24,3072]{1,0:T(8,128)(2,1)} %w_up.1, ...), custom_call_target="tpu_custom_call" | custom-call | flops 1 | bytes 1 | tf_op jit(solution)/shard_map/pack/pallas_call | solution.py:83
  17.7 8.9 %collective-permute-done.4 = bf16[152,768]{1,0:T(8,128)(2,1)S(1)} collective-permute-done((bf16[152,768]{1,0:T(8,128)(2,1)S(1)}, bf16[152,768]{1,0:T(8,128)(2,1)S(1)}, u32[]{:S(2)}, u32[]{:S(2)}) %collective-permute-start.4) | collective-permute-done | bytes 233504 | tf_op jit(solution)/shard_map/ppermute | solution.py:51
  29.8 4.1 %collective-permute-start.8 = (bf16[72,768]{1,0:T(8,128)(2,1)S(1)}, bf16[72,768]{1,0:T(8,128)(2,1)}, u32[]{:S(2)}, u32[]{:S(2)}) collective-permute-start(bf16[72,768]{1,0:T(8,128)(2,1)S(1)} %pad_maximum_fusion.6), channel_id=1, source_target_pairs={{0,8},{8,0},{16,24},{24,16},{1,9},{9,1},{17,25},{25,17},{2,10},{10... | collective-permute-start | bytes 331784 | tf_op jit(solution)/shard_map/ppermute | solution.py:51
  37.1 3.7 %all-to-all-start = ((bf16[16,24,256]{2,1,0:T(8,128)(2,1)}), bf16[16,24,256]{2,1,0:T(8,128)(2,1)S(1)}, u32[]{:S(2)}, u32[]{:S(2)}) async-start(bf16[16,24,256]{2,1,0:T(8,128)(2,1)} %get-tuple-element.116), calls=%async_computation | async-start | bytes 393216 | tf_op jit(solution)/shard_map/all_to_all | solution.py:642
  41.7 7.3 %all-to-all-done = bf16[16,24,256]{2,1,0:T(8,128)(2,1)S(1)} async-done(((bf16[16,24,256]{2,1,0:T(8,128)(2,1)}), bf16[16,24,256]{2,1,0:T(8,128)(2,1)S(1)}, u32[]{:S(2)}, u32[]{:S(2)}) %all-to-all-start) | async-done | bytes 196640 | tf_op jit(solution)/shard_map/all_to_all | solution.py:642
  54.7 13.4 %collective-permute-done.16 = bf16[200,768]{1,0:T(8,128)(2,1)S(1)} collective-permute-done((bf16[200,768]{1,0:T(8,128)(2,1)S(1)}, bf16[200,768]{1,0:T(8,128)(2,1)S(1)}, u32[]{:S(2)}, u32[]{:S(2)}) %collective-permute-start.16) | collective-permute-done | bytes 307232 | tf_op jit(solution)/shard_map/ppermute | solution.py:51
  72.9 15.7 %forward.1 = (bf16[2048,768]{1,0:T(8,128)(2,1)}, bf16[2048,768]{1,0:T(8,128)(2,1)}, bf16[192,2048]{1,0:T(8,128)(2,1)}, bf16[16,64,128]{2,1,0:T(8,128)(2,1)}, f32...) custom-call(s32[5]{0:T(128)} %stack.55.scal, ...), custom_call_target="tpu_custom_call" | custom-call | flops 1 | bytes 1 | tf_op jit(solution)/shard_map/forward/pallas_call | solution.py:83
  88.7 2.9 %collective-permute-done.14.wq_c = bf16[4,72,768]{2,1,0:T(8,128)(2,1)S(1)} collective-permute-done((bf16[4,72,768]{2,1,0:T(8,128)(2,1)S(1)}, bf16[4,72,768]{2,1,0:T(8,128)(2,1)S(1)}, u32[]{:S(2)}, u32[]{:S(2)}) %collective-permute-start.14) | collective-permute-done | bytes 442400 | tf_op jit(solution)/shard_map/ppermute | solution.py:55
  93.1 3.9 %all-to-all-start.1 = ((bf16[16,64,128]{2,1,0:T(8,128)(2,1)}), bf16[16,64,128]{2,1,0:T(8,128)(2,1)S(1)}, u32[]{:S(2)}, u32[]{:S(2)}) async-start(bf16[16,64,128]{2,1,0:T(8,128)(2,1)} %get-tuple-element.128), calls=%async_computation.1 | async-start | bytes 524288 | tf_op jit(solution)/shard_map/all_to_all | solution.py:686
  100.6 7.1 %collective-permute-done.18.dy_b = bf16[128,768]{1,0:T(8,128)(2,1)S(1)} collective-permute-done((bf16[128,768]{1,0:T(8,128)(2,1)S(1)}, bf16[128,768]{1,0:T(8,128)(2,1)S(1)}, u32[]{:S(2)}, u32[]{:S(2)}) %collective-permute-start.18) | collective-permute-done | bytes 196640 | tf_op jit(solution)/shard_map/ppermute | solution.py:55
  112.6 2.7 %middle.1 = (f32[128,768]{1,0:T(8,128)}, bf16[128,768]{1,0:T(8,128)(2,1)}) custom-call(s32[5]{0:T(128)} %stack.55.scal, bf16[16,64,128]{2,1,0:T(8,128)(2,1)} %copy-done.6, bf16[16,24,768]{2,1,0:T(8,128)(2,1)} %get-tuple-element.131.own, bf16[16,24,768]{2,1,0:T(8,128)(2,1)} %copy-done.5, bf16[128,768]{1,0:T(8,128)(2,1)} %bitcast.38, ...), custom_call_target="tpu_custom_call" | custom-call | flops 1 | bytes 1 | tf_op jit(solution)/shard_map/middle/pallas_call | solution.py:83
  118.8 4.1 %collective-permute-done.22.n2_b = bf16[128,768]{1,0:T(8,128)(2,1)S(1)} collective-permute-done((bf16[128,768]{1,0:T(8,128)(2,1)}, bf16[128,768]{1,0:T(8,128)(2,1)S(1)}, u32[]{:S(2)}, u32[]{:S(2)}) %collective-permute-start.22) | collective-permute-done | bytes 196640 | tf_op jit(solution)/shard_map/ppermute | solution.py:55
  123.0 3.8 %collective-permute-done.23.n2_c = bf16[128,768]{1,0:T(8,128)(2,1)S(1)} collective-permute-done((bf16[128,768]{1,0:T(8,128)(2,1)}, bf16[128,768]{1,0:T(8,128)(2,1)S(1)}, u32[]{:S(2)}, u32[]{:S(2)}) %collective-permute-start.23) | collective-permute-done | bytes 196640 | tf_op jit(solution)/shard_map/ppermute | solution.py:55
  127.6 8.7 %feed.1 = (f32[128,768]{1,0:T(8,128)}, bf16[128,768]{1,0:T(8,128)(2,1)}, bf16[128,768]{1,0:T(8,128)(2,1)}, bf16[128,768]{1,0:T(8,128)(2,1)}, f32[128,768]{1,0:T(...) custom-call(s32[5]{0:T(128)} %stack.55.scal, ...), custom_call_target="tpu_custom_call" | custom-call | flops 1 | bytes 1 | tf_op jit(solution)/shard_map/feed/pallas_call | solution.py:83
  139.9 4.4 %collective-permute-done.27.got_b = bf16[128,768]{1,0:T(8,128)(2,1)S(1)} collective-permute-done((bf16[128,768]{1,0:T(8,128)(2,1)}, bf16[128,768]{1,0:T(8,128)(2,1)S(1)}, u32[]{:S(2)}, u32[]{:S(2)}) %collective-permute-start.27) | collective-permute-done | bytes 196640 | tf_op jit(solution)/shard_map/ppermute | solution.py:55
  144.3 3.3 %collective-permute-done.28.got_c = bf16[128,768]{1,0:T(8,128)(2,1)S(1)} collective-permute-done((bf16[128,768]{1,0:T(8,128)(2,1)}, bf16[128,768]{1,0:T(8,128)(2,1)S(1)}, u32[]{:S(2)}, u32[]{:S(2)}) %collective-permute-start.28) | collective-permute-done | bytes 196640 | tf_op jit(solution)/shard_map/ppermute | solution.py:55
  149.2 3.4 %fold.1 = (f32[2,200,768]{2,1,0:T(8,128)}, bf16[2,200,768]{2,1,0:T(8,128)(2,1)}) custom-call(f32[4,200,768]{2,1,0:T(8,128)} %get-tuple-element.139.keep, bf16[4,200,768]{2,1,0:T(8,128)(2,1)} %copy-done.15), custom_call_target="tpu_custom_call" | custom-call | flops 1 | bytes 1 | tf_op jit(solution)/shard_map/fold/pallas_call | solution.py:83
  154.3 4.4 %turn.1 = (f32[128,768]{1,0:T(8,128)}, bf16[8,768]{1,0:T(8,128)(2,1)}, bf16[16,64,128]{2,1,0:T(8,128)(2,1)}, f32[8,768]{1,0:T(8,128)}, f32[16,24,768]{2,1,0:T(8,128)}, /*index=5*/bf16[16,24,768]{2,1,0:T(8,128)(2,1)}) custom-call(s32[5]{0:T(128)} %stack.55.scal, f32[128,768]{1,0:T(8,128)} %get-tuple-element.152.keep, bf16[128,768]{1,0:T(8,128)(2,1)} %copy-done.33, ...), custom_call_target="tpu_custom_call" | custom-call | flops 1 | bytes 1 | tf_op jit(solution)/shard_map/turn/pallas_call | solution.py:83
  158.8 4.9 %all-to-all-start.2 = ((bf16[16,64,128]{2,1,0:T(8,128)(2,1)}), bf16[16,64,128]{2,1,0:T(8,128)(2,1)}, u32[]{:S(2)}, u32[]{:S(2)}) async-start(bf16[16,64,128]{2,1,0:T(8,128)(2,1)} %get-tuple-element.154), calls=%async_computation.2 | async-start | bytes 524288 | tf_op jit(solution)/shard_map/all_to_all | solution.py:744
  163.7 7.3 %collective-permute-done.30.got = bf16[2,200,768]{2,1,0:T(8,128)(2,1)S(1)} collective-permute-done((bf16[2,200,768]{2,1,0:T(8,128)(2,1)}, bf16[2,200,768]{2,1,0:T(8,128)(2,1)S(1)}, u32[]{:S(2)}, u32[]{:S(2)}) %collective-permute-start.30) | collective-permute-done | bytes 614432 | tf_op jit(solution)/shard_map/ppermute | solution.py:51
  175.8 13.1 %backward.1 = (bf16[16,192,128]{2,1,0:T(8,128)(2,1)}, bf16[192,2048]{1,0:T(8,128)(2,1)}) custom-call(s32[5]{0:T(128)} %stack.55.scal, bf16[192,2048]{1,0:T(8,128)(2,1)} %get-tuple-element.150.qkvt, bf16[16,64,128]{2,1,0:T(8,128)(2,1)} %all-to-all-done.2.dcr, f32[64,2048]{1,0:T(8,128)} %get-tuple-element.155.ctxt, f32[1,2048]{1,0:T(1,128)} %get-tuple-element.156.lse), custom_call_target="tpu_custom_call" | custom-call | flops 1 | bytes 1 | tf_op jit(solution)/shard_map/backward/pallas_call | solution.py:83
  188.9 5.4 %all-to-all-start.3 = ((bf16[16,192,128]{2,1,0:T(8,128)(2,1)}), bf16[16,192,128]{2,1,0:T(8,128)(2,1)S(1)}, u32[]{:S(2)}, u32[]{:S(2)}) async-start(bf16[16,192,128]{2,1,0:T(8,128)(2,1)} %get-tuple-element.169), calls=%async_computation.3 | async-start | bytes 1572864 | tf_op jit(solution)/shard_map/all_to_all | solution.py:774
  194.5 6.6 %heads.1 = (f32[16,24,256]{2,1,0:T(8,128)}, bf16[16,24,256]{2,1,0:T(8,128)(2,1)}) custom-call(s32[5]{0:T(128)} %stack.55.scal, bf16[192,2048]{1,0:T(8,128)(2,1)} %get-tuple-element.174.dall, bf16[2048,768]{1,0:T(8,128)(2,1)} %get-tuple-element.180.n1, bf16[2048,768]{1,0:T(8,128)(2,1)} %get-tuple-element.181.n0, bf16[192,768]{1,0:T(8,128)(2,1)} %get-tuple-element.182.wt, ...), custom_call_target="tpu_custom_call" | custom-call | flops 1 | bytes 1 | tf_op jit(solution)/shard_map/heads/pallas_call | solution.py:549
  202.2 3.1 %finish.1 = (f32[96,768]{1,0:T(8,128)}, f32[1,96]{1,0:T(1,128)}, bf16[24,768]{1,0:T(8,128)(2,1)}, f32[4,24,768]{2,1,0:T(8,128)}, bf16[248,768]{1,0:T(8,128)(2,1)...) custom-call(s32[5]{0:T(128)} %stack.55.scal, f32[200,768]{1,0:T(8,128)} %get-tuple-element.147.keep, ...), custom_call_target="tpu_custom_call" | custom-call | flops 1 | bytes 1 | tf_op jit(solution)/shard_map/finish/pallas_call | solution.py:83
  209.5 4.8 %all-to-all-done.3.d_rows = bf16[16,192,128]{2,1,0:T(8,128)(2,1)S(1)} async-done(((bf16[16,192,128]{2,1,0:T(8,128)(2,1)}), bf16[16,192,128]{2,1,0:T(8,128)(2,1)S(1)}, u32[]{:S(2)}, u32[]{:S(2)}) %all-to-all-start.3) | async-done | bytes 786464 | tf_op jit(solution)/shard_map/all_to_all | solution.py:774
  214.3 5.7 %all-to-all-start.4 = ((bf16[16,24,256]{2,1,0:T(8,128)(2,1)}), bf16[16,24,256]{2,1,0:T(8,128)(2,1)S(1)}, u32[]{:S(2)}, u32[]{:S(2)}) async-start(bf16[16,24,256]{2,1,0:T(8,128)(2,1)} %add_convert_fusion), calls=%async_computation.4 | async-start | bytes 393216 | tf_op jit(solution)/shard_map/all_to_all | solution.py:801
  220.0 4.5 %last.1 = f32[128,768]{1,0:T(8,128)} custom-call(s32[5]{0:T(128)} %stack.55.scal, bf16[16,192,128]{2,1,0:T(8,128)(2,1)} %copy-done.2, bf16[4,72,768]{2,1,0:T(8,128)(2,1)} %copy-done.1, bf16[4,72,768]{2,1,0:T(8,128)(2,1)} %copy-done.8, bf16[4,72,768]{2,1,0:T(8,128)(2,1)} %copy-done.10, bf16[4,72,768]{2,1,0:T(8,128)(2,1)} %copy-done.12, ...), custom_call_target="tpu_custom_call" | custom-call | flops 1 | bytes 1 | tf_op jit(solution)/shard_map/last/pallas_call | solution.py:83
  224.5 5.8 %collective-permute-done.34.got_c = bf16[248,768]{1,0:T(8,128)(2,1)} collective-permute-done((bf16[248,768]{1,0:T(8,128)(2,1)}, bf16[248,768]{1,0:T(8,128)(2,1)}, u32[]{:S(2)}, u32[]{:S(2)}) %collective-permute-start.34) | collective-permute-done | bytes 380960 | tf_op jit(solution)/shard_map/ppermute | solution.py:55
  230.3 2.6 %close.1 = (bf16[128,768]{1,0:T(8,128)(2,1)}, f32[24,3072]{1,0:T(8,128)}, f32[24,768]{1,0:T(8,128)}, bf16[24,768]{1,0:T(8,128)(2,1)}, bf16[24,768]{1,0:T(8,128)(2,1)}, /*index=5*/bf16[24,768]{1,0:T(8,128)(2,1)}) custom-call(s32[5]{0:T(128)} %stack.55.scal, bf16[24,768]{1,0:T(8,128)(2,1)} %get-tuple-element.164.own, f32[4,24,768]{2,1,0:T(8,128)} %get-tuple-element.165.wo_own, ...), custom_call_target="tpu_custom_call" | custom-call | flops 1 | bytes 1 | tf_op jit(solution)/shard_map/close/pallas_call | solution.py:83
  232.9 3.7 %collective-permute-start.40 = (bf16[24,768]{1,0:T(8,128)(2,1)}, bf16[24,768]{1,0:T(8,128)(2,1)S(1)}, u32[]{:S(2)}, u32[]{:S(2)}) collective-permute-start(bf16[24,768]{1,0:T(8,128)(2,1)} %get-tuple-element.197), channel_id=1, source_target_pairs={{0,24},{8,16},{16,8},{24,0},{1,25},{9,17},{17,9},{25,1},{2,26},{10... | collective-permute-start | bytes 110600 | tf_op jit(solution)/shard_map/ppermute | solution.py:51
  239.0 2.6 %collective-permute-done.39 = bf16[24,768]{1,0:T(8,128)(2,1)S(1)} collective-permute-done((bf16[24,768]{1,0:T(8,128)(2,1)}, bf16[24,768]{1,0:T(8,128)(2,1)S(1)}, u32[]{:S(2)}, u32[]{:S(2)}) %collective-permute-start.39) | collective-permute-done | bytes 36896 | tf_op jit(solution)/shard_map/ppermute | solution.py:51
  (166 shorter events, 64.1 us)
Async XLA Ops:
  1.6 13.7 %collective-permute-start.5 = (bf16[152,768]{1,0:T(8,128)(2,1)S(1)}, bf16[152,768]{1,0:T(8,128)(2,1)S(1)}, u32[]{:S(2)}, u32[]{:S(2)}) collective-permute-start(bf16[152,768]{1,0:T(8,128)(2,1)S(1)} %pad_maximum_fusion.5.ahead), channel_id=1, source_target_pairs={{0,24},{8,16},{16,8},{24,0},{1,25},{9,17},{17,9},{25,1},{2,26},{10... | collective-permute-start | bytes 700424 | tf_op jit(solution)/shard_map/ppermute | solution.py:51
  6.8 19.9 %collective-permute-start.4 = (bf16[152,768]{1,0:T(8,128)(2,1)S(1)}, bf16[152,768]{1,0:T(8,128)(2,1)S(1)}, u32[]{:S(2)}, u32[]{:S(2)}) collective-permute-start(bf16[152,768]{1,0:T(8,128)(2,1)S(1)} %pad_maximum_fusion.5.ahead), channel_id=1, source_target_pairs={{0,16},{8,24},{16,0},{24,8},{1,17},{9,25},{17,1},{25,9},{2,18},{10... | collective-permute-start | bytes 700424 | tf_op jit(solution)/shard_map/ppermute | solution.py:51
  6.8 19.9 %collective-permute-start.3 = (bf16[152,768]{1,0:T(8,128)(2,1)S(1)}, bf16[152,768]{1,0:T(8,128)(2,1)S(1)}, u32[]{:S(2)}, u32[]{:S(2)}) collective-permute-start(bf16[152,768]{1,0:T(8,128)(2,1)S(1)} %pad_maximum_fusion.5.ahead), channel_id=1, source_target_pairs={{0,8},{8,0},{16,24},{24,16},{1,9},{9,1},{17,25},{25,17},{2,10},{10... | collective-permute-start | bytes 700424 | tf_op jit(solution)/shard_map/ppermute | solution.py:51
  11.2 15.5 %collective-permute-start = (bf16[176,768]{1,0:T(8,128)(2,1)}, bf16[176,768]{1,0:T(8,128)(2,1)S(1)}, u32[]{:S(2)}, u32[]{:S(2)}) collective-permute-start(bf16[176,768]{1,0:T(8,128)(2,1)} %get-tuple-element.111), channel_id=1, source_target_pairs={{0,2},{2,0},{4,6},{6,4},{1,3},{3,1},{5,7},{7,5},{8,10},{10,8},{12,... | collective-permute-start | bytes 811016 | tf_op jit(solution)/shard_map/ppermute | solution.py:55
  12.9 13.9 %collective-permute-start.1 = (bf16[176,768]{1,0:T(8,128)(2,1)}, bf16[176,768]{1,0:T(8,128)(2,1)S(1)}, u32[]{:S(2)}, u32[]{:S(2)}) collective-permute-start(bf16[176,768]{1,0:T(8,128)(2,1)} %get-tuple-element.112), channel_id=1, source_target_pairs={{0,4},{2,6},{4,0},{6,2},{1,5},{3,7},{5,1},{7,3},{8,12},{10,14},{12... | collective-permute-start | bytes 811016 | tf_op jit(solution)/shard_map/ppermute | solution.py:55
  15.3 11.4 %collective-permute-start.2 = (bf16[176,768]{1,0:T(8,128)(2,1)}, bf16[176,768]{1,0:T(8,128)(2,1)}, u32[]{:S(2)}, u32[]{:S(2)}) collective-permute-start(bf16[176,768]{1,0:T(8,128)(2,1)} %get-tuple-element.113), channel_id=1, source_target_pairs={{0,6},{2,4},{4,2},{6,0},{1,7},{3,5},{5,3},{7,1},{8,14},{10,12},{12... | collective-permute-start | bytes 811016 | tf_op jit(solution)/shard_map/ppermute | solution.py:55
  26.8 24.4 %collective-permute-start.6 = (bf16[3,152,768]{2,1,0:T(8,128)(2,1)S(1)}, bf16[3,152,768]{2,1,0:T(8,128)(2,1)S(1)}, u32[]{:S(2)}, u32[]{:S(2)}) collective-permute-start(bf16[3,152,768]{2,1,0:T(8,128)(2,1)S(1)} %pad_maximum_fusion.2.zc), channel_id=1, source_target_pairs={{0,2},{2,0},{1,3},{3,1},{4,6},{6,4},{5,7},{7,5},{8,10},{10,8},{9,1... | collective-permute-start | bytes 2101256 | tf_op jit(solution)/shard_map/ppermute | solution.py:51
  28.3 22.9 %collective-permute-start.7 = (bf16[3,152,768]{2,1,0:T(8,128)(2,1)S(1)}, bf16[3,152,768]{2,1,0:T(8,128)(2,1)S(1)}, u32[]{:S(2)}, u32[]{:S(2)}) collective-permute-start(bf16[3,152,768]{2,1,0:T(8,128)(2,1)S(1)} %pad_maximum_fusion.2.zc), channel_id=1, source_target_pairs={{0,4},{4,0},{1,5},{5,1},{2,6},{6,2},{3,7},{7,3},{8,12},{12,8},{9,1... | collective-permute-start | bytes 2101256 | tf_op jit(solution)/shard_map/ppermute | solution.py:51
  29.8 21.3 %collective-permute-start.8 = (bf16[72,768]{1,0:T(8,128)(2,1)S(1)}, bf16[72,768]{1,0:T(8,128)(2,1)}, u32[]{:S(2)}, u32[]{:S(2)}) collective-permute-start(bf16[72,768]{1,0:T(8,128)(2,1)S(1)} %pad_maximum_fusion.6), channel_id=1, source_target_pairs={{0,8},{8,0},{16,24},{24,16},{1,9},{9,1},{17,25},{25,17},{2,10},{10... | collective-permute-start | bytes 331784 | tf_op jit(solution)/shard_map/ppermute | solution.py:51
  34.0 17.2 %collective-permute-start.9 = (bf16[72,768]{1,0:T(8,128)(2,1)S(1)}, bf16[72,768]{1,0:T(8,128)(2,1)}, u32[]{:S(2)}, u32[]{:S(2)}) collective-permute-start(bf16[72,768]{1,0:T(8,128)(2,1)S(1)} %pad_maximum_fusion.6), channel_id=1, source_target_pairs={{0,16},{8,24},{16,0},{24,8},{1,17},{9,25},{17,1},{25,9},{2,18},{10... | collective-permute-start | bytes 331784 | tf_op jit(solution)/shard_map/ppermute | solution.py:51
  35.6 15.5 %collective-permute-start.10 = (bf16[72,768]{1,0:T(8,128)(2,1)S(1)}, bf16[72,768]{1,0:T(8,128)(2,1)}, u32[]{:S(2)}, u32[]{:S(2)}) collective-permute-start(bf16[72,768]{1,0:T(8,128)(2,1)S(1)} %pad_maximum_fusion.6), channel_id=1, source_target_pairs={{0,24},{8,16},{16,8},{24,0},{1,25},{9,17},{17,9},{25,1},{2,26},{10... | collective-permute-start | bytes 331784 | tf_op jit(solution)/shard_map/ppermute | solution.py:51
  37.1 11.8 %all-to-all-start = ((bf16[16,24,256]{2,1,0:T(8,128)(2,1)}), bf16[16,24,256]{2,1,0:T(8,128)(2,1)S(1)}, u32[]{:S(2)}, u32[]{:S(2)}) async-start(bf16[16,24,256]{2,1,0:T(8,128)(2,1)} %get-tuple-element.116), calls=%async_computation | async-start | bytes 393216 | tf_op jit(solution)/shard_map/all_to_all | solution.py:642
  51.2 16.9 %collective-permute-start.16 = (bf16[200,768]{1,0:T(8,128)(2,1)S(1)}, bf16[200,768]{1,0:T(8,128)(2,1)S(1)}, u32[]{:S(2)}, u32[]{:S(2)}) collective-permute-start(bf16[200,768]{1,0:T(8,128)(2,1)S(1)} %constant_dynamic-update-slice_fusion), channel_id=1, source_target_pairs={{0,16},{8,24},{16,0},{24,8},{1,17},{9,25},{17,1},{25,9},{2,18},{10... | collective-permute-start | bytes 921608 | tf_op jit(solution)/shard_map/ppermute | solution.py:51
  52.4 17.0 %collective-permute-start.11 = (bf16[2,152,768]{2,1,0:T(8,128)(2,1)S(1)}, bf16[2,152,768]{2,1,0:T(8,128)(2,1)}, u32[]{:S(2)}, u32[]{:S(2)}) collective-permute-start(bf16[2,152,768]{2,1,0:T(8,128)(2,1)S(1)} %slice.15), channel_id=1, source_target_pairs={{0,4},{4,0},{1,5},{5,1},{2,6},{6,2},{3,7},{7,3},{8,12},{12,8},{9,1... | collective-permute-start | bytes 1400840 | tf_op jit(solution)/shard_map/ppermute | solution.py:51
  53.6 15.7 %collective-permute-start.12 = (bf16[1,152,768]{2,1,0:T(8,128)(2,1)S(1)}, bf16[1,152,768]{2,1,0:T(8,128)(2,1)S(1)}, u32[]{:S(2)}, u32[]{:S(2)}) collective-permute-start(bf16[1,152,768]{2,1,0:T(8,128)(2,1)S(1)} %slice.16), channel_id=1, source_target_pairs={{0,2},{2,0},{1,3},{3,1},{4,6},{6,4},{5,7},{7,5},{8,10},{10,8},{9,1... | collective-permute-start | bytes 700424 | tf_op jit(solution)/shard_map/ppermute | solution.py:51
  68.2 23.4 %collective-permute-start.17 = (bf16[2,200,768]{2,1,0:T(8,128)(2,1)S(1)}, bf16[2,200,768]{2,1,0:T(8,128)(2,1)S(1)}, u32[]{:S(2)}, u32[]{:S(2)}) collective-permute-start(bf16[2,200,768]{2,1,0:T(8,128)(2,1)S(1)} %pad_maximum_fusion.3), channel_id=1, source_target_pairs={{0,8},{8,0},{16,24},{24,16},{1,9},{9,1},{17,25},{25,17},{2,10},{10... | collective-permute-start | bytes 1843208 | tf_op jit(solution)/shard_map/ppermute | solution.py:51
  69.3 19.3 %collective-permute-start.13 = (bf16[4,72,768]{2,1,0:T(8,128)(2,1)S(1)}, bf16[4,72,768]{2,1,0:T(8,128)(2,1)S(1)}, u32[]{:S(2)}, u32[]{:S(2)}) collective-permute-start(bf16[4,72,768]{2,1,0:T(8,128)(2,1)S(1)} %pad_maximum_fusion.4.wq_a), channel_id=1, source_target_pairs={{0,2},{2,0},{4,6},{6,4},{1,3},{3,1},{5,7},{7,5},{8,10},{10,8},{12,... | collective-permute-start | bytes 1327112 | tf_op jit(solution)/shard_map/ppermute | solution.py:55
  70.2 21.3 %collective-permute-start.14 = (bf16[4,72,768]{2,1,0:T(8,128)(2,1)S(1)}, bf16[4,72,768]{2,1,0:T(8,128)(2,1)S(1)}, u32[]{:S(2)}, u32[]{:S(2)}) collective-permute-start(bf16[4,72,768]{2,1,0:T(8,128)(2,1)S(1)} %pad_maximum_fusion.4.wq_a), channel_id=1, source_target_pairs={{0,4},{2,6},{4,0},{6,2},{1,5},{3,7},{5,1},{7,3},{8,12},{10,14},{12... | collective-permute-start | bytes 1327112 | tf_op jit(solution)/shard_map/ppermute | solution.py:55
  70.8 20.7 %collective-permute-start.15 = (bf16[4,72,768]{2,1,0:T(8,128)(2,1)S(1)}, bf16[4,72,768]{2,1,0:T(8,128)(2,1)S(1)}, u32[]{:S(2)}, u32[]{:S(2)}) collective-permute-start(bf16[4,72,768]{2,1,0:T(8,128)(2,1)S(1)} %pad_maximum_fusion.4.wq_a), channel_id=1, source_target_pairs={{0,6},{2,4},{4,2},{6,0},{1,7},{3,5},{5,3},{7,1},{8,14},{10,12},{12... | collective-permute-start | bytes 1327112 | tf_op jit(solution)/shard_map/ppermute | solution.py:55
  92.5 34.4 %collective-permute-start.25 = (bf16[4,200,768]{2,1,0:T(8,128)(2,1)S(1)}, bf16[4,200,768]{2,1,0:T(8,128)(2,1)}, u32[]{:S(2)}, u32[]{:S(2)}) collective-permute-start(bf16[4,200,768]{2,1,0:T(8,128)(2,1)S(1)} %pad_maximum_fusion.1.ffz), channel_id=1, source_target_pairs={{0,1},{1,0},{2,3},{3,2},{4,5},{5,4},{6,7},{7,6},{8,9},{9,8},{10,11... | collective-permute-start | bytes 3686408 | tf_op jit(solution)/shard_map/ppermute | solution.py:51
  92.6 19.2 %collective-permute-start.21 = (bf16[16,24,768]{2,1,0:T(8,128)(2,1)S(1)}, bf16[16,24,768]{2,1,0:T(8,128)(2,1)S(1)}, u32[]{:S(2)}, u32[]{:S(2)}) collective-permute-start(bf16[16,24,768]{2,1,0:T(8,128)(2,1)S(1)} %copy-done.4), channel_id=1, source_target_pairs={{0,1},{1,0},{2,3},{3,2},{4,5},{5,4},{6,7},{7,6},{8,9},{9,8},{10,11... | collective-permute-start | bytes 1769480 | tf_op jit(solution)/shard_map/ppermute | solution.py:51
  93.1 18.6 %all-to-all-start.1 = ((bf16[16,64,128]{2,1,0:T(8,128)(2,1)}), bf16[16,64,128]{2,1,0:T(8,128)(2,1)S(1)}, u32[]{:S(2)}, u32[]{:S(2)}) async-start(bf16[16,64,128]{2,1,0:T(8,128)(2,1)} %get-tuple-element.128), calls=%async_computation.1 | async-start | bytes 524288 | tf_op jit(solution)/shard_map/all_to_all | solution.py:686
  136.3 11.9 %collective-permute-start.26 = (bf16[4,200,768]{2,1,0:T(8,128)(2,1)}, bf16[4,200,768]{2,1,0:T(8,128)(2,1)S(1)}, u32[]{:S(2)}, u32[]{:S(2)}) collective-permute-start(bf16[4,200,768]{2,1,0:T(8,128)(2,1)} %get-tuple-element.140), channel_id=1, source_target_pairs={{0,1},{1,0},{2,3},{3,2},{4,5},{5,4},{6,7},{7,6},{8,9},{9,8},{10,11... | collective-permute-start | bytes 3686408 | tf_op jit(solution)/shard_map/ppermute | solution.py:51
  152.6 18.4 %collective-permute-start.30 = (bf16[2,200,768]{2,1,0:T(8,128)(2,1)}, bf16[2,200,768]{2,1,0:T(8,128)(2,1)S(1)}, u32[]{:S(2)}, u32[]{:S(2)}) collective-permute-start(bf16[2,200,768]{2,1,0:T(8,128)(2,1)} %get-tuple-element.146), channel_id=1, source_target_pairs={{0,8},{8,0},{16,24},{24,16},{1,9},{9,1},{17,25},{25,17},{2,10},{10... | collective-permute-start | bytes 1843208 | tf_op jit(solution)/shard_map/ppermute | solution.py:51
  158.8 17.0 %all-to-all-start.2 = ((bf16[16,64,128]{2,1,0:T(8,128)(2,1)}), bf16[16,64,128]{2,1,0:T(8,128)(2,1)}, u32[]{:S(2)}, u32[]{:S(2)}) async-start(bf16[16,64,128]{2,1,0:T(8,128)(2,1)} %get-tuple-element.154), calls=%async_computation.2 | async-start | bytes 524288 | tf_op jit(solution)/shard_map/all_to_all | solution.py:744
  174.3 14.6 %collective-permute-start.31 = (bf16[200,768]{1,0:T(8,128)(2,1)}, bf16[200,768]{1,0:T(8,128)(2,1)}, u32[]{:S(2)}, u32[]{:S(2)}) collective-permute-start(bf16[200,768]{1,0:T(8,128)(2,1)} %get-tuple-element.148), channel_id=1, source_target_pairs={{0,16},{8,24},{16,0},{24,8},{1,17},{9,25},{17,1},{25,9},{2,18},{10... | collective-permute-start | bytes 921608 | tf_op jit(solution)/shard_map/ppermute | solution.py:51
  188.9 31.1 %collective-permute-start.36 = (bf16[16,72,768]{2,1,0:T(8,128)(2,1)S(1)}, bf16[16,72,768]{2,1,0:T(8,128)(2,1)}, u32[]{:S(2)}, u32[]{:S(2)}) collective-permute-start(bf16[16,72,768]{2,1,0:T(8,128)(2,1)S(1)} %pad_maximum_fusion), channel_id=1, source_target_pairs={{0,1},{1,0},{2,3},{3,2},{4,5},{5,4},{6,7},{7,6},{8,9},{9,8},{10,11... | collective-permute-start | bytes 5308424 | tf_op jit(solution)/shard_map/ppermute | solution.py:51
  188.9 25.4 %all-to-all-start.3 = ((bf16[16,192,128]{2,1,0:T(8,128)(2,1)}), bf16[16,192,128]{2,1,0:T(8,128)(2,1)S(1)}, u32[]{:S(2)}, u32[]{:S(2)}) async-start(bf16[16,192,128]{2,1,0:T(8,128)(2,1)} %get-tuple-element.169), calls=%async_computation.3 | async-start | bytes 1572864 | tf_op jit(solution)/shard_map/all_to_all | solution.py:774
  205.3 19.2 %collective-permute-start.33 = (bf16[248,768]{1,0:T(8,128)(2,1)}, bf16[248,768]{1,0:T(8,128)(2,1)S(1)}, u32[]{:S(2)}, u32[]{:S(2)}) collective-permute-start(bf16[248,768]{1,0:T(8,128)(2,1)} %get-tuple-element.166), channel_id=1, source_target_pairs={{0,2},{2,0},{4,6},{6,4},{1,3},{3,1},{5,7},{7,5},{8,10},{10,8},{12,... | collective-permute-start | bytes 1142792 | tf_op jit(solution)/shard_map/ppermute | solution.py:55
  207.2 23.1 %collective-permute-start.34 = (bf16[248,768]{1,0:T(8,128)(2,1)}, bf16[248,768]{1,0:T(8,128)(2,1)}, u32[]{:S(2)}, u32[]{:S(2)}) collective-permute-start(bf16[248,768]{1,0:T(8,128)(2,1)} %get-tuple-element.167), channel_id=1, source_target_pairs={{0,4},{2,6},{4,0},{6,2},{1,5},{3,7},{5,1},{7,3},{8,12},{10,14},{12... | collective-permute-start | bytes 1142792 | tf_op jit(solution)/shard_map/ppermute | solution.py:55
  208.7 21.6 %collective-permute-start.35 = (bf16[248,768]{1,0:T(8,128)(2,1)}, bf16[248,768]{1,0:T(8,128)(2,1)}, u32[]{:S(2)}, u32[]{:S(2)}) collective-permute-start(bf16[248,768]{1,0:T(8,128)(2,1)} %get-tuple-element.168), channel_id=1, source_target_pairs={{0,6},{2,4},{4,2},{6,0},{1,7},{3,5},{5,3},{7,1},{8,14},{10,12},{12... | collective-permute-start | bytes 1142792 | tf_op jit(solution)/shard_map/ppermute | solution.py:55
  214.3 28.8 %all-to-all-start.4 = ((bf16[16,24,256]{2,1,0:T(8,128)(2,1)}), bf16[16,24,256]{2,1,0:T(8,128)(2,1)S(1)}, u32[]{:S(2)}, u32[]{:S(2)}) async-start(bf16[16,24,256]{2,1,0:T(8,128)(2,1)} %add_convert_fusion), calls=%async_computation.4 | async-start | bytes 393216 | tf_op jit(solution)/shard_map/all_to_all | solution.py:801
  (51 other events, 711.9 us)

commit v6 on v5

--- a/solution.py
+++ b/solution.py
@@ -59,8 +59,8 @@
     return lax.optimization_barrier((value,) + others)[0]
 
 
-def split(length):
-    return 512 if length % 512 == 0 else length
+def split(length, most=512):
+    return most if length % most == 0 else length
 
 
 SMALL = pl.CostEstimate(flops=1, bytes_accessed=1, transcendentals=0)
@@ -210,42 +210,44 @@
         k_s[sl, :] = jnp.transpose(k_part.astype(F32)).astype(BF16)
     scale = 0.125 * LOG2E
 
+    wide, deep = (split(length, 1024), split(length, 1024))
+
     def one_query(i, carry):
-        first = pl.multiple_of(i * blk, blk)
-        q_now = qkvt[:HD, pl.ds(first, blk)]
+        first = pl.multiple_of(i * wide, wide)
+        q_now = qkvt[:HD, pl.ds(first, wide)]
 
         def step(masked, j, state):
             top, total, acc = state
-            start = pl.multiple_of(j * blk, blk)
-            scores = dot(k_s[pl.ds(start, blk), :], q_now) * scale
+            start = pl.multiple_of(j * deep, deep)
+            scores = dot(k_s[pl.ds(start, deep), :], q_now) * scale
             if masked:
-                key = start + lax.broadcasted_iota(jnp.int32, (blk, blk), 0)
-                query = first + lax.broadcasted_iota(jnp.int32, (blk, blk), 1)
+                key = start + lax.broadcasted_iota(jnp.int32, (deep, wide), 0)
+                query = first + lax.broadcasted_iota(jnp.int32, (deep, wide), 1)
                 scores = jnp.where((key <= query) | (key < prefix), scores, -1e30)
             new_top = jnp.maximum(top, jnp.max(scores, axis=0, keepdims=True))
             prob = jnp.exp2(scores - new_top)
             fade = jnp.exp2(top - new_top)
             total = total * fade + jnp.sum(prob, axis=0, keepdims=True)
-            acc = acc * fade + dot(qkvt[2 * HD :, pl.ds(start, blk)], prob.astype(BF16))
+            acc = acc * fade + dot(qkvt[2 * HD :, pl.ds(start, deep)], prob.astype(BF16))
             return (new_top, total, acc)
 
         state = (
-            jnp.full((1, blk), -1e30, F32),
-            jnp.zeros((1, blk), F32),
-            jnp.zeros((HD, blk), F32),
+            jnp.full((1, wide), -1e30, F32),
+            jnp.zeros((1, wide), F32),
+            jnp.zeros((HD, wide), F32),
         )
-        full = jnp.maximum(prefix // blk, i)
-        needed = jnp.maximum((prefix + blk - 1) // blk, i + 1)
+        full = jnp.maximum(prefix // deep, first // deep)
+        needed = jnp.maximum((prefix + deep - 1) // deep, (first + wide + deep - 1) // deep)
         state = lax.fori_loop(0, full, functools.partial(step, False), state)
         top, total, acc = lax.fori_loop(full, needed, functools.partial(step, True), state)
         out = acc / total
-        ctxt[:, pl.ds(first, blk)] = out
-        lse[:, pl.ds(first, blk)] = top + jnp.log2(total)
-        for r in range(blk // rows):
-            ctxc[i * (blk // rows) + r] = out[:, r * rows : (r + 1) * rows].astype(BF16)
+        ctxt[:, pl.ds(first, wide)] = out
+        lse[:, pl.ds(first, wide)] = top + jnp.log2(total)
+        for r in range(wide // rows):
+            ctxc[i * (wide // rows) + r] = out[:, r * rows : (r + 1) * rows].astype(BF16)
         return carry
 
-    lax.fori_loop(0, length // blk, one_query, 0)
+    lax.fori_loop(0, length // wide, one_query, 0)
     for copy in copies:
         copy.wait()
 
@@ -272,42 +274,44 @@
     dq_s[...] = jnp.zeros_like(dq_s)
     scale = 0.125 * LOG2E
 
+    wide, deep = (split(length, 512), split(length, 512))
+
     def one_key(j, carry):
-        start = pl.multiple_of(j * blk, blk)
+        start = pl.multiple_of(j * deep, deep)
         dk_s[...] = jnp.zeros_like(dk_s)
         dv_s[...] = jnp.zeros_like(dv_s)
 
         def step(masked, i, inner):
-            first = pl.multiple_of(i * blk, blk)
-            here = pl.ds(first, blk)
-            scores = dot(k_s[pl.ds(start, blk), :], qkvt[:HD, here]) * scale
+            first = pl.multiple_of(i * wide, wide)
+            here = pl.ds(first, wide)
+            scores = dot(k_s[pl.ds(start, deep), :], qkvt[:HD, here]) * scale
             prob = jnp.exp2(scores - lse[:, here])
             if masked:
-                key = start + lax.broadcasted_iota(jnp.int32, (blk, blk), 0)
-                query = first + lax.broadcasted_iota(jnp.int32, (blk, blk), 1)
+                key = start + lax.broadcasted_iota(jnp.int32, (deep, wide), 0)
+                query = first + lax.broadcasted_iota(jnp.int32, (deep, wide), 1)
                 prob = jnp.where((key <= query) | (key < prefix), prob, 0.0)
-            d_prob = dot(v_s[pl.ds(start, blk), :], dct_s[:, here])
+            d_prob = dot(v_s[pl.ds(start, deep), :], dct_s[:, here])
             d_score = (prob * (d_prob - del_s[:, here])).astype(BF16)
             dv_s[...] += dot(prob.astype(BF16), dc_s[here, :])
             dk_s[...] += dot(d_score, q_s[here, :])
-            dq_s[:, here] += dot(qkvt[HD : 2 * HD, pl.ds(start, blk)], d_score)
+            dq_s[:, here] += dot(qkvt[HD : 2 * HD, pl.ds(start, deep)], d_score)
             return inner
 
-        begin = jnp.where(start < prefix, 0, j)
-        middle = jnp.where(start + blk <= prefix, begin, j + 1)
+        begin = jnp.where(start < prefix, 0, start // wide)
+        middle = jnp.where(start + deep <= prefix, begin, (start + deep + wide - 2) // wide)
         lax.fori_loop(begin, middle, functools.partial(step, True), 0)
-        lax.fori_loop(middle, count, functools.partial(step, False), 0)
+        lax.fori_loop(middle, length // wide, functools.partial(step, False), 0)
         d_key = jnp.transpose(dk_s[...] * 0.125).astype(BF16)
         d_value = jnp.transpose(dv_s[...]).astype(BF16)
-        dall[HD : 2 * HD, pl.ds(start, blk)] = d_key
-        dall[2 * HD :, pl.ds(start, blk)] = d_value
-        for r in range(blk // rows):
-            at = j * (blk // rows) + r
+        dall[HD : 2 * HD, pl.ds(start, deep)] = d_key
+        dall[2 * HD :, pl.ds(start, deep)] = d_value
+        for r in range(deep // rows):
+            at = j * (deep // rows) + r
             dchunk[at, HD : 2 * HD, :] = d_key[:, r * rows : (r + 1) * rows]
             dchunk[at, 2 * HD :, :] = d_value[:, r * rows : (r + 1) * rows]
         return carry
 
-    lax.fori_loop(0, count, one_key, 0)
+    lax.fori_loop(0, length // deep, one_key, 0)
     for i in range(count):
         sl = slice(i * blk, (i + 1) * blk)
         d_query = (dq_s[:, sl] * 0.125).astype(BF16)
@@ -543,7 +547,7 @@
 
 def head_grads(scal, dall, n1, n0, wt, sums, heads, seq):
     length, width = n1.shape
-    blk = split(length)
+    blk = split(length, 1024)
     cut = width // (2 * seq)
     outs = (like((seq, cut, WIDE), F32), like((seq, cut, WIDE), BF16))
     return pl.pallas_call(
@@ -642,14 +646,14 @@
     head_w = lax.all_to_all(after(send, zc), SEQ, split_axis=0, concat_axis=0, tiled=True)
     wq = after(jnp.concatenate([w_query, w_key, w_value]), zc)
     wq_got = [swap(wq, "z", k) for k in range(1, outer)]
+    b_up_row = jnp.pad(b_up[None], ((0, 7), (0, width - half)))
+    ff = [w_down, up_own] + [part[rows + cut :] for part in first] + [b_up_row]
+    ff = after(jnp.concatenate(ff), *wq_got)
     head_w = lax.all_gather(head_w, "batch", axis=0, tiled=False)
     xc, yc, head_w, wq_got = lax.optimization_barrier((xc, yc, head_w, wq_got))
     xya = swap(xc[: outer // 2], "y")
     xyb = swap(yc[outer // 2 :], "x")
 
-    b_up_row = jnp.pad(b_up[None], ((0, 7), (0, width - half)))
-    ff = [w_down, up_own] + [part[rows + cut :] for part in first] + [b_up_row]
-    ff = after(jnp.concatenate(ff), head_w, xc)
     ff = jnp.stack([ff, swap(ff, "z", 2)])
     ff_got = swap(ff, "z", 1)
     wq = after(jnp.stack([wq] + wq_got), xya, xyb)
@@ -766,8 +770,8 @@
             pltpu.VMEM((HD, length), BF16),
             pltpu.VMEM((1, length), F32),
             pltpu.VMEM((HD, length), F32),
-            pltpu.VMEM((blk, HD), F32),
-            pltpu.VMEM((blk, HD), F32),
+            pltpu.VMEM((split(length, 512), HD), F32),
+            pltpu.VMEM((split(length, 512), HD), F32),
         ],
     )
     back, dchunk = lax.optimization_barrier((back, dchunk))

time: 246 us -> 247 us (level)
  starting transfers between devices: 73.2 us -> 82.8 us
  waiting for transfers between devices: 81.4 us -> 73.6 us
    ppermute x23, starting transfers between devices: 28.1 us -> 36 us  [swap(): return lax.ppermute(value, axis, [(i, i ^ step) for i in range(size)])]
    all_to_all x1, waiting for transfers between devices: 7.27 us -> 0.01 us  [body(): lax.all_to_all(after(send, zc), SEQ, split_axis=0, concat_axis=0, tiled=T...]
    unnamed x79 -> x77, local copies, waits for them, and re-layouts: 9.08 us -> 9.5 us
  transfers between devices with their start and end apart: 46 -> 46, of which waited for: 17 -> 21; matrix products, arithmetic and copies ran while one was open for 3% -> 3% of each run, Pallas kernels for 23% -> 23%
where the time goes in v6:
time: 247 us; the launch traced here: 246 us
  starting transfers between devices  82.8 us (34%)
  waiting for transfers between devices  73.6 us (30%)
  Pallas kernels  69.3 us (28%)
  local copies, waits for them, and re-layouts  10.2 us (4%)
  other arithmetic  5.58 us (2%)
    pallas_call x12, Pallas kernels, once(): pl.pallas_call(kernel, grid=(1,), out_shape=tuple(outs), in_specs=in_spec...  63.4 us
    ppermute x23, starting transfers between devices, swap(): return lax.ppermute(value, axis, [(i, i ^ step) for i in range(size)])  36 us
    ppermute x18, waiting for transfers between devices, swap_plane(): return lax.ppermute(value, ('y', 'x'), [(i, i ^ step) for i in range(4)])  35.7 us
    ppermute x23, waiting for transfers between devices, swap(): return lax.ppermute(value, axis, [(i, i ^ step) for i in range(size)])  32.5 us
    ppermute x18, starting transfers between devices, swap_plane(): return lax.ppermute(value, ('y', 'x'), [(i, i ^ step) for i in range(4)])  21.1 us
    unnamed x77, local copies, waits for them, and re-layouts  9.5 us
    all_to_all x1, starting transfers between devices, body(): ctx = lax.all_to_all(ctxc, SEQ, split_axis=0, concat_axis=0, tiled=True)  6.08 us
    pallas_call x1, Pallas kernels, head_grads(): pl.pallas_call(functools.partial(heads_kernel, heads), out_shape=outs, gr...  5.94 us
  transfers between devices with their start and end apart: 46, of which 21 were waited for; matrix products, arithmetic and copies ran while one was open for 3% of the time, Pallas kernels for 23%

profile of v6, /device:TPU:0, one launch (start us, length us, event | category | flops | bytes accessed | tf_op | source)
XLA Modules:
  0.0 245.7 jit_solution(3948757959166532444)
XLA Ops:
  1.6 5.1 %collective-permute-start.5 = (bf16[152,768]{1,0:T(8,128)(2,1)S(1)}, bf16[152,768]{1,0:T(8,128)(2,1)S(1)}, u32[]{:S(2)}, u32[]{:S(2)}) collective-permute-start(bf16[152,768]{1,0:T(8,128)(2,1)S(1)} %pad_maximum_fusion.5.ahead), channel_id=1, source_target_pairs={{0,24},{8,16},{16,8},{24,0},{1,25},{9,17},{17,9},{25,1},{2,26},{10... | collective-permute-start | bytes 700424 | tf_op jit(solution)/shard_map/ppermute | solution.py:51
  8.7 2.6 %pack.1 = (bf16[24,768]{1,0:T(8,128)(2,1)}, bf16[176,768]{1,0:T(8,128)(2,1)}, bf16[176,768]{1,0:T(8,128)(2,1)}, bf16[176,768]{1,0:T(8,128)(2,1)}, bf16[16,24,256]{2,1,0:T(8,128)(2,1)}) custom-call(s32[5]{0:T(128)} %stack.55.scal, bf16[128,768]{1,0:T(8,128)(2,1)} %bitcast.37, bf16[24,768]{1,0:T(8,128)(2,1)} %w_out.1, bf16[24,3072]{1,0:T(8,128)(2,1)} %w_up.1, ...), custom_call_target="tpu_custom_call" | custom-call | flops 1 | bytes 1 | tf_op jit(solution)/shard_map/pack/pallas_call | solution.py:83
  17.7 9.0 %collective-permute-done.4 = bf16[152,768]{1,0:T(8,128)(2,1)S(1)} collective-permute-done((bf16[152,768]{1,0:T(8,128)(2,1)S(1)}, bf16[152,768]{1,0:T(8,128)(2,1)S(1)}, u32[]{:S(2)}, u32[]{:S(2)}) %collective-permute-start.4) | collective-permute-done | bytes 233504 | tf_op jit(solution)/shard_map/ppermute | solution.py:51
  29.8 4.1 %collective-permute-start.8 = (bf16[72,768]{1,0:T(8,128)(2,1)S(1)}, bf16[72,768]{1,0:T(8,128)(2,1)}, u32[]{:S(2)}, u32[]{:S(2)}) collective-permute-start(bf16[72,768]{1,0:T(8,128)(2,1)S(1)} %pad_maximum_fusion.6), channel_id=1, source_target_pairs={{0,8},{8,0},{16,24},{24,16},{1,9},{9,1},{17,25},{25,17},{2,10},{10... | collective-permute-start | bytes 331784 | tf_op jit(solution)/shard_map/ppermute | solution.py:51
  37.1 3.7 %all-to-all-start = ((bf16[16,24,256]{2,1,0:T(8,128)(2,1)}), bf16[16,24,256]{2,1,0:T(8,128)(2,1)S(1)}, u32[]{:S(2)}, u32[]{:S(2)}) async-start(bf16[16,24,256]{2,1,0:T(8,128)(2,1)} %get-tuple-element.116), calls=%async_computation | async-start | bytes 393216 | tf_op jit(solution)/shard_map/all_to_all | solution.py:646
  44.0 8.8 %collective-permute-start.16 = (bf16[200,768]{1,0:T(8,128)(2,1)S(1)}, bf16[200,768]{1,0:T(8,128)(2,1)S(1)}, u32[]{:S(2)}, u32[]{:S(2)}) collective-permute-start(bf16[200,768]{1,0:T(8,128)(2,1)S(1)} %constant_dynamic-update-slice_fusion), channel_id=1, source_target_pairs={{0,16},{8,24},{16,0},{24,8},{1,17},{9,25},{17,1},{25,9},{2,18},{10... | collective-permute-start | bytes 921608 | tf_op jit(solution)/shard_map/ppermute | solution.py:51
  57.3 3.8 %collective-permute-done.16 = bf16[200,768]{1,0:T(8,128)(2,1)S(1)} collective-permute-done((bf16[200,768]{1,0:T(8,128)(2,1)S(1)}, bf16[200,768]{1,0:T(8,128)(2,1)S(1)}, u32[]{:S(2)}, u32[]{:S(2)}) %collective-permute-start.16) | collective-permute-done | bytes 307232 | tf_op jit(solution)/shard_map/ppermute | solution.py:51
  63.0 4.9 %collective-permute-done.11.xya = bf16[2,152,768]{2,1,0:T(8,128)(2,1)S(1)} collective-permute-done((bf16[2,152,768]{2,1,0:T(8,128)(2,1)S(1)}, bf16[2,152,768]{2,1,0:T(8,128)(2,1)S(1)}, u32[]{:S(2)}, u32[]{:S(2)}) %collective-permute-start.11) | collective-permute-done | bytes 466976 | tf_op jit(solution)/shard_map/ppermute | solution.py:51
  71.4 14.2 %forward.1 = (bf16[2048,768]{1,0:T(8,128)(2,1)}, bf16[2048,768]{1,0:T(8,128)(2,1)}, bf16[192,2048]{1,0:T(8,128)(2,1)}, bf16[16,64,128]{2,1,0:T(8,128)(2,1)}, f32...) custom-call(s32[5]{0:T(128)} %stack.55.scal, ...), custom_call_target="tpu_custom_call" | custom-call | flops 1 | bytes 1 | tf_op jit(solution)/shard_map/forward/pallas_call | solution.py:83
  85.7 3.9 %collective-permute-done.14.wq_c = bf16[4,72,768]{2,1,0:T(8,128)(2,1)S(1)} collective-permute-done((bf16[4,72,768]{2,1,0:T(8,128)(2,1)S(1)}, bf16[4,72,768]{2,1,0:T(8,128)(2,1)S(1)}, u32[]{:S(2)}, u32[]{:S(2)}) %collective-permute-start.14) | collective-permute-done | bytes 442400 | tf_op jit(solution)/shard_map/ppermute | solution.py:55
  91.1 6.1 %all-to-all-start.1 = ((bf16[16,64,128]{2,1,0:T(8,128)(2,1)}), bf16[16,64,128]{2,1,0:T(8,128)(2,1)S(1)}, u32[]{:S(2)}, u32[]{:S(2)}) async-start(bf16[16,64,128]{2,1,0:T(8,128)(2,1)} %get-tuple-element.128), calls=%async_computation.1 | async-start | bytes 524288 | tf_op jit(solution)/shard_map/all_to_all | solution.py:690
  100.8 7.1 %collective-permute-done.18.dy_b = bf16[128,768]{1,0:T(8,128)(2,1)S(1)} collective-permute-done((bf16[128,768]{1,0:T(8,128)(2,1)S(1)}, bf16[128,768]{1,0:T(8,128)(2,1)S(1)}, u32[]{:S(2)}, u32[]{:S(2)}) %collective-permute-start.18) | collective-permute-done | bytes 196640 | tf_op jit(solution)/shard_map/ppermute | solution.py:55
  112.9 2.7 %middle.1 = (f32[128,768]{1,0:T(8,128)}, bf16[128,768]{1,0:T(8,128)(2,1)}) custom-call(s32[5]{0:T(128)} %stack.55.scal, bf16[16,64,128]{2,1,0:T(8,128)(2,1)} %copy-done.6, bf16[16,24,768]{2,1,0:T(8,128)(2,1)} %get-tuple-element.131.own, bf16[16,24,768]{2,1,0:T(8,128)(2,1)} %copy-done.5, bf16[128,768]{1,0:T(8,128)(2,1)} %bitcast.38, ...), custom_call_target="tpu_custom_call" | custom-call | flops 1 | bytes 1 | tf_op jit(solution)/shard_map/middle/pallas_call | solution.py:83
  119.1 4.1 %collective-permute-done.22.n2_b = bf16[128,768]{1,0:T(8,128)(2,1)S(1)} collective-permute-done((bf16[128,768]{1,0:T(8,128)(2,1)}, bf16[128,768]{1,0:T(8,128)(2,1)S(1)}, u32[]{:S(2)}, u32[]{:S(2)}) %collective-permute-start.22) | collective-permute-done | bytes 196640 | tf_op jit(solution)/shard_map/ppermute | solution.py:55
  123.2 3.8 %collective-permute-done.23.n2_c = bf16[128,768]{1,0:T(8,128)(2,1)S(1)} collective-permute-done((bf16[128,768]{1,0:T(8,128)(2,1)}, bf16[128,768]{1,0:T(8,128)(2,1)S(1)}, u32[]{:S(2)}, u32[]{:S(2)}) %collective-permute-start.23) | collective-permute-done | bytes 196640 | tf_op jit(solution)/shard_map/ppermute | solution.py:55
  127.8 8.7 %feed.1 = (f32[128,768]{1,0:T(8,128)}, bf16[128,768]{1,0:T(8,128)(2,1)}, bf16[128,768]{1,0:T(8,128)(2,1)}, bf16[128,768]{1,0:T(8,128)(2,1)}, f32[128,768]{1,0:T(...) custom-call(s32[5]{0:T(128)} %stack.55.scal, ...), custom_call_target="tpu_custom_call" | custom-call | flops 1 | bytes 1 | tf_op jit(solution)/shard_map/feed/pallas_call | solution.py:83
  140.1 4.4 %collective-permute-done.27.got_b = bf16[128,768]{1,0:T(8,128)(2,1)S(1)} collective-permute-done((bf16[128,768]{1,0:T(8,128)(2,1)}, bf16[128,768]{1,0:T(8,128)(2,1)S(1)}, u32[]{:S(2)}, u32[]{:S(2)}) %collective-permute-start.27) | collective-permute-done | bytes 196640 | tf_op jit(solution)/shard_map/ppermute | solution.py:55
  144.5 3.3 %collective-permute-done.28.got_c = bf16[128,768]{1,0:T(8,128)(2,1)S(1)} collective-permute-done((bf16[128,768]{1,0:T(8,128)(2,1)}, bf16[128,768]{1,0:T(8,128)(2,1)S(1)}, u32[]{:S(2)}, u32[]{:S(2)}) %collective-permute-start.28) | collective-permute-done | bytes 196640 | tf_op jit(solution)/shard_map/ppermute | solution.py:55
  149.5 3.4 %fold.1 = (f32[2,200,768]{2,1,0:T(8,128)}, bf16[2,200,768]{2,1,0:T(8,128)(2,1)}) custom-call(f32[4,200,768]{2,1,0:T(8,128)} %get-tuple-element.139.keep, bf16[4,200,768]{2,1,0:T(8,128)(2,1)} %copy-done.15), custom_call_target="tpu_custom_call" | custom-call | flops 1 | bytes 1 | tf_op jit(solution)/shard_map/fold/pallas_call | solution.py:83
  154.5 4.5 %turn.1 = (f32[128,768]{1,0:T(8,128)}, bf16[8,768]{1,0:T(8,128)(2,1)}, bf16[16,64,128]{2,1,0:T(8,128)(2,1)}, f32[8,768]{1,0:T(8,128)}, f32[16,24,768]{2,1,0:T(8,128)}, /*index=5*/bf16[16,24,768]{2,1,0:T(8,128)(2,1)}) custom-call(s32[5]{0:T(128)} %stack.55.scal, f32[128,768]{1,0:T(8,128)} %get-tuple-element.152.keep, bf16[128,768]{1,0:T(8,128)(2,1)} %copy-done.32, ...), custom_call_target="tpu_custom_call" | custom-call | flops 1 | bytes 1 | tf_op jit(solution)/shard_map/turn/pallas_call | solution.py:83
  159.0 4.9 %all-to-all-start.2 = ((bf16[16,64,128]{2,1,0:T(8,128)(2,1)}), bf16[16,64,128]{2,1,0:T(8,128)(2,1)}, u32[]{:S(2)}, u32[]{:S(2)}) async-start(bf16[16,64,128]{2,1,0:T(8,128)(2,1)} %get-tuple-element.154), calls=%async_computation.2 | async-start | bytes 524288 | tf_op jit(solution)/shard_map/all_to_all | solution.py:748
  163.9 7.3 %collective-permute-done.30.got = bf16[2,200,768]{2,1,0:T(8,128)(2,1)S(1)} collective-permute-done((bf16[2,200,768]{2,1,0:T(8,128)(2,1)}, bf16[2,200,768]{2,1,0:T(8,128)(2,1)S(1)}, u32[]{:S(2)}, u32[]{:S(2)}) %collective-permute-start.30) | collective-permute-done | bytes 614432 | tf_op jit(solution)/shard_map/ppermute | solution.py:51
  176.0 13.1 %backward.1 = (bf16[16,192,128]{2,1,0:T(8,128)(2,1)}, bf16[192,2048]{1,0:T(8,128)(2,1)}) custom-call(s32[5]{0:T(128)} %stack.55.scal, bf16[192,2048]{1,0:T(8,128)(2,1)} %get-tuple-element.150.qkvt, bf16[16,64,128]{2,1,0:T(8,128)(2,1)} %all-to-all-done.2.dcr, f32[64,2048]{1,0:T(8,128)} %get-tuple-element.155.ctxt, f32[1,2048]{1,0:T(1,128)} %get-tuple-element.156.lse), custom_call_target="tpu_custom_call" | custom-call | flops 1 | bytes 1 | tf_op jit(solution)/shard_map/backward/pallas_call | solution.py:83
  189.1 5.4 %all-to-all-start.3 = ((bf16[16,192,128]{2,1,0:T(8,128)(2,1)}), bf16[16,192,128]{2,1,0:T(8,128)(2,1)S(1)}, u32[]{:S(2)}, u32[]{:S(2)}) async-start(bf16[16,192,128]{2,1,0:T(8,128)(2,1)} %get-tuple-element.169), calls=%async_computation.3 | async-start | bytes 1572864 | tf_op jit(solution)/shard_map/all_to_all | solution.py:778
  194.7 5.9 %heads.1 = (f32[16,24,256]{2,1,0:T(8,128)}, bf16[16,24,256]{2,1,0:T(8,128)(2,1)}) custom-call(s32[5]{0:T(128)} %stack.55.scal, bf16[192,2048]{1,0:T(8,128)(2,1)} %get-tuple-element.174.dall, bf16[2048,768]{1,0:T(8,128)(2,1)} %get-tuple-element.180.n1, bf16[2048,768]{1,0:T(8,128)(2,1)} %get-tuple-element.181.n0, bf16[192,768]{1,0:T(8,128)(2,1)} %get-tuple-element.182.wt, ...), custom_call_target="tpu_custom_call" | custom-call | flops 1 | bytes 1 | tf_op jit(solution)/shard_map/heads/pallas_call | solution.py:553
  201.8 3.1 %finish.1 = (f32[96,768]{1,0:T(8,128)}, f32[1,96]{1,0:T(1,128)}, bf16[24,768]{1,0:T(8,128)(2,1)}, f32[4,24,768]{2,1,0:T(8,128)}, bf16[248,768]{1,0:T(8,128)(2,1)...) custom-call(s32[5]{0:T(128)} %stack.55.scal, f32[200,768]{1,0:T(8,128)} %get-tuple-element.147.keep, ...), custom_call_target="tpu_custom_call" | custom-call | flops 1 | bytes 1 | tf_op jit(solution)/shard_map/finish/pallas_call | solution.py:83
  209.1 5.4 %all-to-all-done.3.d_rows = bf16[16,192,128]{2,1,0:T(8,128)(2,1)S(1)} async-done(((bf16[16,192,128]{2,1,0:T(8,128)(2,1)}), bf16[16,192,128]{2,1,0:T(8,128)(2,1)S(1)}, u32[]{:S(2)}, u32[]{:S(2)}) %all-to-all-start.3) | async-done | bytes 786464 | tf_op jit(solution)/shard_map/all_to_all | solution.py:778
  214.5 5.7 %all-to-all-start.4 = ((bf16[16,24,256]{2,1,0:T(8,128)(2,1)}), bf16[16,24,256]{2,1,0:T(8,128)(2,1)S(1)}, u32[]{:S(2)}, u32[]{:S(2)}) async-start(bf16[16,24,256]{2,1,0:T(8,128)(2,1)} %add_convert_fusion), calls=%async_computation.4 | async-start | bytes 393216 | tf_op jit(solution)/shard_map/all_to_all | solution.py:805
  220.2 4.5 %last.1 = f32[128,768]{1,0:T(8,128)} custom-call(s32[5]{0:T(128)} %stack.55.scal, bf16[16,192,128]{2,1,0:T(8,128)(2,1)} %copy-done.2, bf16[4,72,768]{2,1,0:T(8,128)(2,1)} %copy-done.1, bf16[4,72,768]{2,1,0:T(8,128)(2,1)} %copy-done.8, bf16[4,72,768]{2,1,0:T(8,128)(2,1)} %copy-done.10, bf16[4,72,768]{2,1,0:T(8,128)(2,1)} %copy-done.12, ...), custom_call_target="tpu_custom_call" | custom-call | flops 1 | bytes 1 | tf_op jit(solution)/shard_map/last/pallas_call | solution.py:83
  224.7 3.9 %collective-permute-done.34.got_c = bf16[248,768]{1,0:T(8,128)(2,1)} collective-permute-done((bf16[248,768]{1,0:T(8,128)(2,1)}, bf16[248,768]{1,0:T(8,128)(2,1)}, u32[]{:S(2)}, u32[]{:S(2)}) %collective-permute-start.34) | collective-permute-done | bytes 380960 | tf_op jit(solution)/shard_map/ppermute | solution.py:55
  232.3 4.2 %collective-permute-start.40 = (bf16[24,768]{1,0:T(8,128)(2,1)}, bf16[24,768]{1,0:T(8,128)(2,1)S(1)}, u32[]{:S(2)}, u32[]{:S(2)}) collective-permute-start(bf16[24,768]{1,0:T(8,128)(2,1)} %get-tuple-element.197), channel_id=1, source_target_pairs={{0,24},{8,16},{16,8},{24,0},{1,25},{9,17},{17,9},{25,1},{2,26},{10... | collective-permute-start | bytes 110600 | tf_op jit(solution)/shard_map/ppermute | solution.py:51
  238.7 2.9 %collective-permute-done.39 = bf16[24,768]{1,0:T(8,128)(2,1)S(1)} collective-permute-done((bf16[24,768]{1,0:T(8,128)(2,1)}, bf16[24,768]{1,0:T(8,128)(2,1)S(1)}, u32[]{:S(2)}, u32[]{:S(2)}) %collective-permute-start.39) | collective-permute-done | bytes 36896 | tf_op jit(solution)/shard_map/ppermute | solution.py:51
  (164 shorter events, 69.2 us)
Async XLA Ops:
  1.6 13.7 %collective-permute-start.5 = (bf16[152,768]{1,0:T(8,128)(2,1)S(1)}, bf16[152,768]{1,0:T(8,128)(2,1)S(1)}, u32[]{:S(2)}, u32[]{:S(2)}) collective-permute-start(bf16[152,768]{1,0:T(8,128)(2,1)S(1)} %pad_maximum_fusion.5.ahead), channel_id=1, source_target_pairs={{0,24},{8,16},{16,8},{24,0},{1,25},{9,17},{17,9},{25,1},{2,26},{10... | collective-permute-start | bytes 700424 | tf_op jit(solution)/shard_map/ppermute | solution.py:51
  6.8 19.9 %collective-permute-start.4 = (bf16[152,768]{1,0:T(8,128)(2,1)S(1)}, bf16[152,768]{1,0:T(8,128)(2,1)S(1)}, u32[]{:S(2)}, u32[]{:S(2)}) collective-permute-start(bf16[152,768]{1,0:T(8,128)(2,1)S(1)} %pad_maximum_fusion.5.ahead), channel_id=1, source_target_pairs={{0,16},{8,24},{16,0},{24,8},{1,17},{9,25},{17,1},{25,9},{2,18},{10... | collective-permute-start | bytes 700424 | tf_op jit(solution)/shard_map/ppermute | solution.py:51
  6.8 19.9 %collective-permute-start.3 = (bf16[152,768]{1,0:T(8,128)(2,1)S(1)}, bf16[152,768]{1,0:T(8,128)(2,1)S(1)}, u32[]{:S(2)}, u32[]{:S(2)}) collective-permute-start(bf16[152,768]{1,0:T(8,128)(2,1)S(1)} %pad_maximum_fusion.5.ahead), channel_id=1, source_target_pairs={{0,8},{8,0},{16,24},{24,16},{1,9},{9,1},{17,25},{25,17},{2,10},{10... | collective-permute-start | bytes 700424 | tf_op jit(solution)/shard_map/ppermute | solution.py:51
  11.2 15.5 %collective-permute-start = (bf16[176,768]{1,0:T(8,128)(2,1)}, bf16[176,768]{1,0:T(8,128)(2,1)S(1)}, u32[]{:S(2)}, u32[]{:S(2)}) collective-permute-start(bf16[176,768]{1,0:T(8,128)(2,1)} %get-tuple-element.111), channel_id=1, source_target_pairs={{0,2},{2,0},{4,6},{6,4},{1,3},{3,1},{5,7},{7,5},{8,10},{10,8},{12,... | collective-permute-start | bytes 811016 | tf_op jit(solution)/shard_map/ppermute | solution.py:55
  12.9 13.9 %collective-permute-start.1 = (bf16[176,768]{1,0:T(8,128)(2,1)}, bf16[176,768]{1,0:T(8,128)(2,1)S(1)}, u32[]{:S(2)}, u32[]{:S(2)}) collective-permute-start(bf16[176,768]{1,0:T(8,128)(2,1)} %get-tuple-element.112), channel_id=1, source_target_pairs={{0,4},{2,6},{4,0},{6,2},{1,5},{3,7},{5,1},{7,3},{8,12},{10,14},{12... | collective-permute-start | bytes 811016 | tf_op jit(solution)/shard_map/ppermute | solution.py:55
  15.3 11.4 %collective-permute-start.2 = (bf16[176,768]{1,0:T(8,128)(2,1)}, bf16[176,768]{1,0:T(8,128)(2,1)}, u32[]{:S(2)}, u32[]{:S(2)}) collective-permute-start(bf16[176,768]{1,0:T(8,128)(2,1)} %get-tuple-element.113), channel_id=1, source_target_pairs={{0,6},{2,4},{4,2},{6,0},{1,7},{3,5},{5,3},{7,1},{8,14},{10,12},{12... | collective-permute-start | bytes 811016 | tf_op jit(solution)/shard_map/ppermute | solution.py:55
  26.8 28.3 %collective-permute-start.6 = (bf16[3,152,768]{2,1,0:T(8,128)(2,1)S(1)}, bf16[3,152,768]{2,1,0:T(8,128)(2,1)S(1)}, u32[]{:S(2)}, u32[]{:S(2)}) collective-permute-start(bf16[3,152,768]{2,1,0:T(8,128)(2,1)S(1)} %pad_maximum_fusion.2.zc), channel_id=1, source_target_pairs={{0,2},{2,0},{1,3},{3,1},{4,6},{6,4},{5,7},{7,5},{8,10},{10,8},{9,1... | collective-permute-start | bytes 2101256 | tf_op jit(solution)/shard_map/ppermute | solution.py:51
  28.3 26.7 %collective-permute-start.7 = (bf16[3,152,768]{2,1,0:T(8,128)(2,1)S(1)}, bf16[3,152,768]{2,1,0:T(8,128)(2,1)S(1)}, u32[]{:S(2)}, u32[]{:S(2)}) collective-permute-start(bf16[3,152,768]{2,1,0:T(8,128)(2,1)S(1)} %pad_maximum_fusion.2.zc), channel_id=1, source_target_pairs={{0,4},{4,0},{1,5},{5,1},{2,6},{6,2},{3,7},{7,3},{8,12},{12,8},{9,1... | collective-permute-start | bytes 2101256 | tf_op jit(solution)/shard_map/ppermute | solution.py:51
  29.8 11.8 %collective-permute-start.8 = (bf16[72,768]{1,0:T(8,128)(2,1)S(1)}, bf16[72,768]{1,0:T(8,128)(2,1)}, u32[]{:S(2)}, u32[]{:S(2)}) collective-permute-start(bf16[72,768]{1,0:T(8,128)(2,1)S(1)} %pad_maximum_fusion.6), channel_id=1, source_target_pairs={{0,8},{8,0},{16,24},{24,16},{1,9},{9,1},{17,25},{25,17},{2,10},{10... | collective-permute-start | bytes 331784 | tf_op jit(solution)/shard_map/ppermute | solution.py:51
  37.1 15.7 %all-to-all-start = ((bf16[16,24,256]{2,1,0:T(8,128)(2,1)}), bf16[16,24,256]{2,1,0:T(8,128)(2,1)S(1)}, u32[]{:S(2)}, u32[]{:S(2)}) async-start(bf16[16,24,256]{2,1,0:T(8,128)(2,1)} %get-tuple-element.116), calls=%async_computation | async-start | bytes 393216 | tf_op jit(solution)/shard_map/all_to_all | solution.py:646
  44.0 17.0 %collective-permute-start.16 = (bf16[200,768]{1,0:T(8,128)(2,1)S(1)}, bf16[200,768]{1,0:T(8,128)(2,1)S(1)}, u32[]{:S(2)}, u32[]{:S(2)}) collective-permute-start(bf16[200,768]{1,0:T(8,128)(2,1)S(1)} %constant_dynamic-update-slice_fusion), channel_id=1, source_target_pairs={{0,16},{8,24},{16,0},{24,8},{1,17},{9,25},{17,1},{25,9},{2,18},{10... | collective-permute-start | bytes 921608 | tf_op jit(solution)/shard_map/ppermute | solution.py:51
  55.1 12.8 %collective-permute-start.11 = (bf16[2,152,768]{2,1,0:T(8,128)(2,1)S(1)}, bf16[2,152,768]{2,1,0:T(8,128)(2,1)S(1)}, u32[]{:S(2)}, u32[]{:S(2)}) collective-permute-start(bf16[2,152,768]{2,1,0:T(8,128)(2,1)S(1)} %slice.15), channel_id=1, source_target_pairs={{0,4},{4,0},{1,5},{5,1},{2,6},{6,2},{3,7},{7,3},{8,12},{12,8},{9,1... | collective-permute-start | bytes 1400840 | tf_op jit(solution)/shard_map/ppermute | solution.py:51
  61.1 24.5 %collective-permute-start.17 = (bf16[2,200,768]{2,1,0:T(8,128)(2,1)S(1)}, bf16[2,200,768]{2,1,0:T(8,128)(2,1)S(1)}, u32[]{:S(2)}, u32[]{:S(2)}) collective-permute-start(bf16[2,200,768]{2,1,0:T(8,128)(2,1)S(1)} %pad_maximum_fusion.3), channel_id=1, source_target_pairs={{0,8},{8,0},{16,24},{24,16},{1,9},{9,1},{17,25},{25,17},{2,10},{10... | collective-permute-start | bytes 1843208 | tf_op jit(solution)/shard_map/ppermute | solution.py:51
  67.9 17.7 %collective-permute-start.13 = (bf16[4,72,768]{2,1,0:T(8,128)(2,1)S(1)}, bf16[4,72,768]{2,1,0:T(8,128)(2,1)S(1)}, u32[]{:S(2)}, u32[]{:S(2)}) collective-permute-start(bf16[4,72,768]{2,1,0:T(8,128)(2,1)S(1)} %pad_maximum_fusion.4.wq_a), channel_id=1, source_target_pairs={{0,2},{2,0},{4,6},{6,4},{1,3},{3,1},{5,7},{7,5},{8,10},{10,8},{12,... | collective-permute-start | bytes 1327112 | tf_op jit(solution)/shard_map/ppermute | solution.py:55
  68.7 20.9 %collective-permute-start.14 = (bf16[4,72,768]{2,1,0:T(8,128)(2,1)S(1)}, bf16[4,72,768]{2,1,0:T(8,128)(2,1)S(1)}, u32[]{:S(2)}, u32[]{:S(2)}) collective-permute-start(bf16[4,72,768]{2,1,0:T(8,128)(2,1)S(1)} %pad_maximum_fusion.4.wq_a), channel_id=1, source_target_pairs={{0,4},{2,6},{4,0},{6,2},{1,5},{3,7},{5,1},{7,3},{8,12},{10,14},{12... | collective-permute-start | bytes 1327112 | tf_op jit(solution)/shard_map/ppermute | solution.py:55
  69.9 19.6 %collective-permute-start.15 = (bf16[4,72,768]{2,1,0:T(8,128)(2,1)S(1)}, bf16[4,72,768]{2,1,0:T(8,128)(2,1)S(1)}, u32[]{:S(2)}, u32[]{:S(2)}) collective-permute-start(bf16[4,72,768]{2,1,0:T(8,128)(2,1)S(1)} %pad_maximum_fusion.4.wq_a), channel_id=1, source_target_pairs={{0,6},{2,4},{4,2},{6,0},{1,7},{3,5},{5,3},{7,1},{8,14},{10,12},{12... | collective-permute-start | bytes 1327112 | tf_op jit(solution)/shard_map/ppermute | solution.py:55
  90.5 36.5 %collective-permute-start.25 = (bf16[4,200,768]{2,1,0:T(8,128)(2,1)S(1)}, bf16[4,200,768]{2,1,0:T(8,128)(2,1)}, u32[]{:S(2)}, u32[]{:S(2)}) collective-permute-start(bf16[4,200,768]{2,1,0:T(8,128)(2,1)S(1)} %pad_maximum_fusion.1.ffz), channel_id=1, source_target_pairs={{0,1},{1,0},{2,3},{3,2},{4,5},{5,4},{6,7},{7,6},{8,9},{9,8},{10,11... | collective-permute-start | bytes 3686408 | tf_op jit(solution)/shard_map/ppermute | solution.py:51
  90.6 21.3 %collective-permute-start.21 = (bf16[16,24,768]{2,1,0:T(8,128)(2,1)S(1)}, bf16[16,24,768]{2,1,0:T(8,128)(2,1)S(1)}, u32[]{:S(2)}, u32[]{:S(2)}) collective-permute-start(bf16[16,24,768]{2,1,0:T(8,128)(2,1)S(1)} %copy-done.4), channel_id=1, source_target_pairs={{0,1},{1,0},{2,3},{3,2},{4,5},{5,4},{6,7},{7,6},{8,9},{9,8},{10,11... | collective-permute-start | bytes 1769480 | tf_op jit(solution)/shard_map/ppermute | solution.py:51
  91.1 20.8 %all-to-all-start.1 = ((bf16[16,64,128]{2,1,0:T(8,128)(2,1)}), bf16[16,64,128]{2,1,0:T(8,128)(2,1)S(1)}, u32[]{:S(2)}, u32[]{:S(2)}) async-start(bf16[16,64,128]{2,1,0:T(8,128)(2,1)} %get-tuple-element.128), calls=%async_computation.1 | async-start | bytes 524288 | tf_op jit(solution)/shard_map/all_to_all | solution.py:690
  99.2 11.1 %collective-permute-start.19 = (bf16[128,768]{1,0:T(8,128)(2,1)S(1)}, bf16[128,768]{1,0:T(8,128)(2,1)S(1)}, u32[]{:S(2)}, u32[]{:S(2)}) collective-permute-start(bf16[128,768]{1,0:T(8,128)(2,1)S(1)} %bitcast.48), channel_id=1, source_target_pairs={{0,4},{2,6},{4,0},{6,2},{1,5},{3,7},{5,1},{7,3},{8,12},{10,14},{12... | collective-permute-start | bytes 589832 | tf_op jit(solution)/shard_map/ppermute | solution.py:55
  100.7 11.2 %collective-permute-start.20 = (bf16[128,768]{1,0:T(8,128)(2,1)S(1)}, bf16[128,768]{1,0:T(8,128)(2,1)}, u32[]{:S(2)}, u32[]{:S(2)}) collective-permute-start(bf16[128,768]{1,0:T(8,128)(2,1)S(1)} %bitcast.49), channel_id=1, source_target_pairs={{0,6},{2,4},{4,2},{6,0},{1,7},{3,5},{5,3},{7,1},{8,14},{10,12},{12... | collective-permute-start | bytes 589832 | tf_op jit(solution)/shard_map/ppermute | solution.py:55
  136.5 11.9 %collective-permute-start.26 = (bf16[4,200,768]{2,1,0:T(8,128)(2,1)}, bf16[4,200,768]{2,1,0:T(8,128)(2,1)S(1)}, u32[]{:S(2)}, u32[]{:S(2)}) collective-permute-start(bf16[4,200,768]{2,1,0:T(8,128)(2,1)} %get-tuple-element.140), channel_id=1, source_target_pairs={{0,1},{1,0},{2,3},{3,2},{4,5},{5,4},{6,7},{7,6},{8,9},{9,8},{10,11... | collective-permute-start | bytes 3686408 | tf_op jit(solution)/shard_map/ppermute | solution.py:51
  137.0 10.8 %collective-permute-start.28 = (bf16[128,768]{1,0:T(8,128)(2,1)}, bf16[128,768]{1,0:T(8,128)(2,1)S(1)}, u32[]{:S(2)}, u32[]{:S(2)}) collective-permute-start(bf16[128,768]{1,0:T(8,128)(2,1)} %get-tuple-element.142), channel_id=1, source_target_pairs={{0,4},{2,6},{4,0},{6,2},{1,5},{3,7},{5,1},{7,3},{8,12},{10,14},{12... | collective-permute-start | bytes 589832 | tf_op jit(solution)/shard_map/ppermute | solution.py:55
  152.9 18.4 %collective-permute-start.30 = (bf16[2,200,768]{2,1,0:T(8,128)(2,1)}, bf16[2,200,768]{2,1,0:T(8,128)(2,1)S(1)}, u32[]{:S(2)}, u32[]{:S(2)}) collective-permute-start(bf16[2,200,768]{2,1,0:T(8,128)(2,1)} %get-tuple-element.146), channel_id=1, source_target_pairs={{0,8},{8,0},{16,24},{24,16},{1,9},{9,1},{17,25},{25,17},{2,10},{10... | collective-permute-start | bytes 1843208 | tf_op jit(solution)/shard_map/ppermute | solution.py:51
  159.0 17.0 %all-to-all-start.2 = ((bf16[16,64,128]{2,1,0:T(8,128)(2,1)}), bf16[16,64,128]{2,1,0:T(8,128)(2,1)}, u32[]{:S(2)}, u32[]{:S(2)}) async-start(bf16[16,64,128]{2,1,0:T(8,128)(2,1)} %get-tuple-element.154), calls=%async_computation.2 | async-start | bytes 524288 | tf_op jit(solution)/shard_map/all_to_all | solution.py:748
  174.5 14.6 %collective-permute-start.31 = (bf16[200,768]{1,0:T(8,128)(2,1)}, bf16[200,768]{1,0:T(8,128)(2,1)}, u32[]{:S(2)}, u32[]{:S(2)}) collective-permute-start(bf16[200,768]{1,0:T(8,128)(2,1)} %get-tuple-element.148), channel_id=1, source_target_pairs={{0,16},{8,24},{16,0},{24,8},{1,17},{9,25},{17,1},{25,9},{2,18},{10... | collective-permute-start | bytes 921608 | tf_op jit(solution)/shard_map/ppermute | solution.py:51
  189.1 31.1 %collective-permute-start.36 = (bf16[16,72,768]{2,1,0:T(8,128)(2,1)S(1)}, bf16[16,72,768]{2,1,0:T(8,128)(2,1)}, u32[]{:S(2)}, u32[]{:S(2)}) collective-permute-start(bf16[16,72,768]{2,1,0:T(8,128)(2,1)S(1)} %pad_maximum_fusion), channel_id=1, source_target_pairs={{0,1},{1,0},{2,3},{3,2},{4,5},{5,4},{6,7},{7,6},{8,9},{9,8},{10,11... | collective-permute-start | bytes 5308424 | tf_op jit(solution)/shard_map/ppermute | solution.py:51
  189.1 25.4 %all-to-all-start.3 = ((bf16[16,192,128]{2,1,0:T(8,128)(2,1)}), bf16[16,192,128]{2,1,0:T(8,128)(2,1)S(1)}, u32[]{:S(2)}, u32[]{:S(2)}) async-start(bf16[16,192,128]{2,1,0:T(8,128)(2,1)} %get-tuple-element.169), calls=%async_computation.3 | async-start | bytes 1572864 | tf_op jit(solution)/shard_map/all_to_all | solution.py:778
  204.9 19.8 %collective-permute-start.33 = (bf16[248,768]{1,0:T(8,128)(2,1)}, bf16[248,768]{1,0:T(8,128)(2,1)S(1)}, u32[]{:S(2)}, u32[]{:S(2)}) collective-permute-start(bf16[248,768]{1,0:T(8,128)(2,1)} %get-tuple-element.166), channel_id=1, source_target_pairs={{0,2},{2,0},{4,6},{6,4},{1,3},{3,1},{5,7},{7,5},{8,10},{10,8},{12,... | collective-permute-start | bytes 1142792 | tf_op jit(solution)/shard_map/ppermute | solution.py:55
  206.8 21.8 %collective-permute-start.34 = (bf16[248,768]{1,0:T(8,128)(2,1)}, bf16[248,768]{1,0:T(8,128)(2,1)}, u32[]{:S(2)}, u32[]{:S(2)}) collective-permute-start(bf16[248,768]{1,0:T(8,128)(2,1)} %get-tuple-element.167), channel_id=1, source_target_pairs={{0,4},{2,6},{4,0},{6,2},{1,5},{3,7},{5,1},{7,3},{8,12},{10,14},{12... | collective-permute-start | bytes 1142792 | tf_op jit(solution)/shard_map/ppermute | solution.py:55
  208.3 21.5 %collective-permute-start.35 = (bf16[248,768]{1,0:T(8,128)(2,1)}, bf16[248,768]{1,0:T(8,128)(2,1)}, u32[]{:S(2)}, u32[]{:S(2)}) collective-permute-start(bf16[248,768]{1,0:T(8,128)(2,1)} %get-tuple-element.168), channel_id=1, source_target_pairs={{0,6},{2,4},{4,2},{6,0},{1,7},{3,5},{5,3},{7,1},{8,14},{10,12},{12... | collective-permute-start | bytes 1142792 | tf_op jit(solution)/shard_map/ppermute | solution.py:55
  214.5 28.6 %all-to-all-start.4 = ((bf16[16,24,256]{2,1,0:T(8,128)(2,1)}), bf16[16,24,256]{2,1,0:T(8,128)(2,1)S(1)}, u32[]{:S(2)}, u32[]{:S(2)}) async-start(bf16[16,24,256]{2,1,0:T(8,128)(2,1)} %add_convert_fusion), calls=%async_computation.4 | async-start | bytes 393216 | tf_op jit(solution)/shard_map/all_to_all | solution.py:805
  (50 other events, 625.0 us)

commit v7 on v5

--- a/solution.py
+++ b/solution.py
@@ -543,7 +543,7 @@
 
 def head_grads(scal, dall, n1, n0, wt, sums, heads, seq):
     length, width = n1.shape
-    blk = split(length)
+    blk = 2 * split(length)
     cut = width // (2 * seq)
     outs = (like((seq, cut, WIDE), F32), like((seq, cut, WIDE), BF16))
     return pl.pallas_call(

time: 246 us -> 246 us (level)
  transfers between devices with their start and end apart: 46 -> 46, of which waited for: 17 -> 18; matrix products, arithmetic and copies ran while one was open for 3% -> 3% of each run, Pallas kernels for 23% -> 23%
where the time goes in v7:
time: 246 us; the launch traced here: 245 us
  waiting for transfers between devices  82.2 us (33%)
  starting transfers between devices  73.6 us (30%)
  Pallas kernels  69.4 us (28%)
  local copies, waits for them, and re-layouts  9.74 us (4%)
  other arithmetic  5.58 us (2%)
    pallas_call x12, Pallas kernels, once(): pl.pallas_call(kernel, grid=(1,), out_shape=tuple(outs), in_specs=in_spec...  63.5 us
    ppermute x18, waiting for transfers between devices, swap_plane(): return lax.ppermute(value, ('y', 'x'), [(i, i ^ step) for i in range(4)])  35.3 us
    ppermute x23, waiting for transfers between devices, swap(): return lax.ppermute(value, axis, [(i, i ^ step) for i in range(size)])  34.1 us
    ppermute x23, starting transfers between devices, swap(): return lax.ppermute(value, axis, [(i, i ^ step) for i in range(size)])  28.5 us
    ppermute x18, starting transfers between devices, swap_plane(): return lax.ppermute(value, ('y', 'x'), [(i, i ^ step) for i in range(4)])  21.6 us
    unnamed x79, local copies, waits for them, and re-layouts  9.08 us
    all_to_all x1, waiting for transfers between devices, body(): lax.all_to_all(after(send, zc), SEQ, split_axis=0, concat_axis=0, tiled=T...  7.27 us
    pallas_call x1, Pallas kernels, head_grads(): pl.pallas_call(functools.partial(heads_kernel, heads), out_shape=outs, gr...  5.94 us
  transfers between devices with their start and end apart: 46, of which 18 were waited for; matrix products, arithmetic and copies ran while one was open for 3% of the time, Pallas kernels for 23%

profile of v7, /device:TPU:0, one launch (start us, length us, event | category | flops | bytes accessed | tf_op | source)
XLA Modules:
  0.0 244.7 jit_solution(764065180083629547)
XLA Ops:
  1.6 5.1 %collective-permute-start.5 = (bf16[152,768]{1,0:T(8,128)(2,1)S(1)}, bf16[152,768]{1,0:T(8,128)(2,1)S(1)}, u32[]{:S(2)}, u32[]{:S(2)}) collective-permute-start(bf16[152,768]{1,0:T(8,128)(2,1)S(1)} %pad_maximum_fusion.5.ahead), channel_id=1, source_target_pairs={{0,24},{8,16},{16,8},{24,0},{1,25},{9,17},{17,9},{25,1},{2,26},{10... | collective-permute-start | bytes 700424 | tf_op jit(solution)/shard_map/ppermute | solution.py:51
  8.7 2.6 %pack.1 = (bf16[24,768]{1,0:T(8,128)(2,1)}, bf16[176,768]{1,0:T(8,128)(2,1)}, bf16[176,768]{1,0:T(8,128)(2,1)}, bf16[176,768]{1,0:T(8,128)(2,1)}, bf16[16,24,256]{2,1,0:T(8,128)(2,1)}) custom-call(s32[5]{0:T(128)} %stack.55.scal, bf16[128,768]{1,0:T(8,128)(2,1)} %bitcast.37, bf16[24,768]{1,0:T(8,128)(2,1)} %w_out.1, bf16[24,3072]{1,0:T(8,128)(2,1)} %w_up.1, ...), custom_call_target="tpu_custom_call" | custom-call | flops 1 | bytes 1 | tf_op jit(solution)/shard_map/pack/pallas_call | solution.py:83
  17.7 8.9 %collective-permute-done.4 = bf16[152,768]{1,0:T(8,128)(2,1)S(1)} collective-permute-done((bf16[152,768]{1,0:T(8,128)(2,1)S(1)}, bf16[152,768]{1,0:T(8,128)(2,1)S(1)}, u32[]{:S(2)}, u32[]{:S(2)}) %collective-permute-start.4) | collective-permute-done | bytes 233504 | tf_op jit(solution)/shard_map/ppermute | solution.py:51
  29.8 4.1 %collective-permute-start.8 = (bf16[72,768]{1,0:T(8,128)(2,1)S(1)}, bf16[72,768]{1,0:T(8,128)(2,1)}, u32[]{:S(2)}, u32[]{:S(2)}) collective-permute-start(bf16[72,768]{1,0:T(8,128)(2,1)S(1)} %pad_maximum_fusion.6), channel_id=1, source_target_pairs={{0,8},{8,0},{16,24},{24,16},{1,9},{9,1},{17,25},{25,17},{2,10},{10... | collective-permute-start | bytes 331784 | tf_op jit(solution)/shard_map/ppermute | solution.py:51
  37.1 3.7 %all-to-all-start = ((bf16[16,24,256]{2,1,0:T(8,128)(2,1)}), bf16[16,24,256]{2,1,0:T(8,128)(2,1)S(1)}, u32[]{:S(2)}, u32[]{:S(2)}) async-start(bf16[16,24,256]{2,1,0:T(8,128)(2,1)} %get-tuple-element.116), calls=%async_computation | async-start | bytes 393216 | tf_op jit(solution)/shard_map/all_to_all | solution.py:642
  41.7 7.3 %all-to-all-done = bf16[16,24,256]{2,1,0:T(8,128)(2,1)S(1)} async-done(((bf16[16,24,256]{2,1,0:T(8,128)(2,1)}), bf16[16,24,256]{2,1,0:T(8,128)(2,1)S(1)}, u32[]{:S(2)}, u32[]{:S(2)}) %all-to-all-start) | async-done | bytes 196640 | tf_op jit(solution)/shard_map/all_to_all | solution.py:642
  54.7 13.4 %collective-permute-done.16 = bf16[200,768]{1,0:T(8,128)(2,1)S(1)} collective-permute-done((bf16[200,768]{1,0:T(8,128)(2,1)S(1)}, bf16[200,768]{1,0:T(8,128)(2,1)S(1)}, u32[]{:S(2)}, u32[]{:S(2)}) %collective-permute-start.16) | collective-permute-done | bytes 307232 | tf_op jit(solution)/shard_map/ppermute | solution.py:51
  72.9 15.0 %forward.1 = (bf16[2048,768]{1,0:T(8,128)(2,1)}, bf16[2048,768]{1,0:T(8,128)(2,1)}, bf16[192,2048]{1,0:T(8,128)(2,1)}, bf16[16,64,128]{2,1,0:T(8,128)(2,1)}, f32...) custom-call(s32[5]{0:T(128)} %stack.55.scal, ...), custom_call_target="tpu_custom_call" | custom-call | flops 1 | bytes 1 | tf_op jit(solution)/shard_map/forward/pallas_call | solution.py:83
  88.0 3.5 %collective-permute-done.14.wq_c = bf16[4,72,768]{2,1,0:T(8,128)(2,1)S(1)} collective-permute-done((bf16[4,72,768]{2,1,0:T(8,128)(2,1)S(1)}, bf16[4,72,768]{2,1,0:T(8,128)(2,1)S(1)}, u32[]{:S(2)}, u32[]{:S(2)}) %collective-permute-start.14) | collective-permute-done | bytes 442400 | tf_op jit(solution)/shard_map/ppermute | solution.py:55
  93.1 3.9 %all-to-all-start.1 = ((bf16[16,64,128]{2,1,0:T(8,128)(2,1)}), bf16[16,64,128]{2,1,0:T(8,128)(2,1)S(1)}, u32[]{:S(2)}, u32[]{:S(2)}) async-start(bf16[16,64,128]{2,1,0:T(8,128)(2,1)} %get-tuple-element.128), calls=%async_computation.1 | async-start | bytes 524288 | tf_op jit(solution)/shard_map/all_to_all | solution.py:686
  100.6 7.1 %collective-permute-done.18.dy_b = bf16[128,768]{1,0:T(8,128)(2,1)S(1)} collective-permute-done((bf16[128,768]{1,0:T(8,128)(2,1)S(1)}, bf16[128,768]{1,0:T(8,128)(2,1)S(1)}, u32[]{:S(2)}, u32[]{:S(2)}) %collective-permute-start.18) | collective-permute-done | bytes 196640 | tf_op jit(solution)/shard_map/ppermute | solution.py:55
  112.6 2.7 %middle.1 = (f32[128,768]{1,0:T(8,128)}, bf16[128,768]{1,0:T(8,128)(2,1)}) custom-call(s32[5]{0:T(128)} %stack.55.scal, bf16[16,64,128]{2,1,0:T(8,128)(2,1)} %copy-done.6, bf16[16,24,768]{2,1,0:T(8,128)(2,1)} %get-tuple-element.131.own, bf16[16,24,768]{2,1,0:T(8,128)(2,1)} %copy-done.5, bf16[128,768]{1,0:T(8,128)(2,1)} %bitcast.38, ...), custom_call_target="tpu_custom_call" | custom-call | flops 1 | bytes 1 | tf_op jit(solution)/shard_map/middle/pallas_call | solution.py:83
  118.8 4.1 %collective-permute-done.22.n2_b = bf16[128,768]{1,0:T(8,128)(2,1)S(1)} collective-permute-done((bf16[128,768]{1,0:T(8,128)(2,1)}, bf16[128,768]{1,0:T(8,128)(2,1)S(1)}, u32[]{:S(2)}, u32[]{:S(2)}) %collective-permute-start.22) | collective-permute-done | bytes 196640 | tf_op jit(solution)/shard_map/ppermute | solution.py:55
  123.0 3.8 %collective-permute-done.23.n2_c = bf16[128,768]{1,0:T(8,128)(2,1)S(1)} collective-permute-done((bf16[128,768]{1,0:T(8,128)(2,1)}, bf16[128,768]{1,0:T(8,128)(2,1)S(1)}, u32[]{:S(2)}, u32[]{:S(2)}) %collective-permute-start.23) | collective-permute-done | bytes 196640 | tf_op jit(solution)/shard_map/ppermute | solution.py:55
  127.6 8.7 %feed.1 = (f32[128,768]{1,0:T(8,128)}, bf16[128,768]{1,0:T(8,128)(2,1)}, bf16[128,768]{1,0:T(8,128)(2,1)}, bf16[128,768]{1,0:T(8,128)(2,1)}, f32[128,768]{1,0:T(...) custom-call(s32[5]{0:T(128)} %stack.55.scal, ...), custom_call_target="tpu_custom_call" | custom-call | flops 1 | bytes 1 | tf_op jit(solution)/shard_map/feed/pallas_call | solution.py:83
  139.9 4.4 %collective-permute-done.27.got_b = bf16[128,768]{1,0:T(8,128)(2,1)S(1)} collective-permute-done((bf16[128,768]{1,0:T(8,128)(2,1)}, bf16[128,768]{1,0:T(8,128)(2,1)S(1)}, u32[]{:S(2)}, u32[]{:S(2)}) %collective-permute-start.27) | collective-permute-done | bytes 196640 | tf_op jit(solution)/shard_map/ppermute | solution.py:55
  144.3 3.3 %collective-permute-done.28.got_c = bf16[128,768]{1,0:T(8,128)(2,1)S(1)} collective-permute-done((bf16[128,768]{1,0:T(8,128)(2,1)}, bf16[128,768]{1,0:T(8,128)(2,1)S(1)}, u32[]{:S(2)}, u32[]{:S(2)}) %collective-permute-start.28) | collective-permute-done | bytes 196640 | tf_op jit(solution)/shard_map/ppermute | solution.py:55
  149.2 3.4 %fold.1 = (f32[2,200,768]{2,1,0:T(8,128)}, bf16[2,200,768]{2,1,0:T(8,128)(2,1)}) custom-call(f32[4,200,768]{2,1,0:T(8,128)} %get-tuple-element.139.keep, bf16[4,200,768]{2,1,0:T(8,128)(2,1)} %copy-done.15), custom_call_target="tpu_custom_call" | custom-call | flops 1 | bytes 1 | tf_op jit(solution)/shard_map/fold/pallas_call | solution.py:83
  154.3 4.4 %turn.1 = (f32[128,768]{1,0:T(8,128)}, bf16[8,768]{1,0:T(8,128)(2,1)}, bf16[16,64,128]{2,1,0:T(8,128)(2,1)}, f32[8,768]{1,0:T(8,128)}, f32[16,24,768]{2,1,0:T(8,128)}, /*index=5*/bf16[16,24,768]{2,1,0:T(8,128)(2,1)}) custom-call(s32[5]{0:T(128)} %stack.55.scal, f32[128,768]{1,0:T(8,128)} %get-tuple-element.152.keep, bf16[128,768]{1,0:T(8,128)(2,1)} %copy-done.33, ...), custom_call_target="tpu_custom_call" | custom-call | flops 1 | bytes 1 | tf_op jit(solution)/shard_map/turn/pallas_call | solution.py:83
  158.8 4.9 %all-to-all-start.2 = ((bf16[16,64,128]{2,1,0:T(8,128)(2,1)}), bf16[16,64,128]{2,1,0:T(8,128)(2,1)}, u32[]{:S(2)}, u32[]{:S(2)}) async-start(bf16[16,64,128]{2,1,0:T(8,128)(2,1)} %get-tuple-element.154), calls=%async_computation.2 | async-start | bytes 524288 | tf_op jit(solution)/shard_map/all_to_all | solution.py:744
  163.7 7.3 %collective-permute-done.30.got = bf16[2,200,768]{2,1,0:T(8,128)(2,1)S(1)} collective-permute-done((bf16[2,200,768]{2,1,0:T(8,128)(2,1)}, bf16[2,200,768]{2,1,0:T(8,128)(2,1)S(1)}, u32[]{:S(2)}, u32[]{:S(2)}) %collective-permute-start.30) | collective-permute-done | bytes 614432 | tf_op jit(solution)/shard_map/ppermute | solution.py:51
  175.8 12.4 %backward.1 = (bf16[16,192,128]{2,1,0:T(8,128)(2,1)}, bf16[192,2048]{1,0:T(8,128)(2,1)}) custom-call(s32[5]{0:T(128)} %stack.55.scal, bf16[192,2048]{1,0:T(8,128)(2,1)} %get-tuple-element.150.qkvt, bf16[16,64,128]{2,1,0:T(8,128)(2,1)} %all-to-all-done.2.dcr, f32[64,2048]{1,0:T(8,128)} %get-tuple-element.155.ctxt, f32[1,2048]{1,0:T(1,128)} %get-tuple-element.156.lse), custom_call_target="tpu_custom_call" | custom-call | flops 1 | bytes 1 | tf_op jit(solution)/shard_map/backward/pallas_call | solution.py:83
  188.1 5.3 %all-to-all-start.3 = ((bf16[16,192,128]{2,1,0:T(8,128)(2,1)}), bf16[16,192,128]{2,1,0:T(8,128)(2,1)S(1)}, u32[]{:S(2)}, u32[]{:S(2)}) async-start(bf16[16,192,128]{2,1,0:T(8,128)(2,1)} %get-tuple-element.169), calls=%async_computation.3 | async-start | bytes 1572864 | tf_op jit(solution)/shard_map/all_to_all | solution.py:774
  193.8 5.9 %heads.1 = (f32[16,24,256]{2,1,0:T(8,128)}, bf16[16,24,256]{2,1,0:T(8,128)(2,1)}) custom-call(s32[5]{0:T(128)} %stack.55.scal, bf16[192,2048]{1,0:T(8,128)(2,1)} %get-tuple-element.174.dall, bf16[2048,768]{1,0:T(8,128)(2,1)} %get-tuple-element.180.n1, bf16[2048,768]{1,0:T(8,128)(2,1)} %get-tuple-element.181.n0, bf16[192,768]{1,0:T(8,128)(2,1)} %get-tuple-element.182.wt, ...), custom_call_target="tpu_custom_call" | custom-call | flops 1 | bytes 1 | tf_op jit(solution)/shard_map/heads/pallas_call | solution.py:549
  200.8 3.1 %finish.1 = (f32[96,768]{1,0:T(8,128)}, f32[1,96]{1,0:T(1,128)}, bf16[24,768]{1,0:T(8,128)(2,1)}, f32[4,24,768]{2,1,0:T(8,128)}, bf16[248,768]{1,0:T(8,128)(2,1)...) custom-call(s32[5]{0:T(128)} %stack.55.scal, f32[200,768]{1,0:T(8,128)} %get-tuple-element.147.keep, ...), custom_call_target="tpu_custom_call" | custom-call | flops 1 | bytes 1 | tf_op jit(solution)/shard_map/finish/pallas_call | solution.py:83
  208.1 5.4 %all-to-all-done.3.d_rows = bf16[16,192,128]{2,1,0:T(8,128)(2,1)S(1)} async-done(((bf16[16,192,128]{2,1,0:T(8,128)(2,1)}), bf16[16,192,128]{2,1,0:T(8,128)(2,1)S(1)}, u32[]{:S(2)}, u32[]{:S(2)}) %all-to-all-start.3) | async-done | bytes 786464 | tf_op jit(solution)/shard_map/all_to_all | solution.py:774
  213.6 5.6 %all-to-all-start.4 = ((bf16[16,24,256]{2,1,0:T(8,128)(2,1)}), bf16[16,24,256]{2,1,0:T(8,128)(2,1)S(1)}, u32[]{:S(2)}, u32[]{:S(2)}) async-start(bf16[16,24,256]{2,1,0:T(8,128)(2,1)} %add_convert_fusion), calls=%async_computation.4 | async-start | bytes 393216 | tf_op jit(solution)/shard_map/all_to_all | solution.py:801
  219.2 4.5 %last.1 = f32[128,768]{1,0:T(8,128)} custom-call(s32[5]{0:T(128)} %stack.55.scal, bf16[16,192,128]{2,1,0:T(8,128)(2,1)} %copy-done.2, bf16[4,72,768]{2,1,0:T(8,128)(2,1)} %copy-done.1, bf16[4,72,768]{2,1,0:T(8,128)(2,1)} %copy-done.8, bf16[4,72,768]{2,1,0:T(8,128)(2,1)} %copy-done.10, bf16[4,72,768]{2,1,0:T(8,128)(2,1)} %copy-done.12, ...), custom_call_target="tpu_custom_call" | custom-call | flops 1 | bytes 1 | tf_op jit(solution)/shard_map/last/pallas_call | solution.py:83
  223.7 3.3 %collective-permute-done.34.got_c = bf16[248,768]{1,0:T(8,128)(2,1)} collective-permute-done((bf16[248,768]{1,0:T(8,128)(2,1)}, bf16[248,768]{1,0:T(8,128)(2,1)}, u32[]{:S(2)}, u32[]{:S(2)}) %collective-permute-start.34) | collective-permute-done | bytes 380960 | tf_op jit(solution)/shard_map/ppermute | solution.py:55
  228.8 2.6 %close.1 = (bf16[128,768]{1,0:T(8,128)(2,1)}, f32[24,3072]{1,0:T(8,128)}, f32[24,768]{1,0:T(8,128)}, bf16[24,768]{1,0:T(8,128)(2,1)}, bf16[24,768]{1,0:T(8,128)(2,1)}, /*index=5*/bf16[24,768]{1,0:T(8,128)(2,1)}) custom-call(s32[5]{0:T(128)} %stack.55.scal, bf16[24,768]{1,0:T(8,128)(2,1)} %get-tuple-element.164.own, f32[4,24,768]{2,1,0:T(8,128)} %get-tuple-element.165.wo_own, ...), custom_call_target="tpu_custom_call" | custom-call | flops 1 | bytes 1 | tf_op jit(solution)/shard_map/close/pallas_call | solution.py:83
  231.4 4.2 %collective-permute-start.40 = (bf16[24,768]{1,0:T(8,128)(2,1)}, bf16[24,768]{1,0:T(8,128)(2,1)S(1)}, u32[]{:S(2)}, u32[]{:S(2)}) collective-permute-start(bf16[24,768]{1,0:T(8,128)(2,1)} %get-tuple-element.197), channel_id=1, source_target_pairs={{0,24},{8,16},{16,8},{24,0},{1,25},{9,17},{17,9},{25,1},{2,26},{10... | collective-permute-start | bytes 110600 | tf_op jit(solution)/shard_map/ppermute | solution.py:51
  237.7 2.9 %collective-permute-done.39 = bf16[24,768]{1,0:T(8,128)(2,1)S(1)} collective-permute-done((bf16[24,768]{1,0:T(8,128)(2,1)}, bf16[24,768]{1,0:T(8,128)(2,1)S(1)}, u32[]{:S(2)}, u32[]{:S(2)}) %collective-permute-start.39) | collective-permute-done | bytes 36896 | tf_op jit(solution)/shard_map/ppermute | solution.py:51
  (166 shorter events, 65.5 us)
Async XLA Ops:
  1.6 13.7 %collective-permute-start.5 = (bf16[152,768]{1,0:T(8,128)(2,1)S(1)}, bf16[152,768]{1,0:T(8,128)(2,1)S(1)}, u32[]{:S(2)}, u32[]{:S(2)}) collective-permute-start(bf16[152,768]{1,0:T(8,128)(2,1)S(1)} %pad_maximum_fusion.5.ahead), channel_id=1, source_target_pairs={{0,24},{8,16},{16,8},{24,0},{1,25},{9,17},{17,9},{25,1},{2,26},{10... | collective-permute-start | bytes 700424 | tf_op jit(solution)/shard_map/ppermute | solution.py:51
  6.8 19.9 %collective-permute-start.4 = (bf16[152,768]{1,0:T(8,128)(2,1)S(1)}, bf16[152,768]{1,0:T(8,128)(2,1)S(1)}, u32[]{:S(2)}, u32[]{:S(2)}) collective-permute-start(bf16[152,768]{1,0:T(8,128)(2,1)S(1)} %pad_maximum_fusion.5.ahead), channel_id=1, source_target_pairs={{0,16},{8,24},{16,0},{24,8},{1,17},{9,25},{17,1},{25,9},{2,18},{10... | collective-permute-start | bytes 700424 | tf_op jit(solution)/shard_map/ppermute | solution.py:51
  6.8 19.9 %collective-permute-start.3 = (bf16[152,768]{1,0:T(8,128)(2,1)S(1)}, bf16[152,768]{1,0:T(8,128)(2,1)S(1)}, u32[]{:S(2)}, u32[]{:S(2)}) collective-permute-start(bf16[152,768]{1,0:T(8,128)(2,1)S(1)} %pad_maximum_fusion.5.ahead), channel_id=1, source_target_pairs={{0,8},{8,0},{16,24},{24,16},{1,9},{9,1},{17,25},{25,17},{2,10},{10... | collective-permute-start | bytes 700424 | tf_op jit(solution)/shard_map/ppermute | solution.py:51
  11.2 15.5 %collective-permute-start = (bf16[176,768]{1,0:T(8,128)(2,1)}, bf16[176,768]{1,0:T(8,128)(2,1)S(1)}, u32[]{:S(2)}, u32[]{:S(2)}) collective-permute-start(bf16[176,768]{1,0:T(8,128)(2,1)} %get-tuple-element.111), channel_id=1, source_target_pairs={{0,2},{2,0},{4,6},{6,4},{1,3},{3,1},{5,7},{7,5},{8,10},{10,8},{12,... | collective-permute-start | bytes 811016 | tf_op jit(solution)/shard_map/ppermute | solution.py:55
  12.9 13.9 %collective-permute-start.1 = (bf16[176,768]{1,0:T(8,128)(2,1)}, bf16[176,768]{1,0:T(8,128)(2,1)S(1)}, u32[]{:S(2)}, u32[]{:S(2)}) collective-permute-start(bf16[176,768]{1,0:T(8,128)(2,1)} %get-tuple-element.112), channel_id=1, source_target_pairs={{0,4},{2,6},{4,0},{6,2},{1,5},{3,7},{5,1},{7,3},{8,12},{10,14},{12... | collective-permute-start | bytes 811016 | tf_op jit(solution)/shard_map/ppermute | solution.py:55
  15.3 11.4 %collective-permute-start.2 = (bf16[176,768]{1,0:T(8,128)(2,1)}, bf16[176,768]{1,0:T(8,128)(2,1)}, u32[]{:S(2)}, u32[]{:S(2)}) collective-permute-start(bf16[176,768]{1,0:T(8,128)(2,1)} %get-tuple-element.113), channel_id=1, source_target_pairs={{0,6},{2,4},{4,2},{6,0},{1,7},{3,5},{5,3},{7,1},{8,14},{10,12},{12... | collective-permute-start | bytes 811016 | tf_op jit(solution)/shard_map/ppermute | solution.py:55
  26.8 24.4 %collective-permute-start.6 = (bf16[3,152,768]{2,1,0:T(8,128)(2,1)S(1)}, bf16[3,152,768]{2,1,0:T(8,128)(2,1)S(1)}, u32[]{:S(2)}, u32[]{:S(2)}) collective-permute-start(bf16[3,152,768]{2,1,0:T(8,128)(2,1)S(1)} %pad_maximum_fusion.2.zc), channel_id=1, source_target_pairs={{0,2},{2,0},{1,3},{3,1},{4,6},{6,4},{5,7},{7,5},{8,10},{10,8},{9,1... | collective-permute-start | bytes 2101256 | tf_op jit(solution)/shard_map/ppermute | solution.py:51
  28.3 22.9 %collective-permute-start.7 = (bf16[3,152,768]{2,1,0:T(8,128)(2,1)S(1)}, bf16[3,152,768]{2,1,0:T(8,128)(2,1)S(1)}, u32[]{:S(2)}, u32[]{:S(2)}) collective-permute-start(bf16[3,152,768]{2,1,0:T(8,128)(2,1)S(1)} %pad_maximum_fusion.2.zc), channel_id=1, source_target_pairs={{0,4},{4,0},{1,5},{5,1},{2,6},{6,2},{3,7},{7,3},{8,12},{12,8},{9,1... | collective-permute-start | bytes 2101256 | tf_op jit(solution)/shard_map/ppermute | solution.py:51
  29.8 21.3 %collective-permute-start.8 = (bf16[72,768]{1,0:T(8,128)(2,1)S(1)}, bf16[72,768]{1,0:T(8,128)(2,1)}, u32[]{:S(2)}, u32[]{:S(2)}) collective-permute-start(bf16[72,768]{1,0:T(8,128)(2,1)S(1)} %pad_maximum_fusion.6), channel_id=1, source_target_pairs={{0,8},{8,0},{16,24},{24,16},{1,9},{9,1},{17,25},{25,17},{2,10},{10... | collective-permute-start | bytes 331784 | tf_op jit(solution)/shard_map/ppermute | solution.py:51
  34.0 17.2 %collective-permute-start.9 = (bf16[72,768]{1,0:T(8,128)(2,1)S(1)}, bf16[72,768]{1,0:T(8,128)(2,1)}, u32[]{:S(2)}, u32[]{:S(2)}) collective-permute-start(bf16[72,768]{1,0:T(8,128)(2,1)S(1)} %pad_maximum_fusion.6), channel_id=1, source_target_pairs={{0,16},{8,24},{16,0},{24,8},{1,17},{9,25},{17,1},{25,9},{2,18},{10... | collective-permute-start | bytes 331784 | tf_op jit(solution)/shard_map/ppermute | solution.py:51
  35.6 15.5 %collective-permute-start.10 = (bf16[72,768]{1,0:T(8,128)(2,1)S(1)}, bf16[72,768]{1,0:T(8,128)(2,1)}, u32[]{:S(2)}, u32[]{:S(2)}) collective-permute-start(bf16[72,768]{1,0:T(8,128)(2,1)S(1)} %pad_maximum_fusion.6), channel_id=1, source_target_pairs={{0,24},{8,16},{16,8},{24,0},{1,25},{9,17},{17,9},{25,1},{2,26},{10... | collective-permute-start | bytes 331784 | tf_op jit(solution)/shard_map/ppermute | solution.py:51
  37.1 11.8 %all-to-all-start = ((bf16[16,24,256]{2,1,0:T(8,128)(2,1)}), bf16[16,24,256]{2,1,0:T(8,128)(2,1)S(1)}, u32[]{:S(2)}, u32[]{:S(2)}) async-start(bf16[16,24,256]{2,1,0:T(8,128)(2,1)} %get-tuple-element.116), calls=%async_computation | async-start | bytes 393216 | tf_op jit(solution)/shard_map/all_to_all | solution.py:642
  51.2 16.9 %collective-permute-start.16 = (bf16[200,768]{1,0:T(8,128)(2,1)S(1)}, bf16[200,768]{1,0:T(8,128)(2,1)S(1)}, u32[]{:S(2)}, u32[]{:S(2)}) collective-permute-start(bf16[200,768]{1,0:T(8,128)(2,1)S(1)} %constant_dynamic-update-slice_fusion), channel_id=1, source_target_pairs={{0,16},{8,24},{16,0},{24,8},{1,17},{9,25},{17,1},{25,9},{2,18},{10... | collective-permute-start | bytes 921608 | tf_op jit(solution)/shard_map/ppermute | solution.py:51
  52.4 17.0 %collective-permute-start.11 = (bf16[2,152,768]{2,1,0:T(8,128)(2,1)S(1)}, bf16[2,152,768]{2,1,0:T(8,128)(2,1)}, u32[]{:S(2)}, u32[]{:S(2)}) collective-permute-start(bf16[2,152,768]{2,1,0:T(8,128)(2,1)S(1)} %slice.15), channel_id=1, source_target_pairs={{0,4},{4,0},{1,5},{5,1},{2,6},{6,2},{3,7},{7,3},{8,12},{12,8},{9,1... | collective-permute-start | bytes 1400840 | tf_op jit(solution)/shard_map/ppermute | solution.py:51
  53.6 15.7 %collective-permute-start.12 = (bf16[1,152,768]{2,1,0:T(8,128)(2,1)S(1)}, bf16[1,152,768]{2,1,0:T(8,128)(2,1)S(1)}, u32[]{:S(2)}, u32[]{:S(2)}) collective-permute-start(bf16[1,152,768]{2,1,0:T(8,128)(2,1)S(1)} %slice.16), channel_id=1, source_target_pairs={{0,2},{2,0},{1,3},{3,1},{4,6},{6,4},{5,7},{7,5},{8,10},{10,8},{9,1... | collective-permute-start | bytes 700424 | tf_op jit(solution)/shard_map/ppermute | solution.py:51
  68.2 23.4 %collective-permute-start.17 = (bf16[2,200,768]{2,1,0:T(8,128)(2,1)S(1)}, bf16[2,200,768]{2,1,0:T(8,128)(2,1)S(1)}, u32[]{:S(2)}, u32[]{:S(2)}) collective-permute-start(bf16[2,200,768]{2,1,0:T(8,128)(2,1)S(1)} %pad_maximum_fusion.3), channel_id=1, source_target_pairs={{0,8},{8,0},{16,24},{24,16},{1,9},{9,1},{17,25},{25,17},{2,10},{10... | collective-permute-start | bytes 1843208 | tf_op jit(solution)/shard_map/ppermute | solution.py:51
  69.3 18.6 %collective-permute-start.13 = (bf16[4,72,768]{2,1,0:T(8,128)(2,1)S(1)}, bf16[4,72,768]{2,1,0:T(8,128)(2,1)S(1)}, u32[]{:S(2)}, u32[]{:S(2)}) collective-permute-start(bf16[4,72,768]{2,1,0:T(8,128)(2,1)S(1)} %pad_maximum_fusion.4.wq_a), channel_id=1, source_target_pairs={{0,2},{2,0},{4,6},{6,4},{1,3},{3,1},{5,7},{7,5},{8,10},{10,8},{12,... | collective-permute-start | bytes 1327112 | tf_op jit(solution)/shard_map/ppermute | solution.py:55
  70.2 21.3 %collective-permute-start.14 = (bf16[4,72,768]{2,1,0:T(8,128)(2,1)S(1)}, bf16[4,72,768]{2,1,0:T(8,128)(2,1)S(1)}, u32[]{:S(2)}, u32[]{:S(2)}) collective-permute-start(bf16[4,72,768]{2,1,0:T(8,128)(2,1)S(1)} %pad_maximum_fusion.4.wq_a), channel_id=1, source_target_pairs={{0,4},{2,6},{4,0},{6,2},{1,5},{3,7},{5,1},{7,3},{8,12},{10,14},{12... | collective-permute-start | bytes 1327112 | tf_op jit(solution)/shard_map/ppermute | solution.py:55
  70.8 20.7 %collective-permute-start.15 = (bf16[4,72,768]{2,1,0:T(8,128)(2,1)S(1)}, bf16[4,72,768]{2,1,0:T(8,128)(2,1)S(1)}, u32[]{:S(2)}, u32[]{:S(2)}) collective-permute-start(bf16[4,72,768]{2,1,0:T(8,128)(2,1)S(1)} %pad_maximum_fusion.4.wq_a), channel_id=1, source_target_pairs={{0,6},{2,4},{4,2},{6,0},{1,7},{3,5},{5,3},{7,1},{8,14},{10,12},{12... | collective-permute-start | bytes 1327112 | tf_op jit(solution)/shard_map/ppermute | solution.py:55
  92.5 34.4 %collective-permute-start.25 = (bf16[4,200,768]{2,1,0:T(8,128)(2,1)S(1)}, bf16[4,200,768]{2,1,0:T(8,128)(2,1)}, u32[]{:S(2)}, u32[]{:S(2)}) collective-permute-start(bf16[4,200,768]{2,1,0:T(8,128)(2,1)S(1)} %pad_maximum_fusion.1.ffz), channel_id=1, source_target_pairs={{0,1},{1,0},{2,3},{3,2},{4,5},{5,4},{6,7},{7,6},{8,9},{9,8},{10,11... | collective-permute-start | bytes 3686408 | tf_op jit(solution)/shard_map/ppermute | solution.py:51
  92.6 19.2 %collective-permute-start.21 = (bf16[16,24,768]{2,1,0:T(8,128)(2,1)S(1)}, bf16[16,24,768]{2,1,0:T(8,128)(2,1)S(1)}, u32[]{:S(2)}, u32[]{:S(2)}) collective-permute-start(bf16[16,24,768]{2,1,0:T(8,128)(2,1)S(1)} %copy-done.4), channel_id=1, source_target_pairs={{0,1},{1,0},{2,3},{3,2},{4,5},{5,4},{6,7},{7,6},{8,9},{9,8},{10,11... | collective-permute-start | bytes 1769480 | tf_op jit(solution)/shard_map/ppermute | solution.py:51
  93.1 18.6 %all-to-all-start.1 = ((bf16[16,64,128]{2,1,0:T(8,128)(2,1)}), bf16[16,64,128]{2,1,0:T(8,128)(2,1)S(1)}, u32[]{:S(2)}, u32[]{:S(2)}) async-start(bf16[16,64,128]{2,1,0:T(8,128)(2,1)} %get-tuple-element.128), calls=%async_computation.1 | async-start | bytes 524288 | tf_op jit(solution)/shard_map/all_to_all | solution.py:686
  136.3 11.9 %collective-permute-start.26 = (bf16[4,200,768]{2,1,0:T(8,128)(2,1)}, bf16[4,200,768]{2,1,0:T(8,128)(2,1)S(1)}, u32[]{:S(2)}, u32[]{:S(2)}) collective-permute-start(bf16[4,200,768]{2,1,0:T(8,128)(2,1)} %get-tuple-element.140), channel_id=1, source_target_pairs={{0,1},{1,0},{2,3},{3,2},{4,5},{5,4},{6,7},{7,6},{8,9},{9,8},{10,11... | collective-permute-start | bytes 3686408 | tf_op jit(solution)/shard_map/ppermute | solution.py:51
  152.6 18.4 %collective-permute-start.30 = (bf16[2,200,768]{2,1,0:T(8,128)(2,1)}, bf16[2,200,768]{2,1,0:T(8,128)(2,1)S(1)}, u32[]{:S(2)}, u32[]{:S(2)}) collective-permute-start(bf16[2,200,768]{2,1,0:T(8,128)(2,1)} %get-tuple-element.146), channel_id=1, source_target_pairs={{0,8},{8,0},{16,24},{24,16},{1,9},{9,1},{17,25},{25,17},{2,10},{10... | collective-permute-start | bytes 1843208 | tf_op jit(solution)/shard_map/ppermute | solution.py:51
  158.8 17.0 %all-to-all-start.2 = ((bf16[16,64,128]{2,1,0:T(8,128)(2,1)}), bf16[16,64,128]{2,1,0:T(8,128)(2,1)}, u32[]{:S(2)}, u32[]{:S(2)}) async-start(bf16[16,64,128]{2,1,0:T(8,128)(2,1)} %get-tuple-element.154), calls=%async_computation.2 | async-start | bytes 524288 | tf_op jit(solution)/shard_map/all_to_all | solution.py:744
  174.3 13.8 %collective-permute-start.31 = (bf16[200,768]{1,0:T(8,128)(2,1)}, bf16[200,768]{1,0:T(8,128)(2,1)}, u32[]{:S(2)}, u32[]{:S(2)}) collective-permute-start(bf16[200,768]{1,0:T(8,128)(2,1)} %get-tuple-element.148), channel_id=1, source_target_pairs={{0,16},{8,24},{16,0},{24,8},{1,17},{9,25},{17,1},{25,9},{2,18},{10... | collective-permute-start | bytes 921608 | tf_op jit(solution)/shard_map/ppermute | solution.py:51
  188.1 31.1 %collective-permute-start.36 = (bf16[16,72,768]{2,1,0:T(8,128)(2,1)S(1)}, bf16[16,72,768]{2,1,0:T(8,128)(2,1)}, u32[]{:S(2)}, u32[]{:S(2)}) collective-permute-start(bf16[16,72,768]{2,1,0:T(8,128)(2,1)S(1)} %pad_maximum_fusion), channel_id=1, source_target_pairs={{0,1},{1,0},{2,3},{3,2},{4,5},{5,4},{6,7},{7,6},{8,9},{9,8},{10,11... | collective-permute-start | bytes 5308424 | tf_op jit(solution)/shard_map/ppermute | solution.py:51
  188.1 25.4 %all-to-all-start.3 = ((bf16[16,192,128]{2,1,0:T(8,128)(2,1)}), bf16[16,192,128]{2,1,0:T(8,128)(2,1)S(1)}, u32[]{:S(2)}, u32[]{:S(2)}) async-start(bf16[16,192,128]{2,1,0:T(8,128)(2,1)} %get-tuple-element.169), calls=%async_computation.3 | async-start | bytes 1572864 | tf_op jit(solution)/shard_map/all_to_all | solution.py:774
  203.9 19.8 %collective-permute-start.33 = (bf16[248,768]{1,0:T(8,128)(2,1)}, bf16[248,768]{1,0:T(8,128)(2,1)S(1)}, u32[]{:S(2)}, u32[]{:S(2)}) collective-permute-start(bf16[248,768]{1,0:T(8,128)(2,1)} %get-tuple-element.166), channel_id=1, source_target_pairs={{0,2},{2,0},{4,6},{6,4},{1,3},{3,1},{5,7},{7,5},{8,10},{10,8},{12,... | collective-permute-start | bytes 1142792 | tf_op jit(solution)/shard_map/ppermute | solution.py:55
  205.8 21.2 %collective-permute-start.34 = (bf16[248,768]{1,0:T(8,128)(2,1)}, bf16[248,768]{1,0:T(8,128)(2,1)}, u32[]{:S(2)}, u32[]{:S(2)}) collective-permute-start(bf16[248,768]{1,0:T(8,128)(2,1)} %get-tuple-element.167), channel_id=1, source_target_pairs={{0,4},{2,6},{4,0},{6,2},{1,5},{3,7},{5,1},{7,3},{8,12},{10,14},{12... | collective-permute-start | bytes 1142792 | tf_op jit(solution)/shard_map/ppermute | solution.py:55
  207.3 21.5 %collective-permute-start.35 = (bf16[248,768]{1,0:T(8,128)(2,1)}, bf16[248,768]{1,0:T(8,128)(2,1)}, u32[]{:S(2)}, u32[]{:S(2)}) collective-permute-start(bf16[248,768]{1,0:T(8,128)(2,1)} %get-tuple-element.168), channel_id=1, source_target_pairs={{0,6},{2,4},{4,2},{6,0},{1,7},{3,5},{5,3},{7,1},{8,14},{10,12},{12... | collective-permute-start | bytes 1142792 | tf_op jit(solution)/shard_map/ppermute | solution.py:55
  213.6 28.6 %all-to-all-start.4 = ((bf16[16,24,256]{2,1,0:T(8,128)(2,1)}), bf16[16,24,256]{2,1,0:T(8,128)(2,1)S(1)}, u32[]{:S(2)}, u32[]{:S(2)}) async-start(bf16[16,24,256]{2,1,0:T(8,128)(2,1)} %add_convert_fusion), calls=%async_computation.4 | async-start | bytes 393216 | tf_op jit(solution)/shard_map/all_to_all | solution.py:801
  (51 other events, 712.7 us)
